TPU v7x, 32 devices: a whole 2x2x4 slice. The times are simulated.
32 devices in a mesh: dp: 16 (over z, y, x), fsdp: 2 (over core).
Axes of the slice: x: 2, y: 2, z: 4, core: 2. Of those that a mesh axis runs over, the one named last changes fastest.
Arguments:
- hidden_in: bfloat16 [16, 1024, 1536], P('dp', 'fsdp'), may hold values from -6 to 6
- text_state: bfloat16 [16, 256, 4096], P('dp', 'fsdp'), may hold values from -6 to 6
- caption_lengths: int32 [16], P('dp'), may hold values from 8 to 256, as said below
- timesteps: int32 [16], P('dp'), may hold values from 0 to 999
- patch_positions: int32 [16, 2, 1024], P('dp', None, 'fsdp'), may hold values from 0 to 127, as said below
- cotangent: bfloat16 [16, 1024, 1536], P('dp', 'fsdp'), may hold values from -6 to 6
- w_ada: bfloat16 [1024, 4, 1536], P('fsdp'), may hold values from -0.1875 to 0.1875
- w_text: bfloat16 [4096, 2, 1536], P('fsdp'), may hold values from -0.09375 to 0.09375
- w_qkv: bfloat16 [1536, 3, 1536], P('fsdp'), may hold values from -0.15625 to 0.15625
- w_out: bfloat16 [1536, 1536], P('fsdp'), may hold values from -3.5 to 3.5
- gains: bfloat16 [5, 1536], P(None, 'fsdp'), may hold values from 0.5 to 1.5
- cross_gate: bfloat16 [24], P('fsdp'), may hold values from 0.25 to 0.75
- w_gate_up: bfloat16 [1536, 2, 4096], P(None, None, 'fsdp'), may hold values from -0.15625 to 0.15625
- w_down: bfloat16 [4096, 1536], P('fsdp'), may hold values from -0.1875 to 0.1875
Outputs:
- output: bfloat16 [16, 1024, 1536], P('dp', 'fsdp')
- grad_input: bfloat16 [16, 1024, 1536], P('dp', 'fsdp')
- grad_text: bfloat16 [16, 256, 4096], P('dp', 'fsdp')
- grad_ada: float32 [1024, 4, 1536], P('fsdp', None, 'dp')
- grad_text_proj: float32 [4096, 2, 1536], P('fsdp', None, 'dp')
- grad_qkv: float32 [1536, 3, 1536], P('fsdp', None, 'dp')
- grad_out: float32 [1536, 1536], P('fsdp', 'dp')
- grad_gains: float32 [5, 1536], P(None, 'fsdp')
- grad_cross_gate: float32 [24], P('fsdp')
- grad_gate_up: float32 [1536, 2, 4096], P('dp', None, 'fsdp')
- grad_down: float32 [4096, 1536], P('fsdp', 'dp')
Inputs may be any that keep to these rules, and one draw needn't show every extreme that they name: `caption_lengths`: each image's caption has at least 8 tokens; in every draw one image's caption fills all 256 slots and another's has exactly 8. `patch_positions`: each image's patches lie row by row on a grid whose width w is 8, 16 or 32: patch p sits at row p // w and column p % w. In every draw some image has width 8 and another width 32.
All inputs are finite; a program needn't handle non-finite values.
Results may differ from a plain program's by a relative error of at most 0.023.
Values may be sent and summed in bfloat16 or wider, within the bound.
A program may use at most 576 MiB of HBM per device.

v0:
```python
import math

import jax
import jax.numpy as jnp
from jax import lax
from jax.sharding import PartitionSpec as P

D = 1536
HEADS = 24
HD = 64
TW = 4096
TE = 1024
PATCHES = 1024
TEXT = 256


EPSILON = 1e-06
PRECISE = lax.Precision.HIGHEST


def time_embed(timesteps):
    half_width = TE // 2
    frequencies = jnp.exp(
        -math.log(10000.0) * jnp.arange(half_width, dtype=jnp.float32) / half_width
    )
    angles = timesteps.astype(jnp.float32)[..., None] * frequencies
    return jnp.concatenate([jnp.cos(angles), jnp.sin(angles)], axis=-1)


def rope_tables(positions):
    quarter = HD // 4
    frequencies = 10000.0 ** (-jnp.arange(quarter, dtype=jnp.float32) / quarter)
    angles = jnp.swapaxes(positions.astype(jnp.float32), -1, -2)[..., None] * frequencies
    return (jnp.cos(angles), jnp.sin(angles))


def rotate(values, cosine_rows, sine_rows):
    lead_shape = values.shape[:-1]
    quarters = values.reshape(lead_shape + (HEADS, 2, 2, HD // 4))
    first_half = quarters[..., 0, :]
    second_half = quarters[..., 1, :]
    cosine_b = cosine_rows[..., None, :, :]
    sine_b = sine_rows[..., None, :, :]
    turned = jnp.stack(
        [
            first_half * cosine_b - second_half * sine_b,
            second_half * cosine_b + first_half * sine_b,
        ],
        axis=-2,
    )
    return turned.reshape(values.shape)


def inverse_rms(values):
    return lax.rsqrt(jnp.mean(values * values, axis=-1, keepdims=True) + EPSILON)


def rms_back(grad_hat, normed, inverse):
    return inverse * (grad_hat - normed * jnp.mean(grad_hat * normed, axis=-1, keepdims=True))


def matmul(left_op, right_op):
    flat_rows = jnp.dot(
        left_op.reshape(-1, left_op.shape[-1]), right_op, preferred_element_type=jnp.float32
    )
    return flat_rows.reshape(left_op.shape[:-1] + (right_op.shape[-1],))


def matmul_t(left_op, right_op):
    flat_rows = lax.dot_general(
        left_op.reshape(-1, left_op.shape[-1]),
        right_op,
        (((1,), (1,)), ((), ())),
        preferred_element_type=jnp.float32,
    )
    return flat_rows.reshape(left_op.shape[:-1] + (right_op.shape[0],))


def outer_sum(left_op, right_op):
    return lax.dot_general(
        left_op.reshape(-1, left_op.shape[-1]),
        right_op.reshape(-1, right_op.shape[-1]),
        (((0,), (0,)), ((), ())),
        preferred_element_type=jnp.float32,
    )


def own_columns(values, width):
    return lax.dynamic_slice_in_dim(values, lax.axis_index("fsdp") * width, width, values.ndim - 1)


def head_split(values):
    return values.reshape(values.shape[:-1] + (HEADS, HD))


def attn_scores(queries_b, keys_b, valid_keys):
    scores = jnp.einsum(
        "iqhd,ikhd->ihqk",
        head_split(queries_b),
        head_split(keys_b),
        preferred_element_type=jnp.float32,
    ) * HD ** (-0.5)
    if valid_keys is not None:
        scores = jnp.where(valid_keys[:, None, None, :], scores, -1e30)
    return scores


def attn_forward(queries_b, keys_b, values_b, valid_keys):
    scores = attn_scores(queries_b, keys_b, valid_keys)
    row_peak = jnp.max(scores, axis=-1, keepdims=True)
    exp_scores = jnp.exp(scores - row_peak)
    row_total = jnp.sum(exp_scores, axis=-1, keepdims=True)
    probs_low = (exp_scores / row_total).astype(jnp.bfloat16)
    context = jnp.einsum(
        "ihqk,ikhd->iqhd", probs_low, head_split(values_b), preferred_element_type=jnp.float32
    )
    return (context.reshape(queries_b.shape), row_peak + jnp.log(row_total))


def attn_backward(queries_b, keys_b, values_b, valid_keys, log_total, grad_b):
    scores = attn_scores(queries_b, keys_b, valid_keys)
    attn_probs = jnp.exp(scores - log_total)
    probs_low = attn_probs.astype(jnp.bfloat16)
    grad_heads = head_split(grad_b)
    grad_probs = jnp.einsum(
        "iqhd,ikhd->ihqk", grad_heads, head_split(values_b), preferred_element_type=jnp.float32
    )
    row_delta = jnp.sum(attn_probs * grad_probs, axis=-1, keepdims=True)
    grad_scores = (attn_probs * (grad_probs - row_delta)).astype(jnp.bfloat16)
    score_scale = HD ** (-0.5)
    grad_queries = (
        jnp.einsum(
            "ihqk,ikhd->iqhd", grad_scores, head_split(keys_b), preferred_element_type=jnp.float32
        )
        * score_scale
    )
    grad_keys = (
        jnp.einsum(
            "ihqk,iqhd->ikhd",
            grad_scores,
            head_split(queries_b),
            preferred_element_type=jnp.float32,
        )
        * score_scale
    )
    grad_values = jnp.einsum(
        "ihqk,iqhd->ikhd", probs_low, grad_heads, preferred_element_type=jnp.float32
    )
    return (
        grad_queries.reshape(queries_b.shape),
        grad_keys.reshape(keys_b.shape),
        grad_values.reshape(values_b.shape),
    )


def swiglu_back(gate_pre, up_pre, grad_hidden):
    sigmoid_gate = jax.nn.sigmoid(gate_pre)
    grad_gate = (
        grad_hidden * up_pre * (sigmoid_gate + gate_pre * sigmoid_gate * (1.0 - sigmoid_gate))
    )
    grad_up = grad_hidden * gate_pre * sigmoid_gate
    return (grad_gate.astype(jnp.bfloat16), grad_up.astype(jnp.bfloat16))


def attn_weights(w_text, w_qkv, w_out, gains, cross_gate):
    return (
        lax.all_gather(w_text, "fsdp", axis=0, tiled=True),
        lax.all_gather(w_qkv, "fsdp", axis=0, tiled=True),
        lax.all_gather(w_out, "fsdp", axis=0, tiled=True),
        lax.all_gather(gains, "fsdp", axis=1, tiled=True),
        lax.all_gather(cross_gate, "fsdp", axis=0, tiled=True),
    )


def group_rows(values):
    return lax.all_gather(values, "fsdp", axis=1, tiled=True)


def group_sums(values):
    return lax.psum_scatter(
        values.astype(jnp.bfloat16), "fsdp", scatter_dimension=1, tiled=True
    ).astype(jnp.float32)


def on_device(
    hidden_in,
    text_state,
    caption_lengths,
    timesteps,
    patch_positions,
    cotangent,
    w_ada,
    w_text,
    w_qkv,
    w_out,
    gains,
    cross_gate,
    w_gate_up,
    w_down,
):
    images = hidden_in.shape[0]
    patch_dev = hidden_in.shape[1]
    time_low = jax.nn.silu(time_embed(timesteps)).astype(jnp.bfloat16)
    ada_full = lax.all_gather(w_ada, "fsdp", axis=0, tiled=True)
    modulation = matmul(time_low, ada_full.reshape(TE, 4 * D)).reshape(images, 4, D)
    scale_attn = modulation[:, 0][:, None]
    gate_attn = jnp.tanh(modulation[:, 1])[:, None]
    scale_ffn = modulation[:, 2][:, None]
    gate_ffn = jnp.tanh(modulation[:, 3])[:, None]
    text_full, qkv_full, out_full, gains_full, gate_full = attn_weights(
        w_text, w_qkv, w_out, gains, cross_gate
    )
    gain_rows = gains_full.astype(jnp.float32)
    head_gates = jnp.repeat(jnp.tanh(gate_full.astype(jnp.float32)), HD)
    cosine_rows, sine_rows = rope_tables(patch_positions)
    inputs_f = hidden_in.astype(jnp.float32)
    inverse_one = inverse_rms(inputs_f)
    normed_one = inputs_f * inverse_one
    first_norm = (normed_one * gain_rows[0] * (1.0 + scale_attn)).astype(jnp.bfloat16)
    projected = matmul(first_norm, qkv_full.reshape(D, 3 * D)).reshape(images, patch_dev, 3, D)
    query_pre = projected[:, :, 0]
    key_pre = projected[:, :, 1]
    inverse_q = inverse_rms(query_pre)
    normed_q = query_pre * inverse_q
    inverse_k = inverse_rms(key_pre)
    normed_k = key_pre * inverse_k
    queries_b = rotate(normed_q * gain_rows[2], cosine_rows, sine_rows).astype(jnp.bfloat16)
    keys_b = rotate(normed_k * gain_rows[3], cosine_rows, sine_rows).astype(jnp.bfloat16)
    values_b = projected[:, :, 2].astype(jnp.bfloat16)
    text_proj = matmul(text_state, text_full.reshape(TW, 2 * D)).reshape(
        images, text_state.shape[1], 2, D
    )
    inverse_t = inverse_rms(text_proj[:, :, 0])
    normed_t = text_proj[:, :, 0] * inverse_t
    text_keys_b = (normed_t * gain_rows[4]).astype(jnp.bfloat16)
    text_values_b = text_proj[:, :, 1].astype(jnp.bfloat16)
    keys_all, values_all, text_keys_all, text_values_all = (
        lax.all_gather(keys_b, "fsdp", axis=1, tiled=True),
        lax.all_gather(values_b, "fsdp", axis=1, tiled=True),
        lax.all_gather(text_keys_b, "fsdp", axis=1, tiled=True),
        lax.all_gather(text_values_b, "fsdp", axis=1, tiled=True),
    )
    valid_text = jnp.arange(TEXT)[None, :] < caption_lengths[:, None]
    self_out, self_lse = attn_forward(queries_b, keys_all, values_all, None)
    cross_out, cross_lse = attn_forward(queries_b, text_keys_all, text_values_all, valid_text)
    mixed_b = (self_out + head_gates * cross_out).astype(jnp.bfloat16)
    attn_branch = matmul(mixed_b, out_full)
    after_attn = inputs_f + gate_attn * attn_branch
    inverse_two = inverse_rms(after_attn)
    normed_two = after_attn * inverse_two
    second_norm = (normed_two * gain_rows[1] * (1.0 + scale_ffn)).astype(jnp.bfloat16)
    ffn_local = w_gate_up.shape[2]
    second_all = group_rows(second_norm)
    pair_pre = matmul(second_all, w_gate_up.reshape(D, 2 * ffn_local)).reshape(
        images, PATCHES, 2, ffn_local
    )
    gate_pre = pair_pre[:, :, 0]
    up_pre = pair_pre[:, :, 1]
    hidden_b = (jax.nn.silu(gate_pre) * up_pre).astype(jnp.bfloat16)
    ffn_branch = group_sums(matmul(hidden_b, w_down))
    output = (after_attn + gate_ffn * ffn_branch).astype(jnp.bfloat16)
    grad_out = cotangent.astype(jnp.float32)
    grad_gate_ffn = jnp.sum(grad_out * ffn_branch, axis=1) * (1.0 - gate_ffn[:, 0] * gate_ffn[:, 0])
    grad_branch_b = (gate_ffn * grad_out).astype(jnp.bfloat16)
    grad_branch_all = group_rows(grad_branch_b)
    grad_hidden = matmul_t(grad_branch_all, w_down)
    grad_gate_b, grad_up_b = swiglu_back(gate_pre, up_pre, grad_hidden)
    grad_pair = jnp.concatenate([grad_gate_b, grad_up_b], axis=-1)
    grad_down_s = outer_sum(hidden_b, grad_branch_all)
    grad_gate_up_s = outer_sum(second_all, grad_pair).reshape(D, 2, ffn_local)
    grad_second = group_sums(matmul_t(grad_pair, w_gate_up.reshape(D, 2 * ffn_local)))
    gate_up_grad, down_grad = (
        lax.psum_scatter(
            grad_gate_up_s.astype(jnp.bfloat16), "dp", scatter_dimension=0, tiled=True
        ).astype(jnp.float32),
        lax.psum_scatter(
            grad_down_s.astype(jnp.bfloat16), "dp", scatter_dimension=1, tiled=True
        ).astype(jnp.float32),
    )
    text_back, qkv_back, out_back, gains_back, gate_back = attn_weights(
        w_text, w_qkv, w_out, gains, cross_gate
    )
    gain_back_rows = gains_back.astype(jnp.float32)
    head_tanh = jnp.tanh(gate_back.astype(jnp.float32))
    head_gates_back = jnp.repeat(head_tanh, HD)
    grad_scale_ffn = jnp.sum(grad_second * normed_two * gain_back_rows[1], axis=1)
    grad_gain_two = jnp.sum(grad_second * normed_two * (1.0 + scale_ffn), axis=(0, 1))
    grad_after = grad_out + rms_back(
        grad_second * gain_back_rows[1] * (1.0 + scale_ffn), normed_two, inverse_two
    )
    grad_gate_attn = jnp.sum(grad_after * attn_branch, axis=1) * (
        1.0 - gate_attn[:, 0] * gate_attn[:, 0]
    )
    grad_attn_b = (gate_attn * grad_after).astype(jnp.bfloat16)
    grad_mixed = matmul_t(grad_attn_b, out_back)
    grad_head_gates = jnp.sum(
        (grad_mixed * cross_out).reshape(images, patch_dev, HEADS, HD), axis=(0, 1, 3)
    ) * (1.0 - head_tanh * head_tanh)
    grad_self_b = grad_mixed.astype(jnp.bfloat16)
    grad_cross_b = (grad_mixed * head_gates_back).astype(jnp.bfloat16)
    grad_q_self, grad_k_part, grad_v_part = attn_backward(
        queries_b, keys_all, values_all, None, self_lse, grad_self_b
    )
    grad_q_cross, grad_tk_part, grad_tv_part = attn_backward(
        queries_b, text_keys_all, text_values_all, valid_text, cross_lse, grad_cross_b
    )
    grad_keys, grad_values, grad_text_keys, grad_text_values = (
        lax.psum_scatter(
            grad_k_part.astype(jnp.bfloat16), "fsdp", scatter_dimension=1, tiled=True
        ).astype(jnp.float32),
        lax.psum_scatter(
            grad_v_part.astype(jnp.bfloat16), "fsdp", scatter_dimension=1, tiled=True
        ).astype(jnp.float32),
        lax.psum_scatter(
            grad_tk_part.astype(jnp.bfloat16), "fsdp", scatter_dimension=1, tiled=True
        ).astype(jnp.float32),
        lax.psum_scatter(
            grad_tv_part.astype(jnp.bfloat16), "fsdp", scatter_dimension=1, tiled=True
        ).astype(jnp.float32),
    )
    grad_queries_r = rotate(grad_q_self + grad_q_cross, cosine_rows, -sine_rows)
    grad_gain_query = jnp.sum(grad_queries_r * normed_q, axis=(0, 1))
    grad_query_pre = rms_back(grad_queries_r * gain_back_rows[2], normed_q, inverse_q).astype(
        jnp.bfloat16
    )
    grad_keys_r = rotate(grad_keys, cosine_rows, -sine_rows)
    grad_gain_key = jnp.sum(grad_keys_r * normed_k, axis=(0, 1))
    grad_key_pre = rms_back(grad_keys_r * gain_back_rows[3], normed_k, inverse_k).astype(
        jnp.bfloat16
    )
    grad_value_pre = grad_values.astype(jnp.bfloat16)
    grad_gain_text = jnp.sum(grad_text_keys * normed_t, axis=(0, 1))
    grad_text_key_pre = rms_back(grad_text_keys * gain_back_rows[4], normed_t, inverse_t).astype(
        jnp.bfloat16
    )
    grad_text_value_pre = grad_text_values.astype(jnp.bfloat16)
    grad_qkv_pre = jnp.concatenate([grad_query_pre, grad_key_pre, grad_value_pre], axis=-1)
    grad_first = matmul_t(grad_qkv_pre, qkv_back.reshape(D, 3 * D))
    grad_text_pair = jnp.concatenate([grad_text_key_pre, grad_text_value_pre], axis=-1)
    grad_text_in = matmul_t(grad_text_pair, text_back.reshape(TW, 2 * D)).astype(jnp.bfloat16)
    grad_scale_attn = jnp.sum(grad_first * normed_one * gain_back_rows[0], axis=1)
    grad_gain_one = jnp.sum(grad_first * normed_one * (1.0 + scale_attn), axis=(0, 1))
    grad_input = (
        grad_after
        + rms_back(grad_first * gain_back_rows[0] * (1.0 + scale_attn), normed_one, inverse_one)
    ).astype(jnp.bfloat16)
    grad_modulation = jnp.stack(
        [grad_scale_attn, grad_gate_attn, grad_scale_ffn, grad_gate_ffn], axis=1
    )
    grad_gain_rows = jnp.stack(
        [grad_gain_one, grad_gain_two, grad_gain_query, grad_gain_key, grad_gain_text]
    )
    width_shard = D // lax.axis_size("fsdp")
    first_all, qkv_pre_all, mixed_all, attn_grad_all, text_all, text_pair_all = (
        lax.all_gather(first_norm, "fsdp", axis=1, tiled=True),
        lax.all_gather(grad_qkv_pre, "fsdp", axis=1, tiled=True),
        lax.all_gather(mixed_b, "fsdp", axis=1, tiled=True),
        lax.all_gather(grad_attn_b, "fsdp", axis=1, tiled=True),
        lax.all_gather(text_state, "fsdp", axis=1, tiled=True),
        lax.all_gather(grad_text_pair, "fsdp", axis=1, tiled=True),
    )
    mod_parts, gain_parts, gate_parts = (
        lax.all_gather(
            grad_modulation[:, None].astype(jnp.bfloat16), "fsdp", axis=1, tiled=True
        ).astype(jnp.float32),
        lax.all_gather(
            grad_gain_rows[:, None].astype(jnp.bfloat16), "fsdp", axis=1, tiled=True
        ).astype(jnp.float32),
        lax.all_gather(
            grad_head_gates[:, None].astype(jnp.bfloat16), "fsdp", axis=1, tiled=True
        ).astype(jnp.float32),
    )
    qkv_s = outer_sum(own_columns(first_all, width_shard), qkv_pre_all).reshape(width_shard, 3, D)
    out_s = outer_sum(own_columns(mixed_all, width_shard), attn_grad_all)
    text_shard = TW // lax.axis_size("fsdp")
    text_s = outer_sum(own_columns(text_all, text_shard), text_pair_all).reshape(text_shard, 2, D)
    mod_total = jnp.sum(mod_parts, axis=1)
    time_shard = own_columns(time_low.astype(jnp.float32), TE // lax.axis_size("fsdp"))
    ada_s = jnp.dot(time_shard.T, mod_total.reshape(images, 4 * D), precision=PRECISE).reshape(
        time_shard.shape[1], 4, D
    )
    gains_s = own_columns(jnp.sum(gain_parts, axis=1), width_shard)
    gate_s = own_columns(jnp.sum(gate_parts, axis=1), HEADS // lax.axis_size("fsdp"))
    gains_grad, gate_grad = lax.psum((gains_s, gate_s), "dp")
    ada_grad, text_grad, qkv_grad, out_grad = (
        lax.psum_scatter(ada_s.astype(jnp.bfloat16), "dp", scatter_dimension=2, tiled=True).astype(
            jnp.float32
        ),
        lax.psum_scatter(text_s.astype(jnp.bfloat16), "dp", scatter_dimension=2, tiled=True).astype(
            jnp.float32
        ),
        lax.psum_scatter(qkv_s.astype(jnp.bfloat16), "dp", scatter_dimension=2, tiled=True).astype(
            jnp.float32
        ),
        lax.psum_scatter(out_s.astype(jnp.bfloat16), "dp", scatter_dimension=1, tiled=True).astype(
            jnp.float32
        ),
    )
    return (
        output,
        grad_input,
        grad_text_in,
        ada_grad,
        text_grad,
        qkv_grad,
        out_grad,
        gains_grad,
        gate_grad,
        gate_up_grad,
        down_grad,
    )


def solution(mesh):
    return jax.shard_map(
        on_device,
        mesh=mesh,
        in_specs=(
            P("dp", "fsdp", None),
            P("dp", "fsdp", None),
            P("dp"),
            P("dp"),
            P("dp", None, "fsdp"),
            P("dp", "fsdp", None),
            P("fsdp", None, None),
            P("fsdp", None, None),
            P("fsdp", None, None),
            P("fsdp", None),
            P(None, "fsdp"),
            P("fsdp"),
            P(None, None, "fsdp"),
            P("fsdp", None),
        ),
        out_specs=(
            P("dp", "fsdp", None),
            P("dp", "fsdp", None),
            P("dp", "fsdp", None),
            P("fsdp", None, "dp"),
            P("fsdp", None, "dp"),
            P("fsdp", None, "dp"),
            P("fsdp", "dp"),
            P(None, "fsdp"),
            P("fsdp"),
            P("dp", None, "fsdp"),
            P("fsdp", "dp"),
        ),
        check_vma=False,
    )
```

profile of v0, /device:TPU:0, one launch (start us, length us, event | category | flops | bytes accessed | tf_op | source)
XLA Modules:
  0.0 1710.0 jit_solution(16764344963530457315)
XLA Ops:
  50.1 16.3 all-gather.21.cloned.1.call-done
  106.2 23.1 %multiply_reduce_fusion.1 = (f32[24,512]{1,0:T(8,128)S(1)}, f32[24,512,1024]{2,1,0:T(8,128)}) fusion(bf16[512,24,64]{0,2,1:T(8,128)(2,1)S(1)} %bitcast.365, bf16[1024,24,64]{0,2,1:T(8,128)(2,1)} %bitcast.375), kind=kOutput, calls=%fused_computation.6 | convolution fusion | flops 1635766272 | bytes 55099392 | tf_op jit(solution)/shard_map/iqhd,ikhd->ihqk/dot_general | solution.py:97
  129.3 29.0 %fusion = f32[24,512]{1,0:T(8,128)S(1)} fusion(f32[24,512,1024]{2,1,0:T(8,128)} %get-tuple-element.115, f32[24,512]{1,0:T(8,128)S(1)} %get-tuple-element.114), kind=kLoop, calls=%fused_computation.5 | loop fusion | flops 37736448 | bytes 50429952 | tf_op jit(solution)/shard_map/reduce_sum | solution.py:112
  163.0 23.5 %fusion.6 = f32[24,64,512]{2,1,0:T(8,128)} fusion(bf16[1024,24,64]{0,2,1:T(8,128)(2,1)} %bitcast.381, f32[24,512,1024]{2,1,0:T(8,128)} %get-tuple-element.115, f32[24,512]{1,0:T(8,128)S(1)} %fusion, f32[24,512]{1,0:T(8,128)S(1)} %get-tuple-element.114), kind=kOutput, calls=%fused_computation.11 | convolution fusion | flops 1660944384 | bytes 56721408 | tf_op jit(solution)/shard_map/ihqk,ikhd->iqhd/dot_general | solution.py:114
  190.1 24.7 %copy.167 = bf16[512,8,2,1536]{3,1,2,0:T(8,128)(2,1)} copy(bf16[512,8,2,1536]{3,2,1,0:T(2,128)(2,1)} %bitcast.377) | data formatting | bytes 50331648
  214.8 30.1 %copy.124 = bf16[4096,3072]{0,1:T(8,128)(2,1)} copy(bf16[4096,3072]{1,0:T(8,128)(2,1)} %bitcast.362) | data formatting | bytes 50331648 | tf_op jit(solution)/shard_map/reshape | solution.py:230
  310.2 16.8 copy.130
  327.0 20.4 %convolution_bitcast_fusion = f32[1,1024,2,2048]{3,1,2,0:T(8,128)} fusion(bf16[2,2048,1536]{2,1,0:T(8,128)(2,1)} %bitcast.387, bf16[1,1024,1536]{2,1,0:T(8,128)(2,1)} %all-gather.29.cloned.1.call-done), kind=kOutput, calls=%fused_computation.46 | convolution fusion | flops 12884901888 | bytes 32505856 | tf_op jit(solution)/shard_map/dot_general | solution.py:63
  347.4 16.8 fusion.40
  366.3 18.5 %fusion.53 = bf16[1,1024,1536]{2,1,0:T(8,128)(2,1)} fusion(bf16[1536,4096]{1,0:T(8,128)(2,1)} %bitcast.370, bf16[1,1024,2048]{2,1,0:T(8,128)(2,1)} %get-tuple-element.87, bf16[1,1024,2048]{2,1,0:T(8,128)(2,1)S(1)} %get-tuple-element.86), kind=kOutput, calls=%fused_computation.80 | convolution fusion | flops 12903251968 | bytes 24117248 | tf_op jit(solution)/shard_map/dot_general | solution.py:70
  465.6 34.6 %multiply_reduce_fusion = (f32[24,512]{1,0:T(8,128)S(1)}, f32[24,512,1024]{2,1,0:T(8,128)}) fusion(f32[24,512,1024]{2,1,0:T(8,128)} %get-tuple-element.115, f32[24,512]{1,0:T(8,128)S(1)} %log_add_fusion.1, bf16[512,24,64]{0,2,1:T(8,128)(2,1)S(1)} %bitcast.378, bf16[1024,24,64]{0,2,1:T(8,128)(2,1)} %bitcast.382), kind=kOutput, calls=%fused_computation.1 | convolution fusion | flops 1660932096 | bytes 105480192 | tf_op jit(solution)/shard_map/iqhd,ikhd->ihqk/dot_general | solution.py:125
  500.2 40.5 %multiply_convert_fusion = bf16[24,512,1024]{2,1,0:T(8,128)(2,1)} fusion(f32[24,512,1024]{2,1,0:T(8,128)} %get-tuple-element.121, f32[24,512,1024]{2,1,0:T(8,128)} %get-tuple-element.115, f32[24,512]{1,0:T(8,128)S(1)} %get-tuple-element.120, f32[24,512]{1,0:T(8,128)S(1)} %log_add_fusion.1), kind=kLoop, calls=%fused_computation | loop fusion | flops 62914560 | bytes 125927424 | tf_op jit(solution)/shard_map/convert_element_type | solution.py:129
  540.7 14.3 multiply_convert_fusion.4
  555.0 22.0 %fusion.92 = bf16[24,64,1024]{2,1,0:T(8,128)(2,1)} fusion(bf16[512,24,64]{0,2,1:T(8,128)(2,1)S(1)} %bitcast.379, f32[24,512,1024]{2,1,0:T(8,128)} %get-tuple-element.115, f32[24,512]{1,0:T(8,128)S(1)} %log_add_fusion.1), kind=kOutput, calls=%fused_computation.145 | convolution fusion | flops 1649934336 | bytes 55099392 | tf_op jit(solution)/shard_map/ihqk,iqhd->ikhd/dot_general | solution.py:146
  595.5 14.2 fusion.142
  693.5 19.3 %convolution_convert_fusion = bf16[1536,2,2048]{2,0,1:T(8,128)(2,1)} fusion(bf16[2,2048,1024]{2,1,0:T(8,128)(2,1)} %bitcast.395, bf16[1,1024,1536]{2,1,0:T(8,128)(2,1)S(1)} %copy-done.68), kind=kOutput, calls=%fused_computation.25 | convolution fusion | flops 12891193344 | bytes 24117248 | tf_op jit(solution)/shard_map/dot_general | solution.py:80
  714.9 15.8 multiply_reduce_fusion.7
  792.3 49.9 %reduce-scatter.35.cloned.1.call-done = bf16[2048,96]{0,1:T(8,128)(2,1)} async-done(((bf16[2048,1536]{0,1:T(8,128)(2,1)}), bf16[2048,96]{0,1:T(8,128)(2,1)}) %reduce-scatter.35.cloned.1.call-update) | async-done | bytes 393232 | tf_op jit(solution)/shard_map/reduce_scatter | solution.py:276
  846.0 75.0 %all-reduce.1 = (f32[5,768]{1,0:T(8,128)}, f32[12]{0:T(128)}) all-reduce(f32[5,768]{1,0:T(8,128)S(1)} %constant_dynamic-slice_fusion, f32[12]{0:T(128)} %dynamic_slice.23), channel_id=1, replica_groups=mesh['dp'=16,'fsdp'=2] {'dp'}, use_global_device_ids=true, to_apply=%region_37.38 | all-reduce | flops 3852 | bytes 30816 | tf_op jit(solution)/shard_map/psum | solution.py:384
  926.2 48.6 %reduce-scatter.31.cloned.1.call-done = bf16[768,96]{0,1:T(8,128)(2,1)} async-done(((bf16[768,1536]{0,1:T(8,128)(2,1)}), bf16[768,96]{0,1:T(8,128)(2,1)}) %reduce-scatter.31.cloned.1.call-update) | async-done | bytes 147472 | tf_op jit(solution)/shard_map/reduce_scatter | solution.py:395
  976.4 208.1 %reduce-scatter.33.cloned.1.call-done = bf16[96,2,2048]{2,0,1:T(8,128)(2,1)} async-done(((bf16[1536,2,2048]{2,0,1:T(8,128)(2,1)}), bf16[96,2,2048]{2,0,1:T(8,128)(2,1)}) %reduce-scatter.33.cloned.1.call-update) | async-done | bytes 786448 | tf_op jit(solution)/shard_map/reduce_scatter | solution.py:273
  1187.7 147.5 %reduce-scatter.25.cloned.1.call-done = bf16[512,4,96]{0,2,1:T(8,128)(2,1)} async-done(((bf16[512,4,1536]{0,2,1:T(8,128)(2,1)}), bf16[512,4,96]{0,2,1:T(8,128)(2,1)}) %reduce-scatter.25.cloned.1.call-update) | async-done | bytes 393232 | tf_op jit(solution)/shard_map/reduce_scatter | solution.py:386
  1337.1 206.8 %reduce-scatter.27.cloned.1.call-done = bf16[2048,2,96]{0,2,1:T(8,128)(2,1)} async-done(((bf16[2048,2,1536]{0,2,1:T(8,128)(2,1)}), bf16[2048,2,96]{0,2,1:T(8,128)(2,1)}) %reduce-scatter.27.cloned.1.call-update) | async-done | bytes 786448 | tf_op jit(solution)/shard_map/reduce_scatter | solution.py:389
  1546.4 154.7 %reduce-scatter.29.cloned.1.call-done = bf16[768,3,96]{0,2,1:T(8,128)(2,1)} async-done(((bf16[768,3,1536]{0,2,1:T(8,128)(2,1)}), bf16[768,3,96]{0,2,1:T(8,128)(2,1)}) %reduce-scatter.29.cloned.1.call-update) | async-done | bytes 442384 | tf_op jit(solution)/shard_map/reduce_scatter | solution.py:392
  (360 shorter events, 421.9 us)
Async XLA Ops:
  7.9 58.5 %all-gather.21.cloned.1.call-start = ((), (), s32[]{:S(2)}) async-start(), calls=%async_computation.13 | async-start | bytes 21233664 | tf_op jit(solution)/shard_map/all_gather | solution.py:168
  18.3 88.0 %all-gather.23.cloned.1.call-start = ((), (), s32[]{:S(2)}) async-start(), calls=%async_computation.14 | async-start | bytes 4718592 | tf_op jit(solution)/shard_map/all_gather | solution.py:238
  92.8 65.6 %all-gather.45.cloned.1.call-start = ((), (), s32[]{:S(2)}) async-start(), calls=%async_computation.37 | async-start | bytes 4718592 | tf_op jit(solution)/shard_map/all_gather | solution.py:239
  96.5 93.5 %all-gather.25.cloned.1.call-start = ((), (), s32[]{:S(2)}) async-start(), calls=%async_computation.15 | async-start | bytes 37748736 | tf_op jit(solution)/shard_map/all_gather | solution.py:167
  97.1 185.5 %all-gather.27.cloned.1.call-start = ((), (), s32[]{:S(2)}) async-start(), calls=%async_computation.16 | async-start | bytes 7077888 | tf_op jit(solution)/shard_map/all_gather | solution.py:169
  97.7 229.3 %all-gather.29.cloned.1.call-start = ((), (), s32[]{:S(2)}) async-start(), calls=%async_computation.17 | async-start | bytes 4718592 | tf_op jit(solution)/shard_map/all_gather | solution.py:176
  293.4 54.1 %all-gather.31.cloned.1.call-start = ((), (), s32[]{:S(2)}) async-start(), calls=%async_computation.19 | async-start | bytes 4718592 | tf_op jit(solution)/shard_map/all_gather | solution.py:176
  296.2 102.1 %reduce-scatter.15.cloned.1.call-start = ((), (), s32[]{:S(2)}) async-start(), calls=%async_computation.20 | async-start | bytes 4718592 | tf_op jit(solution)/shard_map/reduce_scatter | solution.py:180
  398.2 189.8 %reduce-scatter.21.cloned.1.call-start = ((), (), s32[]{:S(2)}) async-start(), calls=%async_computation.23 | async-start | bytes 1179648 | tf_op jit(solution)/shard_map/reduce_scatter | solution.py:314
  453.9 138.8 %reduce-scatter.23.cloned.1.call-start = ((), (), s32[]{:S(2)}) async-start(), calls=%async_computation.24 | async-start | bytes 1179648 | tf_op jit(solution)/shard_map/reduce_scatter | solution.py:317
  465.6 149.2 %reduce-scatter.17.cloned.1.call-start = ((), (), s32[]{:S(2)}) async-start(), calls=%async_computation.21 | async-start | bytes 4718592 | tf_op jit(solution)/shard_map/reduce_scatter | solution.py:308
  555.0 93.2 %reduce-scatter.19.cloned.1.call-start = ((), (), s32[]{:S(2)}) async-start(), calls=%async_computation.22 | async-start | bytes 4718592 | tf_op jit(solution)/shard_map/reduce_scatter | solution.py:311
  581.7 84.7 %all-gather.41.cloned.1.call-start = ((), (), s32[]{:S(2)}) async-start(), calls=%async_computation.32 | async-start | bytes 4718592 | tf_op jit(solution)/shard_map/all_gather | solution.py:357
  586.9 79.5 %all-gather.43.cloned.1.call-start = ((), (), s32[]{:S(2)}) async-start(), calls=%async_computation.33 | async-start | bytes 4718592 | tf_op jit(solution)/shard_map/all_gather | solution.py:358
  587.5 148.5 %all-gather.35.cloned.1.call-start = ((), (), s32[]{:S(2)}) async-start(), calls=%async_computation.27 | async-start | bytes 2359296 | tf_op jit(solution)/shard_map/all_gather | solution.py:360
  594.9 142.9 %all-gather.33.cloned.1.call-start = ((), (), s32[]{:S(2)}) async-start(), calls=%async_computation.26 | async-start | bytes 3145728 | tf_op jit(solution)/shard_map/all_gather | solution.py:359
  595.4 150.2 %all-gather.39.cloned.1.call-start = ((), (), s32[]{:S(2)}) async-start(), calls=%async_computation.30 | async-start | bytes 14155776 | tf_op jit(solution)/shard_map/all_gather | solution.py:356
  652.1 106.3 %all-gather.37.cloned.1.call-start = ((), (), s32[]{:S(2)}) async-start(), calls=%async_computation.29 | async-start | bytes 4718592 | tf_op jit(solution)/shard_map/all_gather | solution.py:355
  652.7 189.5 %reduce-scatter.35.cloned.1.call-start = ((), (), s32[]{:S(2)}) async-start(), calls=%async_computation.36 | async-start | bytes 6684672 | tf_op jit(solution)/shard_map/reduce_scatter | solution.py:276
  666.3 308.5 %reduce-scatter.31.cloned.1.call-start = ((), (), s32[]{:S(2)}) async-start(), calls=%async_computation.34 | async-start | bytes 2506752 | tf_op jit(solution)/shard_map/reduce_scatter | solution.py:395
  673.5 511.1 %reduce-scatter.33.cloned.1.call-start = ((), (), s32[]{:S(2)}) async-start(), calls=%async_computation.35 | async-start | bytes 13369344 | tf_op jit(solution)/shard_map/reduce_scatter | solution.py:273
  713.0 622.2 %reduce-scatter.25.cloned.1.call-start = ((), (), s32[]{:S(2)}) async-start(), calls=%async_computation.25 | async-start | bytes 6684672 | tf_op jit(solution)/shard_map/reduce_scatter | solution.py:386
  736.0 808.0 %reduce-scatter.27.cloned.1.call-start = ((), (), s32[]{:S(2)}) async-start(), calls=%async_computation.28 | async-start | bytes 13369344 | tf_op jit(solution)/shard_map/reduce_scatter | solution.py:389
  745.6 955.5 %reduce-scatter.29.cloned.1.call-start = ((), (), s32[]{:S(2)}) async-start(), calls=%async_computation.31 | async-start | bytes 7520256 | tf_op jit(solution)/shard_map/reduce_scatter | solution.py:392
  (79 other events, 871.2 us)
Sparse Core Ops, SparseCore 0:
  9.6 27.5 all-gather.18
  38.8 27.5 all-gather.20
  92.9 13.2 all-gather.22
  108.2 13.2 all-gather.44
  122.9 41.4 all-gather.24
  165.8 15.5 all-gather.26
  293.5 13.2 all-gather.28
  308.9 13.2 all-gather.30
  384.9 12.0 reduce-scatter.14
  399.2 12.0 reduce-scatter.12
  555.1 12.0 reduce-scatter.16
  581.8 12.0 reduce-scatter.18
  595.9 13.2 all-gather.40
  610.6 13.2 all-gather.42
  625.9 10.9 all-gather.34
  638.3 11.7 all-gather.32
  652.2 22.9 all-gather.38
  676.6 13.2 all-gather.36
  695.1 146.9 reduce-scatter.34
  847.1 127.6 reduce-scatter.30
  981.4 203.1 reduce-scatter.32
  1189.7 145.4 reduce-scatter.24
  1340.8 203.0 reduce-scatter.26
  1550.0 151.0 reduce-scatter.28
  (2 shorter events, 18.7 us)
where the time goes:
time: 1720 us; the launch traced here: 1710 us
  waiting for transfers between devices  860 us (50%)
  matrix products  374 us (22%)
  local copies, waits for them, and re-layouts  203 us (12%)
  other arithmetic  162 us (9%)
  blocking collectives  90.1 us (5%)
  between operations  17.7 us (1%)
    reduce_scatter x1, waiting for transfers between devices, on_device(): lax.psum_scatter(grad_gate_up_s.astype(jnp.bfloat16), 'dp', scatter_dimen...  208 us
    reduce_scatter x1, waiting for transfers between devices, on_device(): lax.psum_scatter(text_s.astype(jnp.bfloat16), 'dp', scatter_dimension=2,...  207 us
    reduce_scatter x1, waiting for transfers between devices, on_device(): lax.psum_scatter(qkv_s.astype(jnp.bfloat16), 'dp', scatter_dimension=2, t...  155 us
    reduce_scatter x1, waiting for transfers between devices, on_device(): lax.psum_scatter(ada_s.astype(jnp.bfloat16), 'dp', scatter_dimension=2, t...  147 us
    dot_general x6, matrix products, matmul(): jnp.dot(left_op.reshape(-1, left_op.shape[-1]), right_op, preferred_eleme...  77.8 us
    psum x1, blocking collectives, on_device(): gains_grad, gate_grad = lax.psum((gains_s, gate_s), 'dp')  75 us
    dot_general x5, matrix products, matmul_t(): lax.dot_general(left_op.reshape(-1, left_op.shape[-1]), right_op, (((1,),...  73.3 us
    unnamed x161, local copies, waits for them, and re-layouts  71 us
  transfers between devices with their start and end apart: 26, of which 10 were waited for; matrix products, arithmetic and copies ran while one was open for 36% of the time, Pallas kernels for 0%

commit v1 on v0

v1 whole, which is shorter than its diff:
```python
import functools
import math

import jax
import jax.numpy as jnp
from jax import lax
from jax.experimental import pallas as pl
from jax.experimental.pallas import tpu as pltpu
from jax.sharding import PartitionSpec as P

D = 1536
HEADS = 24
HD = 64
TW = 4096
TE = 1024
PATCHES = 1024
TEXT = 256
EPSILON = 1e-06
F32 = jnp.float32
BF16 = jnp.bfloat16
QC = 256


def dot(a, b, ca=1, cb=0):
    return lax.dot_general(a, b, (((ca,), (cb,)), ((), ())), preferred_element_type=F32)


def from_behind(value, step):
    n = lax.axis_size("fsdp")
    return lax.ppermute(value, "fsdp", [(i, (i + step) % n) for i in range(n)])


def gather_rot(value):
    return [value] + [from_behind(value, r) for r in range(1, lax.axis_size("fsdp"))]


def pair_sum(value):
    return functools.reduce(lambda a, b: a + b, gather_rot(value))


def row_sum(value):
    n = lax.axis_size("fsdp")
    rows = value.shape[-1] // n
    total = value
    for r in range(1, n):
        total = total + jnp.roll(from_behind(value, r), r * rows, axis=-1)
    return total


def scatter_rot(blocks):
    n = lax.axis_size("fsdp")
    total = blocks[0].astype(F32)
    for r in range(1, n):
        got = lax.ppermute(blocks[r], "fsdp", [(i, (i - r) % n) for i in range(n)])
        total = total + got.astype(F32)
    return total


def rot_blocks(value, axis):
    n, f = lax.axis_size("fsdp"), lax.axis_index("fsdp")
    return [lax.dynamic_index_in_dim(value, (f - r) % n, axis, keepdims=False) for r in range(n)]


def dp_bits():
    return int(lax.axis_size("dp")).bit_length() - 1


def dp_swap(value, bit):
    n = lax.axis_size("dp")
    return lax.ppermute(value, "dp", [(i, i ^ (1 << bit)) for i in range(n)])


def orders():
    bits = list(range(dp_bits()))
    return bits, bits[:2][::-1] + bits[2:], bits[2:] + bits[:2]


def split_bit(value, axis, bit):
    mine = (lax.axis_index("dp") >> bit) & 1
    keep = lax.dynamic_index_in_dim(value, mine, axis, keepdims=False)
    send = lax.dynamic_index_in_dim(value, 1 - mine, axis, keepdims=False)
    return keep, send


def dp_scatter(value, order):
    nb = dp_bits()
    rows = value.shape[0] >> nb
    cur = value.reshape((2,) * nb + (rows, value.shape[1]))
    labels = list(range(nb))[::-1]
    for i, bit in enumerate(order):
        keep, send = split_bit(cur, labels.index(bit), bit)
        labels.remove(bit)
        total = keep.astype(F32) + dp_swap(send, bit).astype(F32)
        cur = total if i == nb - 1 else total.astype(BF16)
    return cur


def dp_exchange(value, order):
    nb = dp_bits()
    cur = value.reshape((2,) * nb + value.shape[1:])
    for bit in order:
        axis = nb - 1 - bit
        keep, send = split_bit(cur, axis, bit)
        cur = jnp.stack([keep, dp_swap(send, bit)], axis=axis)
    return cur.reshape(value.shape)


def dp_total(value):
    for bit in range(dp_bits()):
        value = value + dp_swap(value, bit)
    return value


def dp_gather(value, order):
    pieces = [([0], value[None])]
    for bit in order[::-1]:
        pieces = pieces + [([p ^ (1 << bit) for p in pos], dp_swap(a, bit)) for pos, a in pieces]
    return pieces


def rope_block(value, cosine, sine, sign):
    width = value.shape[1]
    lane = lax.broadcasted_iota(jnp.int32, value.shape, 1)
    partner = jnp.where(
        lane % 32 < 16, pltpu.roll(value, width - 16, 1), pltpu.roll(value, 16, 1)
    )
    return value * cosine + sign * (partner * sine)


def masked(value, head):
    lane = lax.broadcasted_iota(jnp.int32, value.shape, 1)
    return jnp.where(lane // HD == head, value, jnp.zeros_like(value))


def attn_fwd_kernel(
    len_ref, qp_ref, kp_ref, vp_ref, iq_ref, ik_ref, gq_ref, gk_ref, cos_ref, sin_ref,
    tk_ref, tv_ref, gate_ref,
    q_ref, k_ref, v_ref, mixed_ref, so_ref, co_ref, ls_ref, lc_ref, vt_ref, tvt_ref,
):
    tokens, width = qp_ref.shape
    heads = width // HD
    q = rope_block(qp_ref[...] * iq_ref[...] * gq_ref[...], cos_ref[...], sin_ref[...], 1.0)
    q_ref[...] = q.astype(BF16)
    k = rope_block(kp_ref[...] * ik_ref[...] * gk_ref[...], cos_ref[...], sin_ref[...], 1.0)
    k_ref[...] = k.astype(BF16)
    v_ref[...] = vp_ref[...].astype(BF16)
    vt_ref[...] = vp_ref[...].T.astype(BF16)
    tvt_ref[...] = tv_ref[...].astype(F32).T.astype(BF16)
    length = len_ref[0]

    def one(keys, values_t, qm, head, limit):
        s = dot(keys, qm, 1, 1)
        if limit is not None:
            slot = lax.broadcasted_iota(jnp.int32, s.shape, 0)
            s = jnp.where(slot < limit, s, -1e30)
        peak = jnp.max(s, axis=0, keepdims=True)
        e = jnp.exp(s - peak)
        total = jnp.sum(e, axis=0, keepdims=True)
        o = dot(values_t[head * HD : (head + 1) * HD, :], e.astype(BF16))
        return o * (1.0 / total), peak + jnp.log(total)

    def chunk(c, carry):
        rows = pl.ds(pl.multiple_of(c * QC, QC), QC)
        qc = q_ref[rows, :] * jnp.asarray(HD**-0.5, BF16)
        selfs, crosses = [], []
        for h in range(heads):
            qm = masked(qc, h)
            o, lse = one(k_ref[...], vt_ref, qm, h, None)
            selfs.append(o)
            ls_ref[0, h : h + 1, rows] = lse
            o, lse = one(tk_ref[...], tvt_ref, qm, h, length)
            crosses.append(o)
            lc_ref[0, h : h + 1, rows] = lse
        so = jnp.concatenate(selfs, axis=0)
        co = jnp.concatenate(crosses, axis=0)
        so_ref[:, rows] = so
        co_ref[:, rows] = co
        mixed_ref[rows, :] = (so + gate_ref[...] * co).T.astype(BF16)
        return carry

    lax.fori_loop(0, tokens // QC, chunk, 0)


def attn_bwd_kernel(
    len_ref, q_ref, k_ref, v_ref, tk_ref, tv_ref, g_ref, so_ref, co_ref, ls_ref, lc_ref,
    qp_ref, kp_ref, iq_ref, ik_ref, gq_ref, gk_ref, cos_ref, sin_ref, gate_ref, gate_row_ref,
    dq_ref, dk_ref, dv_ref, dtk_ref, dtv_ref, rq_ref, rk_ref, gainq_ref, gaink_ref, gateg_ref,
    gs_ref, gc_ref, ds_ref, dc_ref, kt_ref, tkt_ref, dqt_ref, dk_acc, dv_acc,
):
    tokens, width = q_ref.shape
    heads = width // HD
    scale = jnp.asarray(HD**-0.5, BF16)

    @pl.when(pl.program_id(0) == 0)
    def _():
        rq_ref[...] = jnp.zeros_like(rq_ref)
        rk_ref[...] = jnp.zeros_like(rk_ref)

    g = g_ref[...]
    gs_ref[...] = g.astype(BF16)
    gc_ref[...] = (g * gate_row_ref[...]).astype(BF16)
    gt = g.T
    co = co_ref[...]
    prod_c = gt * co
    gateg_ref[...] = jnp.sum(prod_c, axis=1, keepdims=True)
    prod_s = gt * so_ref[...]
    prod_c = prod_c * gate_ref[...]
    for h in range(heads):
        ds_ref[h : h + 1, :] = jnp.sum(prod_s[h * HD : (h + 1) * HD], axis=0, keepdims=True)
        dc_ref[h : h + 1, :] = jnp.sum(prod_c[h * HD : (h + 1) * HD], axis=0, keepdims=True)
    kt_ref[...] = k_ref[...].astype(F32).T.astype(BF16)
    tkt_ref[...] = tk_ref[...].astype(F32).T.astype(BF16)
    dk_acc[...] = jnp.zeros_like(dk_acc)
    dv_acc[...] = jnp.zeros_like(dv_acc)
    dtk_ref[...] = jnp.zeros_like(dtk_ref)
    dtv_ref[...] = jnp.zeros_like(dtv_ref)
    length = len_ref[0]

    def one(keys, keys_t, values, qm, gm, lse, delta, head, limit):
        s = dot(keys, qm, 1, 1)
        p = jnp.exp(s - lse)
        if limit is not None:
            slot = lax.broadcasted_iota(jnp.int32, s.shape, 0)
            p = jnp.where(slot < limit, p, 0.0)
        dp = dot(values, gm, 1, 1)
        ds = (p * (dp - delta)).astype(BF16)
        dq = dot(keys_t[head * HD : (head + 1) * HD, :], ds)
        return dq, dot(ds, qm), dot(p.astype(BF16), gm)

    def chunk(c, carry):
        rows = pl.ds(pl.multiple_of(c * QC, QC), QC)
        qc = q_ref[rows, :] * scale
        for h in range(heads):
            qm = masked(qc, h)
            dq, dk, dv = one(
                k_ref[...], kt_ref, v_ref[...], qm, masked(gs_ref[rows, :], h),
                ls_ref[0, h : h + 1, rows], ds_ref[h : h + 1, rows], h, None,
            )
            dk_acc[...] += dk
            dv_acc[...] += dv
            dq2, dk, dv = one(
                tk_ref[...], tkt_ref, tv_ref[...], qm, masked(gc_ref[rows, :], h),
                lc_ref[0, h : h + 1, rows], dc_ref[h : h + 1, rows], h, length,
            )
            dtk_ref[...] += dk
            dtv_ref[...] += dv
            dqt_ref[h * HD : (h + 1) * HD, rows] = (dq + dq2) * HD**-0.5
        return carry

    lax.fori_loop(0, tokens // QC, chunk, 0)
    dq = rope_block(dqt_ref[...].T, cos_ref[...], sin_ref[...], -1.0)
    dq_ref[...] = dq
    prod = dq * (qp_ref[...] * iq_ref[...])
    gainq_ref[...] = jnp.sum(prod, axis=0, keepdims=True)
    rq_ref[...] += prod * gq_ref[...]
    dk = rope_block(dk_acc[...], cos_ref[...], sin_ref[...], -1.0)
    dk_ref[...] = dk
    prod = dk * (kp_ref[...] * ik_ref[...])
    gaink_ref[...] = jnp.sum(prod, axis=0, keepdims=True)
    rk_ref[...] += prod * gk_ref[...]
    dv_ref[...] = dv_acc[...].astype(BF16)


def specs(tokens, text, width, heads):
    col = pl.BlockSpec((tokens, width), lambda i: (0, i))
    tcol = pl.BlockSpec((text, width), lambda i: (0, i))
    row = pl.BlockSpec((width, tokens), lambda i: (i, 0))
    stat = pl.BlockSpec((tokens, 1), lambda i: (0, 0))
    gain = pl.BlockSpec((1, width), lambda i: (0, i))
    gcol = pl.BlockSpec((width, 1), lambda i: (i, 0))
    table = pl.BlockSpec((tokens, width), lambda i: (0, 0))
    lse = pl.BlockSpec((1, heads, tokens), lambda i: (i, 0, 0))
    scalar = pl.BlockSpec(memory_space=pltpu.SMEM)
    return col, tcol, row, stat, gain, gcol, table, lse, scalar


def sds(shape, dtype=F32):
    return jax.ShapeDtypeStruct(shape, dtype)


def attn_forward(length, qp, kp, vp, iq, ik, gq, gk, cosine, sine, tk, tv, gate):
    tokens, columns = qp.shape
    text, width = tk.shape[0], cosine.shape[1]
    heads, blocks = width // HD, columns // width
    col, tcol, row, stat, gain, gcol, table, lse, scalar = specs(tokens, text, width, heads)
    pairs = columns // HD * tokens * (tokens + text)
    return pl.pallas_call(
        attn_fwd_kernel,
        grid=(blocks,),
        in_specs=[scalar, col, col, col, stat, stat, gain, gain, table, table, tcol, tcol, gcol],
        out_specs=[col, col, col, col, row, row, lse, lse],
        out_shape=[
            sds(qp.shape, BF16), sds(qp.shape, BF16), sds(qp.shape, BF16), sds(qp.shape, BF16),
            sds((columns, tokens)), sds((columns, tokens)),
            sds((blocks, heads, tokens)), sds((blocks, heads, tokens)),
        ],
        scratch_shapes=[pltpu.VMEM((width, tokens), BF16), pltpu.VMEM((width, text), BF16)],
        cost_estimate=pl.CostEstimate(
            flops=16 * pairs * HD, transcendentals=pairs, bytes_accessed=28 * tokens * columns
        ),
    )(length, qp, kp, vp, iq, ik, gq, gk, cosine, sine, tk, tv, gate)


def attn_backward(length, q, k, v, tk, tv, g, so, co, ls, lc, qp, kp, iq, ik, gq, gk, cosine, sine, gate):
    tokens, columns = q.shape
    text, width = tk.shape[0], cosine.shape[1]
    heads, blocks = width // HD, columns // width
    col, tcol, row, stat, gain, gcol, table, lse, scalar = specs(tokens, text, width, heads)
    pairs = columns // HD * tokens * (tokens + text)
    return pl.pallas_call(
        attn_bwd_kernel,
        grid=(blocks,),
        in_specs=[scalar, col, col, col, tcol, tcol, col, row, row, lse, lse,
                  col, col, stat, stat, gain, gain, table, table, gcol, gain],
        out_specs=[col, col, col, tcol, tcol, table, table, gain, gain, gcol],
        out_shape=[
            sds(q.shape), sds(q.shape), sds(q.shape, BF16), sds(tk.shape), sds(tk.shape),
            sds((tokens, width)), sds((tokens, width)),
            sds((1, columns)), sds((1, columns)), sds((columns, 1)),
        ],
        scratch_shapes=[
            pltpu.VMEM((tokens, width), BF16), pltpu.VMEM((tokens, width), BF16),
            pltpu.VMEM((heads, tokens), F32), pltpu.VMEM((heads, tokens), F32),
            pltpu.VMEM((width, tokens), BF16), pltpu.VMEM((width, text), BF16),
            pltpu.VMEM((width, tokens), F32),
            pltpu.VMEM((tokens, width), F32), pltpu.VMEM((tokens, width), F32),
        ],
        cost_estimate=pl.CostEstimate(
            flops=40 * pairs * HD, transcendentals=pairs, bytes_accessed=44 * tokens * columns
        ),
    )(length, q, k, v, tk, tv, g, so, co, ls, lc, qp, kp, iq, ik, gq, gk, cosine, sine,
      gate, gate.reshape(1, columns))


def time_embed(timesteps):
    half = TE // 2
    frequencies = jnp.exp(-math.log(10000.0) * jnp.arange(half, dtype=F32) / half)
    angles = timesteps.astype(F32)[:, None] * frequencies
    waves = jnp.concatenate([jnp.cos(angles), jnp.sin(angles)], axis=-1)
    return jax.nn.silu(waves).astype(BF16)


def rope_tables(positions, width):
    lane = jnp.arange(width)
    quarter = HD // 4
    frequencies = 10000.0 ** (-(lane % quarter).astype(F32) / quarter)
    place = jnp.where(lane % HD < HD // 2, positions[0][:, None], positions[1][:, None])
    angles = place.astype(F32) * frequencies
    return jnp.cos(angles), jnp.where(lane % 32 < 16, -1.0, 1.0) * jnp.sin(angles)


def inverse_rms(values):
    return lax.rsqrt(jnp.mean(values * values, axis=-1, keepdims=True) + EPSILON)


def rms_back(grad_hat, normed, inverse):
    return inverse * (grad_hat - normed * jnp.mean(grad_hat * normed, axis=-1, keepdims=True))


def pad_cols(value, width):
    extra = -value.shape[-1] % width
    return value if extra == 0 else jnp.pad(value, [(0, 0)] * (value.ndim - 1) + [(0, extra)])


def on_device(
    hidden_in, text_state, caption_lengths, timesteps, patch_positions, cotangent,
    w_ada, w_text, w_qkv, w_out, gains, cross_gate, w_gate_up, w_down,
):
    n, f = lax.axis_size("fsdp"), lax.axis_index("fsdp")
    dpn, me = lax.axis_size("dp"), lax.axis_index("dp")
    order_a, order_b, order_c = orders()
    own_d = D // n
    local = hidden_in.shape[1]
    width = 2 * HD
    x_bf, dy_bf = hidden_in[0], cotangent[0]

    x_all = jnp.concatenate(gather_rot(x_bf), axis=0)
    dy_all = jnp.concatenate(gather_rot(dy_bf), axis=0)
    places = jnp.concatenate(gather_rot(patch_positions[0]), axis=1)
    w_heads = lax.all_to_all(w_qkv, "fsdp", split_axis=2, concat_axis=0, tiled=True)
    text_cols = lax.all_to_all(text_state[0], "fsdp", split_axis=1, concat_axis=0, tiled=True)
    gain_full = lax.all_gather(gains, "fsdp", axis=1, tiled=True).astype(F32)
    gain_own = gains.astype(F32)
    times_all = lax.all_gather(timesteps, "dp", axis=0, tiled=True)

    time_low = time_embed(timesteps)
    own_te = TE // n
    time_own = lax.dynamic_slice_in_dim(time_low[0], f * own_te, own_te, 0)
    modulation = pair_sum(
        jnp.einsum("k,kjd->jd", time_own, w_ada, preferred_element_type=F32)
    )
    scale_attn, gate_attn = modulation[0:1], jnp.tanh(modulation[1:2])
    scale_ffn, gate_ffn = modulation[2:3], jnp.tanh(modulation[3:4])

    x_f = x_all.astype(F32)
    normed_all = x_f * inverse_rms(x_f)
    first_all = (normed_all * gain_full[0] * (1.0 + scale_attn)).astype(BF16)
    q_pre, k_pre, v_pre = (dot(first_all, w_heads[:, j]) for j in range(3))
    squares = row_sum(jnp.stack([jnp.sum(q_pre * q_pre, -1), jnp.sum(k_pre * k_pre, -1)]))
    inverse = lax.rsqrt(squares / D + EPSILON)
    inv_q, inv_k = inverse[0][:, None], inverse[1][:, None]

    text_part = jnp.stack([dot(text_cols, w_text[:, j]) for j in range(2)])
    text_pre = scatter_rot(rot_blocks(text_part.reshape(2, TEXT, n, own_d), 2))
    inv_t = lax.rsqrt(
        pair_sum(jnp.sum(text_pre[0] * text_pre[0], -1, keepdims=True)) / D + EPSILON
    )
    normed_t = text_pre[0] * inv_t
    tk = (normed_t * gain_own[4]).astype(BF16)
    tv = text_pre[1].astype(BF16)
    half = text_cols.shape[1] // 2
    text_a = dp_gather(text_cols[:, :half], order_a)
    text_b = dp_gather(text_cols[:, half:], order_b)

    head_tanh = jnp.tanh(cross_gate.astype(F32))
    gate_col = pad_cols(jnp.repeat(head_tanh, HD)[None], width).T
    cosine, sine = rope_tables(places, width)
    gq, gk = pad_cols(gain_own[2:3], width), pad_cols(gain_own[3:4], width)
    qp, kp, vp = (pad_cols(v, width) for v in (q_pre, k_pre, v_pre))
    tkp, tvp = pad_cols(tk, width), pad_cols(tv, width)
    q, k, v, mixed_p, so, co, ls, lc = attn_forward(
        caption_lengths, qp, kp, vp, inv_q, inv_k, gq, gk, cosine, sine, tkp, tvp, gate_col
    )
    mixed = mixed_p[:, :own_d]
    parts = [dot(mixed[r * local : (r + 1) * local], w_out) for r in range(n)]
    attn_branch = scatter_rot([parts[0]] + [p.astype(BF16) for p in parts[1:]])
    x_own = x_bf.astype(F32)
    after_attn = x_own + gate_attn * attn_branch
    inverse_two = inverse_rms(after_attn)
    normed_two = after_attn * inverse_two
    second = (normed_two * gain_full[1] * (1.0 + scale_ffn)).astype(BF16)

    second_all = jnp.concatenate(gather_rot(second), axis=0)
    branch_all = (gate_ffn * dy_all.astype(F32)).astype(BF16)
    w_gate, w_up = w_gate_up[:, 0], w_gate_up[:, 1]
    gate_pre = dot(second_all, w_gate)
    up_pre = dot(second_all, w_up)
    grad_hidden = dot(branch_all, w_down, 1, 1)
    sig = jax.nn.sigmoid(gate_pre)
    hidden = (gate_pre * sig * up_pre).astype(BF16)
    grad_gate = (grad_hidden * up_pre * (sig + gate_pre * sig * (1.0 - sig))).astype(BF16)
    grad_up = (grad_hidden * gate_pre * sig).astype(BF16)
    down_grad = dp_scatter(dot(branch_all, hidden, 0, 0).astype(BF16), order_c)
    gate_grad = dp_scatter(dot(second_all, grad_gate, 0, 0).astype(BF16), order_a)
    up_grad = dp_scatter(dot(second_all, grad_up, 0, 0).astype(BF16), order_b)

    def rows(value, r):
        return value[r * local : (r + 1) * local]

    back = [
        dot(rows(grad_gate, r), w_gate, 1, 1) + dot(rows(grad_up, r), w_up, 1, 1) for r in range(n)
    ]
    grad_second = scatter_rot([back[0]] + [b.astype(BF16) for b in back[1:]])
    parts = [dot(rows(hidden, r), w_down) for r in range(n)]
    ffn_branch = scatter_rot([parts[0]] + [p.astype(BF16) for p in parts[1:]])
    output = (after_attn + gate_ffn * ffn_branch).astype(BF16)
    dy = dy_bf.astype(F32)
    d_gate_ffn = jnp.sum(dy * ffn_branch, axis=0) * (1.0 - gate_ffn[0] * gate_ffn[0])

    scaled = grad_second * normed_two
    d_scale_ffn = jnp.sum(scaled * gain_full[1], axis=0)
    gain_two = jnp.sum(scaled * (1.0 + scale_ffn), axis=0)
    grad_after = dy + rms_back(
        grad_second * gain_full[1] * (1.0 + scale_ffn), normed_two, inverse_two
    )
    d_gate_attn = jnp.sum(grad_after * attn_branch, axis=0) * (1.0 - gate_attn[0] * gate_attn[0])
    grad_attn = (gate_attn * grad_after).astype(BF16)
    grad_attn_all = jnp.concatenate(gather_rot(grad_attn), axis=0)
    grad_mixed = dot(grad_attn_all, w_out, 1, 1)
    out_local = dot(grad_attn_all, mixed, 0, 0).astype(BF16)
    half_d = own_d // 2
    out_grad = jnp.concatenate(
        [dp_scatter(out_local[:, :half_d], order_a), dp_scatter(out_local[:, half_d:], order_b)],
        axis=1,
    )
    dq, dk, dv, dtk, dtv, rq, rk, gain_q, gain_k, gate_g = attn_backward(
        caption_lengths, q, k, v, tkp, tvp, pad_cols(grad_mixed, width), so, co, ls, lc, qp, kp,
        inv_q, inv_k, gq, gk, cosine, sine, gate_col,
    )
    dq, dk, dv, dtk, dtv = (v_[:, :own_d] for v_ in (dq, dk, dv, dtk, dtv))
    gate_total = jnp.sum(gate_g[:own_d].reshape(HEADS // n, HD), axis=1) * (
        1.0 - head_tanh * head_tanh
    )
    text_hat = dtk * gain_own[4]
    gain_text = jnp.sum(dtk * normed_t, axis=0, keepdims=True)
    means = row_sum(jnp.stack([jnp.sum(rq, -1), jnp.sum(rk, -1)])) / D
    mean_t = pair_sum(jnp.sum(text_hat * normed_t, -1, keepdims=True)) / D
    grad_q = (inv_q * (dq * gain_own[2] - q_pre * inv_q * means[0][:, None])).astype(BF16)
    grad_k = (inv_k * (dk * gain_own[3] - k_pre * inv_k * means[1][:, None])).astype(BF16)

    grads = (grad_q, grad_k, dv)
    wide = jnp.stack([dot(g, first_all, 0, 0).astype(BF16) for g in grads])
    wide = lax.all_to_all(wide, "fsdp", split_axis=2, concat_axis=1, tiled=True)
    q_grad = dp_scatter(wide[0], order_a)
    k_grad = dp_scatter(wide[1], order_b)
    v_grad = jnp.concatenate(
        [
            dp_scatter(wide[2][:, :half_d], order_a),
            dp_scatter(wide[2][:, half_d:], order_b),
        ],
        axis=1,
    )
    parts = [
        sum(dot(rows(g, r), w_heads[:, j], 1, 1) for j, g in enumerate(grads)) for r in range(n)
    ]
    grad_first = scatter_rot([parts[0]] + [p.astype(BF16) for p in parts[1:]])
    inverse_one = inverse_rms(x_own)
    normed_one = x_own * inverse_one
    scaled = grad_first * normed_one
    d_scale_attn = jnp.sum(scaled * gain_full[0], axis=0)
    gain_one = jnp.sum(scaled * (1.0 + scale_attn), axis=0)
    grad_input = (
        grad_after
        + rms_back(grad_first * gain_full[0] * (1.0 + scale_attn), normed_one, inverse_one)
    ).astype(BF16)

    grad_tk = (inv_t * (text_hat - normed_t * mean_t)).astype(BF16)
    text_pair = jnp.concatenate([grad_tk, dtv.astype(BF16)], axis=0).reshape(2, TEXT, own_d)
    pair_all = lax.all_gather(text_pair, "fsdp", axis=2, tiled=True)
    text_in = dot(pair_all[0], w_text[:, 0], 1, 1) + dot(pair_all[1], w_text[:, 1], 1, 1)
    text_in = lax.all_to_all(text_in.astype(BF16), "fsdp", split_axis=0, concat_axis=1, tiled=True)
    share = D // dpn
    outgoing = pair_all.reshape(2, TEXT, dpn, share).transpose(2, 0, 1, 3)
    pair_cols = dp_exchange(outgoing, order_a)
    halves = []
    for pieces in (text_a, text_b):
        total = 0.0
        for where, piece in pieces:
            for i, r in enumerate(where):
                total = total + jnp.einsum(
                    "jts,tk->jsk", pair_cols[r], piece[i], preferred_element_type=F32
                )
        halves.append(total)
    text_grad = jnp.concatenate(halves, axis=2)

    mods = jnp.stack([d_scale_attn, d_gate_attn, d_scale_ffn, d_gate_ffn])
    mods = pair_sum(dp_exchange(mods.reshape(4, dpn, share).transpose(1, 0, 2), order_a))
    times = time_embed(jnp.take(times_all, me ^ jnp.arange(dpn)))
    times = lax.dynamic_slice_in_dim(times, f * own_te, own_te, 1).astype(F32)
    ada_grad = lax.dot_general(
        mods.reshape(dpn, 4 * share), times, (((0,), (0,)), ((), ())),
        precision=lax.Precision.HIGHEST,
    ).reshape(4, share, own_te)
    two = scatter_rot(rot_blocks(jnp.stack([gain_one, gain_two]).reshape(2, n, own_d), 1))
    gate_row = jnp.pad(gate_total, (0, own_d - gate_total.shape[0]))[None]
    small = dp_total(
        jnp.concatenate([two, gain_q[:, :own_d], gain_k[:, :own_d], gain_text, gate_row], axis=0)
    )
    return (
        output[None],
        grad_input[None],
        text_in[None],
        ada_grad.transpose(2, 0, 1),
        text_grad.transpose(2, 0, 1),
        jnp.stack([q_grad, k_grad, v_grad]).transpose(2, 0, 1),
        out_grad.T,
        small[:5],
        small[5, : HEADS // n],
        jnp.stack([gate_grad, up_grad], axis=1),
        down_grad.T,
    )


def solution(mesh):
    return jax.shard_map(
        on_device,
        mesh=mesh,
        in_specs=(
            P("dp", "fsdp", None),
            P("dp", "fsdp", None),
            P("dp"),
            P("dp"),
            P("dp", None, "fsdp"),
            P("dp", "fsdp", None),
            P("fsdp", None, None),
            P("fsdp", None, None),
            P("fsdp", None, None),
            P("fsdp", None),
            P(None, "fsdp"),
            P("fsdp"),
            P(None, None, "fsdp"),
            P("fsdp", None),
        ),
        out_specs=(
            P("dp", "fsdp", None),
            P("dp", "fsdp", None),
            P("dp", "fsdp", None),
            P("fsdp", None, "dp"),
            P("fsdp", None, "dp"),
            P("fsdp", None, "dp"),
            P("fsdp", "dp"),
            P(None, "fsdp"),
            P("fsdp"),
            P("dp", None, "fsdp"),
            P("fsdp", "dp"),
        ),
        check_vma=False,
    )
```

time: 1720 us -> 1300 us (0.76)
  waiting for transfers between devices: 860 us -> 401 us
  matrix products: 374 us -> 245 us
  Pallas kernels: 0 us -> 128 us
  starting transfers between devices: 2.31 us -> 106 us
  other arithmetic: 162 us -> 78.2 us
  local copies, waits for them, and re-layouts: 203 us -> 262 us
  blocking collectives: 90.1 us -> 47.2 us
    reduce_scatter x12 -> x0, waiting for transfers between devices: 825 us -> none  [the longest x1 208 us: on_device(): lax.psum_scatter(grad_gate_up_s.astype(jnp.bfloat16), 'dp', scatter_dimen...]
    ppermute x0 -> x95, waiting for transfers between devices: none -> 400 us  [the longest x78 400 us: dp_swap(): return lax.ppermute(value, 'dp', [(i, i ^ 1 << bit) for i in range(n)])]
    dot_general x28 -> x66, matrix products: 374 us -> 245 us  [the longest x32 228 us: dot(): lax.dot_general(a, b, (((ca,), (cb,)), ((), ())), preferred_element_type=...]
    pallas_call x0 -> x2, Pallas kernels: none -> 128 us  [the longest x1 64.2 us: attn_backward(): pl.pallas_call(attn_bwd_kernel, grid=(blocks,), in_specs=[scalar, col, co...]
    ppermute x0 -> x95, starting transfers between devices: none -> 95.1 us  [the longest x78 91.6 us: dp_swap(): return lax.ppermute(value, 'dp', [(i, i ^ 1 << bit) for i in range(n)])]
    psum x1 -> x0, blocking collectives: 75 us -> none  [on_device(): gains_grad, gate_grad = lax.psum((gains_s, gate_s), 'dp')]
    slice x6 -> x15, local copies, waits for them, and re-layouts: 13.3 us -> 65.2 us  [the longest x1 24.7 us: on_device(): text_part = jnp.stack([dot(text_cols, w_text[:, j]) for j in range(2)])]
    convert_element_type x19 -> x37, other arithmetic: 81.4 us -> 32.7 us  [the longest x27 23.1 us: dp_scatter(): cur = total if i == nb - 1 else total.astype(BF16)]
  transfers between devices with their start and end apart: 26 -> 98, of which waited for: 10 -> 42; matrix products, arithmetic and copies ran while one was open for 36% -> 43% of each run, Pallas kernels for 0% -> 5%
where the time goes in v1:
time: 1300 us; the launch traced here: 1280 us
  waiting for transfers between devices  401 us (31%)
  local copies, waits for them, and re-layouts  262 us (20%)
  matrix products  245 us (19%)
  Pallas kernels  128 us (10%)
  starting transfers between devices  106 us (8%)
  other arithmetic  78.2 us (6%)
  blocking collectives  47.2 us (4%)
  between operations  17.8 us (1%)
    ppermute x78, waiting for transfers between devices, dp_swap(): return lax.ppermute(value, 'dp', [(i, i ^ 1 << bit) for i in range(n)])  400 us
    dot_general x32, matrix products, dot(): lax.dot_general(a, b, (((ca,), (cb,)), ((), ())), preferred_element_type=...  228 us
    ppermute x78, starting transfers between devices, dp_swap(): return lax.ppermute(value, 'dp', [(i, i ^ 1 << bit) for i in range(n)])  91.6 us
    dot_general x4, local copies, waits for them, and re-layouts, dot(): lax.dot_general(a, b, (((ca,), (cb,)), ((), ())), preferred_element_type=...  66.2 us
    pallas_call x1, Pallas kernels, attn_backward(): pl.pallas_call(attn_bwd_kernel, grid=(blocks,), in_specs=[scalar, col, co...  64.2 us
    pallas_call x1, Pallas kernels, attn_forward(): pl.pallas_call(attn_fwd_kernel, grid=(blocks,), in_specs=[scalar, col, co...  63.3 us
    unnamed x212, local copies, waits for them, and re-layouts  29.4 us
  transfers between devices with their start and end apart: 98, of which 42 were waited for; matrix products, arithmetic and copies ran while one was open for 43% of the time, Pallas kernels for 5%

profile of v1, /device:TPU:0, one launch (start us, length us, event | category | flops | bytes accessed | tf_op | source)
XLA Modules:
  0.0 1284.4 jit_solution(9771119748057208516)
XLA Ops:
  14.1 24.7 %fusion.224 = (bf16[2048,1,1536]{2,1,0:T(2,128)(2,1)}, bf16[2048,1,1536]{2,1,0:T(2,128)(2,1)}) fusion(bf16[2048,2,1536]{2,1,0:T(2,128)(2,1)} %param.21), kind=kLoop, calls=%fused_computation.517 | loop fusion | bytes 25165824 | tf_op jit(solution)/shard_map/slice | solution.py:403
  38.9 29.6 %copy.242 = bf16[2048,1,1536]{0,2,1:T(8,128)(2,1)} copy(bf16[2048,1,1536]{2,1,0:T(2,128)(2,1)} %get-tuple-element.119) | data formatting | bytes 12582912 | tf_op jit(solution)/shard_map/dot_general | solution.py:25
  68.4 29.6 %copy.241 = bf16[2048,1,1536]{0,2,1:T(8,128)(2,1)} copy(bf16[2048,1,1536]{2,1,0:T(2,128)(2,1)} %get-tuple-element.120) | data formatting | bytes 12582912 | tf_op jit(solution)/shard_map/dot_general | solution.py:25
  116.2 14.8 %copy.177 = bf16[768,3,1536]{0,1,2:T(4,128)(2,1)} copy(bf16[768,3,1536]{2,0,1:T(8,128)(2,1)} %param.22) | data formatting | bytes 14155776 | tf_op args[8]
  209.5 63.3 %shard_map.221 = (bf16[1024,768]{1,0:T(8,128)(2,1)}, bf16[1024,768]{1,0:T(8,128)(2,1)}, bf16[1024,768]{1,0:T(8,128)(2,1)}, bf16[1024,768]{1,0:T(8,128)(2,1)}, f3...) custom-call(s32[1]{0:T(128)S(6)} %copy.314.len_ref, ...), custom_call_target="tpu_custom_call" | custom-call | flops 16106127360 | bytes 22020096 | tf_op jit(solution)/shard_map/pallas_call | solution.py:287
  290.0 19.1 %fusion.223 = (bf16[1536,1,2048]{2,1,0:T(2,128)(2,1)}, bf16[1536,1,2048]{2,1,0:T(2,128)(2,1)}) fusion(bf16[1536,2,2048]{2,1,0:T(2,128)(2,1)S(1)} %bitcast.652), kind=kLoop, calls=%fused_computation.516 | loop fusion | bytes 25165824 | tf_op jit(solution)/shard_map/slice | solution.py:435
  311.1 15.1 %all-reduce.1 = s32[16]{0:T(128)S(1)} all-reduce(s32[16]{0:T(128)S(1)} %dynamic-update-slice), channel_id=1, replica_groups=mesh['dp'=16,'fsdp'=2] {'dp'}, use_global_device_ids=true, to_apply=%add.1 | all-reduce | flops 16 | bytes 128
  328.3 13.2 %fusion.215 = f32[1024,2048]{1,0:T(8,128)} fusion(bf16[512,1536]{1,0:T(8,128)(2,1)} %collective-permute-done.7, bf16[512,1536]{1,0:T(8,128)(2,1)} %multiply_convert_fusion.7, bf16[1536,1,2048]{2,1,0:T(2,128)(2,1)} %get-tuple-element.118), kind=kOutput, calls=%fused_computation.514 | convolution fusion | flops 6448742400 | bytes 17825792 | tf_op jit(solution)/shard_map/dot_general | solution.py:25
  352.6 17.7 %multiply_convert_fusion = (bf16[1024,2048]{1,0:T(8,128)(2,1)}, bf16[1024,2048]{1,0:T(8,128)(2,1)}, bf16[1024,2048]{1,0:T(8,128)(2,1)}) fusion(f32[1024,2048]{1,0:T(8,128)} %fusion.216, f32[1024,2048]{1,0:T(8,128)} %fusion.215, bf16[2048,1536]{1,0:T(8,128)(2,1)} %param.27, bf16[512,1536]{1,0:T(8,128)(2,1)} %collective-permute-done.9, ...), kind=kOutput, calls=%fused_computation.1 | convolution fusion | flops 6483345408 | bytes 38803456 | tf_op jit(solution)/shard_map/dot_general | solution.py:25
  461.5 14.1 %multiply_reduce_fusion = (f32[1536]{0:T(1024)S(1)}, f32[512]{0:T(512)S(1)}, f32[1536]{0:T(1024)S(1)}, f32[512,1536]{1,0:T(8,128)}) fusion(f32[1536]{0:T(1024)S(1)} %copy-done.60, f32[512,1536]{1,0:T(8,128)S(1)} %copy-done.3, f32[512]{0:T(512)S(1)} %copy-done.71, f32[1536]{0:T(1024)S(1)} %copy-done.56, bf16[512,1536]{1,0:T(8,128)(2,1)} %copy-done.82, ...), kind=kOutput, calls=%fused_computation.75 | convolution fusion | flops 3231445504 | bytes 25718784 | tf_op jit(solution)/shard_map/dot_general | solution.py:25
  499.4 31.7 %collective-permute-done.87 = bf16[2,2,2,96,2048]{4,3,0,1,2:T(8,128)(2,1)} collective-permute-done((bf16[2,2,2,96,2048]{4,3,0,1,2:T(8,128)(2,1)}, bf16[2,2,2,96,2048]{4,3,0,1,2:T(8,128)(2,1)}, u32[]{:S(2)}, u32[]{:S(2)}) %collective-permute-start.87) | collective-permute-done | bytes 3145760 | tf_op jit(solution)/shard_map/ppermute | solution.py:70
  542.1 64.2 %shard_map.222 = (f32[1024,768]{1,0:T(8,128)}, f32[1024,768]{1,0:T(8,128)}, bf16[1024,768]{1,0:T(8,128)(2,1)}, f32[256,768]{1,0:T(8,128)}, f32[256,768]{1,0:T(8,...) custom-call(s32[1]{0:T(128)S(6)} %copy.314.len_ref, ...), custom_call_target="tpu_custom_call" | custom-call | flops 40265318400 | bytes 34603008 | tf_op jit(solution)/shard_map/pallas_call | solution.py:310
  662.5 14.8 %copy.204 = bf16[3,768,1536]{1,0,2:T(4,128)(2,1)} copy(bf16[3,768,1536]{2,1,0:T(8,128)(2,1)} %pad_maximum_fusion) | data formatting | bytes 14155776 | tf_op jit(solution)/shard_map/stack | solution.py:492
  677.2 20.2 %all_to_all.65 = bf16[3,768,1536]{1,0,2:T(4,128)(2,1)} all-to-all(bf16[3,768,1536]{1,0,2:T(4,128)(2,1)} %copy.204), channel_id=1, replica_groups=mesh['dp'=16,'fsdp'=2] {'fsdp'}, dimensions={2} | all-to-all | bytes 14155776 | tf_op jit(solution)/shard_map/all_to_all | solution.py:493
  737.6 15.0 %collective-permute-done.62 = bf16[2,2,2,96,384]{4,3,0,1,2:T(8,128)(2,1)S(1)} collective-permute-done((bf16[2,2,2,96,384]{4,3,0,1,2:T(8,128)(2,1)S(1)}, bf16[2,2,2,96,384]{4,3,0,1,2:T(8,128)(2,1)S(1)}, u32[]{:S(2)}, u32[]{:S(2)}) %collective-permute-start.62) | collective-permute-done | bytes 589856 | tf_op jit(solution)/shard_map/ppermute | solution.py:70
  826.4 22.3 %collective-permute-done.84 = bf16[2,2,96,2048]{3,2,0,1:T(8,128)(2,1)S(1)} collective-permute-done((bf16[2,2,96,2048]{3,2,0,1:T(8,128)(2,1)S(1)}, bf16[2,2,96,2048]{3,2,0,1:T(8,128)(2,1)S(1)}, u32[]{:S(2)}, u32[]{:S(2)}) %collective-permute-start.84) | collective-permute-done | bytes 1572896 | tf_op jit(solution)/shard_map/ppermute | solution.py:70
  932.4 17.5 %collective-permute-done.56 = bf16[2,96,768]{2,1,0:T(8,128)(2,1)S(1)} collective-permute-done((bf16[2,96,768]{2,1,0:T(8,128)(2,1)S(1)}, bf16[2,96,768]{2,1,0:T(8,128)(2,1)S(1)}, u32[]{:S(2)}, u32[]{:S(2)}) %collective-permute-start.56) | collective-permute-done | bytes 294944 | tf_op jit(solution)/shard_map/ppermute | solution.py:70
  989.6 14.1 %collective-permute-done.89 = bf16[2,96,2048]{2,1,0:T(8,128)(2,1)S(1)} collective-permute-done((bf16[2,96,2048]{2,1,0:T(8,128)(2,1)S(1)}, bf16[2,96,2048]{2,1,0:T(8,128)(2,1)S(1)}, u32[]{:S(2)}, u32[]{:S(2)}) %collective-permute-start.89) | collective-permute-done | bytes 786464 | tf_op jit(solution)/shard_map/ppermute | solution.py:70
  1032.0 16.9 %collective-permute-done.86 = bf16[96,2048]{1,0:T(8,128)(2,1)S(1)} collective-permute-done((bf16[96,2048]{1,0:T(8,128)(2,1)S(1)}, bf16[96,2048]{1,0:T(8,128)(2,1)S(1)}, u32[]{:S(2)}, u32[]{:S(2)}) %collective-permute-start.86) | collective-permute-done | bytes 393248 | tf_op jit(solution)/shard_map/ppermute | solution.py:70
  1049.0 16.7 %collective-permute-done.90 = bf16[96,2048]{1,0:T(8,128)(2,1)S(1)} collective-permute-done((bf16[96,2048]{1,0:T(8,128)(2,1)S(1)}, bf16[96,2048]{1,0:T(8,128)(2,1)S(1)}, u32[]{:S(2)}, u32[]{:S(2)}) %collective-permute-start.90) | collective-permute-done | bytes 393248 | tf_op jit(solution)/shard_map/ppermute | solution.py:70
  1071.2 17.9 %collective-permute-done.23 = bf16[2,2,2,2,256,96]{4,5,3,2,1,0:T(8,128)(2,1)S(1)} collective-permute-done((bf16[2,2,2,2,256,96]{4,5,3,2,1,0:T(8,128)(2,1)S(1)}, bf16[2,2,2,2,256,96]{4,5,3,2,1,0:T(8,128)(2,1)S(1)}, u32[]{:S(2)}, u32[]{:S(2)}) %collective-permute-start.23) | collective-permute-done | bytes 786464 | tf_op jit(solution)/shard_map/ppermute | solution.py:70
  1096.5 19.3 %collective-permute-done.26 = bf16[1,256,1024]{2,1,0:T(8,128)(2,1)S(1)} collective-permute-done((bf16[1,256,1024]{2,1,0:T(8,128)(2,1)}, bf16[1,256,1024]{2,1,0:T(8,128)(2,1)S(1)}, u32[]{:S(2)}, u32[]{:S(2)}) %collective-permute-start.26) | collective-permute-done | bytes 524320 | tf_op jit(solution)/shard_map/ppermute | solution.py:70
  1159.0 22.2 %collective-permute-done.37 = bf16[1,256,1024]{2,1,0:T(8,128)(2,1)S(1)} collective-permute-done((bf16[1,256,1024]{2,1,0:T(8,128)(2,1)S(1)}, bf16[1,256,1024]{2,1,0:T(8,128)(2,1)S(1)}, u32[]{:S(2)}, u32[]{:S(2)}) %collective-permute-start.37) | collective-permute-done | bytes 524320 | tf_op jit(solution)/shard_map/ppermute | solution.py:70
  1184.3 19.3 %collective-permute-done.36 = bf16[1,256,1024]{2,1,0:T(8,128)(2,1)S(1)} collective-permute-done((bf16[1,256,1024]{2,1,0:T(8,128)(2,1)S(1)}, bf16[1,256,1024]{2,1,0:T(8,128)(2,1)S(1)}, u32[]{:S(2)}, u32[]{:S(2)}) %collective-permute-start.36) | collective-permute-done | bytes 524320 | tf_op jit(solution)/shard_map/ppermute | solution.py:70
  (665 shorter events, 713.4 us)
Async XLA Ops:
  10.5 87.5 %all-to-all-start.1 = ((bf16[128,2,2048]{2,0,1:T(8,128)(2,1)}), bf16[128,2,2048]{2,0,1:T(8,128)(2,1)S(1)}, u32[]{:S(2)}, u32[]{:S(2)}) async-start(bf16[128,2,2048]{2,0,1:T(8,128)(2,1)} %copy.180), calls=%async_computation.1 | async-start | bytes 2097152 | tf_op jit(solution)/shard_map/all_to_all | solution.py:381
  109.9 61.5 %collective-permute-start.4 = (f32[2,256,768]{2,1,0:T(8,128)}, f32[2,256,768]{2,1,0:T(8,128)}, u32[]{:S(2)}, u32[]{:S(2)}) collective-permute-start(f32[2,256,768]{2,1,0:T(8,128)} %fusion.55), channel_id=1, source_target_pairs={{0,1},{1,0},{2,3},{3,2},{4,5},{5,4},{6,7},{7,6},{8,9},{9,8},{10,11... | collective-permute-start | bytes 4718600 | tf_op jit(solution)/shard_map/ppermute | solution.py:54
  115.6 55.1 %collective-permute-start = (f32[4,1536]{1,0:T(4,128)S(1)}, f32[4,1536]{1,0:T(4,128)S(1)}, u32[]{:S(2)}, u32[]{:S(2)}) collective-permute-start(f32[4,1536]{1,0:T(4,128)S(1)} %bitcast.739), channel_id=1, source_target_pairs={{0,1},{1,0},{2,3},{3,2},{4,5},{5,4},{6,7},{7,6},{8,9},{9,8},{10,11... | collective-permute-start | bytes 73736 | tf_op jit(solution)/shard_map/ppermute | solution.py:30
  115.7 59.8 %collective-permute-start.1 = (bf16[512,1536]{1,0:T(8,128)(2,1)}, bf16[512,1536]{1,0:T(8,128)(2,1)}, u32[]{:S(2)}, u32[]{:S(2)}) collective-permute-start(bf16[512,1536]{1,0:T(8,128)(2,1)} %bitcast), channel_id=1, source_target_pairs={{0,1},{1,0},{2,3},{3,2},{4,5},{5,4},{6,7},{7,6},{8,9},{9,8},{10,11... | collective-permute-start | bytes 4718600 | tf_op jit(solution)/shard_map/ppermute | solution.py:30
  138.5 714.2 %all-gather.2.cloned.1.call-start = ((), (), s32[]{:S(2)}) async-start(), calls=%async_computation.4 | async-start | bytes 2359296 | tf_op jit(solution)/shard_map/all_gather | solution.py:519
  276.0 76.7 %collective-permute-start.9 = (bf16[512,1536]{1,0:T(8,128)(2,1)}, bf16[512,1536]{1,0:T(8,128)(2,1)}, u32[]{:S(2)}, u32[]{:S(2)}) collective-permute-start(bf16[512,1536]{1,0:T(8,128)(2,1)} %bitcast.40), channel_id=1, source_target_pairs={{0,1},{1,0},{2,3},{3,2},{4,5},{5,4},{6,7},{7,6},{8,9},{9,8},{10,11... | collective-permute-start | bytes 4718600 | tf_op jit(solution)/shard_map/ppermute | solution.py:30
  277.2 812.4 %collective-permute-start.24 = (bf16[1,256,1024]{2,1,0:T(8,128)(2,1)}, bf16[1,256,1024]{2,1,0:T(8,128)(2,1)}, u32[]{:S(2)}, u32[]{:S(2)}) collective-permute-start(bf16[1,256,1024]{2,1,0:T(8,128)(2,1)} %get-tuple-element.157), channel_id=1, source_target_pairs={{0,16},{2,18},{4,20},{6,22},{8,24},{10,26},{12,28},{14,30},{16,0},... | collective-permute-start | bytes 1572872 | tf_op jit(solution)/shard_map/ppermute | solution.py:70
  392.1 94.9 %collective-permute-start.91 = (bf16[2,2,2,96,2048]{4,3,1,2,0:T(8,128)(2,1)}, bf16[2,2,2,96,2048]{4,3,1,2,0:T(8,128)(2,1)}, u32[]{:S(2)}, u32[]{:S(2)}) collective-permute-start(bf16[2,2,2,96,2048]{4,3,1,2,0:T(8,128)(2,1)} %bitcast.640), channel_id=1, source_target_pairs={{0,8},{2,10},{4,12},{6,14},{8,0},{10,2},{12,4},{14,6},{16,24},{18,... | collective-permute-start | bytes 9437192 | tf_op jit(solution)/shard_map/ppermute | solution.py:70
  418.9 73.8 %collective-permute-start.83 = (bf16[2,2,2,96,2048]{4,3,0,1,2:T(8,128)(2,1)}, bf16[2,2,2,96,2048]{4,3,0,1,2:T(8,128)(2,1)}, u32[]{:S(2)}, u32[]{:S(2)}) collective-permute-start(bf16[2,2,2,96,2048]{4,3,0,1,2:T(8,128)(2,1)} %bitcast.642), channel_id=1, source_target_pairs={{0,2},{2,0},{4,6},{6,4},{8,10},{10,8},{12,14},{14,12},{16,18},{18,... | collective-permute-start | bytes 9437192 | tf_op jit(solution)/shard_map/ppermute | solution.py:70
  461.0 70.1 %collective-permute-start.87 = (bf16[2,2,2,96,2048]{4,3,0,1,2:T(8,128)(2,1)}, bf16[2,2,2,96,2048]{4,3,0,1,2:T(8,128)(2,1)}, u32[]{:S(2)}, u32[]{:S(2)}) collective-permute-start(bf16[2,2,2,96,2048]{4,3,0,1,2:T(8,128)(2,1)} %bitcast.641), channel_id=1, source_target_pairs={{0,4},{2,6},{4,0},{6,2},{8,12},{10,14},{12,8},{14,10},{16,20},{18,... | collective-permute-start | bytes 9437192 | tf_op jit(solution)/shard_map/ppermute | solution.py:70
  484.3 51.4 %collective-permute-start.11 = (bf16[512,1536]{1,0:T(8,128)(2,1)}, bf16[512,1536]{1,0:T(8,128)(2,1)}, u32[]{:S(2)}, u32[]{:S(2)}) collective-permute-start(bf16[512,1536]{1,0:T(8,128)(2,1)} %multiply_convert_fusion.6), channel_id=1, source_target_pairs={{0,1},{1,0},{2,3},{3,2},{4,5},{5,4},{6,7},{7,6},{8,9},{9,8},{10,11... | collective-permute-start | bytes 4718600 | tf_op jit(solution)/shard_map/ppermute | solution.py:30
  492.5 330.7 %collective-permute-start.92 = (bf16[2,2,96,2048]{3,2,0,1:T(8,128)(2,1)}, bf16[2,2,96,2048]{3,2,0,1:T(8,128)(2,1)}, u32[]{:S(2)}, u32[]{:S(2)}) collective-permute-start(bf16[2,2,96,2048]{3,2,0,1:T(8,128)(2,1)} %dynamic-slice_bitcast_fusion), channel_id=1, source_target_pairs={{0,16},{2,18},{4,20},{6,22},{8,24},{10,26},{12,28},{14,30},{16,0},... | collective-permute-start | bytes 4718600 | tf_op jit(solution)/shard_map/ppermute | solution.py:70
  620.4 111.5 %collective-permute-start.70 = (bf16[2,2,2,96,384]{4,3,0,1,2:T(8,128)(2,1)}, bf16[2,2,2,96,384]{4,3,0,1,2:T(8,128)(2,1)}, u32[]{:S(2)}, u32[]{:S(2)}) collective-permute-start(bf16[2,2,2,96,384]{4,3,0,1,2:T(8,128)(2,1)} %bitcast.646), channel_id=1, source_target_pairs={{0,2},{2,0},{4,6},{6,4},{8,10},{10,8},{12,14},{14,12},{16,18},{18,... | collective-permute-start | bytes 1769480 | tf_op jit(solution)/shard_map/ppermute | solution.py:70
  630.2 104.6 %collective-permute-start.74 = (bf16[2,2,2,96,384]{4,3,0,1,2:T(8,128)(2,1)}, bf16[2,2,2,96,384]{4,3,0,1,2:T(8,128)(2,1)}, u32[]{:S(2)}, u32[]{:S(2)}) collective-permute-start(bf16[2,2,2,96,384]{4,3,0,1,2:T(8,128)(2,1)} %bitcast.645), channel_id=1, source_target_pairs={{0,4},{2,6},{4,0},{6,2},{8,12},{10,14},{12,8},{14,10},{16,20},{18,... | collective-permute-start | bytes 1769480 | tf_op jit(solution)/shard_map/ppermute | solution.py:70
  711.7 107.2 %collective-permute-start.54 = (bf16[2,2,2,96,768]{4,3,2,1,0:T(8,128)(2,1)}, bf16[2,2,2,96,768]{4,3,2,1,0:T(8,128)(2,1)}, u32[]{:S(2)}, u32[]{:S(2)}) collective-permute-start(bf16[2,2,2,96,768]{4,3,2,1,0:T(8,128)(2,1)} %dynamic-slice_bitcast_fusion.3), channel_id=1, source_target_pairs={{0,2},{2,0},{4,6},{6,4},{8,10},{10,8},{12,14},{14,12},{16,18},{18,... | collective-permute-start | bytes 3538952 | tf_op jit(solution)/shard_map/ppermute | solution.py:70
  768.1 50.1 %collective-permute-start.58 = (bf16[2,2,2,96,768]{4,3,0,1,2:T(8,128)(2,1)S(1)}, bf16[2,2,2,96,768]{4,3,0,1,2:T(8,128)(2,1)S(1)}, u32[]{:S(2)}, u32[]{:S(2)}) collective-permute-start(bf16[2,2,2,96,768]{4,3,0,1,2:T(8,128)(2,1)S(1)} %bitcast.723), channel_id=1, source_target_pairs={{0,4},{2,6},{4,0},{6,2},{8,12},{10,14},{12,8},{14,10},{16,20},{18,... | collective-permute-start | bytes 3538952 | tf_op jit(solution)/shard_map/ppermute | solution.py:70
  814.4 276.6 %collective-permute-start.25 = (bf16[1,256,1024]{2,1,0:T(8,128)(2,1)}, bf16[1,256,1024]{2,1,0:T(8,128)(2,1)}, u32[]{:S(2)}, u32[]{:S(2)}) collective-permute-start(bf16[1,256,1024]{2,1,0:T(8,128)(2,1)} %get-tuple-element.157), channel_id=1, source_target_pairs={{0,8},{2,10},{4,12},{6,14},{8,0},{10,2},{12,4},{14,6},{16,24},{18,... | collective-permute-start | bytes 1572872 | tf_op jit(solution)/shard_map/ppermute | solution.py:70
  848.7 75.6 %collective-permute-start.55 = (bf16[2,2,96,768]{3,2,1,0:T(8,128)(2,1)}, bf16[2,2,96,768]{3,2,1,0:T(8,128)(2,1)}, u32[]{:S(2)}, u32[]{:S(2)}) collective-permute-start(bf16[2,2,96,768]{3,2,1,0:T(8,128)(2,1)} %dynamic-slice_bitcast_fusion.8), channel_id=1, source_target_pairs={{0,4},{2,6},{4,0},{6,2},{8,12},{10,14},{12,8},{14,10},{16,20},{18,... | collective-permute-start | bytes 1769480 | tf_op jit(solution)/shard_map/ppermute | solution.py:70
  922.4 53.0 %collective-permute-start.93 = (bf16[2,96,2048]{2,1,0:T(8,128)(2,1)}, bf16[2,96,2048]{2,1,0:T(8,128)(2,1)S(1)}, u32[]{:S(2)}, u32[]{:S(2)}) collective-permute-start(bf16[2,96,2048]{2,1,0:T(8,128)(2,1)} %dynamic-slice_bitcast_fusion.4), channel_id=1, source_target_pairs={{0,2},{2,0},{4,6},{6,4},{8,10},{10,8},{12,14},{14,12},{16,18},{18,... | collective-permute-start | bytes 2359304 | tf_op jit(solution)/shard_map/ppermute | solution.py:70
  924.2 65.0 %collective-permute-start.85 = (bf16[2,96,2048]{2,1,0:T(8,128)(2,1)}, bf16[2,96,2048]{2,1,0:T(8,128)(2,1)S(1)}, u32[]{:S(2)}, u32[]{:S(2)}) collective-permute-start(bf16[2,96,2048]{2,1,0:T(8,128)(2,1)} %dynamic-slice_bitcast_fusion.6), channel_id=1, source_target_pairs={{0,8},{2,10},{4,12},{6,14},{8,0},{10,2},{12,4},{14,6},{16,24},{18,... | collective-permute-start | bytes 2359304 | tf_op jit(solution)/shard_map/ppermute | solution.py:70
  975.4 118.9 %collective-permute-start.27 = (bf16[1,256,1024]{2,1,0:T(8,128)(2,1)}, bf16[1,256,1024]{2,1,0:T(8,128)(2,1)S(1)}, u32[]{:S(2)}, u32[]{:S(2)}) collective-permute-start(bf16[1,256,1024]{2,1,0:T(8,128)(2,1)} %get-tuple-element.157), channel_id=1, source_target_pairs={{0,4},{2,6},{4,0},{6,2},{8,12},{10,14},{12,8},{14,10},{16,20},{18,... | collective-permute-start | bytes 1572872 | tf_op jit(solution)/shard_map/ppermute | solution.py:70
  1065.7 66.6 %collective-permute-start.31 = (bf16[1,256,1024]{2,1,0:T(8,128)(2,1)}, bf16[1,256,1024]{2,1,0:T(8,128)(2,1)S(1)}, u32[]{:S(2)}, u32[]{:S(2)}) collective-permute-start(bf16[1,256,1024]{2,1,0:T(8,128)(2,1)} %get-tuple-element.157), channel_id=1, source_target_pairs={{0,2},{2,0},{4,6},{6,4},{8,10},{10,8},{12,14},{14,12},{16,18},{18,... | collective-permute-start | bytes 1572872 | tf_op jit(solution)/shard_map/ppermute | solution.py:70
  1089.1 92.3 %collective-permute-start.39 = (bf16[1,256,1024]{2,1,0:T(8,128)(2,1)S(1)}, bf16[1,256,1024]{2,1,0:T(8,128)(2,1)S(1)}, u32[]{:S(2)}, u32[]{:S(2)}) collective-permute-start(bf16[1,256,1024]{2,1,0:T(8,128)(2,1)S(1)} %copy-done.50), channel_id=1, source_target_pairs={{0,16},{2,18},{4,20},{6,22},{8,24},{10,26},{12,28},{14,30},{16,0},... | collective-permute-start | bytes 1572872 | tf_op jit(solution)/shard_map/ppermute | solution.py:70
  1089.6 93.3 %collective-permute-start.40 = (bf16[1,256,1024]{2,1,0:T(8,128)(2,1)S(1)}, bf16[1,256,1024]{2,1,0:T(8,128)(2,1)S(1)}, u32[]{:S(2)}, u32[]{:S(2)}) collective-permute-start(bf16[1,256,1024]{2,1,0:T(8,128)(2,1)S(1)} %copy-done.50), channel_id=1, source_target_pairs={{0,8},{2,10},{4,12},{6,14},{8,0},{10,2},{12,4},{14,6},{16,24},{18,... | collective-permute-start | bytes 1572872 | tf_op jit(solution)/shard_map/ppermute | solution.py:70
  (178 other events, 3657.4 us)
Sparse Core Ops, SparseCore 0:
  632.3 8.1 all-gather.1

commit v2 on v1

v2 whole, which is shorter than its diff:
```python
import functools
import math

import jax
import jax.numpy as jnp
from jax import lax
from jax.experimental import pallas as pl
from jax.experimental.pallas import tpu as pltpu
from jax.sharding import PartitionSpec as P

D = 1536
HEADS = 24
HD = 64
TW = 4096
TE = 1024
PATCHES = 1024
TEXT = 256
EPSILON = 1e-06
F32 = jnp.float32
BF16 = jnp.bfloat16
QC = 256


def dot(a, b, ca=1, cb=0):
    return lax.dot_general(a, b, (((ca,), (cb,)), ((), ())), preferred_element_type=F32)


def from_behind(value, step):
    n = lax.axis_size("fsdp")
    return lax.ppermute(value, "fsdp", [(i, (i + step) % n) for i in range(n)])


def gather_rot(value):
    return [value] + [from_behind(value, r) for r in range(1, lax.axis_size("fsdp"))]


def pair_sum(value):
    return functools.reduce(lambda a, b: a + b, gather_rot(value))


def row_sum(value):
    n = lax.axis_size("fsdp")
    rows = value.shape[-1] // n
    total = value
    for r in range(1, n):
        total = total + jnp.roll(from_behind(value, r), r * rows, axis=-1)
    return total


def scatter_rot(blocks):
    n = lax.axis_size("fsdp")
    total = blocks[0].astype(F32)
    for r in range(1, n):
        got = lax.ppermute(blocks[r], "fsdp", [(i, (i - r) % n) for i in range(n)])
        total = total + got.astype(F32)
    return total


def rot_blocks(value, axis):
    n, f = lax.axis_size("fsdp"), lax.axis_index("fsdp")
    return [lax.dynamic_index_in_dim(value, (f - r) % n, axis, keepdims=False) for r in range(n)]


def exchange_rot(value, axis):
    n, f = lax.axis_size("fsdp"), lax.axis_index("fsdp")
    out = []
    for r in range(n):
        send = lax.dynamic_index_in_dim(value, (f + r) % n, axis, keepdims=False)
        out.append(from_behind(send, r) if r else send)
    return out


def gather_natural(value):
    n, f = lax.axis_size("fsdp"), lax.axis_index("fsdp")
    blocks = jnp.stack(gather_rot(value))
    order = [lax.dynamic_index_in_dim(blocks, (f - g) % n, 0, keepdims=False) for g in range(n)]
    return jnp.concatenate(order, axis=-1)


def exchange(value):
    n, f = lax.axis_size("fsdp"), lax.axis_index("fsdp")
    sends = rot_blocks(value, 0)
    got = [sends[0]]
    for r in range(1, n):
        got.append(lax.ppermute(sends[r], "fsdp", [(i, (i - r) % n) for i in range(n)]))
    if n == 2:
        return [jnp.where(f == 0, got[0], got[1]), jnp.where(f == 0, got[1], got[0])]
    got = jnp.stack(got)
    return [lax.dynamic_index_in_dim(got, (g - f) % n, 0, keepdims=False) for g in range(n)]


def dp_bits():
    return int(lax.axis_size("dp")).bit_length() - 1


def dp_swap(value, bit):
    n = lax.axis_size("dp")
    return lax.ppermute(value, "dp", [(i, i ^ (1 << bit)) for i in range(n)])


def orders():
    bits = list(range(dp_bits()))
    return bits, bits[:2][::-1] + bits[2:], bits[2:3] + bits[:2][::-1] + bits[3:]


def split_bit(value, axis, bit):
    mine = (lax.axis_index("dp") >> bit) & 1
    keep = lax.dynamic_index_in_dim(value, mine, axis, keepdims=False)
    send = lax.dynamic_index_in_dim(value, 1 - mine, axis, keepdims=False)
    return keep, send


class Halving:
    def __init__(self, value, order, flip=0):
        nb = dp_bits()
        self.cur = value.reshape((2,) * nb + value.shape[1:])
        self.labels = list(range(nb))[::-1]
        self.order, self.flip = list(order), flip
        self.keep = self.got = None
        self.start()

    def start(self):
        if not self.order:
            return
        bit = self.order.pop(0)
        axis = self.labels.index(bit)
        mine = (lax.axis_index("dp") >> bit) & 1
        if bit == dp_bits() - 1:
            mine = mine ^ self.flip
        self.labels.remove(bit)
        self.keep = lax.dynamic_index_in_dim(self.cur, mine, axis, keepdims=False)
        send = lax.dynamic_index_in_dim(self.cur, 1 - mine, axis, keepdims=False)
        self.got = dp_swap(send, bit)

    def step(self):
        if self.got is None:
            return
        total = self.keep.astype(F32) + self.got.astype(F32)
        self.cur = total.astype(BF16) if self.order else total
        self.got = None
        self.start()


def advance(chains, value):
    live = [c for c in chains if c.got is not None]
    value, got = lax.optimization_barrier((value, [c.got for c in live]))
    for c, g in zip(live, got):
        c.got = g
        c.step()
    return value


def dp_exchange(value, order):
    nb = dp_bits()
    cur = value.reshape((2,) * nb + value.shape[1:])
    for bit in order:
        axis = nb - 1 - bit
        keep, send = split_bit(cur, axis, bit)
        cur = jnp.stack([keep, dp_swap(send, bit)], axis=axis)
    return cur.reshape(value.shape)


def dp_total(value):
    for bit in range(dp_bits()):
        value = value + dp_swap(value, bit)
    return value


def rope_block(value, cosine, sine, sign):
    width = value.shape[1]
    lane = lax.broadcasted_iota(jnp.int32, value.shape, 1)
    partner = jnp.where(
        lane % 32 < 16, pltpu.roll(value, width - 16, 1), pltpu.roll(value, 16, 1)
    )
    return value * cosine + sign * (partner * sine)


def masked(value, head):
    lane = lax.broadcasted_iota(jnp.int32, value.shape, 1)
    return jnp.where(lane // HD == head, value, jnp.zeros_like(value))


def attn_fwd_kernel(
    len_ref, qp_ref, kp_ref, vp_ref, iq_ref, ik_ref, gq_ref, gk_ref, cos_ref, sin_ref,
    tk_ref, tv_ref, gate_ref,
    q_ref, k_ref, v_ref, mixed_ref, so_ref, co_ref, ls_ref, lc_ref,
):
    tokens, width = qp_ref.shape
    heads = width // HD
    q = rope_block(qp_ref[...] * iq_ref[...] * gq_ref[...], cos_ref[...], sin_ref[...], 1.0)
    q_ref[...] = q.astype(BF16)
    k = rope_block(kp_ref[...] * ik_ref[...] * gk_ref[...], cos_ref[...], sin_ref[...], 1.0)
    k_ref[...] = k.astype(BF16)
    v_ref[...] = vp_ref[...].astype(BF16)
    length = len_ref[0]

    def one(keys, values, qm, limit):
        s = dot(qm, keys, 1, 1)
        if limit is not None:
            slot = lax.broadcasted_iota(jnp.int32, s.shape, 1)
            s = jnp.where(slot < limit, s, -1e30)
        peak = jnp.max(s, axis=1, keepdims=True)
        e = jnp.exp(s - peak)
        total = jnp.sum(e, axis=1, keepdims=True)
        o = dot(e.astype(BF16), values)
        return o * (1.0 / total), peak + jnp.log(total)

    lane = lax.broadcasted_iota(jnp.int32, (tokens, width), 1)
    qs = q_ref[...] * jnp.asarray(HD**-0.5, BF16)
    so = co = stats = jnp.zeros((tokens, width), F32)
    for h in range(heads):
        qm = masked(qs, h)
        o, lse = one(k_ref[...], v_ref[...], qm, None)
        so = jnp.where(lane // HD == h, o, so)
        stats = jnp.where(lane == h, lse, stats)
        o, lse = one(tk_ref[...], tv_ref[...], qm, length)
        co = jnp.where(lane // HD == h, o, co)
        stats = jnp.where(lane == heads + h, lse, stats)
    so_ref[...] = so
    co_ref[...] = co
    mixed_ref[...] = (so + gate_ref[...] * co).astype(BF16)
    stats = stats.T
    ls_ref[0] = stats[:heads]
    lc_ref[0] = stats[heads : 2 * heads]


def attn_bwd_kernel(
    len_ref, q_ref, k_ref, v_ref, tk_ref, tv_ref, g_ref, so_ref, co_ref, ls_ref, lc_ref,
    qp_ref, kp_ref, iq_ref, ik_ref, gq_ref, gk_ref, cos_ref, sin_ref, gate_ref,
    dq_ref, dk_ref, dv_ref, dtk_ref, dtv_ref, rq_ref, rk_ref, gainq_ref, gaink_ref, gateg_ref,
    gs_ref, gc_ref, ds_ref, dc_ref, kt_ref, tkt_ref, dqt_ref, dk_acc, dv_acc,
):
    tokens, width = q_ref.shape
    heads = width // HD
    scale = jnp.asarray(HD**-0.5, BF16)

    @pl.when(pl.program_id(0) == 0)
    def _():
        rq_ref[...] = jnp.zeros_like(rq_ref)
        rk_ref[...] = jnp.zeros_like(rk_ref)

    g = g_ref[...]
    gs_ref[...] = g.astype(BF16)
    gc_ref[...] = (g * gate_ref[...]).astype(BF16)
    prod_c = g * co_ref[...]
    gateg_ref[...] = jnp.sum(prod_c, axis=0, keepdims=True)
    prod_s = (g * so_ref[...]).T
    prod_c = (prod_c * gate_ref[...]).T
    for h in range(heads):
        ds_ref[h : h + 1, :] = jnp.sum(prod_s[h * HD : (h + 1) * HD], axis=0, keepdims=True)
        dc_ref[h : h + 1, :] = jnp.sum(prod_c[h * HD : (h + 1) * HD], axis=0, keepdims=True)
    kt_ref[...] = k_ref[...].astype(F32).T.astype(BF16)
    tkt_ref[...] = tk_ref[...].astype(F32).T.astype(BF16)
    dk_acc[...] = jnp.zeros_like(dk_acc)
    dv_acc[...] = jnp.zeros_like(dv_acc)
    dtk_ref[...] = jnp.zeros_like(dtk_ref)
    dtv_ref[...] = jnp.zeros_like(dtv_ref)
    length = len_ref[0]

    def one(keys, keys_t, values, qm, gm, lse, delta, head, limit):
        s = dot(keys, qm, 1, 1)
        p = jnp.exp(s - lse)
        if limit is not None:
            slot = lax.broadcasted_iota(jnp.int32, s.shape, 0)
            p = jnp.where(slot < limit, p, 0.0)
        dp = dot(values, gm, 1, 1)
        ds = (p * (dp - delta)).astype(BF16)
        dq = dot(keys_t[head * HD : (head + 1) * HD, :], ds)
        return dq, dot(ds, qm), dot(p.astype(BF16), gm)

    def chunk(c, carry):
        rows = pl.ds(pl.multiple_of(c * QC, QC), QC)
        qc = q_ref[rows, :] * scale
        for h in range(heads):
            qm = masked(qc, h)
            dq, dk, dv = one(
                k_ref[...], kt_ref, v_ref[...], qm, masked(gs_ref[rows, :], h),
                ls_ref[0, h : h + 1, rows], ds_ref[h : h + 1, rows], h, None,
            )
            dk_acc[...] += dk
            dv_acc[...] += dv
            dq2, dk, dv = one(
                tk_ref[...], tkt_ref, tv_ref[...], qm, masked(gc_ref[rows, :], h),
                lc_ref[0, h : h + 1, rows], dc_ref[h : h + 1, rows], h, length,
            )
            dtk_ref[...] += dk
            dtv_ref[...] += dv
            dqt_ref[h * HD : (h + 1) * HD, rows] = (dq + dq2) * HD**-0.5
        return carry

    lax.fori_loop(0, tokens // QC, chunk, 0)
    dq = rope_block(dqt_ref[...].T, cos_ref[...], sin_ref[...], -1.0)
    dq_ref[...] = dq
    prod = dq * (qp_ref[...] * iq_ref[...])
    gainq_ref[...] = jnp.sum(prod, axis=0, keepdims=True)
    rq_ref[...] += prod * gq_ref[...]
    dk = rope_block(dk_acc[...], cos_ref[...], sin_ref[...], -1.0)
    dk_ref[...] = dk
    prod = dk * (kp_ref[...] * ik_ref[...])
    gaink_ref[...] = jnp.sum(prod, axis=0, keepdims=True)
    rk_ref[...] += prod * gk_ref[...]
    dv_ref[...] = dv_acc[...].astype(BF16)


def specs(tokens, text, width, heads):
    col = pl.BlockSpec((tokens, width), lambda i: (0, i))
    tcol = pl.BlockSpec((text, width), lambda i: (0, i))
    stat = pl.BlockSpec((tokens, 1), lambda i: (0, 0))
    gain = pl.BlockSpec((1, width), lambda i: (0, i))
    table = pl.BlockSpec((tokens, width), lambda i: (0, 0))
    lse = pl.BlockSpec((1, heads, tokens), lambda i: (i, 0, 0))
    scalar = pl.BlockSpec(memory_space=pltpu.SMEM)
    return col, tcol, stat, gain, table, lse, scalar


def sds(shape, dtype=F32):
    return jax.ShapeDtypeStruct(shape, dtype)


def attn_forward(length, qp, kp, vp, iq, ik, gq, gk, cosine, sine, tk, tv, gate):
    tokens, columns = qp.shape
    text, width = tk.shape[0], cosine.shape[1]
    heads, blocks = width // HD, columns // width
    col, tcol, stat, gain, table, lse, scalar = specs(tokens, text, width, heads)
    return pl.pallas_call(
        attn_fwd_kernel,
        grid=(blocks,),
        in_specs=[scalar, col, col, col, stat, stat, gain, gain, table, table, tcol, tcol, gain],
        out_specs=[col, col, col, col, col, col, lse, lse],
        out_shape=[
            sds(qp.shape, BF16), sds(qp.shape, BF16), sds(qp.shape, BF16), sds(qp.shape, BF16),
            sds(qp.shape), sds(qp.shape),
            sds((blocks, heads, tokens)), sds((blocks, heads, tokens)),
        ],
    )(length, qp, kp, vp, iq, ik, gq, gk, cosine, sine, tk, tv, gate)


def attn_backward(length, q, k, v, tk, tv, g, so, co, ls, lc, qp, kp, iq, ik, gq, gk, cosine, sine, gate):
    tokens, columns = q.shape
    text, width = tk.shape[0], cosine.shape[1]
    heads, blocks = width // HD, columns // width
    col, tcol, stat, gain, table, lse, scalar = specs(tokens, text, width, heads)
    return pl.pallas_call(
        attn_bwd_kernel,
        grid=(blocks,),
        in_specs=[scalar, col, col, col, tcol, tcol, col, col, col, lse, lse,
                  col, col, stat, stat, gain, gain, table, table, gain],
        out_specs=[col, col, col, tcol, tcol, table, table, gain, gain, gain],
        out_shape=[
            sds(q.shape), sds(q.shape), sds(q.shape, BF16), sds(tk.shape), sds(tk.shape),
            sds((tokens, width)), sds((tokens, width)),
            sds((1, columns)), sds((1, columns)), sds((1, columns)),
        ],
        scratch_shapes=[
            pltpu.VMEM((tokens, width), BF16), pltpu.VMEM((tokens, width), BF16),
            pltpu.VMEM((heads, tokens), F32), pltpu.VMEM((heads, tokens), F32),
            pltpu.VMEM((width, tokens), BF16), pltpu.VMEM((width, text), BF16),
            pltpu.VMEM((width, tokens), F32),
            pltpu.VMEM((tokens, width), F32), pltpu.VMEM((tokens, width), F32),
        ],
    )(length, q, k, v, tk, tv, g, so, co, ls, lc, qp, kp, iq, ik, gq, gk, cosine, sine,
      gate)


def pick(rows, cols, step, part):
    i = lax.broadcasted_iota(jnp.int32, (rows, cols), 0)
    j = lax.broadcasted_iota(jnp.int32, (rows, cols), 1)
    hit = (j == step * i + part) if cols > rows else (i == step * j + part)
    return jnp.where(hit, 1.0, 0.0).astype(BF16)

def text_fwd_kernel(x_ref, w_ref, o_ref):
    @pl.when(pl.program_id(0) == 0)
    def _():
        o_ref[...] = jnp.zeros_like(o_ref)
    for b in range(w_ref.shape[0] // 128):
        rows = slice(b * 128, (b + 1) * 128)
        w = w_ref[rows].reshape(256, w_ref.shape[2])
        x = x_ref[:, rows]
        for j in range(2):
            spread = dot(x, pick(128, 256, 2, j)).astype(BF16)
            o_ref[j] += dot(spread, w)

def text_fwd(x, w):
    depth, _, cols = w.shape
    bk = 256
    return pl.pallas_call(
        text_fwd_kernel, grid=(depth // bk,),
        in_specs=[pl.BlockSpec((x.shape[0], bk), lambda i: (0, i)), pl.BlockSpec((bk, 2, cols), lambda i: (i, 0, 0))],
        out_specs=pl.BlockSpec((2, x.shape[0], cols), lambda i: (0, 0, 0)),
        out_shape=sds((2, x.shape[0], cols)),
    )(x, w)

def text_bwd_kernel(g_ref, w_ref, o_ref):
    for b in range(w_ref.shape[0] // 128):
        rows = slice(b * 128, (b + 1) * 128)
        w = w_ref[rows].reshape(256, w_ref.shape[2])
        total = 0.0
        for j in range(2):
            total = total + dot(g_ref[j], dot(pick(128, 256, 2, j), w).astype(BF16), 1, 1)
        o_ref[:, rows] = total.astype(BF16)

def text_bwd(g, w):
    depth, _, cols = w.shape
    bk = 256
    return pl.pallas_call(
        text_bwd_kernel, grid=(depth // bk,),
        in_specs=[pl.BlockSpec(g.shape, lambda i: (0, 0, 0)), pl.BlockSpec((bk, 2, cols), lambda i: (i, 0, 0))],
        out_specs=pl.BlockSpec((g.shape[1], bk), lambda i: (0, i)),
        out_shape=sds((g.shape[1], depth), BF16),
    )(g, w)

def ffn_kernel(
    s_ref, b_ref, w_ref, d_ref, wgo_ref, wuo_ref, wdo_ref, fo_ref, fp_ref, so_ref, sp_ref,
    st, bt, wg, wu, facc, sacc,
):
    step = pl.program_id(0)
    depth, _, cols = w_ref.shape
    own = fo_ref.shape[0]
    @pl.when(step == 0)
    def _():
        for c in range(depth // 256):
            part = slice(c * 256, (c + 1) * 256)
            st[part, :] = s_ref[:, part].astype(F32).T.astype(BF16)
            bt[part, :] = b_ref[:, part].astype(F32).T.astype(BF16)
        facc[...] = jnp.zeros_like(facc)
        sacc[...] = jnp.zeros_like(sacc)
    for c in range(depth // 128):
        part = slice(c * 128, (c + 1) * 128)
        w = w_ref[part].reshape(256, cols)
        wg[part, :] = dot(pick(128, 256, 2, 0), w).astype(BF16)
        wu[part, :] = dot(pick(128, 256, 2, 1), w).astype(BF16)
    s, b = s_ref[...], b_ref[...]
    gate = dot(s, wg[...])
    up = dot(s, wu[...])
    back = dot(b, d_ref[...], 1, 1)
    sig = jax.nn.sigmoid(gate)
    silu = gate * sig
    hidden = (silu * up).astype(BF16)
    g_gate = (back * up * (sig + silu * (1.0 - sig))).astype(BF16)
    g_up = (back * silu).astype(BF16)
    dp, rows, _ = wgo_ref.shape
    for out, left, right in ((wgo_ref, st, g_gate), (wuo_ref, st, g_up), (wdo_ref, bt, hidden)):
        out[...] = dot(left[...], right).astype(BF16).reshape(dp, rows, cols)
    facc[...] += dot(hidden, d_ref[...])
    sacc[...] += dot(g_gate, wg[...], 1, 1) + dot(g_up, wu[...], 1, 1)
    @pl.when(step == pl.num_programs(0) - 1)
    def _():
        fo_ref[...] = facc[:own]
        fp_ref[...] = facc[own:].astype(BF16)
        so_ref[...] = sacc[:own]
        sp_ref[...] = sacc[own:].astype(BF16)

def ffn(s, b, w, d, local, dp):
    tokens, depth = s.shape
    hid = d.shape[0]
    bc = min(256, hid)
    rest = max(tokens - local, 8)
    once = functools.partial(pl.BlockSpec, pipeline_mode=pl.Buffered(1))
    const = lambda i: (0, 0)
    return pl.pallas_call(
        ffn_kernel, grid=(hid // bc,),
        in_specs=[once((tokens, depth), const), once((tokens, depth), const),
                  pl.BlockSpec((depth, 2, bc), lambda i: (0, 0, i)), pl.BlockSpec((bc, depth), lambda i: (i, 0))],
        out_specs=[pl.BlockSpec((dp, depth // dp, bc), lambda i: (0, 0, i))] * 3 + [
                   once((local, depth), const), once((rest, depth), const), once((local, depth), const), once((rest, depth), const)],
        out_shape=[sds((dp, depth // dp, hid), BF16)] * 3 + [sds((local, depth)), sds((rest, depth), BF16), sds((local, depth)), sds((rest, depth), BF16)],
        scratch_shapes=[pltpu.VMEM((depth, tokens), BF16)] * 2 + [pltpu.VMEM((depth, bc), BF16)] * 2 + [pltpu.VMEM((tokens, depth), F32)] * 2,
        compiler_params=pltpu.CompilerParams(vmem_limit_bytes=62 << 20),
    )(s, b, w, d)


def time_embed(timesteps):
    half = TE // 2
    frequencies = jnp.exp(-math.log(10000.0) * jnp.arange(half, dtype=F32) / half)
    angles = timesteps.astype(F32)[:, None] * frequencies
    waves = jnp.concatenate([jnp.cos(angles), jnp.sin(angles)], axis=-1)
    return jax.nn.silu(waves).astype(BF16)


def rope_tables(positions, width):
    lane = jnp.arange(width)
    quarter = HD // 4
    frequencies = 10000.0 ** (-(lane % quarter).astype(F32) / quarter)
    place = jnp.where(lane % HD < HD // 2, positions[0][:, None], positions[1][:, None])
    angles = place.astype(F32) * frequencies
    return jnp.cos(angles), jnp.where(lane % 32 < 16, -1.0, 1.0) * jnp.sin(angles)


def inverse_rms(values):
    return lax.rsqrt(jnp.mean(values * values, axis=-1, keepdims=True) + EPSILON)


def rms_back(grad_hat, normed, inverse):
    return inverse * (grad_hat - normed * jnp.mean(grad_hat * normed, axis=-1, keepdims=True))


def pad_cols(value, width):
    extra = -value.shape[-1] % width
    return value if extra == 0 else jnp.pad(value, [(0, 0)] * (value.ndim - 1) + [(0, extra)])


def on_device(
    hidden_in, text_state, caption_lengths, timesteps, patch_positions, cotangent,
    w_ada, w_text, w_qkv, w_out, gains, cross_gate, w_gate_up, w_down,
):
    n, f = lax.axis_size("fsdp"), lax.axis_index("fsdp")
    dpn, me = lax.axis_size("dp"), lax.axis_index("dp")
    order_a, order_b, order_c = orders()
    own_d = D // n
    local = hidden_in.shape[1]
    width = 2 * HD
    share = D // dpn
    x_bf, dy_bf = hidden_in[0], cotangent[0]

    time_low = time_embed(timesteps)
    own_te = TE // n
    time_own = lax.dynamic_slice_in_dim(time_low[0], f * own_te, own_te, 0)
    modulation = pair_sum(
        jnp.einsum("k,kjd->jd", time_own, w_ada, preferred_element_type=F32)
    )
    scale_attn, gate_attn = modulation[0:1], jnp.tanh(modulation[1:2])
    scale_ffn, gate_ffn = modulation[2:3], jnp.tanh(modulation[3:4])

    x_all = jnp.concatenate(gather_rot(x_bf), axis=0)
    dy_all = jnp.concatenate(gather_rot(dy_bf), axis=0)
    places = jnp.concatenate(gather_rot(patch_positions[0]), axis=1)
    w_parts = exchange_rot(jnp.moveaxis(w_qkv, 1, 0).reshape(3, own_d, n, own_d), 2)
    w_heads = jnp.concatenate(w_parts, axis=1)
    text_cols = exchange(jnp.moveaxis(text_state[0].reshape(-1, n, TW // n), 1, 0))
    text_cols = jnp.concatenate(text_cols, axis=0)
    text_all = lax.all_gather(text_cols, "dp", axis=0, tiled=True)
    gain_full = lax.all_gather(gains, "fsdp", axis=1, tiled=True).astype(F32)
    gain_own = gains.astype(F32)
    times_all = timesteps
    for bit in range(dp_bits()):
        times_all = jnp.concatenate([times_all, dp_swap(times_all, bit)])

    x_f = x_all.astype(F32)
    inverse_all = inverse_rms(x_f)
    x_rot = jnp.concatenate(rot_blocks(x_all.reshape(-1, n, own_d), 1), axis=1).astype(F32)
    front = (gain_full[0] * (1.0 + scale_attn)).reshape(1, n, own_d)
    front = jnp.concatenate(rot_blocks(front, 1), axis=1)
    first_all = (x_rot * inverse_all * front).astype(BF16)
    q_pre, k_pre, v_pre = (dot(first_all, w_heads[j]) for j in range(3))
    squares = row_sum(jnp.stack([jnp.sum(q_pre * q_pre, -1), jnp.sum(k_pre * k_pre, -1)]))
    inverse = lax.rsqrt(squares / D + EPSILON)
    inv_q, inv_k = inverse[0][:, None], inverse[1][:, None]

    text_part = text_fwd(text_cols, w_text)
    text_pre = scatter_rot(rot_blocks(text_part.reshape(2, TEXT, n, own_d), 2))
    inv_t = lax.rsqrt(
        pair_sum(jnp.sum(text_pre[0] * text_pre[0], -1, keepdims=True)) / D + EPSILON
    )
    normed_t = text_pre[0] * inv_t
    tk = (normed_t * gain_own[4]).astype(BF16)
    tv = text_pre[1].astype(BF16)

    head_tanh = jnp.tanh(cross_gate.astype(F32))
    gate_row = pad_cols(jnp.repeat(head_tanh, HD)[None], width)
    cosine, sine = rope_tables(places, width)
    gq, gk = pad_cols(gain_own[2:3], width), pad_cols(gain_own[3:4], width)
    qp, kp, vp = (pad_cols(v, width) for v in (q_pre, k_pre, v_pre))
    tkp, tvp = pad_cols(tk, width), pad_cols(tv, width)
    q, k, v, mixed_p, so, co, ls, lc = attn_forward(
        caption_lengths, qp, kp, vp, inv_q, inv_k, gq, gk, cosine, sine, tkp, tvp, gate_row
    )
    mixed = mixed_p[:, :own_d]

    def rows(value, r):
        return value[r * local : (r + 1) * local]

    parts = [dot(rows(mixed, r), w_out) for r in range(n)]
    attn_branch = scatter_rot([parts[0]] + [p.astype(BF16) for p in parts[1:]])
    x_own = x_bf.astype(F32)
    after_attn = x_own + gate_attn * attn_branch
    inverse_two = inverse_rms(after_attn)
    normed_two = after_attn * inverse_two
    second = (normed_two * gain_full[1] * (1.0 + scale_ffn)).astype(BF16)

    second_all = jnp.concatenate(gather_rot(second), axis=0)
    branch_all = (gate_ffn * dy_all.astype(F32)).astype(BF16)
    d_gate, d_up, d_down, ffn_own, ffn_rest, back_own, back_rest = ffn(
        second_all, branch_all, w_gate_up, w_down, local, dpn
    )
    chains = [Halving(d_gate, order_a), Halving(d_up, order_b), Halving(d_down, order_c)]
    gate_chain, up_chain, down_chain = chains
    grad_second = scatter_rot([back_own] + [rows(back_rest, r) for r in range(n - 1)])
    ffn_branch = scatter_rot([ffn_own] + [rows(ffn_rest, r) for r in range(n - 1)])
    output = (after_attn + gate_ffn * ffn_branch).astype(BF16)
    dy = dy_bf.astype(F32)
    d_gate_ffn = jnp.sum(dy * ffn_branch, axis=0) * (1.0 - gate_ffn[0] * gate_ffn[0])

    scaled = grad_second * normed_two
    d_scale_ffn = jnp.sum(scaled * gain_full[1], axis=0)
    gain_two = jnp.sum(scaled * (1.0 + scale_ffn), axis=0)
    grad_after = dy + rms_back(
        grad_second * gain_full[1] * (1.0 + scale_ffn), normed_two, inverse_two
    )
    d_gate_attn = jnp.sum(grad_after * attn_branch, axis=0) * (1.0 - gate_attn[0] * gate_attn[0])
    grad_attn = (gate_attn * grad_after).astype(BF16)
    grad_attn_all = jnp.concatenate(gather_rot(grad_attn), axis=0)
    grad_mixed = dot(grad_attn_all, w_out, 1, 1)
    d_out = dot(grad_attn_all, mixed, 0, 0).astype(BF16)
    out_chain = Halving(d_out.reshape(dpn, share, own_d), order_c)
    chains.append(out_chain)
    dq, dk, dv, dtk, dtv, rq, rk, gain_q, gain_k, gate_g = attn_backward(
        caption_lengths, q, k, v, tkp, tvp, pad_cols(grad_mixed, width), so, co, ls, lc, qp, kp,
        inv_q, inv_k, gq, gk, cosine, sine, gate_row,
    )
    rq, rk, dtk = advance(chains, (rq, rk, dtk))
    dq, dk, dv, dtk, dtv = (v_[:, :own_d] for v_ in (dq, dk, dv, dtk, dtv))
    gate_total = jnp.sum(gate_g[0, :own_d].reshape(HEADS // n, HD), axis=1) * (
        1.0 - head_tanh * head_tanh
    )
    text_hat = dtk * gain_own[4]
    gain_text = jnp.sum(dtk * normed_t, axis=0, keepdims=True)
    means = row_sum(jnp.stack([jnp.sum(rq, -1), jnp.sum(rk, -1)])) / D
    mean_t = pair_sum(jnp.sum(text_hat * normed_t, -1, keepdims=True)) / D
    grad_q = (inv_q * (dq * gain_own[2] - q_pre * inv_q * means[0][:, None])).astype(BF16)
    grad_k = (inv_k * (dk * gain_own[3] - k_pre * inv_k * means[1][:, None])).astype(BF16)

    grads = (grad_q, grad_k, dv)
    wide = []
    for g in grads:
        blocks = [
            dot(g, first_all[:, r * own_d : (r + 1) * own_d], 0, 0).astype(BF16) for r in range(n)
        ]
        got = [blocks[0]]
        for r in range(1, n):
            got.append(lax.ppermute(blocks[r], "fsdp", [(i, (i - r) % n) for i in range(n)]))
        got = jnp.stack(got)
        if n != 2 or dpn == 1:
            got = jnp.stack(
                [lax.dynamic_index_in_dim(got, (g_ - f) % n, 0, keepdims=False) for g_ in range(n)]
            )
        wide.append(got.reshape(dpn, share, own_d))
    flip = f if n == 2 else 0
    qkv_chains = [
        Halving(w_, o, flip) for w_, o in zip(wide, (order_a, order_b, order_c))
    ]
    chains += qkv_chains

    grad_tk = (inv_t * (text_hat - normed_t * mean_t)).astype(BF16)
    text_pair = jnp.stack([grad_tk, dtv.astype(BF16)])
    pair_all = gather_natural(text_pair)
    text_in = text_bwd(pair_all, w_text)
    text_in = exchange(text_in.reshape(n, -1, TW // n))
    text_in = jnp.concatenate(text_in, axis=1)
    outgoing = pair_all.reshape(2, TEXT, dpn, share).transpose(2, 0, 1, 3)
    pair_cols = dp_exchange(outgoing, order_a)
    pair_cols = jnp.take(pair_cols, me ^ jnp.arange(dpn), axis=0)
    pair_cols = pair_cols.transpose(0, 2, 1, 3).reshape(dpn * TEXT, 2 * share)
    text_grad = dot(pair_cols, text_all, 0, 0).reshape(2, share, TW // n)

    parts = [
        sum(dot(rows(g, r), w_heads[j], 1, 1) for j, g in enumerate(grads)) for r in range(n)
    ]
    parts = [jnp.concatenate(rot_blocks(p.reshape(-1, n, own_d), 1), axis=1) for p in parts]
    grad_first = scatter_rot([parts[0]] + [p.astype(BF16) for p in parts[1:]])
    inverse_one = inverse_rms(x_own)
    normed_one = x_own * inverse_one
    scaled = grad_first * normed_one
    d_scale_attn = jnp.sum(scaled * gain_full[0], axis=0)
    gain_one = jnp.sum(scaled * (1.0 + scale_attn), axis=0)
    grad_input = (
        grad_after
        + rms_back(grad_first * gain_full[0] * (1.0 + scale_attn), normed_one, inverse_one)
    ).astype(BF16)

    mods = jnp.stack([d_scale_attn, d_gate_attn, d_scale_ffn, d_gate_ffn])
    mods = pair_sum(dp_exchange(mods.reshape(4, dpn, share).transpose(1, 0, 2), order_a))
    times = time_embed(times_all)
    times = lax.dynamic_slice_in_dim(times, f * own_te, own_te, 1).astype(F32)
    ada_grad = lax.dot_general(
        mods.reshape(dpn, 4 * share), times, (((0,), (0,)), ((), ())),
        precision=lax.Precision.HIGHEST,
    ).reshape(4, share, own_te)
    two = scatter_rot(rot_blocks(jnp.stack([gain_one, gain_two]).reshape(2, n, own_d), 1))
    gate_pad = jnp.pad(gate_total, (0, own_d - gate_total.shape[0]))[None]
    small = dp_total(
        jnp.concatenate([two, gain_q[:, :own_d], gain_k[:, :own_d], gain_text, gate_pad], axis=0)
    )
    while any(c.got is not None for c in chains):
        advance(chains, ())
    return (
        output[None],
        grad_input[None],
        text_in[None],
        ada_grad.transpose(2, 0, 1),
        text_grad.transpose(2, 0, 1),
        jnp.stack([c.cur for c in qkv_chains]).transpose(2, 0, 1),
        out_chain.cur.T,
        small[:5],
        small[5, : HEADS // n],
        jnp.stack([gate_chain.cur, up_chain.cur], axis=1),
        down_chain.cur.T,
    )


def solution(mesh):
    return jax.shard_map(
        on_device,
        mesh=mesh,
        in_specs=(
            P("dp", "fsdp", None),
            P("dp", "fsdp", None),
            P("dp"),
            P("dp"),
            P("dp", None, "fsdp"),
            P("dp", "fsdp", None),
            P("fsdp", None, None),
            P("fsdp", None, None),
            P("fsdp", None, None),
            P("fsdp", None),
            P(None, "fsdp"),
            P("fsdp"),
            P(None, None, "fsdp"),
            P("fsdp", None),
        ),
        out_specs=(
            P("dp", "fsdp", None),
            P("dp", "fsdp", None),
            P("dp", "fsdp", None),
            P("fsdp", None, "dp"),
            P("fsdp", None, "dp"),
            P("fsdp", None, "dp"),
            P("fsdp", "dp"),
            P(None, "fsdp"),
            P("fsdp"),
            P("dp", None, "fsdp"),
            P("fsdp", "dp"),
        ),
        check_vma=False,
    )
```

time: 1300 us -> 968 us (0.74)
  matrix products: 245 us -> 89.9 us
  local copies, waits for them, and re-layouts: 262 us -> 154 us
  waiting for transfers between devices: 401 us -> 304 us
  Pallas kernels: 128 us -> 218 us
  starting transfers between devices: 106 us -> 59.5 us
  blocking collectives: 47.2 us -> 1.98 us
  other arithmetic: 78.2 us -> 114 us
    dot_general x32 -> x20, matrix products: 228 us -> 83.9 us  [dot(): lax.dot_general(a, b, (((ca,), (cb,)), ((), ())), preferred_element_type=...]
    pallas_call x0 -> x3, Pallas kernels: none -> 120 us  [the longest x1 89.4 us: ffn(): pl.pallas_call(ffn_kernel, grid=(hid // bc,), in_specs=[once((tokens, dep...]
    ppermute x78 -> x44, waiting for transfers between devices: 400 us -> 299 us  [dp_swap(): return lax.ppermute(value, 'dp', [(i, i ^ 1 << bit) for i in range(n)])]
    slice x10 -> x1, local copies, waits for them, and re-layouts: 63.4 us -> 0.01 us  [on_device(): means[0][:, None]]
    dot_general x4 -> x2, local copies, waits for them, and re-layouts: 66.2 us -> 5.96 us  [dot(): lax.dot_general(a, b, (((ca,), (cb,)), ((), ())), preferred_element_type=...]
    dynamic_slice x8 -> x18, local copies, waits for them, and re-layouts: 14.4 us -> 53.1 us  [the longest x5 17.7 us: rot_blocks(): lax.dynamic_index_in_dim(value, (f - r) % n, axis, keepdims=False)]
    ppermute x78 -> x44, starting transfers between devices: 91.6 us -> 54 us  [dp_swap(): return lax.ppermute(value, 'dp', [(i, i ^ 1 << bit) for i in range(n)])]
    pallas_call x1, Pallas kernels: 63.3 us -> 33.3 us  [attn_forward(): pl.pallas_call(attn_fwd_kernel, grid=(blocks,), in_specs=[scalar, col, co...]
  transfers between devices with their start and end apart: 98 -> 69, of which waited for: 42 -> 30; matrix products, arithmetic and copies ran while one was open for 43% -> 31% of each run, Pallas kernels for 5% -> 10%
where the time goes in v2:
time: 968 us; the launch traced here: 959 us
  waiting for transfers between devices  304 us (31%)
  Pallas kernels  218 us (23%)
  local copies, waits for them, and re-layouts  154 us (16%)
  other arithmetic  114 us (12%)
  matrix products  89.9 us (9%)
  starting transfers between devices  59.5 us (6%)
  between operations  17.3 us (2%)
    ppermute x44, waiting for transfers between devices, dp_swap(): return lax.ppermute(value, 'dp', [(i, i ^ 1 << bit) for i in range(n)])  299 us
    pallas_call x1, Pallas kernels, ffn(): pl.pallas_call(ffn_kernel, grid=(hid // bc,), in_specs=[once((tokens, dep...  89.4 us
    dot_general x20, matrix products, dot(): lax.dot_general(a, b, (((ca,), (cb,)), ((), ())), preferred_element_type=...  83.9 us
    pallas_call x1, Pallas kernels, attn_backward(): pl.pallas_call(attn_bwd_kernel, grid=(blocks,), in_specs=[scalar, col, co...  64.7 us
    ppermute x44, starting transfers between devices, dp_swap(): return lax.ppermute(value, 'dp', [(i, i ^ 1 << bit) for i in range(n)])  54 us
    unnamed x256, local copies, waits for them, and re-layouts  44.1 us
    pallas_call x1, Pallas kernels, attn_forward(): pl.pallas_call(attn_fwd_kernel, grid=(blocks,), in_specs=[scalar, col, co...  33.3 us
    convert_element_type x21, other arithmetic, step(): self.cur = total.astype(BF16) if self.order else total  25 us
  transfers between devices with their start and end apart: 69, of which 30 were waited for; matrix products, arithmetic and copies ran while one was open for 31% of the time, Pallas kernels for 10%

profile of v2, /device:TPU:0, one launch (start us, length us, event | category | flops | bytes accessed | tf_op | source)
XLA Modules:
  0.0 959.3 jit_solution(1644840502862791961)
XLA Ops:
  13.8 10.4 %copy.102 = bf16[768,3,1536]{0,2,1:T(8,128)(2,1)} copy(bf16[768,3,1536]{2,0,1:T(8,128)(2,1)} %param.22) | data formatting | bytes 14155776 | tf_op args[8]
  64.1 15.9 %shard_map.221 = f32[2,256,1536]{2,1,0:T(8,128)} custom-call(bf16[256,2048]{1,0:T(8,128)(2,1)} %pad_maximum_fusion.10.x_ref, bf16[2048,2,1536]{2,1,0:T(2,128)(2,1)} %w_ref.5), custom_call_target="tpu_custom_call" | custom-call | tf_op jit(solution)/shard_map/pallas_call | solution.py:386
  85.3 7.2 constant_dynamic-slice_fusion.20
  126.2 5.7 multiply_reduce_fusion.9
  147.9 33.3 %shard_map.222 = (bf16[1024,768]{1,0:T(8,128)(2,1)}, bf16[1024,768]{1,0:T(8,128)(2,1)}, bf16[1024,768]{1,0:T(8,128)(2,1)}, bf16[1024,768]{1,0:T(8,128)(2,1)}, f3...) custom-call(s32[1]{0:T(128)S(6)} %copy.233.len_ref, ...), custom_call_target="tpu_custom_call" | custom-call | tf_op jit(solution)/shard_map/pallas_call | solution.py:325
  199.2 89.4 %shard_map.223 = (bf16[16,96,2048]{2,1,0:T(8,128)(2,1)}, bf16[16,96,2048]{2,1,0:T(8,128)(2,1)}, bf16[16,96,2048]{2,1,0:T(8,128)(2,1)}, f32[512,1536]{1,0:T(8,128...) custom-call(bf16[1024,1536]{1,0:T(8,128)(2,1)} %pad_maximum_fusion.s_ref, ...), custom_call_target="tpu_custom_call" | custom-call | tf_op jit(solution)/shard_map/pallas_call | solution.py:460
  313.4 6.0 fusion.12
  346.3 6.3 fusion.31.g_ref
  352.6 64.7 %shard_map.224 = (f32[1024,768]{1,0:T(8,128)}, f32[1024,768]{1,0:T(8,128)}, bf16[1024,768]{1,0:T(8,128)(2,1)}, f32[256,768]{1,0:T(8,128)}, f32[256,768]{1,0:T(8,...) custom-call(s32[1]{0:T(128)S(6)} %copy.233.len_ref, ...), custom_call_target="tpu_custom_call" | custom-call | tf_op jit(solution)/shard_map/pallas_call | solution.py:343
  443.8 28.2 %collective-permute-done.16 = bf16[2,2,2,96,2048]{4,3,0,2,1:T(8,128)(2,1)} collective-permute-done((bf16[2,2,2,96,2048]{4,3,0,2,1:T(8,128)(2,1)}, bf16[2,2,2,96,2048]{4,3,0,2,1:T(8,128)(2,1)}, u32[]{:S(2)}, u32[]{:S(2)}) %collective-permute-start.16) | collective-permute-done | bytes 3145760 | tf_op jit(solution)/shard_map/ppermute | solution.py:98
  472.1 68.5 %collective-permute-done.17 = bf16[2,2,2,96,768]{4,3,0,2,1:T(8,128)(2,1)} collective-permute-done((bf16[2,2,2,96,768]{4,3,0,2,1:T(8,128)(2,1)}, bf16[2,2,2,96,768]{4,3,0,2,1:T(8,128)(2,1)}, u32[]{:S(2)}, u32[]{:S(2)}) %collective-permute-start.17) | collective-permute-done | bytes 1179680 | tf_op jit(solution)/shard_map/ppermute | solution.py:98
  634.4 14.8 %shard_map.225 = bf16[256,2048]{1,0:T(8,128)(2,1)} custom-call(bf16[2,256,1536]{2,1,0:T(8,128)(2,1)} %pad_maximum_fusion.6.g_ref, bf16[2048,2,1536]{2,1,0:T(2,128)(2,1)} %w_ref.5), custom_call_target="tpu_custom_call" | custom-call | tf_op jit(solution)/shard_map/pallas_call | solution.py:405
  664.8 6.4 collective-permute-done.27
  682.0 32.8 %collective-permute-done.65 = f32[6,768]{1,0:T(8,128)S(1)} collective-permute-done((f32[6,768]{1,0:T(8,128)S(1)}, f32[6,768]{1,0:T(8,128)S(1)}, u32[]{:S(2)}, u32[]{:S(2)}) %collective-permute-start.65) | collective-permute-done | bytes 18464 | tf_op jit(solution)/shard_map/ppermute | solution.py:98
  730.5 21.8 %collective-permute-done.38 = bf16[2,2,96,2048]{3,2,0,1:T(8,128)(2,1)S(1)} collective-permute-done((bf16[2,2,96,2048]{3,2,0,1:T(8,128)(2,1)}, bf16[2,2,96,2048]{3,2,0,1:T(8,128)(2,1)S(1)}, u32[]{:S(2)}, u32[]{:S(2)}) %collective-permute-start.38) | collective-permute-done | bytes 1572896 | tf_op jit(solution)/shard_map/ppermute | solution.py:98
  755.4 23.0 %collective-permute-done.43 = bf16[2,2,2,96,768]{4,3,0,1,2:T(8,128)(2,1)S(1)} collective-permute-done((bf16[2,2,2,96,768]{4,3,0,1,2:T(8,128)(2,1)S(1)}, bf16[2,2,2,96,768]{4,3,0,1,2:T(8,128)(2,1)S(1)}, u32[]{:S(2)}, u32[]{:S(2)}) %collective-permute-start.43) | collective-permute-done | bytes 1179680 | tf_op jit(solution)/shard_map/ppermute | solution.py:98
  811.3 11.5 %collective-permute-done.51 = bf16[2,2,96,768]{3,2,0,1:T(8,128)(2,1)} collective-permute-done((bf16[2,2,96,768]{3,2,0,1:T(8,128)(2,1)}, bf16[2,2,96,768]{3,2,0,1:T(8,128)(2,1)}, u32[]{:S(2)}, u32[]{:S(2)}) %collective-permute-start.51) | collective-permute-done | bytes 589856 | tf_op jit(solution)/shard_map/ppermute | solution.py:98
  823.5 17.8 %collective-permute-done.46 = bf16[2,96,2048]{2,1,0:T(8,128)(2,1)} collective-permute-done((bf16[2,96,2048]{2,1,0:T(8,128)(2,1)}, bf16[2,96,2048]{2,1,0:T(8,128)(2,1)}, u32[]{:S(2)}, u32[]{:S(2)}) %collective-permute-start.46) | collective-permute-done | bytes 786464 | tf_op jit(solution)/shard_map/ppermute | solution.py:98
  857.1 8.9 collective-permute-done.56
  868.6 13.6 %collective-permute-done.58 = bf16[2,96,768]{2,1,0:T(8,128)(2,1)S(1)} collective-permute-done((bf16[2,96,768]{2,1,0:T(8,128)(2,1)S(1)}, bf16[2,96,768]{2,1,0:T(8,128)(2,1)S(1)}, u32[]{:S(2)}, u32[]{:S(2)}) %collective-permute-start.58) | collective-permute-done | bytes 294944 | tf_op jit(solution)/shard_map/ppermute | solution.py:98
  888.5 22.0 %collective-permute-done.54 = bf16[96,2048]{1,0:T(8,128)(2,1)S(1)} collective-permute-done((bf16[96,2048]{1,0:T(8,128)(2,1)S(1)}, bf16[96,2048]{1,0:T(8,128)(2,1)S(1)}, u32[]{:S(2)}, u32[]{:S(2)}) %collective-permute-start.54) | collective-permute-done | bytes 393248 | tf_op jit(solution)/shard_map/ppermute | solution.py:98
  910.5 8.4 collective-permute-done.53
  926.9 9.4 collective-permute-done.62
  943.5 8.7 fusion
  (600 shorter events, 407.3 us)
Async XLA Ops:
  7.2 936.3 %all-gather.2.cloned.1.call-start = ((), (), s32[]{:S(2)}) async-start(), calls=%async_computation | async-start | bytes 17825792 | tf_op jit(solution)/shard_map/all_gather | solution.py:531
  13.3 48.0 %collective-permute-start.5 = (bf16[128,2048]{1,0:T(8,128)(2,1)}, bf16[128,2048]{1,0:T(8,128)(2,1)}, u32[]{:S(2)}, u32[]{:S(2)}) collective-permute-start(bf16[128,2048]{1,0:T(8,128)(2,1)} %bitcast.410), channel_id=1, source_target_pairs={{0,1},{1,0},{2,3},{3,2},{4,5},{5,4},{6,7},{7,6},{8,9},{9,8},{10,11... | collective-permute-start | bytes 1572872 | tf_op jit(solution)/shard_map/ppermute | solution.py:85
  33.2 87.4 %collective-permute-start.2 = (bf16[3,768,768]{2,1,0:T(8,128)(2,1)}, bf16[3,768,768]{2,1,0:T(8,128)(2,1)}, u32[]{:S(2)}, u32[]{:S(2)}) collective-permute-start(bf16[3,768,768]{2,1,0:T(8,128)(2,1)} %bitcast.449), channel_id=1, source_target_pairs={{0,1},{1,0},{2,3},{3,2},{4,5},{5,4},{6,7},{7,6},{8,9},{9,8},{10,11... | collective-permute-start | bytes 10616840 | tf_op jit(solution)/shard_map/ppermute | solution.py:30
  33.2 66.4 %collective-permute-start.1 = (bf16[512,1536]{1,0:T(8,128)(2,1)}, bf16[512,1536]{1,0:T(8,128)(2,1)}, u32[]{:S(2)}, u32[]{:S(2)}) collective-permute-start(bf16[512,1536]{1,0:T(8,128)(2,1)} %bitcast), channel_id=1, source_target_pairs={{0,1},{1,0},{2,3},{3,2},{4,5},{5,4},{6,7},{7,6},{8,9},{9,8},{10,11... | collective-permute-start | bytes 4718600 | tf_op jit(solution)/shard_map/ppermute | solution.py:30
  40.2 53.8 %collective-permute-start = (f32[4,1536]{1,0:T(4,128)}, f32[4,1536]{1,0:T(4,128)}, u32[]{:S(2)}, u32[]{:S(2)}) collective-permute-start(f32[4,1536]{1,0:T(4,128)} %bitcast.411), channel_id=1, source_target_pairs={{0,1},{1,0},{2,3},{3,2},{4,5},{5,4},{6,7},{7,6},{8,9},{9,8},{10,11... | collective-permute-start | bytes 73736 | tf_op jit(solution)/shard_map/ppermute | solution.py:30
  330.4 113.4 %collective-permute-start.14 = (bf16[2,2,2,96,2048]{4,3,0,1,2:T(8,128)(2,1)}, bf16[2,2,2,96,2048]{4,3,0,1,2:T(8,128)(2,1)}, u32[]{:S(2)}, u32[]{:S(2)}) collective-permute-start(bf16[2,2,2,96,2048]{4,3,0,1,2:T(8,128)(2,1)} %bitcast.402), channel_id=1, source_target_pairs={{0,2},{2,0},{4,6},{6,4},{8,10},{10,8},{12,14},{14,12},{16,18},{18,... | collective-permute-start | bytes 9437192 | tf_op jit(solution)/shard_map/ppermute | solution.py:98
  336.7 107.1 %collective-permute-start.15 = (bf16[2,2,2,96,2048]{4,3,0,1,2:T(8,128)(2,1)}, bf16[2,2,2,96,2048]{4,3,0,1,2:T(8,128)(2,1)}, u32[]{:S(2)}, u32[]{:S(2)}) collective-permute-start(bf16[2,2,2,96,2048]{4,3,0,1,2:T(8,128)(2,1)} %bitcast.401), channel_id=1, source_target_pairs={{0,4},{2,6},{4,0},{6,2},{8,12},{10,14},{12,8},{14,10},{16,20},{18,... | collective-permute-start | bytes 9437192 | tf_op jit(solution)/shard_map/ppermute | solution.py:98
  342.7 129.4 %collective-permute-start.16 = (bf16[2,2,2,96,2048]{4,3,0,2,1:T(8,128)(2,1)}, bf16[2,2,2,96,2048]{4,3,0,2,1:T(8,128)(2,1)}, u32[]{:S(2)}, u32[]{:S(2)}) collective-permute-start(bf16[2,2,2,96,2048]{4,3,0,2,1:T(8,128)(2,1)} %bitcast.400), channel_id=1, source_target_pairs={{0,8},{2,10},{4,12},{6,14},{8,0},{10,2},{12,4},{14,6},{16,24},{18,... | collective-permute-start | bytes 9437192 | tf_op jit(solution)/shard_map/ppermute | solution.py:98
  427.1 113.5 %collective-permute-start.17 = (bf16[2,2,2,96,768]{4,3,0,2,1:T(8,128)(2,1)}, bf16[2,2,2,96,768]{4,3,0,2,1:T(8,128)(2,1)}, u32[]{:S(2)}, u32[]{:S(2)}) collective-permute-start(bf16[2,2,2,96,768]{4,3,0,2,1:T(8,128)(2,1)} %bitcast.408), channel_id=1, source_target_pairs={{0,8},{2,10},{4,12},{6,14},{8,0},{10,2},{12,4},{14,6},{16,24},{18,... | collective-permute-start | bytes 3538952 | tf_op jit(solution)/shard_map/ppermute | solution.py:98
  442.4 274.6 %collective-permute-start.45 = (bf16[2,2,2,96,768]{4,3,0,2,1:T(8,128)(2,1)}, bf16[2,2,2,96,768]{4,3,0,2,1:T(8,128)(2,1)}, u32[]{:S(2)}, u32[]{:S(2)}) collective-permute-start(bf16[2,2,2,96,768]{4,3,0,2,1:T(8,128)(2,1)} %fusion.49), channel_id=1, source_target_pairs={{0,8},{2,10},{4,12},{6,14},{8,0},{10,2},{12,4},{14,6},{16,24},{18,... | collective-permute-start | bytes 3538952 | tf_op jit(solution)/shard_map/ppermute | solution.py:98
  570.1 51.2 %collective-permute-start.21 = (bf16[2,256,768]{2,1,0:T(8,128)(2,1)}, bf16[2,256,768]{2,1,0:T(8,128)(2,1)}, u32[]{:S(2)}, u32[]{:S(2)}) collective-permute-start(bf16[2,256,768]{2,1,0:T(8,128)(2,1)} %get-tuple-element.212), channel_id=1, source_target_pairs={{0,1},{1,0},{2,3},{3,2},{4,5},{5,4},{6,7},{7,6},{8,9},{9,8},{10,11... | collective-permute-start | bytes 2359304 | tf_op jit(solution)/shard_map/ppermute | solution.py:30
  574.6 76.5 %collective-permute-start.42 = (bf16[768,768]{1,0:T(8,128)(2,1)}, bf16[768,768]{1,0:T(8,128)(2,1)}, u32[]{:S(2)}, u32[]{:S(2)}) collective-permute-start(bf16[768,768]{1,0:T(8,128)(2,1)} %convolution_convert_fusion.4), channel_id=1, source_target_pairs={{0,1},{1,0},{2,3},{3,2},{4,5},{5,4},{6,7},{7,6},{8,9},{9,8},{10,11... | collective-permute-start | bytes 3538952 | tf_op jit(solution)/shard_map/ppermute | solution.py:630
  579.1 77.0 %collective-permute-start.36 = (bf16[768,768]{1,0:T(8,128)(2,1)}, bf16[768,768]{1,0:T(8,128)(2,1)}, u32[]{:S(2)}, u32[]{:S(2)}) collective-permute-start(bf16[768,768]{1,0:T(8,128)(2,1)} %convolution_convert_fusion.6), channel_id=1, source_target_pairs={{0,1},{1,0},{2,3},{3,2},{4,5},{5,4},{6,7},{7,6},{8,9},{9,8},{10,11... | collective-permute-start | bytes 3538952 | tf_op jit(solution)/shard_map/ppermute | solution.py:630
  613.5 46.7 %collective-permute-start.19 = (bf16[512,1536]{1,0:T(8,128)(2,1)}, bf16[512,1536]{1,0:T(8,128)(2,1)}, u32[]{:S(2)}, u32[]{:S(2)}) collective-permute-start(bf16[512,1536]{1,0:T(8,128)(2,1)} %pad_maximum_fusion.5), channel_id=1, source_target_pairs={{0,1},{1,0},{2,3},{3,2},{4,5},{5,4},{6,7},{7,6},{8,9},{9,8},{10,11... | collective-permute-start | bytes 4718600 | tf_op jit(solution)/shard_map/ppermute | solution.py:54
  621.3 94.4 %collective-permute-start.40 = (bf16[2,2,96,768]{3,2,0,1:T(8,128)(2,1)}, bf16[2,2,96,768]{3,2,0,1:T(8,128)(2,1)}, u32[]{:S(2)}, u32[]{:S(2)}) collective-permute-start(bf16[2,2,96,768]{3,2,0,1:T(8,128)(2,1)} %dynamic-slice_bitcast_fusion.9), channel_id=1, source_target_pairs={{0,4},{2,6},{4,0},{6,2},{8,12},{10,14},{12,8},{14,10},{16,20},{18,... | collective-permute-start | bytes 1769480 | tf_op jit(solution)/shard_map/ppermute | solution.py:98
  651.1 68.2 %collective-permute-start.32 = (bf16[2,2,2,2,256,96]{4,5,3,2,1,0:T(8,128)(2,1)}, bf16[2,2,2,2,256,96]{4,5,3,2,1,0:T(8,128)(2,1)}, u32[]{:S(2)}, u32[]{:S(2)}) collective-permute-start(bf16[2,2,2,2,256,96]{4,5,3,2,1,0:T(8,128)(2,1)} %bitcast.460), channel_id=1, source_target_pairs={{0,2},{2,0},{4,6},{6,4},{8,10},{10,8},{12,14},{14,12},{16,18},{18,... | collective-permute-start | bytes 2359304 | tf_op jit(solution)/shard_map/ppermute | solution.py:98
  679.9 49.6 %collective-permute-start.39 = (bf16[2,2,96,2048]{3,2,0,1:T(8,128)(2,1)}, bf16[2,2,96,2048]{3,2,0,1:T(8,128)(2,1)S(1)}, u32[]{:S(2)}, u32[]{:S(2)}) collective-permute-start(bf16[2,2,96,2048]{3,2,0,1:T(8,128)(2,1)} %dynamic-slice_bitcast_fusion), channel_id=1, source_target_pairs={{0,4},{2,6},{4,0},{6,2},{8,12},{10,14},{12,8},{14,10},{16,20},{18,... | collective-permute-start | bytes 4718600 | tf_op jit(solution)/shard_map/ppermute | solution.py:98
  721.6 56.8 %collective-permute-start.43 = (bf16[2,2,2,96,768]{4,3,0,1,2:T(8,128)(2,1)S(1)}, bf16[2,2,2,96,768]{4,3,0,1,2:T(8,128)(2,1)S(1)}, u32[]{:S(2)}, u32[]{:S(2)}) collective-permute-start(bf16[2,2,2,96,768]{4,3,0,1,2:T(8,128)(2,1)S(1)} %bitcast.458), channel_id=1, source_target_pairs={{0,4},{2,6},{4,0},{6,2},{8,12},{10,14},{12,8},{14,10},{16,20},{18,... | collective-permute-start | bytes 3538952 | tf_op jit(solution)/shard_map/ppermute | solution.py:98
  723.1 55.2 %collective-permute-start.41 = (bf16[2,2,2,96,768]{4,3,0,1,2:T(8,128)(2,1)}, bf16[2,2,2,96,768]{4,3,0,1,2:T(8,128)(2,1)S(1)}, u32[]{:S(2)}, u32[]{:S(2)}) collective-permute-start(bf16[2,2,2,96,768]{4,3,0,1,2:T(8,128)(2,1)} %bitcast.459), channel_id=1, source_target_pairs={{0,2},{2,0},{4,6},{6,4},{8,10},{10,8},{12,14},{14,12},{16,18},{18,... | collective-permute-start | bytes 3538952 | tf_op jit(solution)/shard_map/ppermute | solution.py:98
  729.5 66.8 %collective-permute-start.33 = (bf16[2,2,2,2,256,96]{4,5,3,1,0,2:T(8,128)(2,1)S(1)}, bf16[2,2,2,2,256,96]{4,5,3,1,0,2:T(8,128)(2,1)S(1)}, u32[]{:S(2)}, u32[]{:S(2)}) collective-permute-start(bf16[2,2,2,2,256,96]{4,5,3,1,0,2:T(8,128)(2,1)S(1)} %get-tuple-element.197), channel_id=1, source_target_pairs={{0,4},{2,6},{4,0},{6,2},{8,12},{10,14},{12,8},{14,10},{16,20},{18,... | collective-permute-start | bytes 2359304 | tf_op jit(solution)/shard_map/ppermute | solution.py:98
  796.3 44.9 %collective-permute-start.46 = (bf16[2,96,2048]{2,1,0:T(8,128)(2,1)}, bf16[2,96,2048]{2,1,0:T(8,128)(2,1)}, u32[]{:S(2)}, u32[]{:S(2)}) collective-permute-start(bf16[2,96,2048]{2,1,0:T(8,128)(2,1)} %dynamic-slice_bitcast_fusion.5), channel_id=1, source_target_pairs={{0,8},{2,10},{4,12},{6,14},{8,0},{10,2},{12,4},{14,6},{16,24},{18,... | collective-permute-start | bytes 2359304 | tf_op jit(solution)/shard_map/ppermute | solution.py:98
  851.9 58.6 %collective-permute-start.54 = (bf16[96,2048]{1,0:T(8,128)(2,1)S(1)}, bf16[96,2048]{1,0:T(8,128)(2,1)S(1)}, u32[]{:S(2)}, u32[]{:S(2)}) collective-permute-start(bf16[96,2048]{1,0:T(8,128)(2,1)S(1)} %dynamic-slice_bitcast_fusion.12), channel_id=1, source_target_pairs={{0,16},{2,18},{4,20},{6,22},{8,24},{10,26},{12,28},{14,30},{16,0},... | collective-permute-start | bytes 1179656 | tf_op jit(solution)/shard_map/ppermute | solution.py:98
  856.3 62.6 %collective-permute-start.53 = (bf16[96,2048]{1,0:T(8,128)(2,1)S(1)}, bf16[96,2048]{1,0:T(8,128)(2,1)S(1)}, u32[]{:S(2)}, u32[]{:S(2)}) collective-permute-start(bf16[96,2048]{1,0:T(8,128)(2,1)S(1)} %dynamic-slice_bitcast_fusion.13), channel_id=1, source_target_pairs={{0,16},{2,18},{4,20},{6,22},{8,24},{10,26},{12,28},{14,30},{16,0},... | collective-permute-start | bytes 1179656 | tf_op jit(solution)/shard_map/ppermute | solution.py:98
  882.2 58.4 %collective-permute-start.35 = (bf16[2,2,2,2,256,96]{4,5,3,1,0,2:T(8,128)(2,1)S(1)}, bf16[2,2,2,2,256,96]{4,5,3,1,0,2:T(8,128)(2,1)S(1)}, u32[]{:S(2)}, u32[]{:S(2)}) collective-permute-start(bf16[2,2,2,2,256,96]{4,5,3,1,0,2:T(8,128)(2,1)S(1)} %get-tuple-element.194), channel_id=1, source_target_pairs={{0,16},{2,18},{4,20},{6,22},{8,24},{10,26},{12,28},{14,30},{16,0},... | collective-permute-start | bytes 2359304 | tf_op jit(solution)/shard_map/ppermute | solution.py:98
  (166 other events, 2199.4 us)
Sparse Core Ops, SparseCore 0:
  322.6 290.1 all-gather.1

commit v3 on v2

--- a/solution.py
+++ b/solution.py
@@ -56,37 +56,30 @@
     return total
 
 
+def block_of(value, index, axis):
+    size = value.shape[axis] // lax.axis_size("fsdp")
+    return lax.dynamic_slice_in_dim(value, index * size, size, axis)
+
+
 def rot_blocks(value, axis):
     n, f = lax.axis_size("fsdp"), lax.axis_index("fsdp")
-    return [lax.dynamic_index_in_dim(value, (f - r) % n, axis, keepdims=False) for r in range(n)]
+    return [block_of(value, (f - r) % n, axis) for r in range(n)]
 
 
 def exchange_rot(value, axis):
     n, f = lax.axis_size("fsdp"), lax.axis_index("fsdp")
-    out = []
-    for r in range(n):
-        send = lax.dynamic_index_in_dim(value, (f + r) % n, axis, keepdims=False)
-        out.append(from_behind(send, r) if r else send)
+    out = [block_of(value, f, axis)]
+    for r in range(1, n):
+        out.append(from_behind(block_of(value, (f + r) % n, axis), r))
     return out
 
 
-def gather_natural(value):
+def natural(got):
     n, f = lax.axis_size("fsdp"), lax.axis_index("fsdp")
-    blocks = jnp.stack(gather_rot(value))
-    order = [lax.dynamic_index_in_dim(blocks, (f - g) % n, 0, keepdims=False) for g in range(n)]
-    return jnp.concatenate(order, axis=-1)
-
-
-def exchange(value):
-    n, f = lax.axis_size("fsdp"), lax.axis_index("fsdp")
-    sends = rot_blocks(value, 0)
-    got = [sends[0]]
-    for r in range(1, n):
-        got.append(lax.ppermute(sends[r], "fsdp", [(i, (i - r) % n) for i in range(n)]))
     if n == 2:
         return [jnp.where(f == 0, got[0], got[1]), jnp.where(f == 0, got[1], got[0])]
     got = jnp.stack(got)
-    return [lax.dynamic_index_in_dim(got, (g - f) % n, 0, keepdims=False) for g in range(n)]
+    return [lax.dynamic_index_in_dim(got, (f - g) % n, 0, keepdims=False) for g in range(n)]
 
 
 def dp_bits():
@@ -98,45 +91,45 @@
     return lax.ppermute(value, "dp", [(i, i ^ (1 << bit)) for i in range(n)])
 
 
-def orders():
-    bits = list(range(dp_bits()))
+def orders(bits):
     return bits, bits[:2][::-1] + bits[2:], bits[2:3] + bits[:2][::-1] + bits[3:]
 
 
-def split_bit(value, axis, bit):
-    mine = (lax.axis_index("dp") >> bit) & 1
-    keep = lax.dynamic_index_in_dim(value, mine, axis, keepdims=False)
-    send = lax.dynamic_index_in_dim(value, 1 - mine, axis, keepdims=False)
-    return keep, send
+def relative(value):
+    return jnp.take(value, lax.axis_index("dp") ^ jnp.arange(lax.axis_size("dp")), axis=0)
 
 
 class Halving:
-    def __init__(self, value, order, flip=0):
-        nb = dp_bits()
-        self.cur = value.reshape((2,) * nb + value.shape[1:])
-        self.labels = list(range(nb))[::-1]
-        self.order, self.flip = list(order), flip
+    def __init__(self, bits, order, whole=None, pair=None):
+        self.labels, self.order = list(bits)[::-1], list(order)
         self.keep = self.got = None
-        self.start()
+        if pair is None:
+            self.cur = whole
+            self.start()
+        else:
+            bit = self.order.pop(0)
+            self.labels.remove(bit)
+            self.keep, self.got = pair[0], dp_swap(pair[1], bit)
 
     def start(self):
         if not self.order:
             return
         bit = self.order.pop(0)
         axis = self.labels.index(bit)
-        mine = (lax.axis_index("dp") >> bit) & 1
-        if bit == dp_bits() - 1:
-            mine = mine ^ self.flip
+        cur = self.cur.reshape((2,) * len(self.labels) + self.cur.shape[1:])
         self.labels.remove(bit)
-        self.keep = lax.dynamic_index_in_dim(self.cur, mine, axis, keepdims=False)
-        send = lax.dynamic_index_in_dim(self.cur, 1 - mine, axis, keepdims=False)
+        self.keep, send = (
+            lax.index_in_dim(cur, i, axis, keepdims=False).reshape((-1,) + self.cur.shape[1:])
+            for i in range(2)
+        )
         self.got = dp_swap(send, bit)
 
     def step(self):
         if self.got is None:
             return
         total = self.keep.astype(F32) + self.got.astype(F32)
-        self.cur = total.astype(BF16) if self.order else total
+        self.cur = total.astype(BF16)
+        self.last = total
         self.got = None
         self.start()
 
@@ -155,7 +148,7 @@
     cur = value.reshape((2,) * nb + value.shape[1:])
     for bit in order:
         axis = nb - 1 - bit
-        keep, send = split_bit(cur, axis, bit)
+        keep, send = (lax.index_in_dim(cur, i, axis, keepdims=False) for i in range(2))
         cur = jnp.stack([keep, dp_swap(send, bit)], axis=axis)
     return cur.reshape(value.shape)
 
@@ -175,23 +168,28 @@
     return value * cosine + sign * (partner * sine)
 
 
+def column(ref, index, width):
+    row = ref[index : index + 1, :] if isinstance(index, int) else ref[pl.ds(index, 1), :]
+    return jnp.broadcast_to(row, (width, row.shape[1])).T
+
+
 def masked(value, head):
     lane = lax.broadcasted_iota(jnp.int32, value.shape, 1)
     return jnp.where(lane // HD == head, value, jnp.zeros_like(value))
 
 
 def attn_fwd_kernel(
-    len_ref, qp_ref, kp_ref, vp_ref, iq_ref, ik_ref, gq_ref, gk_ref, cos_ref, sin_ref,
-    tk_ref, tv_ref, gate_ref,
+    len_ref, pre_ref, inv_ref, gq_ref, gk_ref, cos_ref, sin_ref, tk_ref, tv_ref, gate_ref,
     q_ref, k_ref, v_ref, mixed_ref, so_ref, co_ref, ls_ref, lc_ref,
 ):
-    tokens, width = qp_ref.shape
+    _, tokens, width = pre_ref.shape
     heads = width // HD
-    q = rope_block(qp_ref[...] * iq_ref[...] * gq_ref[...], cos_ref[...], sin_ref[...], 1.0)
+    iq, ik = column(inv_ref, 0, width), column(inv_ref, 1, width)
+    q = rope_block(pre_ref[0] * iq * gq_ref[...], cos_ref[...], sin_ref[...], 1.0)
     q_ref[...] = q.astype(BF16)
-    k = rope_block(kp_ref[...] * ik_ref[...] * gk_ref[...], cos_ref[...], sin_ref[...], 1.0)
+    k = rope_block(pre_ref[1] * ik * gk_ref[...], cos_ref[...], sin_ref[...], 1.0)
     k_ref[...] = k.astype(BF16)
-    v_ref[...] = vp_ref[...].astype(BF16)
+    v_ref[...] = pre_ref[2].astype(BF16)
     length = len_ref[0]
 
     def one(keys, values, qm, limit):
@@ -226,8 +224,8 @@
 
 def attn_bwd_kernel(
     len_ref, q_ref, k_ref, v_ref, tk_ref, tv_ref, g_ref, so_ref, co_ref, ls_ref, lc_ref,
-    qp_ref, kp_ref, iq_ref, ik_ref, gq_ref, gk_ref, cos_ref, sin_ref, gate_ref,
-    dq_ref, dk_ref, dv_ref, dtk_ref, dtv_ref, rq_ref, rk_ref, gainq_ref, gaink_ref, gateg_ref,
+    pre_ref, inv_ref, gq_ref, gk_ref, cos_ref, sin_ref, gate_ref,
+    d_ref, dtk_ref, dtv_ref, rq_ref, rk_ref, gainq_ref, gaink_ref, gateg_ref,
     gs_ref, gc_ref, ds_ref, dc_ref, kt_ref, tkt_ref, dqt_ref, dk_acc, dv_acc,
 ):
     tokens, width = q_ref.shape
@@ -290,64 +288,62 @@
 
     lax.fori_loop(0, tokens // QC, chunk, 0)
     dq = rope_block(dqt_ref[...].T, cos_ref[...], sin_ref[...], -1.0)
-    dq_ref[...] = dq
-    prod = dq * (qp_ref[...] * iq_ref[...])
+    d_ref[0] = dq
+    prod = dq * (pre_ref[0] * column(inv_ref, 0, width))
     gainq_ref[...] = jnp.sum(prod, axis=0, keepdims=True)
     rq_ref[...] += prod * gq_ref[...]
     dk = rope_block(dk_acc[...], cos_ref[...], sin_ref[...], -1.0)
-    dk_ref[...] = dk
-    prod = dk * (kp_ref[...] * ik_ref[...])
+    d_ref[1] = dk
+    prod = dk * (pre_ref[1] * column(inv_ref, 1, width))
     gaink_ref[...] = jnp.sum(prod, axis=0, keepdims=True)
     rk_ref[...] += prod * gk_ref[...]
-    dv_ref[...] = dv_acc[...].astype(BF16)
+    d_ref[2] = dv_acc[...]
 
 
 def specs(tokens, text, width, heads):
     col = pl.BlockSpec((tokens, width), lambda i: (0, i))
+    three = pl.BlockSpec((3, tokens, width), lambda i: (0, 0, i))
     tcol = pl.BlockSpec((text, width), lambda i: (0, i))
-    stat = pl.BlockSpec((tokens, 1), lambda i: (0, 0))
+    stat = pl.BlockSpec((8, tokens), lambda i: (0, 0))
     gain = pl.BlockSpec((1, width), lambda i: (0, i))
     table = pl.BlockSpec((tokens, width), lambda i: (0, 0))
     lse = pl.BlockSpec((1, heads, tokens), lambda i: (i, 0, 0))
     scalar = pl.BlockSpec(memory_space=pltpu.SMEM)
-    return col, tcol, stat, gain, table, lse, scalar
+    return col, three, tcol, stat, gain, table, lse, scalar
 
 
 def sds(shape, dtype=F32):
     return jax.ShapeDtypeStruct(shape, dtype)
 
 
-def attn_forward(length, qp, kp, vp, iq, ik, gq, gk, cosine, sine, tk, tv, gate):
-    tokens, columns = qp.shape
+def attn_forward(length, pre, inv, gq, gk, cosine, sine, tk, tv, gate):
+    _, tokens, columns = pre.shape
     text, width = tk.shape[0], cosine.shape[1]
     heads, blocks = width // HD, columns // width
-    col, tcol, stat, gain, table, lse, scalar = specs(tokens, text, width, heads)
+    col, three, tcol, stat, gain, table, lse, scalar = specs(tokens, text, width, heads)
+    flat = (tokens, columns)
     return pl.pallas_call(
         attn_fwd_kernel,
         grid=(blocks,),
-        in_specs=[scalar, col, col, col, stat, stat, gain, gain, table, table, tcol, tcol, gain],
+        in_specs=[scalar, three, stat, gain, gain, table, table, tcol, tcol, gain],
         out_specs=[col, col, col, col, col, col, lse, lse],
-        out_shape=[
-            sds(qp.shape, BF16), sds(qp.shape, BF16), sds(qp.shape, BF16), sds(qp.shape, BF16),
-            sds(qp.shape), sds(qp.shape),
-            sds((blocks, heads, tokens)), sds((blocks, heads, tokens)),
-        ],
-    )(length, qp, kp, vp, iq, ik, gq, gk, cosine, sine, tk, tv, gate)
-
-
-def attn_backward(length, q, k, v, tk, tv, g, so, co, ls, lc, qp, kp, iq, ik, gq, gk, cosine, sine, gate):
+        out_shape=[sds(flat, BF16)] * 4 + [sds(flat)] * 2 + [sds((blocks, heads, tokens))] * 2,
+    )(length, pre, inv, gq, gk, cosine, sine, tk, tv, gate)
+
+
+def attn_backward(length, q, k, v, tk, tv, g, so, co, ls, lc, pre, inv, gq, gk, cosine, sine, gate):
     tokens, columns = q.shape
     text, width = tk.shape[0], cosine.shape[1]
     heads, blocks = width // HD, columns // width
-    col, tcol, stat, gain, table, lse, scalar = specs(tokens, text, width, heads)
+    col, three, tcol, stat, gain, table, lse, scalar = specs(tokens, text, width, heads)
     return pl.pallas_call(
         attn_bwd_kernel,
         grid=(blocks,),
         in_specs=[scalar, col, col, col, tcol, tcol, col, col, col, lse, lse,
-                  col, col, stat, stat, gain, gain, table, table, gain],
-        out_specs=[col, col, col, tcol, tcol, table, table, gain, gain, gain],
+                  three, stat, gain, gain, table, table, gain],
+        out_specs=[three, tcol, tcol, table, table, gain, gain, gain],
         out_shape=[
-            sds(q.shape), sds(q.shape), sds(q.shape, BF16), sds(tk.shape), sds(tk.shape),
+            sds(pre.shape), sds(tk.shape), sds(tk.shape),
             sds((tokens, width)), sds((tokens, width)),
             sds((1, columns)), sds((1, columns)), sds((1, columns)),
         ],
@@ -358,8 +354,7 @@
             pltpu.VMEM((width, tokens), F32),
             pltpu.VMEM((tokens, width), F32), pltpu.VMEM((tokens, width), F32),
         ],
-    )(length, q, k, v, tk, tv, g, so, co, ls, lc, qp, kp, iq, ik, gq, gk, cosine, sine,
-      gate)
+    )(length, q, k, v, tk, tv, g, so, co, ls, lc, pre, inv, gq, gk, cosine, sine, gate)
 
 
 def pick(rows, cols, step, part):
@@ -409,21 +404,41 @@
         out_shape=sds((g.shape[1], depth), BF16),
     )(g, w)
 
+def put_relative(dst, src, me, count):
+    rows = dst.shape[0] // count
+    for p in range(count):
+        start = pl.multiple_of((me ^ p) * rows, 16)
+        dst[p * rows : (p + 1) * rows, :] = src[pl.ds(start, rows), :]
+
+
+def put_halves(keep, send, value, count, bit):
+    rows = value.shape[0] // count
+    low = (1 << bit) - 1
+    for p in range(count):
+        place = (p & low) | (p >> (bit + 1) << bit)
+        (send if p >> bit & 1 else keep)[place] = value[p * rows : (p + 1) * rows]
+
+
 def ffn_kernel(
-    s_ref, b_ref, w_ref, d_ref, wgo_ref, wuo_ref, wdo_ref, fo_ref, fp_ref, so_ref, sp_ref,
-    st, bt, wg, wu, facc, sacc,
+    bits, id_ref, s_ref, b_ref, w_ref, d_ref,
+    gk_ref, gs_ref, uk_ref, us_ref, dk_ref, ds_ref, fo_ref, fp_ref, so_ref, sp_ref,
+    st, bt, tmp, wg, wu, facc, sacc,
 ):
     step = pl.program_id(0)
     depth, _, cols = w_ref.shape
     own = fo_ref.shape[0]
+    count = 2 * gk_ref.shape[0]
+
     @pl.when(step == 0)
     def _():
-        for c in range(depth // 256):
-            part = slice(c * 256, (c + 1) * 256)
-            st[part, :] = s_ref[:, part].astype(F32).T.astype(BF16)
-            bt[part, :] = b_ref[:, part].astype(F32).T.astype(BF16)
+        for src, dst in ((s_ref, st), (b_ref, bt)):
+            for c in range(depth // 256):
+                part = slice(c * 256, (c + 1) * 256)
+                tmp[part, :] = src[:, part].astype(F32).T.astype(BF16)
+            put_relative(dst, tmp, id_ref[0], count)
         facc[...] = jnp.zeros_like(facc)
         sacc[...] = jnp.zeros_like(sacc)
+
     for c in range(depth // 128):
         part = slice(c * 128, (c + 1) * 128)
         w = w_ref[part].reshape(256, cols)
@@ -438,11 +453,12 @@
     hidden = (silu * up).astype(BF16)
     g_gate = (back * up * (sig + silu * (1.0 - sig))).astype(BF16)
     g_up = (back * silu).astype(BF16)
-    dp, rows, _ = wgo_ref.shape
-    for out, left, right in ((wgo_ref, st, g_gate), (wuo_ref, st, g_up), (wdo_ref, bt, hidden)):
-        out[...] = dot(left[...], right).astype(BF16).reshape(dp, rows, cols)
+    put_halves(gk_ref, gs_ref, dot(st[...], g_gate).astype(BF16), count, bits[0])
+    put_halves(uk_ref, us_ref, dot(st[...], g_up).astype(BF16), count, bits[1])
+    put_halves(dk_ref, ds_ref, dot(bt[...], hidden).astype(BF16), count, bits[2])
     facc[...] += dot(hidden, d_ref[...])
     sacc[...] += dot(g_gate, wg[...], 1, 1) + dot(g_up, wu[...], 1, 1)
+
     @pl.when(step == pl.num_programs(0) - 1)
     def _():
         fo_ref[...] = facc[:own]
@@ -450,23 +466,165 @@
         so_ref[...] = sacc[:own]
         sp_ref[...] = sacc[own:].astype(BF16)
 
-def ffn(s, b, w, d, local, dp):
+
+def ffn(ids, s, b, w, d, local, dp, bits):
     tokens, depth = s.shape
     hid = d.shape[0]
     bc = min(256, hid)
-    rest = max(tokens - local, 8)
+    rest = tokens - local
     once = functools.partial(pl.BlockSpec, pipeline_mode=pl.Buffered(1))
     const = lambda i: (0, 0)
+    half = pl.BlockSpec((dp // 2, depth // dp, bc), lambda i: (0, 0, i))
     return pl.pallas_call(
-        ffn_kernel, grid=(hid // bc,),
-        in_specs=[once((tokens, depth), const), once((tokens, depth), const),
-                  pl.BlockSpec((depth, 2, bc), lambda i: (0, 0, i)), pl.BlockSpec((bc, depth), lambda i: (i, 0))],
-        out_specs=[pl.BlockSpec((dp, depth // dp, bc), lambda i: (0, 0, i))] * 3 + [
-                   once((local, depth), const), once((rest, depth), const), once((local, depth), const), once((rest, depth), const)],
-        out_shape=[sds((dp, depth // dp, hid), BF16)] * 3 + [sds((local, depth)), sds((rest, depth), BF16), sds((local, depth)), sds((rest, depth), BF16)],
-        scratch_shapes=[pltpu.VMEM((depth, tokens), BF16)] * 2 + [pltpu.VMEM((depth, bc), BF16)] * 2 + [pltpu.VMEM((tokens, depth), F32)] * 2,
+        functools.partial(ffn_kernel, bits),
+        grid=(hid // bc,),
+        in_specs=[
+            pl.BlockSpec(memory_space=pltpu.SMEM),
+            once((tokens, depth), const), once((tokens, depth), const),
+            pl.BlockSpec((depth, 2, bc), lambda i: (0, 0, i)),
+            pl.BlockSpec((bc, depth), lambda i: (i, 0)),
+        ],
+        out_specs=[half] * 6 + [
+            once((local, depth), const), once((rest, depth), const),
+            once((local, depth), const), once((rest, depth), const),
+        ],
+        out_shape=[sds((dp // 2, depth // dp, hid), BF16)] * 6 + [
+            sds((local, depth)), sds((rest, depth), BF16),
+            sds((local, depth)), sds((rest, depth), BF16),
+        ],
+        scratch_shapes=[
+            pltpu.VMEM((depth, tokens), BF16), pltpu.VMEM((depth, tokens), BF16),
+            pltpu.VMEM((depth, tokens), BF16),
+            pltpu.VMEM((depth, bc), BF16), pltpu.VMEM((depth, bc), BF16),
+            pltpu.VMEM((tokens, depth), F32), pltpu.VMEM((tokens, depth), F32),
+        ],
         compiler_params=pltpu.CompilerParams(vmem_limit_bytes=62 << 20),
-    )(s, b, w, d)
+    )(ids, s, b, w, d)
+
+
+def project_kernel(id_ref, xo_ref, xp_ref, front_ref, w_ref, got_ref, first_ref, pre_ref, sq_ref):
+    j = pl.program_id(0)
+    local, depth = xo_ref.shape
+    own = got_ref.shape[2]
+    f = id_ref[1]
+
+    @pl.when(j == 0)
+    def _():
+        for i, ref in enumerate((xo_ref, xp_ref)):
+            x = ref[...].astype(F32)
+            inv = lax.rsqrt(jnp.sum(x * x, axis=1, keepdims=True) * (1.0 / depth) + EPSILON)
+            first_ref[i * local : (i + 1) * local, :] = (x * inv * front_ref[...]).astype(BF16)
+        sq_ref[...] = jnp.zeros_like(sq_ref)
+
+    mine = pl.ds(pl.multiple_of(f * own, 128), own)
+    other = pl.ds(pl.multiple_of((1 - f) * own, 128), own)
+    out = dot(first_ref[:, mine], w_ref[0, :, mine]) + dot(first_ref[:, other], got_ref[0])
+    pre_ref[0] = out
+    square = out * out
+    part = square[:, :128]
+    for c in range(1, own // 128):
+        part = part + square[:, c * 128 : (c + 1) * 128]
+    sq_ref[pl.ds(j, 1), :] = jnp.sum(part.T, axis=0, keepdims=True)
+
+
+def project(ids, xo, xp, front, w, got):
+    local, depth = xo.shape
+    own = got.shape[2]
+    tokens = 2 * local
+    const = lambda j: (0, 0)
+    return pl.pallas_call(
+        project_kernel,
+        grid=(3,),
+        in_specs=[
+            pl.BlockSpec(memory_space=pltpu.SMEM),
+            pl.BlockSpec((local, depth), const), pl.BlockSpec((local, depth), const),
+            pl.BlockSpec((1, depth), const),
+            pl.BlockSpec((1, own, depth), lambda j: (j, 0, 0)),
+            pl.BlockSpec((1, own, own), lambda j: (j, 0, 0)),
+        ],
+        out_specs=[
+            pl.BlockSpec((tokens, depth), const),
+            pl.BlockSpec((1, tokens, own), lambda j: (j, 0, 0)),
+            pl.BlockSpec((8, tokens), const),
+        ],
+        out_shape=[sds((tokens, depth), BF16), sds((3, tokens, own)), sds((8, tokens))],
+    )(ids, xo, xp, front, w, got)
+
+
+def project_back_kernel(
+    bits, id_ref, d_ref, pre_ref, stat_ref, gain_ref, first_ref, w_ref, got_ref,
+    qk_ref, qs_ref, kk_ref, ks_ref, vk_ref, vs_ref, own_ref, peer_ref, gt, tmp, acc,
+):
+    j = pl.program_id(0)
+    tokens, own = d_ref.shape[1:]
+    local = own_ref.shape[0]
+    f = id_ref[1]
+    count = 2 * qk_ref.shape[0]
+    inv, mean = column(stat_ref, j, 128), column(stat_ref, j + 3, 128)
+    grads = []
+    for c in range(own // 128):
+        part = slice(c * 128, (c + 1) * 128)
+        g = inv * (d_ref[0, :, part] * gain_ref[0, :, part] - pre_ref[0, :, part] * inv * mean)
+        tmp[part, :] = g.T.astype(BF16)
+        grads.append(g.astype(BF16))
+    g = jnp.concatenate(grads, axis=1)
+    put_relative(gt, tmp, id_ref[0] % count, count)
+
+    mine = pl.ds(pl.multiple_of(f * own, 128), own)
+    other = pl.ds(pl.multiple_of((1 - f) * own, 128), own)
+    wide = dot(gt[...], first_ref[...]).astype(BF16)
+    refs = ((qk_ref, qs_ref), (kk_ref, ks_ref), (vk_ref, vs_ref))
+    for i, (keep, send) in enumerate(refs):
+
+        @pl.when(j == i)
+        def _(i=i, keep=keep, send=send):
+            put_halves(keep, send, wide, count, bits[i])
+
+    @pl.when(j == 0)
+    def _():
+        acc[...] = jnp.zeros_like(acc)
+
+    acc[:, mine] += dot(g, w_ref[0, :, mine], 1, 1)
+    acc[:, other] += dot(g, got_ref[0], 1, 1)
+
+    @pl.when(j == 2)
+    def _():
+        own_ref[...] = acc[:local]
+        peer_ref[...] = acc[local:].astype(BF16)
+
+
+def project_back(ids, d, pre, stats, gain, first, w, got, dp, bits):
+    _, tokens, own = d.shape
+    depth = first.shape[1]
+    local = tokens // 2
+    share = depth // dp
+    const = lambda j: (0, 0)
+    block = lambda j: (j, 0, 0)
+    half = pl.BlockSpec((dp // 4, share, depth), lambda j: (0, 0, 0), pipeline_mode=pl.Buffered(1))
+    return pl.pallas_call(
+        functools.partial(project_back_kernel, bits),
+        grid=(3,),
+        in_specs=[
+            pl.BlockSpec(memory_space=pltpu.SMEM),
+            pl.BlockSpec((1, tokens, own), block), pl.BlockSpec((1, tokens, own), block),
+            pl.BlockSpec((8, tokens), const),
+            pl.BlockSpec((1, 1, own), block),
+            pl.BlockSpec((tokens, depth), const, pipeline_mode=pl.Buffered(1)),
+            pl.BlockSpec((1, own, depth), block), pl.BlockSpec((1, own, own), block),
+        ],
+        out_specs=[half] * 6 + [
+            pl.BlockSpec((local, depth), const, pipeline_mode=pl.Buffered(1)),
+            pl.BlockSpec((local, depth), const, pipeline_mode=pl.Buffered(1)),
+        ],
+        out_shape=[sds((dp // 4, share, depth), BF16)] * 6 + [
+            sds((local, depth)), sds((local, depth), BF16),
+        ],
+        scratch_shapes=[
+            pltpu.VMEM((own, tokens), BF16), pltpu.VMEM((own, tokens), BF16),
+            pltpu.VMEM((tokens, depth), F32),
+        ],
+        compiler_params=pltpu.CompilerParams(vmem_limit_bytes=62 << 20),
+    )(ids, d, pre, stats, gain, first, w, got)
 
 
 def time_embed(timesteps):
@@ -505,11 +663,16 @@
 ):
     n, f = lax.axis_size("fsdp"), lax.axis_index("fsdp")
     dpn, me = lax.axis_size("dp"), lax.axis_index("dp")
-    order_a, order_b, order_c = orders()
+    bits = list(range(dp_bits()))
+    order_a, order_b, order_c = orders(bits)
+    low_bits = bits[:-1]
     own_d = D // n
     local = hidden_in.shape[1]
+    tokens = n * local
     width = 2 * HD
     share = D // dpn
+    paired = n == 2 and dpn >= 4
+    ids = jnp.stack([me, f]).astype(jnp.int32)
     x_bf, dy_bf = hidden_in[0], cotangent[0]
 
     time_low = time_embed(timesteps)
@@ -521,33 +684,29 @@
     scale_attn, gate_attn = modulation[0:1], jnp.tanh(modulation[1:2])
     scale_ffn, gate_ffn = modulation[2:3], jnp.tanh(modulation[3:4])
 
-    x_all = jnp.concatenate(gather_rot(x_bf), axis=0)
+    w_flat = jnp.moveaxis(w_qkv, 1, 0)
+    w_parts = exchange_rot(w_flat, 2)
+    x_parts = gather_rot(x_bf)
     dy_all = jnp.concatenate(gather_rot(dy_bf), axis=0)
     places = jnp.concatenate(gather_rot(patch_positions[0]), axis=1)
-    w_parts = exchange_rot(jnp.moveaxis(w_qkv, 1, 0).reshape(3, own_d, n, own_d), 2)
-    w_heads = jnp.concatenate(w_parts, axis=1)
-    text_cols = exchange(jnp.moveaxis(text_state[0].reshape(-1, n, TW // n), 1, 0))
-    text_cols = jnp.concatenate(text_cols, axis=0)
+    text_cols = jnp.concatenate(natural(exchange_rot(text_state[0], 1)), axis=0)
     text_all = lax.all_gather(text_cols, "dp", axis=0, tiled=True)
     gain_full = lax.all_gather(gains, "fsdp", axis=1, tiled=True).astype(F32)
     gain_own = gains.astype(F32)
-    times_all = timesteps
-    for bit in range(dp_bits()):
-        times_all = jnp.concatenate([times_all, dp_swap(times_all, bit)])
-
-    x_f = x_all.astype(F32)
-    inverse_all = inverse_rms(x_f)
-    x_rot = jnp.concatenate(rot_blocks(x_all.reshape(-1, n, own_d), 1), axis=1).astype(F32)
-    front = (gain_full[0] * (1.0 + scale_attn)).reshape(1, n, own_d)
-    front = jnp.concatenate(rot_blocks(front, 1), axis=1)
-    first_all = (x_rot * inverse_all * front).astype(BF16)
-    q_pre, k_pre, v_pre = (dot(first_all, w_heads[j]) for j in range(3))
-    squares = row_sum(jnp.stack([jnp.sum(q_pre * q_pre, -1), jnp.sum(k_pre * k_pre, -1)]))
-    inverse = lax.rsqrt(squares / D + EPSILON)
-    inv_q, inv_k = inverse[0][:, None], inverse[1][:, None]
+
+    front = gain_full[0] * (1.0 + scale_attn)
+    if paired:
+        first_all, pre, squares = project(ids, *x_parts, front, w_flat, w_parts[1])
+    else:
+        w_heads = jnp.concatenate(natural(w_parts), axis=1)
+        x_f = jnp.concatenate(x_parts, axis=0).astype(F32)
+        first_all = (x_f * inverse_rms(x_f) * front).astype(BF16)
+        pre = jnp.stack([dot(first_all, w_heads[j]) for j in range(3)])
+        squares = jnp.pad(jnp.sum(pre[:2] * pre[:2], -1), ((0, 6), (0, 0)))
+    inverse = lax.rsqrt(row_sum(squares) / D + EPSILON)
 
     text_part = text_fwd(text_cols, w_text)
-    text_pre = scatter_rot(rot_blocks(text_part.reshape(2, TEXT, n, own_d), 2))
+    text_pre = scatter_rot(rot_blocks(text_part, 2))
     inv_t = lax.rsqrt(
         pair_sum(jnp.sum(text_pre[0] * text_pre[0], -1, keepdims=True)) / D + EPSILON
     )
@@ -559,10 +718,9 @@
     gate_row = pad_cols(jnp.repeat(head_tanh, HD)[None], width)
     cosine, sine = rope_tables(places, width)
     gq, gk = pad_cols(gain_own[2:3], width), pad_cols(gain_own[3:4], width)
-    qp, kp, vp = (pad_cols(v, width) for v in (q_pre, k_pre, v_pre))
-    tkp, tvp = pad_cols(tk, width), pad_cols(tv, width)
+    pre_p, tkp, tvp = pad_cols(pre, width), pad_cols(tk, width), pad_cols(tv, width)
     q, k, v, mixed_p, so, co, ls, lc = attn_forward(
-        caption_lengths, qp, kp, vp, inv_q, inv_k, gq, gk, cosine, sine, tkp, tvp, gate_row
+        caption_lengths, pre_p, inverse, gq, gk, cosine, sine, tkp, tvp, gate_row
     )
     mixed = mixed_p[:, :own_d]
 
@@ -579,11 +737,18 @@
 
     second_all = jnp.concatenate(gather_rot(second), axis=0)
     branch_all = (gate_ffn * dy_all.astype(F32)).astype(BF16)
-    d_gate, d_up, d_down, ffn_own, ffn_rest, back_own, back_rest = ffn(
-        second_all, branch_all, w_gate_up, w_down, local, dpn
-    )
-    chains = [Halving(d_gate, order_a), Halving(d_up, order_b), Halving(d_down, order_c)]
-    gate_chain, up_chain, down_chain = chains
+    firsts = (order_a[0], order_b[0], order_c[0]) if bits else (0, 0, 0)
+    *halves, ffn_own, ffn_rest, back_own, back_rest = ffn(
+        ids, second_all, branch_all, w_gate_up, w_down, local, dpn, firsts
+    )
+    (ffn_own, ffn_rest, back_own, back_rest), text_all = lax.optimization_barrier(
+        ((ffn_own, ffn_rest, back_own, back_rest), text_all)
+    )
+    chains = [
+        Halving(bits, o, pair=halves[2 * i : 2 * i + 2])
+        for i, o in enumerate((order_a, order_b, order_c))
+    ]
+    ffn_chains = list(chains)
     grad_second = scatter_rot([back_own] + [rows(back_rest, r) for r in range(n - 1)])
     ffn_branch = scatter_rot([ffn_own] + [rows(ffn_rest, r) for r in range(n - 1)])
     output = (after_attn + gate_ffn * ffn_branch).astype(BF16)
@@ -600,15 +765,14 @@
     grad_attn = (gate_attn * grad_after).astype(BF16)
     grad_attn_all = jnp.concatenate(gather_rot(grad_attn), axis=0)
     grad_mixed = dot(grad_attn_all, w_out, 1, 1)
+    d, dtk, dtv, rq, rk, gain_q, gain_k, gate_g = attn_backward(
+        caption_lengths, q, k, v, tkp, tvp, pad_cols(grad_mixed, width), so, co, ls, lc, pre_p,
+        inverse, gq, gk, cosine, sine, gate_row,
+    )
+    rq, rk, dtk = advance(chains, (rq, rk, dtk))
     d_out = dot(grad_attn_all, mixed, 0, 0).astype(BF16)
-    out_chain = Halving(d_out.reshape(dpn, share, own_d), order_c)
-    chains.append(out_chain)
-    dq, dk, dv, dtk, dtv, rq, rk, gain_q, gain_k, gate_g = attn_backward(
-        caption_lengths, q, k, v, tkp, tvp, pad_cols(grad_mixed, width), so, co, ls, lc, qp, kp,
-        inv_q, inv_k, gq, gk, cosine, sine, gate_row,
-    )
-    rq, rk, dtk = advance(chains, (rq, rk, dtk))
-    dq, dk, dv, dtk, dtv = (v_[:, :own_d] for v_ in (dq, dk, dv, dtk, dtv))
+    out_chain = Halving(bits, order_c, whole=relative(d_out.reshape(dpn, share, own_d)))
+    d, dtk, dtv = d[:, :, :own_d], dtk[:, :own_d], dtv[:, :own_d]
     gate_total = jnp.sum(gate_g[0, :own_d].reshape(HEADS // n, HD), axis=1) * (
         1.0 - head_tanh * head_tanh
     )
@@ -616,47 +780,45 @@
     gain_text = jnp.sum(dtk * normed_t, axis=0, keepdims=True)
     means = row_sum(jnp.stack([jnp.sum(rq, -1), jnp.sum(rk, -1)])) / D
     mean_t = pair_sum(jnp.sum(text_hat * normed_t, -1, keepdims=True)) / D
-    grad_q = (inv_q * (dq * gain_own[2] - q_pre * inv_q * means[0][:, None])).astype(BF16)
-    grad_k = (inv_k * (dk * gain_own[3] - k_pre * inv_k * means[1][:, None])).astype(BF16)
-
-    grads = (grad_q, grad_k, dv)
-    wide = []
-    for g in grads:
-        blocks = [
-            dot(g, first_all[:, r * own_d : (r + 1) * own_d], 0, 0).astype(BF16) for r in range(n)
-        ]
-        got = [blocks[0]]
-        for r in range(1, n):
-            got.append(lax.ppermute(blocks[r], "fsdp", [(i, (i - r) % n) for i in range(n)]))
-        got = jnp.stack(got)
-        if n != 2 or dpn == 1:
-            got = jnp.stack(
-                [lax.dynamic_index_in_dim(got, (g_ - f) % n, 0, keepdims=False) for g_ in range(n)]
-            )
-        wide.append(got.reshape(dpn, share, own_d))
-    flip = f if n == 2 else 0
-    qkv_chains = [
-        Halving(w_, o, flip) for w_, o in zip(wide, (order_a, order_b, order_c))
-    ]
-    chains += qkv_chains
 
     grad_tk = (inv_t * (text_hat - normed_t * mean_t)).astype(BF16)
     text_pair = jnp.stack([grad_tk, dtv.astype(BF16)])
-    pair_all = gather_natural(text_pair)
+    pair_all = jnp.concatenate(natural(gather_rot(text_pair)), axis=-1)
+    outgoing = block_of(pair_all, f, 1).reshape(2, TEXT // n, dpn, share).transpose(2, 0, 1, 3)
+    pair_cols = dp_exchange(relative(outgoing), order_a)
+
+    ones, zeros = jnp.ones((1, tokens), F32), jnp.zeros((1, tokens), F32)
+    if paired:
+        stats = jnp.concatenate([inverse[:2], ones, means, zeros, zeros, zeros], axis=0)
+        gain3 = jnp.stack([gain_own[2:3], gain_own[3:4], jnp.ones_like(gain_own[2:3])])
+        low_orders = orders(low_bits)
+        *halves, own_part, peer_part = project_back(
+            ids, d, pre, stats, gain3, first_all, w_flat, w_parts[1], dpn,
+            tuple(o[0] for o in low_orders),
+        )
+        qkv_chains = [
+            Halving(low_bits, o, pair=halves[2 * i : 2 * i + 2]) for i, o in enumerate(low_orders)
+        ]
+        parts = [own_part, peer_part]
+    else:
+        inv, mean = inverse[:2, :, None], means[:, :, None]
+        hat = d[:2] * gain_own[2:4][:, None] - pre[:2] * inv * mean
+        grads = [(inv[0] * hat[0]).astype(BF16), (inv[1] * hat[1]).astype(BF16), d[2].astype(BF16)]
+        wide = [dot(g, first_all, 0, 0).astype(BF16) for g in grads]
+        wide = [jnp.concatenate(natural(exchange_rot(w_, 1)), axis=0) for w_ in wide]
+        qkv_chains = [
+            Halving(bits, o, whole=relative(w_.reshape(dpn, share, own_d)))
+            for w_, o in zip(wide, (order_a, order_b, order_c))
+        ]
+        parts = [
+            sum(dot(rows(g, r), w_heads[j], 1, 1) for j, g in enumerate(grads)) for r in range(n)
+        ]
+        parts = [parts[0]] + [p.astype(BF16) for p in parts[1:]]
+    grad_first = scatter_rot(parts)
+
     text_in = text_bwd(pair_all, w_text)
-    text_in = exchange(text_in.reshape(n, -1, TW // n))
-    text_in = jnp.concatenate(text_in, axis=1)
-    outgoing = pair_all.reshape(2, TEXT, dpn, share).transpose(2, 0, 1, 3)
-    pair_cols = dp_exchange(outgoing, order_a)
-    pair_cols = jnp.take(pair_cols, me ^ jnp.arange(dpn), axis=0)
-    pair_cols = pair_cols.transpose(0, 2, 1, 3).reshape(dpn * TEXT, 2 * share)
-    text_grad = dot(pair_cols, text_all, 0, 0).reshape(2, share, TW // n)
-
-    parts = [
-        sum(dot(rows(g, r), w_heads[j], 1, 1) for j, g in enumerate(grads)) for r in range(n)
-    ]
-    parts = [jnp.concatenate(rot_blocks(p.reshape(-1, n, own_d), 1), axis=1) for p in parts]
-    grad_first = scatter_rot([parts[0]] + [p.astype(BF16) for p in parts[1:]])
+    text_in = jnp.concatenate(natural(exchange_rot(text_in, 0)), axis=1)
+
     inverse_one = inverse_rms(x_own)
     normed_one = x_own * inverse_one
     scaled = grad_first * normed_one
@@ -668,32 +830,48 @@
     ).astype(BF16)
 
     mods = jnp.stack([d_scale_attn, d_gate_attn, d_scale_ffn, d_gate_ffn])
-    mods = pair_sum(dp_exchange(mods.reshape(4, dpn, share).transpose(1, 0, 2), order_a))
-    times = time_embed(times_all)
+    mods = mods.reshape(4, dpn, share).transpose(1, 0, 2)
+    stamp = jnp.full((dpn, 1, share), timesteps[0].astype(F32) / n)
+    mods = pair_sum(dp_exchange(relative(jnp.concatenate([mods, stamp], axis=1)), order_a))
+    times = time_embed(jnp.round(mods[:, 4, 0]))
     times = lax.dynamic_slice_in_dim(times, f * own_te, own_te, 1).astype(F32)
     ada_grad = lax.dot_general(
-        mods.reshape(dpn, 4 * share), times, (((0,), (0,)), ((), ())),
+        mods[:, :4].reshape(dpn, 4 * share), times, (((0,), (0,)), ((), ())),
         precision=lax.Precision.HIGHEST,
     ).reshape(4, share, own_te)
-    two = scatter_rot(rot_blocks(jnp.stack([gain_one, gain_two]).reshape(2, n, own_d), 1))
+    two = scatter_rot(rot_blocks(jnp.stack([gain_one, gain_two]), 1))
     gate_pad = jnp.pad(gate_total, (0, own_d - gate_total.shape[0]))[None]
     small = dp_total(
         jnp.concatenate([two, gain_q[:, :own_d], gain_k[:, :own_d], gain_text, gate_pad], axis=0)
     )
+
+    pair_cols = jnp.concatenate(natural(gather_rot(pair_cols)), axis=2)
+    pair_cols = relative(pair_cols).transpose(0, 2, 1, 3).reshape(dpn * TEXT, 2 * share)
+    text_grad = dot(pair_cols, text_all, 0, 0).reshape(2, share, TW // n)
+
+    chains += [out_chain] + qkv_chains
     while any(c.got is not None for c in chains):
-        advance(chains, ())
+        for c in chains:
+            c.step()
+    qkv_grad = [c.last[0] for c in qkv_chains]
+    if paired:
+        own_side = f == (me >> low_bits[-1] + 1)
+        for i, c in enumerate(qkv_chains):
+            mine, got = exchange_rot(c.cur[0], 1)
+            keep, send = jnp.where(own_side, mine, got), jnp.where(own_side, got, mine)
+            qkv_grad[i] = keep.astype(F32) + dp_swap(send, bits[-1]).astype(F32)
     return (
         output[None],
         grad_input[None],
         text_in[None],
         ada_grad.transpose(2, 0, 1),
         text_grad.transpose(2, 0, 1),
-        jnp.stack([c.cur for c in qkv_chains]).transpose(2, 0, 1),
-        out_chain.cur.T,
+        jnp.stack(qkv_grad).transpose(2, 0, 1),
+        out_chain.last[0].T,
         small[:5],
         small[5, : HEADS // n],
-        jnp.stack([gate_chain.cur, up_chain.cur], axis=1),
-        down_chain.cur.T,
+        jnp.stack([ffn_chains[0].last[0], ffn_chains[1].last[0]], axis=1),
+        ffn_chains[2].last[0].T,
     )
 
 

time: 968 us -> 694 us (0.72)
  waiting for transfers between devices: 304 us -> 168 us
  local copies, waits for them, and re-layouts: 154 us -> 54.6 us
  matrix products: 89.9 us -> 35 us
  Pallas kernels: 218 us -> 264 us
  other arithmetic: 114 us -> 98.7 us
  starting transfers between devices: 59.5 us -> 48.2 us
    ppermute x44 -> x40, waiting for transfers between devices: 299 us -> 158 us  [dp_swap(): return lax.ppermute(value, 'dp', [(i, i ^ 1 << bit) for i in range(n)])]
    dot_general x20 -> x5, matrix products: 83.9 us -> 28.1 us  [dot(): lax.dot_general(a, b, (((ca,), (cb,)), ((), ())), preferred_element_type=...]
    pallas_call x2 -> x4, Pallas kernels: 123 us -> 169 us  [the longest x1 90.1 us: ffn(): pl.pallas_call(functools.partial(ffn_kernel, bits), grid=(hid // bc,), in...]
    dynamic_slice x21 -> x8, local copies, waits for them, and re-layouts: 54.2 us -> 9.33 us  [block_of(): return lax.dynamic_slice_in_dim(value, index * size, size, axis)]
    unnamed x256 -> x132, local copies, waits for them, and re-layouts: 44.1 us -> 10.1 us
    reshape x4 -> x2, local copies, waits for them, and re-layouts: 11.1 us -> 0.16 us  [the longest x1 0.08 us: on_device(): mods[:, :4].reshape(dpn, 4 * share)]
    ppermute x44 -> x40, starting transfers between devices: 54 us -> 43.3 us  [dp_swap(): return lax.ppermute(value, 'dp', [(i, i ^ 1 << bit) for i in range(n)])]
    convert_element_type x26 -> x21, other arithmetic: 29.3 us -> 26.2 us  [step(): self.cur = total.astype(BF16)]
  transfers between devices with their start and end apart: 69 -> 66, of which waited for: 30 -> 24; matrix products, arithmetic and copies ran while one was open for 31% -> 24% of each run, Pallas kernels for 10% -> 38%
where the time goes in v3:
time: 694 us; the launch traced here: 688 us
  Pallas kernels  264 us (38%)
  waiting for transfers between devices  168 us (24%)
  other arithmetic  98.7 us (14%)
  local copies, waits for them, and re-layouts  54.6 us (8%)
  starting transfers between devices  48.2 us (7%)
  matrix products  35 us (5%)
  between operations  16.9 us (2%)
    ppermute x40, waiting for transfers between devices, dp_swap(): return lax.ppermute(value, 'dp', [(i, i ^ 1 << bit) for i in range(n)])  158 us
    pallas_call x1, Pallas kernels, ffn(): pl.pallas_call(functools.partial(ffn_kernel, bits), grid=(hid // bc,), in...  90.1 us
    pallas_call x1, Pallas kernels, attn_backward(): pl.pallas_call(attn_bwd_kernel, grid=(blocks,), in_specs=[scalar, col, co...  64.7 us
    ppermute x40, starting transfers between devices, dp_swap(): return lax.ppermute(value, 'dp', [(i, i ^ 1 << bit) for i in range(n)])  43.3 us
    pallas_call x1, Pallas kernels, attn_forward(): pl.pallas_call(attn_fwd_kernel, grid=(blocks,), in_specs=[scalar, three,...  32.1 us
    pallas_call x1, Pallas kernels, project_back(): pl.pallas_call(functools.partial(project_back_kernel, bits), grid=(3,), i...  31.8 us
    dot_general x5, matrix products, dot(): lax.dot_general(a, b, (((ca,), (cb,)), ((), ())), preferred_element_type=...  28.1 us
    convert_element_type x21, other arithmetic, step(): self.cur = total.astype(BF16)  26.2 us
  transfers between devices with their start and end apart: 66, of which 24 were waited for; matrix products, arithmetic and copies ran while one was open for 24% of the time, Pallas kernels for 38%

profile of v3, /device:TPU:0, one launch (start us, length us, event | category | flops | bytes accessed | tf_op | source)
XLA Modules:
  0.0 687.7 jit_solution(10096816562272342596)
XLA Ops:
  23.3 16.2 %shard_map.222 = f32[2,256,1536]{2,1,0:T(8,128)} custom-call(bf16[256,2048]{1,0:T(8,128)(2,1)} %pad_maximum_fusion.7.x_ref, bf16[2048,2,1536]{2,1,0:T(2,128)(2,1)} %w_ref.5), custom_call_target="tpu_custom_call" | custom-call | tf_op jit(solution)/shard_map/pallas_call | solution.py:381
  53.6 14.6 %shard_map.221 = (bf16[1024,1536]{1,0:T(8,128)(2,1)}, f32[3,1024,768]{2,1,0:T(8,128)}, f32[8,1024]{1,0:T(8,128)}) custom-call(s32[2]{0:T(128)} %pad_add_fusion.1.id_ref, bf16[512,1536]{1,0:T(8,128)(2,1)} %bitcast.281, bf16[512,1536]{1,0:T(8,128)(2,1)} %collective-permute-done.1.xp_ref, f32[1,1536]{1,0:T(1,128)} %get-tuple-element.193.front_ref, ...), custom_call_target="tpu_custom_call" | custom-call | tf_op jit(solution)/shard_map/pallas_call | solution.py:535
  71.0 32.1 %shard_map.223 = (bf16[1024,768]{1,0:T(8,128)(2,1)}, bf16[1024,768]{1,0:T(8,128)(2,1)}, bf16[1024,768]{1,0:T(8,128)(2,1)}, bf16[1024,768]{1,0:T(8,128)(2,1)}, f3...) custom-call(s32[1]{0:T(128)S(6)} %copy.134.len_ref, ...), custom_call_target="tpu_custom_call" | custom-call | tf_op jit(solution)/shard_map/pallas_call | solution.py:325
  120.1 90.1 %shard_map.224 = (bf16[8,96,2048]{2,1,0:T(8,128)(2,1)}, bf16[8,96,2048]{2,1,0:T(8,128)(2,1)}, bf16[8,96,2048]{2,1,0:T(8,128)(2,1)}, bf16[8,96,2048]{2,1,0:T(8,12...) custom-call(s32[2]{0:T(128)} %pad_add_fusion.1.id_ref, ...), custom_call_target="tpu_custom_call" | custom-call | tf_op jit(solution)/shard_map/pallas_call | solution.py:478
  216.8 5.0 multiply_reduce_fusion
  221.8 5.5 fusion.7
  237.4 6.9 %fusion.18.g_ref = f32[1024,768]{1,0:T(8,128)} fusion(bf16[768,1536]{1,0:T(8,128)(2,1)} %param.23, bf16[512,1536]{1,0:T(8,128)(2,1)} %collective-permute-done.13, bf16[512,1536]{1,0:T(8,128)(2,1)} %get-tuple-element.162), kind=kOutput, calls=%fused_computation.61 | convolution fusion | flops 2422210560 | bytes 8650752 | tf_op jit(solution)/shard_map/dot_general | solution.py:25
  244.3 64.7 %shard_map.225 = (f32[3,1024,768]{2,1,0:T(8,128)}, f32[256,768]{1,0:T(8,128)}, f32[256,768]{1,0:T(8,128)}, f32[1024,128]{1,0:T(8,128)}, f32[1024,128]{1,0:T(8,12...) custom-call(s32[1]{0:T(128)S(6)} %copy.134.len_ref, bf16[1024,768]{1,0:T(8,128)(2,1)} %get-tuple-element.70.q_ref, ...), custom_call_target="tpu_custom_call" | custom-call | tf_op jit(solution)/shard_map/pallas_call | solution.py:339
  314.8 6.0 convolution_convert_fusion
  356.1 31.8 %shard_map.226 = (bf16[4,96,1536]{2,1,0:T(8,128)(2,1)}, bf16[4,96,1536]{2,1,0:T(8,128)(2,1)}, bf16[4,96,1536]{2,1,0:T(8,128)(2,1)}, bf16[4,96,1536]{2,1,0:T(8,12...) custom-call(s32[2]{0:T(128)} %pad_add_fusion.1.id_ref, ...), custom_call_target="tpu_custom_call" | custom-call | tf_op jit(solution)/shard_map/pallas_call | solution.py:604
  392.2 14.8 %shard_map.227 = bf16[256,2048]{1,0:T(8,128)(2,1)} custom-call(bf16[2,256,1536]{2,1,0:T(8,128)(2,1)} %pad_maximum_fusion.4.g_ref, bf16[2048,2,1536]{2,1,0:T(2,128)(2,1)} %w_ref.5), custom_call_target="tpu_custom_call" | custom-call | tf_op jit(solution)/shard_map/pallas_call | solution.py:400
  415.8 7.0 %collective-permute-done.27 = bf16[2,2,2,2,128,96]{4,5,3,2,1,0:T(8,128)(2,1)S(1)} collective-permute-done((bf16[2,2,2,2,128,96]{4,5,3,2,1,0:T(8,128)(2,1)S(1)}, bf16[2,2,2,2,128,96]{4,5,3,2,1,0:T(8,128)(2,1)S(1)}, u32[]{:S(2)}, u32[]{:S(2)}) %collective-permute-start.27) | collective-permute-done | bytes 393248 | tf_op jit(solution)/shard_map/ppermute | solution.py:91
  429.5 20.4 %collective-permute-done.32 = bf16[4,96,1536]{2,1,0:T(8,128)(2,1)S(1)} collective-permute-done((bf16[4,96,1536]{2,1,0:T(8,128)(2,1)S(1)}, bf16[4,96,1536]{2,1,0:T(8,128)(2,1)S(1)}, u32[]{:S(2)}, u32[]{:S(2)}) %collective-permute-start.32) | collective-permute-done | bytes 1179680 | tf_op jit(solution)/shard_map/ppermute | solution.py:91
  500.5 4.7 fusion.20
  527.3 30.6 %collective-permute-done.29 = bf16[2,2,2,2,128,96]{4,5,3,2,1,0:T(8,128)(2,1)S(1)} collective-permute-done((bf16[2,2,2,2,128,96]{4,5,3,2,1,0:T(8,128)(2,1)S(1)}, bf16[2,2,2,2,128,96]{4,5,3,2,1,0:T(8,128)(2,1)S(1)}, u32[]{:S(2)}, u32[]{:S(2)}) %collective-permute-start.29) | collective-permute-done | bytes 393248 | tf_op jit(solution)/shard_map/ppermute | solution.py:91
  560.2 6.2 collective-permute-done.44
  567.9 10.3 %collective-permute-done.34 = bf16[1,96,1536]{2,1,0:T(8,128)(2,1)S(1)} collective-permute-done((bf16[1,96,1536]{2,1,0:T(8,128)(2,1)S(1)}, bf16[1,96,1536]{2,1,0:T(8,128)(2,1)S(1)}, u32[]{:S(2)}, u32[]{:S(2)}) %collective-permute-start.34) | collective-permute-done | bytes 294944 | tf_op jit(solution)/shard_map/ppermute | solution.py:91
  579.1 13.2 %collective-permute-done.50 = bf16[1,96,768]{2,1,0:T(8,128)(2,1)S(1)} collective-permute-done((bf16[1,96,768]{2,1,0:T(8,128)(2,1)S(1)}, bf16[1,96,768]{2,1,0:T(8,128)(2,1)S(1)}, u32[]{:S(2)}, u32[]{:S(2)}) %collective-permute-start.50) | collective-permute-done | bytes 147488 | tf_op jit(solution)/shard_map/ppermute | solution.py:91
  603.7 24.2 %collective-permute-done.46 = bf16[96,768]{1,0:T(8,128)(2,1)S(1)} collective-permute-done((bf16[96,768]{1,0:T(8,128)(2,1)S(1)}, bf16[96,768]{1,0:T(8,128)(2,1)S(1)}, u32[]{:S(2)}, u32[]{:S(2)}) %collective-permute-start.46) | collective-permute-done | bytes 147488 | tf_op jit(solution)/shard_map/ppermute | solution.py:91
  631.1 11.5 %collective-permute-done.36 = bf16[96,768]{1,0:T(8,128)(2,1)S(1)} collective-permute-done((bf16[96,768]{1,0:T(8,128)(2,1)S(1)}, bf16[96,768]{1,0:T(8,128)(2,1)S(1)}, u32[]{:S(2)}, u32[]{:S(2)}) %collective-permute-start.36) | collective-permute-done | bytes 147488 | tf_op jit(solution)/shard_map/ppermute | solution.py:91
  643.7 7.4 %collective-permute-done.61 = bf16[1,96,2048]{2,1,0:T(8,128)(2,1)S(1)} collective-permute-done((bf16[1,96,2048]{2,1,0:T(8,128)(2,1)S(1)}, bf16[1,96,2048]{2,1,0:T(8,128)(2,1)S(1)}, u32[]{:S(2)}, u32[]{:S(2)}) %collective-permute-start.61) | collective-permute-done | bytes 393248 | tf_op jit(solution)/shard_map/ppermute | solution.py:91
  651.2 8.3 %collective-permute-done.58 = bf16[1,96,2048]{2,1,0:T(8,128)(2,1)S(1)} collective-permute-done((bf16[1,96,2048]{2,1,0:T(8,128)(2,1)S(1)}, bf16[1,96,2048]{2,1,0:T(8,128)(2,1)S(1)}, u32[]{:S(2)}, u32[]{:S(2)}) %collective-permute-start.58) | collective-permute-done | bytes 393248 | tf_op jit(solution)/shard_map/ppermute | solution.py:91
  662.1 5.8 collective-permute-done.64
  671.8 8.7 %fusion = f32[2048,2,96]{0,2,1:T(8,128)} fusion(bf16[2,96,4096]{2,1,0:T(8,128)(2,1)S(1)} %bitcast.308, bf16[4096,2048]{1,0:T(8,128)(2,1)} %all-gather.2.cloned.1.call-done), kind=kOutput, calls=%fused_computation.4 | convolution fusion | flops 3221225472 | bytes 19922944 | tf_op jit(solution)/shard_map/dot_general | solution.py:25
  (436 shorter events, 224.9 us)
Async XLA Ops:
  7.2 203.0 %all-gather.2.cloned.1.call-start = ((), (), s32[]{:S(2)}) async-start(), calls=%async_computation | async-start | bytes 17825792 | tf_op jit(solution)/shard_map/all_gather | solution.py:693
  12.8 40.8 %collective-permute-start.1 = (bf16[512,1536]{1,0:T(8,128)(2,1)S(1)}, bf16[512,1536]{1,0:T(8,128)(2,1)}, u32[]{:S(2)}, u32[]{:S(2)}) collective-permute-start(bf16[512,1536]{1,0:T(8,128)(2,1)S(1)} %bitcast.282), channel_id=1, source_target_pairs={{0,1},{1,0},{2,3},{3,2},{4,5},{5,4},{6,7},{7,6},{8,9},{9,8},{10,11... | collective-permute-start | bytes 4718600 | tf_op jit(solution)/shard_map/ppermute | solution.py:30
  210.8 98.2 %collective-permute-start.14 = (bf16[8,96,2048]{2,1,0:T(8,128)(2,1)}, bf16[8,96,2048]{2,1,0:T(8,128)(2,1)}, u32[]{:S(2)}, u32[]{:S(2)}) collective-permute-start(bf16[8,96,2048]{2,1,0:T(8,128)(2,1)} %get-tuple-element.81), channel_id=1, source_target_pairs={{0,2},{2,0},{4,6},{6,4},{8,10},{10,8},{12,14},{14,12},{16,18},{18,... | collective-permute-start | bytes 9437192 | tf_op jit(solution)/shard_map/ppermute | solution.py:91
  213.8 95.2 %collective-permute-start.15 = (bf16[8,96,2048]{2,1,0:T(8,128)(2,1)}, bf16[8,96,2048]{2,1,0:T(8,128)(2,1)}, u32[]{:S(2)}, u32[]{:S(2)}) collective-permute-start(bf16[8,96,2048]{2,1,0:T(8,128)(2,1)} %get-tuple-element.82), channel_id=1, source_target_pairs={{0,4},{2,6},{4,0},{6,2},{8,12},{10,14},{12,8},{14,10},{16,20},{18,... | collective-permute-start | bytes 9437192 | tf_op jit(solution)/shard_map/ppermute | solution.py:91
  215.3 93.7 %collective-permute-start.16 = (bf16[8,96,2048]{2,1,0:T(8,128)(2,1)}, bf16[8,96,2048]{2,1,0:T(8,128)(2,1)}, u32[]{:S(2)}, u32[]{:S(2)}) collective-permute-start(bf16[8,96,2048]{2,1,0:T(8,128)(2,1)} %get-tuple-element.83), channel_id=1, source_target_pairs={{0,8},{2,10},{4,12},{6,14},{8,0},{10,2},{12,4},{14,6},{16,24},{18,... | collective-permute-start | bytes 9437192 | tf_op jit(solution)/shard_map/ppermute | solution.py:91
  312.3 41.0 %collective-permute-start.17 = (f32[2,1024]{1,0:T(2,128)}, f32[2,1024]{1,0:T(2,128)}, u32[]{:S(2)}, u32[]{:S(2)}) collective-permute-start(f32[2,1024]{1,0:T(2,128)} %pad_maximum_fusion.17), channel_id=1, source_target_pairs={{0,1},{1,0},{2,3},{3,2},{4,5},{5,4},{6,7},{7,6},{8,9},{9,8},{10,11... | collective-permute-start | bytes 24584 | tf_op jit(solution)/shard_map/ppermute | solution.py:30
  328.5 83.3 %collective-permute-start.47 = (bf16[8,96,768]{2,1,0:T(8,128)(2,1)}, bf16[8,96,768]{2,1,0:T(8,128)(2,1)}, u32[]{:S(2)}, u32[]{:S(2)}) collective-permute-start(bf16[8,96,768]{2,1,0:T(8,128)(2,1)} %bitcast.82), channel_id=1, source_target_pairs={{0,8},{2,10},{4,12},{6,14},{8,0},{10,2},{12,4},{14,6},{16,24},{18,... | collective-permute-start | bytes 3538952 | tf_op jit(solution)/shard_map/ppermute | solution.py:91
  334.8 120.3 %collective-permute-start.59 = (bf16[4,96,2048]{2,1,0:T(8,128)(2,1)}, bf16[4,96,2048]{2,1,0:T(8,128)(2,1)}, u32[]{:S(2)}, u32[]{:S(2)}) collective-permute-start(bf16[4,96,2048]{2,1,0:T(8,128)(2,1)} %bitcast.101), channel_id=1, source_target_pairs={{0,2},{2,0},{4,6},{6,4},{8,10},{10,8},{12,14},{14,12},{16,18},{18,... | collective-permute-start | bytes 4718600 | tf_op jit(solution)/shard_map/ppermute | solution.py:91
  341.1 117.2 %collective-permute-start.56 = (bf16[4,96,2048]{2,1,0:T(8,128)(2,1)}, bf16[4,96,2048]{2,1,0:T(8,128)(2,1)}, u32[]{:S(2)}, u32[]{:S(2)}) collective-permute-start(bf16[4,96,2048]{2,1,0:T(8,128)(2,1)} %bitcast.94), channel_id=1, source_target_pairs={{0,4},{2,6},{4,0},{6,2},{8,12},{10,14},{12,8},{14,10},{16,20},{18,... | collective-permute-start | bytes 4718600 | tf_op jit(solution)/shard_map/ppermute | solution.py:91
  349.6 39.0 %collective-permute-start.20 = (bf16[2,256,768]{2,1,0:T(8,128)(2,1)}, bf16[2,256,768]{2,1,0:T(8,128)(2,1)}, u32[]{:S(2)}, u32[]{:S(2)}) collective-permute-start(bf16[2,256,768]{2,1,0:T(8,128)(2,1)} %pad_maximum_fusion.8), channel_id=1, source_target_pairs={{0,1},{1,0},{2,3},{3,2},{4,5},{5,4},{6,7},{7,6},{8,9},{9,8},{10,11... | collective-permute-start | bytes 2359304 | tf_op jit(solution)/shard_map/ppermute | solution.py:30
  388.5 38.8 %collective-permute-start.37 = (bf16[4,96,1536]{2,1,0:T(8,128)(2,1)}, bf16[4,96,1536]{2,1,0:T(8,128)(2,1)}, u32[]{:S(2)}, u32[]{:S(2)}) collective-permute-start(bf16[4,96,1536]{2,1,0:T(8,128)(2,1)} %get-tuple-element.95), channel_id=1, source_target_pairs={{0,4},{2,6},{4,0},{6,2},{8,12},{10,14},{12,8},{14,10},{16,20},{18,... | collective-permute-start | bytes 3538952 | tf_op jit(solution)/shard_map/ppermute | solution.py:91
  424.7 38.7 %collective-permute-start.62 = (bf16[4,96,2048]{2,1,0:T(8,128)(2,1)S(1)}, bf16[4,96,2048]{2,1,0:T(8,128)(2,1)S(1)}, u32[]{:S(2)}, u32[]{:S(2)}) collective-permute-start(bf16[4,96,2048]{2,1,0:T(8,128)(2,1)S(1)} %bitcast.309), channel_id=1, source_target_pairs={{0,4},{2,6},{4,0},{6,2},{8,12},{10,14},{12,8},{14,10},{16,20},{18,... | collective-permute-start | bytes 4718600 | tf_op jit(solution)/shard_map/ppermute | solution.py:91
  427.4 38.8 %collective-permute-start.18 = (bf16[512,1536]{1,0:T(8,128)(2,1)S(1)}, bf16[512,1536]{1,0:T(8,128)(2,1)S(1)}, u32[]{:S(2)}, u32[]{:S(2)}) collective-permute-start(bf16[512,1536]{1,0:T(8,128)(2,1)S(1)} %copy-done.61), channel_id=1, source_target_pairs={{0,1},{1,0},{2,3},{3,2},{4,5},{5,4},{6,7},{7,6},{8,9},{9,8},{10,11... | collective-permute-start | bytes 4718600 | tf_op jit(solution)/shard_map/ppermute | solution.py:54
  452.8 65.1 %collective-permute-start.48 = (bf16[4,96,768]{2,1,0:T(8,128)(2,1)}, bf16[4,96,768]{2,1,0:T(8,128)(2,1)}, u32[]{:S(2)}, u32[]{:S(2)}) collective-permute-start(bf16[4,96,768]{2,1,0:T(8,128)(2,1)} %bitcast.85), channel_id=1, source_target_pairs={{0,4},{2,6},{4,0},{6,2},{8,12},{10,14},{12,8},{14,10},{16,20},{18,... | collective-permute-start | bytes 1769480 | tf_op jit(solution)/shard_map/ppermute | solution.py:91
  458.3 62.1 %collective-permute-start.43 = (bf16[2,96,1536]{2,1,0:T(8,128)(2,1)}, bf16[2,96,1536]{2,1,0:T(8,128)(2,1)}, u32[]{:S(2)}, u32[]{:S(2)}) collective-permute-start(bf16[2,96,1536]{2,1,0:T(8,128)(2,1)} %slice.381), channel_id=1, source_target_pairs={{0,4},{2,6},{4,0},{6,2},{8,12},{10,14},{12,8},{14,10},{16,20},{18,... | collective-permute-start | bytes 1769480 | tf_op jit(solution)/shard_map/ppermute | solution.py:91
  463.4 59.3 %collective-permute-start.38 = (bf16[2,96,1536]{2,1,0:T(8,128)(2,1)}, bf16[2,96,1536]{2,1,0:T(8,128)(2,1)}, u32[]{:S(2)}, u32[]{:S(2)}) collective-permute-start(bf16[2,96,1536]{2,1,0:T(8,128)(2,1)} %slice_bitcast_fusion.7), channel_id=1, source_target_pairs={{0,2},{2,0},{4,6},{6,4},{8,10},{10,8},{12,14},{14,12},{16,18},{18,... | collective-permute-start | bytes 1769480 | tf_op jit(solution)/shard_map/ppermute | solution.py:91
  512.8 83.7 %collective-permute-start.60 = (bf16[2,96,2048]{2,1,0:T(8,128)(2,1)}, bf16[2,96,2048]{2,1,0:T(8,128)(2,1)S(1)}, u32[]{:S(2)}, u32[]{:S(2)}) collective-permute-start(bf16[2,96,2048]{2,1,0:T(8,128)(2,1)} %slice_bitcast_fusion.2), channel_id=1, source_target_pairs={{0,8},{2,10},{4,12},{6,14},{8,0},{10,2},{12,4},{14,6},{16,24},{18,... | collective-permute-start | bytes 2359304 | tf_op jit(solution)/shard_map/ppermute | solution.py:91
  517.9 82.0 %collective-permute-start.57 = (bf16[2,96,2048]{2,1,0:T(8,128)(2,1)}, bf16[2,96,2048]{2,1,0:T(8,128)(2,1)S(1)}, u32[]{:S(2)}, u32[]{:S(2)}) collective-permute-start(bf16[2,96,2048]{2,1,0:T(8,128)(2,1)} %slice_bitcast_fusion.4), channel_id=1, source_target_pairs={{0,8},{2,10},{4,12},{6,14},{8,0},{10,2},{12,4},{14,6},{16,24},{18,... | collective-permute-start | bytes 2359304 | tf_op jit(solution)/shard_map/ppermute | solution.py:91
  520.4 79.8 %collective-permute-start.63 = (bf16[2,96,2048]{2,1,0:T(8,128)(2,1)S(1)}, bf16[2,96,2048]{2,1,0:T(8,128)(2,1)S(1)}, u32[]{:S(2)}, u32[]{:S(2)}) collective-permute-start(bf16[2,96,2048]{2,1,0:T(8,128)(2,1)S(1)} %copy-done.42), channel_id=1, source_target_pairs={{0,2},{2,0},{4,6},{6,4},{8,10},{10,8},{12,14},{14,12},{16,18},{18,... | collective-permute-start | bytes 2359304 | tf_op jit(solution)/shard_map/ppermute | solution.py:91
  599.9 42.8 %collective-permute-start.36 = (bf16[96,768]{1,0:T(8,128)(2,1)S(1)}, bf16[96,768]{1,0:T(8,128)(2,1)S(1)}, u32[]{:S(2)}, u32[]{:S(2)}) collective-permute-start(bf16[96,768]{1,0:T(8,128)(2,1)S(1)} %bitcast_select_fusion.6), channel_id=1, source_target_pairs={{0,16},{2,18},{4,20},{6,22},{8,24},{10,26},{12,28},{14,30},{16,0},... | collective-permute-start | bytes 442376 | tf_op jit(solution)/shard_map/ppermute | solution.py:91
  600.2 50.8 %collective-permute-start.61 = (bf16[1,96,2048]{2,1,0:T(8,128)(2,1)S(1)}, bf16[1,96,2048]{2,1,0:T(8,128)(2,1)S(1)}, u32[]{:S(2)}, u32[]{:S(2)}) collective-permute-start(bf16[1,96,2048]{2,1,0:T(8,128)(2,1)S(1)} %slice.405), channel_id=1, source_target_pairs={{0,16},{2,18},{4,20},{6,22},{8,24},{10,26},{12,28},{14,30},{16,0},... | collective-permute-start | bytes 1179656 | tf_op jit(solution)/shard_map/ppermute | solution.py:91
  603.5 55.9 %collective-permute-start.58 = (bf16[1,96,2048]{2,1,0:T(8,128)(2,1)S(1)}, bf16[1,96,2048]{2,1,0:T(8,128)(2,1)S(1)}, u32[]{:S(2)}, u32[]{:S(2)}) collective-permute-start(bf16[1,96,2048]{2,1,0:T(8,128)(2,1)S(1)} %slice.399), channel_id=1, source_target_pairs={{0,16},{2,18},{4,20},{6,22},{8,24},{10,26},{12,28},{14,30},{16,0},... | collective-permute-start | bytes 1179656 | tf_op jit(solution)/shard_map/ppermute | solution.py:91
  627.9 40.0 %collective-permute-start.64 = (bf16[1,96,2048]{2,1,0:T(8,128)(2,1)S(1)}, bf16[1,96,2048]{2,1,0:T(8,128)(2,1)S(1)}, u32[]{:S(2)}, u32[]{:S(2)}) collective-permute-start(bf16[1,96,2048]{2,1,0:T(8,128)(2,1)S(1)} %slice.411), channel_id=1, source_target_pairs={{0,16},{2,18},{4,20},{6,22},{8,24},{10,26},{12,28},{14,30},{16,0},... | collective-permute-start | bytes 1179656 | tf_op jit(solution)/shard_map/ppermute | solution.py:91
  631.1 37.8 %collective-permute-start.31 = (bf16[16,2,128,96]{2,3,1,0:T(8,128)(2,1)S(1)}, bf16[16,2,128,96]{2,3,1,0:T(8,128)(2,1)S(1)}, u32[]{:S(2)}, u32[]{:S(2)}) collective-permute-start(bf16[16,2,128,96]{2,3,1,0:T(8,128)(2,1)S(1)} %bitcast.304), channel_id=1, source_target_pairs={{0,1},{1,0},{2,3},{3,2},{4,5},{5,4},{6,7},{7,6},{8,9},{9,8},{10,11... | collective-permute-start | bytes 2359304 | tf_op jit(solution)/shard_map/ppermute | solution.py:30
  (107 other events, 1736.0 us)
Sparse Core Ops, SparseCore 0:
  12.9 194.2 all-gather.1

commit v4 on v3

--- a/solution.py
+++ b/solution.py
@@ -86,52 +86,104 @@
     return int(lax.axis_size("dp")).bit_length() - 1
 
 
+def swapped(p):
+    return (p & ~3) | ((p & 1) << 1) | ((p >> 1) & 1)
+
+
+def turned(p, f):
+    return p if dp_bits() < 3 else jnp.where(f % 2 == 0, p, swapped(p))
+
+
 def dp_swap(value, bit):
-    n = lax.axis_size("dp")
-    return lax.ppermute(value, "dp", [(i, i ^ (1 << bit)) for i in range(n)])
-
-
-def orders(bits):
-    return bits, bits[:2][::-1] + bits[2:], bits[2:3] + bits[:2][::-1] + bits[3:]
+    n, dpn = lax.axis_size("fsdp"), lax.axis_size("dp")
+    pairs = []
+    for i in range(dpn):
+        for f in range(n):
+            flip = 1 << bit if dp_bits() < 3 or f % 2 == 0 else swapped(1 << bit)
+            pairs.append((i * n + f, (i ^ flip) * n + f))
+    return lax.ppermute(value, ("dp", "fsdp"), pairs)
 
 
 def relative(value):
-    return jnp.take(value, lax.axis_index("dp") ^ jnp.arange(lax.axis_size("dp")), axis=0)
+    places = turned(jnp.arange(lax.axis_size("dp")), lax.axis_index("fsdp"))
+    return jnp.take(value, lax.axis_index("dp") ^ places, axis=0)
+
+
+def absolute(value):
+    places = lax.axis_index("dp") ^ jnp.arange(lax.axis_size("dp"))
+    return jnp.take(value, turned(places, lax.axis_index("fsdp")), axis=0)
 
 
 class Halving:
-    def __init__(self, bits, order, whole=None, pair=None):
+    def __init__(self, bits, order, pair):
         self.labels, self.order = list(bits)[::-1], list(order)
-        self.keep = self.got = None
-        if pair is None:
-            self.cur = whole
-            self.start()
-        else:
-            bit = self.order.pop(0)
-            self.labels.remove(bit)
-            self.keep, self.got = pair[0], dp_swap(pair[1], bit)
-
-    def start(self):
+        bit = self.order.pop(0)
+        self.labels.remove(bit)
+        self.keep, self.got = pair[0], dp_swap(pair[1], bit)
+
+    def step(self):
+        if self.got is None:
+            return
+
+        def add(keep, got):
+            return keep.astype(F32) + got.astype(F32)
+
         if not self.order:
+            self.last = add(self.keep, self.got)
+            self.got = None
             return
         bit = self.order.pop(0)
         axis = self.labels.index(bit)
-        cur = self.cur.reshape((2,) * len(self.labels) + self.cur.shape[1:])
+        tail = self.keep.shape[1:]
+        parts = [v.reshape((2,) * len(self.labels) + tail) for v in (self.keep, self.got)]
         self.labels.remove(bit)
         self.keep, send = (
-            lax.index_in_dim(cur, i, axis, keepdims=False).reshape((-1,) + self.cur.shape[1:])
+            add(*(lax.index_in_dim(v, i, axis, keepdims=False) for v in parts))
+            .astype(BF16)
+            .reshape((-1,) + tail)
             for i in range(2)
         )
         self.got = dp_swap(send, bit)
 
+
+class Exchange:
+    def __init__(self, value):
+        self.bits, self.shape = list(range(dp_bits())), value.shape
+        self.cur = value.reshape((2,) * dp_bits() + value.shape[1:])
+        self.keep = self.got = None
+        self.start()
+
+    def start(self):
+        if self.bits:
+            self.bit = self.bits.pop(0)
+            self.axis = dp_bits() - 1 - self.bit
+            self.keep, send = (
+                lax.index_in_dim(self.cur, i, self.axis, keepdims=False) for i in range(2)
+            )
+            self.got = dp_swap(send, self.bit)
+
     def step(self):
-        if self.got is None:
-            return
-        total = self.keep.astype(F32) + self.got.astype(F32)
-        self.cur = total.astype(BF16)
-        self.last = total
+        if self.got is not None:
+            self.cur = jnp.stack([self.keep, self.got], axis=self.axis)
+            self.got = None
+            self.start()
+
+
+class Gather:
+    def __init__(self, value):
+        self.bits, self.cur = list(range(dp_bits())), value[None]
         self.got = None
         self.start()
+
+    def start(self):
+        if self.bits:
+            self.got = dp_swap(self.cur, self.bits.pop(0))
+
+    def step(self):
+        if self.got is not None:
+            self.cur = jnp.concatenate([self.cur, self.got], axis=0)
+            self.got = None
+            self.start()
 
 
 def advance(chains, value):
@@ -140,22 +192,6 @@
     for c, g in zip(live, got):
         c.got = g
         c.step()
-    return value
-
-
-def dp_exchange(value, order):
-    nb = dp_bits()
-    cur = value.reshape((2,) * nb + value.shape[1:])
-    for bit in order:
-        axis = nb - 1 - bit
-        keep, send = (lax.index_in_dim(cur, i, axis, keepdims=False) for i in range(2))
-        cur = jnp.stack([keep, dp_swap(send, bit)], axis=axis)
-    return cur.reshape(value.shape)
-
-
-def dp_total(value):
-    for bit in range(dp_bits()):
-        value = value + dp_swap(value, bit)
     return value
 
 
@@ -225,8 +261,8 @@
 def attn_bwd_kernel(
     len_ref, q_ref, k_ref, v_ref, tk_ref, tv_ref, g_ref, so_ref, co_ref, ls_ref, lc_ref,
     pre_ref, inv_ref, gq_ref, gk_ref, cos_ref, sin_ref, gate_ref,
-    d_ref, dtk_ref, dtv_ref, rq_ref, rk_ref, gainq_ref, gaink_ref, gateg_ref,
-    gs_ref, gc_ref, ds_ref, dc_ref, kt_ref, tkt_ref, dqt_ref, dk_acc, dv_acc,
+    d_ref, dtk_ref, dtv_ref, stat_ref, gainq_ref, gaink_ref, gateg_ref,
+    gs_ref, gc_ref, ds_ref, dc_ref, kt_ref, tkt_ref, dqt_ref, dk_acc, dv_acc, rq_ref, rk_ref,
 ):
     tokens, width = q_ref.shape
     heads = width // HD
@@ -299,15 +335,21 @@
     rk_ref[...] += prod * gk_ref[...]
     d_ref[2] = dv_acc[...]
 
-
-def specs(tokens, text, width, heads):
-    col = pl.BlockSpec((tokens, width), lambda i: (0, i))
-    three = pl.BlockSpec((3, tokens, width), lambda i: (0, 0, i))
-    tcol = pl.BlockSpec((text, width), lambda i: (0, i))
+    @pl.when(pl.program_id(0) == pl.num_programs(0) - 1)
+    def _():
+        stat_ref[...] = jnp.zeros_like(stat_ref)
+        for i, ref in enumerate((rq_ref, rk_ref)):
+            stat_ref[i : i + 1, :] = jnp.sum(ref[...].T, axis=0, keepdims=True)
+
+
+def specs(tokens, text, width, heads, at=0):
+    col = pl.BlockSpec((tokens, width), lambda i: (0, i + at))
+    three = pl.BlockSpec((3, tokens, width), lambda i: (0, 0, i + at))
+    tcol = pl.BlockSpec((text, width), lambda i: (0, i + at))
     stat = pl.BlockSpec((8, tokens), lambda i: (0, 0))
-    gain = pl.BlockSpec((1, width), lambda i: (0, i))
+    gain = pl.BlockSpec((1, width), lambda i: (0, i + at))
     table = pl.BlockSpec((tokens, width), lambda i: (0, 0))
-    lse = pl.BlockSpec((1, heads, tokens), lambda i: (i, 0, 0))
+    lse = pl.BlockSpec((1, heads, tokens), lambda i: (i + at, 0, 0))
     scalar = pl.BlockSpec(memory_space=pltpu.SMEM)
     return col, three, tcol, stat, gain, table, lse, scalar
 
@@ -331,27 +373,28 @@
     )(length, pre, inv, gq, gk, cosine, sine, tk, tv, gate)
 
 
-def attn_backward(length, q, k, v, tk, tv, g, so, co, ls, lc, pre, inv, gq, gk, cosine, sine, gate):
-    tokens, columns = q.shape
+def attn_backward(at, blocks, length, q, k, v, tk, tv, g, so, co, ls, lc, pre, inv, gq, gk, cosine, sine, gate):
+    tokens = q.shape[0]
     text, width = tk.shape[0], cosine.shape[1]
-    heads, blocks = width // HD, columns // width
-    col, three, tcol, stat, gain, table, lse, scalar = specs(tokens, text, width, heads)
+    heads, columns = width // HD, blocks * width
+    col, three, tcol, stat, gain, table, lse, scalar = specs(tokens, text, width, heads, at)
+    _, three_o, tcol_o, _, gain_o, _, _, _ = specs(tokens, text, width, heads)
     return pl.pallas_call(
         attn_bwd_kernel,
         grid=(blocks,),
         in_specs=[scalar, col, col, col, tcol, tcol, col, col, col, lse, lse,
                   three, stat, gain, gain, table, table, gain],
-        out_specs=[three, tcol, tcol, table, table, gain, gain, gain],
+        out_specs=[three_o, tcol_o, tcol_o, stat, gain_o, gain_o, gain_o],
         out_shape=[
-            sds(pre.shape), sds(tk.shape), sds(tk.shape),
-            sds((tokens, width)), sds((tokens, width)),
-            sds((1, columns)), sds((1, columns)), sds((1, columns)),
+            sds((3, tokens, columns)), sds((text, columns)), sds((text, columns)),
+            sds((8, tokens)), sds((1, columns)), sds((1, columns)), sds((1, columns)),
         ],
         scratch_shapes=[
             pltpu.VMEM((tokens, width), BF16), pltpu.VMEM((tokens, width), BF16),
             pltpu.VMEM((heads, tokens), F32), pltpu.VMEM((heads, tokens), F32),
             pltpu.VMEM((width, tokens), BF16), pltpu.VMEM((width, text), BF16),
             pltpu.VMEM((width, tokens), F32),
+            pltpu.VMEM((tokens, width), F32), pltpu.VMEM((tokens, width), F32),
             pltpu.VMEM((tokens, width), F32), pltpu.VMEM((tokens, width), F32),
         ],
     )(length, q, k, v, tk, tv, g, so, co, ls, lc, pre, inv, gq, gk, cosine, sine, gate)
@@ -404,30 +447,31 @@
         out_shape=sds((g.shape[1], depth), BF16),
     )(g, w)
 
-def put_relative(dst, src, me, count):
+def put_relative(dst, src, me, f, count):
     rows = dst.shape[0] // count
     for p in range(count):
-        start = pl.multiple_of((me ^ p) * rows, 16)
+        start = pl.multiple_of((me ^ turned(p, f)) * rows, 16)
         dst[p * rows : (p + 1) * rows, :] = src[pl.ds(start, rows), :]
 
 
-def put_halves(keep, send, value, count, bit):
+def put_halves(keep, send, value, count, bit, slot=None):
     rows = value.shape[0] // count
     low = (1 << bit) - 1
     for p in range(count):
         place = (p & low) | (p >> (bit + 1) << bit)
-        (send if p >> bit & 1 else keep)[place] = value[p * rows : (p + 1) * rows]
+        where = place if slot is None else (place, slot)
+        (send if p >> bit & 1 else keep)[where] = value[p * rows : (p + 1) * rows]
 
 
 def ffn_kernel(
     bits, id_ref, s_ref, b_ref, w_ref, d_ref,
-    gk_ref, gs_ref, uk_ref, us_ref, dk_ref, ds_ref, fo_ref, fp_ref, so_ref, sp_ref,
+    wk_ref, ws_ref, dk_ref, ds_ref, fo_ref, fp_ref, so_ref, sp_ref,
     st, bt, tmp, wg, wu, facc, sacc,
 ):
     step = pl.program_id(0)
     depth, _, cols = w_ref.shape
     own = fo_ref.shape[0]
-    count = 2 * gk_ref.shape[0]
+    count = 2 * dk_ref.shape[0]
 
     @pl.when(step == 0)
     def _():
@@ -435,7 +479,7 @@
             for c in range(depth // 256):
                 part = slice(c * 256, (c + 1) * 256)
                 tmp[part, :] = src[:, part].astype(F32).T.astype(BF16)
-            put_relative(dst, tmp, id_ref[0], count)
+            put_relative(dst, tmp, id_ref[0], id_ref[1], count)
         facc[...] = jnp.zeros_like(facc)
         sacc[...] = jnp.zeros_like(sacc)
 
@@ -453,9 +497,9 @@
     hidden = (silu * up).astype(BF16)
     g_gate = (back * up * (sig + silu * (1.0 - sig))).astype(BF16)
     g_up = (back * silu).astype(BF16)
-    put_halves(gk_ref, gs_ref, dot(st[...], g_gate).astype(BF16), count, bits[0])
-    put_halves(uk_ref, us_ref, dot(st[...], g_up).astype(BF16), count, bits[1])
-    put_halves(dk_ref, ds_ref, dot(bt[...], hidden).astype(BF16), count, bits[2])
+    put_halves(wk_ref, ws_ref, dot(st[...], g_gate).astype(BF16), count, bits[0], 0)
+    put_halves(wk_ref, ws_ref, dot(st[...], g_up).astype(BF16), count, bits[0], 1)
+    put_halves(dk_ref, ds_ref, dot(bt[...], hidden).astype(BF16), count, bits[1])
     facc[...] += dot(hidden, d_ref[...])
     sacc[...] += dot(g_gate, wg[...], 1, 1) + dot(g_up, wu[...], 1, 1)
 
@@ -474,7 +518,9 @@
     rest = tokens - local
     once = functools.partial(pl.BlockSpec, pipeline_mode=pl.Buffered(1))
     const = lambda i: (0, 0)
-    half = pl.BlockSpec((dp // 2, depth // dp, bc), lambda i: (0, 0, i))
+    share = depth // dp
+    half = pl.BlockSpec((dp // 2, share, bc), lambda i: (0, 0, i))
+    halves = pl.BlockSpec((dp // 2, 2, share, bc), lambda i: (0, 0, 0, i))
     return pl.pallas_call(
         functools.partial(ffn_kernel, bits),
         grid=(hid // bc,),
@@ -484,11 +530,11 @@
             pl.BlockSpec((depth, 2, bc), lambda i: (0, 0, i)),
             pl.BlockSpec((bc, depth), lambda i: (i, 0)),
         ],
-        out_specs=[half] * 6 + [
+        out_specs=[halves] * 2 + [half] * 2 + [
             once((local, depth), const), once((rest, depth), const),
             once((local, depth), const), once((rest, depth), const),
         ],
-        out_shape=[sds((dp // 2, depth // dp, hid), BF16)] * 6 + [
+        out_shape=[sds((dp // 2, 2, share, hid), BF16)] * 2 + [sds((dp // 2, share, hid), BF16)] * 2 + [
             sds((local, depth)), sds((rest, depth), BF16),
             sds((local, depth)), sds((rest, depth), BF16),
         ],
@@ -552,38 +598,34 @@
 
 
 def project_back_kernel(
-    bits, id_ref, d_ref, pre_ref, stat_ref, gain_ref, first_ref, w_ref, got_ref,
-    qk_ref, qs_ref, kk_ref, ks_ref, vk_ref, vs_ref, own_ref, peer_ref, gt, tmp, acc,
+    id_ref, da_ref, db_ref, pre_ref, stat_ref, gain_ref, first_ref, w_ref, got_ref,
+    keep_ref, send_ref, own_ref, peer_ref, gt, tmp, acc,
 ):
     j = pl.program_id(0)
-    tokens, own = d_ref.shape[1:]
+    tokens, own = pre_ref.shape[1:]
+    cut = da_ref.shape[2]
     local = own_ref.shape[0]
     f = id_ref[1]
-    count = 2 * qk_ref.shape[0]
+    count = 2 * keep_ref.shape[0]
     inv, mean = column(stat_ref, j, 128), column(stat_ref, j + 3, 128)
     grads = []
     for c in range(own // 128):
         part = slice(c * 128, (c + 1) * 128)
-        g = inv * (d_ref[0, :, part] * gain_ref[0, :, part] - pre_ref[0, :, part] * inv * mean)
+        here = slice(c * 128 - cut, (c + 1) * 128 - cut) if c * 128 >= cut else part
+        d = (db_ref if c * 128 >= cut else da_ref)[0, :, here]
+        g = inv * (d * gain_ref[0, :, part] - pre_ref[0, :, part] * inv * mean)
         tmp[part, :] = g.T.astype(BF16)
         grads.append(g.astype(BF16))
     g = jnp.concatenate(grads, axis=1)
-    put_relative(gt, tmp, id_ref[0] % count, count)
-
-    mine = pl.ds(pl.multiple_of(f * own, 128), own)
-    other = pl.ds(pl.multiple_of((1 - f) * own, 128), own)
-    wide = dot(gt[...], first_ref[...]).astype(BF16)
-    refs = ((qk_ref, qs_ref), (kk_ref, ks_ref), (vk_ref, vs_ref))
-    for i, (keep, send) in enumerate(refs):
-
-        @pl.when(j == i)
-        def _(i=i, keep=keep, send=send):
-            put_halves(keep, send, wide, count, bits[i])
+    put_relative(gt, tmp, id_ref[0] % count, f, count)
+    put_halves(keep_ref, send_ref, dot(gt[...], first_ref[...]).astype(BF16), count, 0, j)
 
     @pl.when(j == 0)
     def _():
         acc[...] = jnp.zeros_like(acc)
 
+    mine = pl.ds(pl.multiple_of(f * own, 128), own)
+    other = pl.ds(pl.multiple_of((1 - f) * own, 128), own)
     acc[:, mine] += dot(g, w_ref[0, :, mine], 1, 1)
     acc[:, other] += dot(g, got_ref[0], 1, 1)
 
@@ -593,30 +635,29 @@
         peer_ref[...] = acc[local:].astype(BF16)
 
 
-def project_back(ids, d, pre, stats, gain, first, w, got, dp, bits):
-    _, tokens, own = d.shape
+def project_back(ids, da, db, pre, stats, gain, first, w, got, dp):
+    _, tokens, own = pre.shape
     depth = first.shape[1]
     local = tokens // 2
     share = depth // dp
     const = lambda j: (0, 0)
     block = lambda j: (j, 0, 0)
-    half = pl.BlockSpec((dp // 4, share, depth), lambda j: (0, 0, 0), pipeline_mode=pl.Buffered(1))
+    once = functools.partial(pl.BlockSpec, pipeline_mode=pl.Buffered(1))
+    half = once((dp // 4, 3, share, depth), lambda j: (0, 0, 0, 0))
     return pl.pallas_call(
-        functools.partial(project_back_kernel, bits),
+        project_back_kernel,
         grid=(3,),
         in_specs=[
             pl.BlockSpec(memory_space=pltpu.SMEM),
-            pl.BlockSpec((1, tokens, own), block), pl.BlockSpec((1, tokens, own), block),
+            pl.BlockSpec((1,) + da.shape[1:], block), pl.BlockSpec((1,) + db.shape[1:], block),
+            pl.BlockSpec((1, tokens, own), block),
             pl.BlockSpec((8, tokens), const),
             pl.BlockSpec((1, 1, own), block),
-            pl.BlockSpec((tokens, depth), const, pipeline_mode=pl.Buffered(1)),
+            once((tokens, depth), const),
             pl.BlockSpec((1, own, depth), block), pl.BlockSpec((1, own, own), block),
         ],
-        out_specs=[half] * 6 + [
-            pl.BlockSpec((local, depth), const, pipeline_mode=pl.Buffered(1)),
-            pl.BlockSpec((local, depth), const, pipeline_mode=pl.Buffered(1)),
-        ],
-        out_shape=[sds((dp // 4, share, depth), BF16)] * 6 + [
+        out_specs=[half, half, once((local, depth), const), once((local, depth), const)],
+        out_shape=[sds((dp // 4, 3, share, depth), BF16)] * 2 + [
             sds((local, depth)), sds((local, depth), BF16),
         ],
         scratch_shapes=[
@@ -624,7 +665,40 @@
             pltpu.VMEM((tokens, depth), F32),
         ],
         compiler_params=pltpu.CompilerParams(vmem_limit_bytes=62 << 20),
-    )(ids, d, pre, stats, gain, first, w, got)
+    )(ids, da, db, pre, stats, gain, first, w, got)
+
+
+def out_back_kernel(id_ref, *refs):
+    n = len(refs) - 8
+    blocks, (w_ref, mixed_ref, g_ref, keep_ref, send_ref, all_ref, gt, tmp) = refs[:n], refs[n:]
+    local = blocks[0].shape[0]
+    for r, ref in enumerate(blocks):
+        all_ref[r * local : (r + 1) * local, :] = ref[...]
+    grad = all_ref[...]
+    g_ref[...] = dot(grad, w_ref[...], 1, 1)
+    for c in range(grad.shape[1] // 256):
+        part = slice(c * 256, (c + 1) * 256)
+        tmp[part, :] = grad[:, part].astype(F32).T.astype(BF16)
+    count = 2 * keep_ref.shape[0]
+    put_relative(gt, tmp, id_ref[0], id_ref[1], count)
+    put_halves(keep_ref, send_ref, dot(gt[...], mixed_ref[...]).astype(BF16), count, 0)
+
+
+def out_back(ids, blocks, w, mixed, dp):
+    tokens, own = mixed.shape
+    depth = w.shape[1]
+    vmem = pl.BlockSpec(memory_space=pltpu.VMEM)
+    half = sds((dp // 2, depth // dp, own), BF16)
+    return pl.pallas_call(
+        out_back_kernel,
+        in_specs=[pl.BlockSpec(memory_space=pltpu.SMEM)] + [vmem] * (len(blocks) + 2),
+        out_specs=[vmem] * 3,
+        out_shape=[sds((tokens, own)), half, half],
+        scratch_shapes=[
+            pltpu.VMEM((tokens, depth), BF16),
+            pltpu.VMEM((depth, tokens), BF16), pltpu.VMEM((depth, tokens), BF16),
+        ],
+    )(ids, *blocks, w, mixed)
 
 
 def time_embed(timesteps):
@@ -664,8 +738,8 @@
     n, f = lax.axis_size("fsdp"), lax.axis_index("fsdp")
     dpn, me = lax.axis_size("dp"), lax.axis_index("dp")
     bits = list(range(dp_bits()))
-    order_a, order_b, order_c = orders(bits)
     low_bits = bits[:-1]
+    late = bits[2:] + bits[:2]
     own_d = D // n
     local = hidden_in.shape[1]
     tokens = n * local
@@ -737,18 +811,14 @@
 
     second_all = jnp.concatenate(gather_rot(second), axis=0)
     branch_all = (gate_ffn * dy_all.astype(F32)).astype(BF16)
-    firsts = (order_a[0], order_b[0], order_c[0]) if bits else (0, 0, 0)
-    *halves, ffn_own, ffn_rest, back_own, back_rest = ffn(
-        ids, second_all, branch_all, w_gate_up, w_down, local, dpn, firsts
+    wide_keep, wide_send, down_keep, down_send, ffn_own, ffn_rest, back_own, back_rest = ffn(
+        ids, second_all, branch_all, w_gate_up, w_down, local, dpn, (bits[0], late[0])
     )
     (ffn_own, ffn_rest, back_own, back_rest), text_all = lax.optimization_barrier(
         ((ffn_own, ffn_rest, back_own, back_rest), text_all)
     )
-    chains = [
-        Halving(bits, o, pair=halves[2 * i : 2 * i + 2])
-        for i, o in enumerate((order_a, order_b, order_c))
-    ]
-    ffn_chains = list(chains)
+    wide_chain = Halving(bits, bits, (wide_keep, wide_send))
+    down_chain = Halving(bits, late, (down_keep, down_send))
     grad_second = scatter_rot([back_own] + [rows(back_rest, r) for r in range(n - 1)])
     ffn_branch = scatter_rot([ffn_own] + [rows(ffn_rest, r) for r in range(n - 1)])
     output = (after_attn + gate_ffn * ffn_branch).astype(BF16)
@@ -763,60 +833,64 @@
     )
     d_gate_attn = jnp.sum(grad_after * attn_branch, axis=0) * (1.0 - gate_attn[0] * gate_attn[0])
     grad_attn = (gate_attn * grad_after).astype(BF16)
-    grad_attn_all = jnp.concatenate(gather_rot(grad_attn), axis=0)
-    grad_mixed = dot(grad_attn_all, w_out, 1, 1)
-    d, dtk, dtv, rq, rk, gain_q, gain_k, gate_g = attn_backward(
-        caption_lengths, q, k, v, tkp, tvp, pad_cols(grad_mixed, width), so, co, ls, lc, pre_p,
-        inverse, gq, gk, cosine, sine, gate_row,
-    )
-    rq, rk, dtk = advance(chains, (rq, rk, dtk))
-    d_out = dot(grad_attn_all, mixed, 0, 0).astype(BF16)
-    out_chain = Halving(bits, order_c, whole=relative(d_out.reshape(dpn, share, own_d)))
-    d, dtk, dtv = d[:, :, :own_d], dtk[:, :own_d], dtv[:, :own_d]
-    gate_total = jnp.sum(gate_g[0, :own_d].reshape(HEADS // n, HD), axis=1) * (
+    grad_mixed, *halves = out_back(ids, gather_rot(grad_attn), w_out, mixed, dpn)
+    out_chain = Halving(bits, bits, halves)
+    blocks = pre_p.shape[2] // width
+    cut = max(1, 2 * blocks // 3)
+    grad_mixed = pad_cols(grad_mixed, width)
+    inputs = (so, co, ls, lc, pre_p, inverse, gq, gk, cosine, sine, gate_row)
+    part_a = attn_backward(0, cut, caption_lengths, q, k, v, tkp, tvp, grad_mixed, *inputs)
+    part_a, grad_mixed = lax.optimization_barrier((part_a, grad_mixed))
+    grad_mixed = advance([wide_chain, down_chain], grad_mixed)
+    part_b = attn_backward(
+        cut, blocks - cut, caption_lengths, q, k, v, tkp, tvp, grad_mixed, *inputs
+    )
+    dtk, dtv, gain_q, gain_k, gate_g = (
+        jnp.concatenate([part_a[i], part_b[i]], axis=1)[:, :own_d] for i in (1, 2, 4, 5, 6)
+    )
+    means = row_sum(part_a[3] + part_b[3])[:2] / D
+    gate_total = jnp.sum(gate_g[0].reshape(HEADS // n, HD), axis=1) * (
         1.0 - head_tanh * head_tanh
     )
     text_hat = dtk * gain_own[4]
     gain_text = jnp.sum(dtk * normed_t, axis=0, keepdims=True)
-    means = row_sum(jnp.stack([jnp.sum(rq, -1), jnp.sum(rk, -1)])) / D
     mean_t = pair_sum(jnp.sum(text_hat * normed_t, -1, keepdims=True)) / D
 
     grad_tk = (inv_t * (text_hat - normed_t * mean_t)).astype(BF16)
     text_pair = jnp.stack([grad_tk, dtv.astype(BF16)])
     pair_all = jnp.concatenate(natural(gather_rot(text_pair)), axis=-1)
     outgoing = block_of(pair_all, f, 1).reshape(2, TEXT // n, dpn, share).transpose(2, 0, 1, 3)
-    pair_cols = dp_exchange(relative(outgoing), order_a)
+    pair_chain = Exchange(relative(outgoing))
 
     ones, zeros = jnp.ones((1, tokens), F32), jnp.zeros((1, tokens), F32)
     if paired:
         stats = jnp.concatenate([inverse[:2], ones, means, zeros, zeros, zeros], axis=0)
         gain3 = jnp.stack([gain_own[2:3], gain_own[3:4], jnp.ones_like(gain_own[2:3])])
-        low_orders = orders(low_bits)
         *halves, own_part, peer_part = project_back(
-            ids, d, pre, stats, gain3, first_all, w_flat, w_parts[1], dpn,
-            tuple(o[0] for o in low_orders),
+            ids, part_a[0], part_b[0], pre, stats, gain3, first_all, w_flat, w_parts[1], dpn
         )
-        qkv_chains = [
-            Halving(low_bits, o, pair=halves[2 * i : 2 * i + 2]) for i, o in enumerate(low_orders)
-        ]
+        qkv_chain = Halving(low_bits, low_bits, halves)
         parts = [own_part, peer_part]
     else:
+        d = jnp.concatenate([part_a[0], part_b[0]], axis=2)[:, :, :own_d]
         inv, mean = inverse[:2, :, None], means[:, :, None]
         hat = d[:2] * gain_own[2:4][:, None] - pre[:2] * inv * mean
         grads = [(inv[0] * hat[0]).astype(BF16), (inv[1] * hat[1]).astype(BF16), d[2].astype(BF16)]
         wide = [dot(g, first_all, 0, 0).astype(BF16) for g in grads]
         wide = [jnp.concatenate(natural(exchange_rot(w_, 1)), axis=0) for w_ in wide]
-        qkv_chains = [
-            Halving(bits, o, whole=relative(w_.reshape(dpn, share, own_d)))
-            for w_, o in zip(wide, (order_a, order_b, order_c))
-        ]
+        wide = relative(jnp.stack([w_.reshape(dpn, share, own_d) for w_ in wide], axis=1))
+        wide = wide.reshape((dpn // 2, 2) + wide.shape[1:])
+        qkv_chain = Halving(bits, bits, (wide[:, 0], wide[:, 1]))
         parts = [
             sum(dot(rows(g, r), w_heads[j], 1, 1) for j, g in enumerate(grads)) for r in range(n)
         ]
         parts = [parts[0]] + [p.astype(BF16) for p in parts[1:]]
+    chains = [wide_chain, down_chain, out_chain]
+    parts = advance([wide_chain, down_chain, out_chain, pair_chain], parts)
     grad_first = scatter_rot(parts)
 
     text_in = text_bwd(pair_all, w_text)
+    text_in = advance([out_chain, pair_chain], text_in)
     text_in = jnp.concatenate(natural(exchange_rot(text_in, 0)), axis=1)
 
     inverse_one = inverse_rms(x_own)
@@ -829,49 +903,56 @@
         + rms_back(grad_first * gain_full[0] * (1.0 + scale_attn), normed_one, inverse_one)
     ).astype(BF16)
 
-    mods = jnp.stack([d_scale_attn, d_gate_attn, d_scale_ffn, d_gate_ffn])
-    mods = mods.reshape(4, dpn, share).transpose(1, 0, 2)
-    stamp = jnp.full((dpn, 1, share), timesteps[0].astype(F32) / n)
-    mods = pair_sum(dp_exchange(relative(jnp.concatenate([mods, stamp], axis=1)), order_a))
-    times = time_embed(jnp.round(mods[:, 4, 0]))
+    grad_input = advance([wide_chain, down_chain, qkv_chain], grad_input)
+
+    sums = [d_scale_attn, d_gate_attn, d_scale_ffn, d_gate_ffn, gain_one, gain_two]
+    sums = pair_sum(jnp.stack(sums))
+    stamp = jnp.full((1, D), timesteps[0].astype(F32))
+    gate_pad = jnp.pad(gate_total, (0, own_d - gate_total.shape[0]))[None]
+    small = jnp.concatenate([block_of(sums[4:], f, 1), gain_q, gain_k, gain_text, gate_pad], axis=0)
+    small_chain = Gather(
+        jnp.concatenate([sums[:4], stamp, jnp.pad(small, ((0, 0), (0, D - own_d)))], axis=0)
+    )
+
+    def rest(chain):
+        while chain.got is not None:
+            chain.step()
+
+    advance([pair_chain, out_chain, small_chain], ())
+    rest(pair_chain)
+    pair_cols = absolute(pair_chain.cur.reshape(pair_chain.shape))
+    pair_cols = jnp.concatenate(natural(gather_rot(pair_cols)), axis=2)
+    pair_cols = pair_cols.transpose(0, 2, 1, 3).reshape(dpn * TEXT, 2 * share)
+    text_grad = dot(pair_cols, text_all, 0, 0).reshape(2, share, TW // n)
+    text_grad = advance([qkv_chain, small_chain, wide_chain, down_chain], text_grad)
+    for chain in (small_chain, qkv_chain, out_chain, wide_chain, down_chain):
+        rest(chain)
+    total = jnp.sum(small_chain.cur[:, 5:, :own_d], axis=0)
+    mods = lax.dynamic_slice_in_dim(small_chain.cur[:, :4], me * share, share, 2)
+    times = time_embed(small_chain.cur[:, 4, 0])
     times = lax.dynamic_slice_in_dim(times, f * own_te, own_te, 1).astype(F32)
     ada_grad = lax.dot_general(
-        mods[:, :4].reshape(dpn, 4 * share), times, (((0,), (0,)), ((), ())),
+        mods.reshape(dpn, 4 * share), times, (((0,), (0,)), ((), ())),
         precision=lax.Precision.HIGHEST,
     ).reshape(4, share, own_te)
-    two = scatter_rot(rot_blocks(jnp.stack([gain_one, gain_two]), 1))
-    gate_pad = jnp.pad(gate_total, (0, own_d - gate_total.shape[0]))[None]
-    small = dp_total(
-        jnp.concatenate([two, gain_q[:, :own_d], gain_k[:, :own_d], gain_text, gate_pad], axis=0)
-    )
-
-    pair_cols = jnp.concatenate(natural(gather_rot(pair_cols)), axis=2)
-    pair_cols = relative(pair_cols).transpose(0, 2, 1, 3).reshape(dpn * TEXT, 2 * share)
-    text_grad = dot(pair_cols, text_all, 0, 0).reshape(2, share, TW // n)
-
-    chains += [out_chain] + qkv_chains
-    while any(c.got is not None for c in chains):
-        for c in chains:
-            c.step()
-    qkv_grad = [c.last[0] for c in qkv_chains]
+    qkv_grad = qkv_chain.last[0]
     if paired:
         own_side = f == (me >> low_bits[-1] + 1)
-        for i, c in enumerate(qkv_chains):
-            mine, got = exchange_rot(c.cur[0], 1)
-            keep, send = jnp.where(own_side, mine, got), jnp.where(own_side, got, mine)
-            qkv_grad[i] = keep.astype(F32) + dp_swap(send, bits[-1]).astype(F32)
+        mine, got = exchange_rot(qkv_grad.astype(BF16), 2)
+        keep, send = jnp.where(own_side, mine, got), jnp.where(own_side, got, mine)
+        qkv_grad = keep.astype(F32) + dp_swap(send, bits[-1]).astype(F32)
     return (
         output[None],
         grad_input[None],
         text_in[None],
         ada_grad.transpose(2, 0, 1),
         text_grad.transpose(2, 0, 1),
-        jnp.stack(qkv_grad).transpose(2, 0, 1),
+        qkv_grad.transpose(2, 0, 1),
         out_chain.last[0].T,
-        small[:5],
-        small[5, : HEADS // n],
-        jnp.stack([ffn_chains[0].last[0], ffn_chains[1].last[0]], axis=1),
-        ffn_chains[2].last[0].T,
+        total[:5],
+        total[5, : HEADS // n],
+        wide_chain.last[0].transpose(1, 0, 2),
+        down_chain.last[0].T,
     )
 
 

time: 694 us -> 648 us (0.934)
  waiting for transfers between devices: 168 us -> 131 us
  Pallas kernels: 264 us -> 277 us
  matrix products: 35 us -> 22.2 us
  starting transfers between devices: 48.2 us -> 35.6 us
  other arithmetic: 98.7 us -> 108 us
    ppermute x40 -> x24, waiting for transfers between devices: 158 us -> 122 us  [dp_swap(): return lax.ppermute(value, ('dp', 'fsdp'), pairs)]
    convert_element_type x21 -> x18, other arithmetic: 26.2 us -> 58.3 us  [the longest x14 51.1 us: step(): self.keep, send = (add(*(lax.index_in_dim(v, i, axis, keepdims=False) for...]
    ppermute x40 -> x24, starting transfers between devices: 43.3 us -> 30 us  [dp_swap(): return lax.ppermute(value, ('dp', 'fsdp'), pairs)]
    dot_general x5 -> x3, matrix products: 28.1 us -> 16.2 us  [dot(): lax.dot_general(a, b, (((ca,), (cb,)), ((), ())), preferred_element_type=...]
    pallas_call x1 -> x2, Pallas kernels: 31.8 us -> 39.7 us  [the longest x1 30.2 us: project_back(): pl.pallas_call(project_back_kernel, grid=(3,), in_specs=[pl.BlockSpec(mem...]
    convert_element_type x0 -> x1, local copies, waits for them, and re-layouts: none -> 6.95 us  [step(): self.keep, send = (add(*(lax.index_in_dim(v, i, axis, keepdims=False) for...]
    pallas_call x1 -> x2, Pallas kernels: 64.7 us -> 69.2 us  [attn_backward(): pl.pallas_call(attn_bwd_kernel, grid=(blocks,), in_specs=[scalar, col, co...]
  transfers between devices with their start and end apart: 66 -> 47, of which waited for: 24 -> 14; matrix products, arithmetic and copies ran while one was open for 24% -> 24% of each run, Pallas kernels for 38% -> 39%
where the time goes in v4:
time: 648 us; the launch traced here: 643 us
  Pallas kernels  277 us (43%)
  waiting for transfers between devices  131 us (20%)
  other arithmetic  108 us (17%)
  local copies, waits for them, and re-layouts  50.3 us (8%)
  starting transfers between devices  35.6 us (5%)
  matrix products  22.2 us (3%)
  between operations  16.7 us (3%)
    ppermute x24, waiting for transfers between devices, dp_swap(): return lax.ppermute(value, ('dp', 'fsdp'), pairs)  122 us
    pallas_call x1, Pallas kernels, ffn(): pl.pallas_call(functools.partial(ffn_kernel, bits), grid=(hid // bc,), in...  90.3 us
    pallas_call x2, Pallas kernels, attn_backward(): pl.pallas_call(attn_bwd_kernel, grid=(blocks,), in_specs=[scalar, col, co...  69.2 us
    convert_element_type x14, other arithmetic, step(): self.keep, send = (add(*(lax.index_in_dim(v, i, axis, keepdims=False) for...  51.1 us
    pallas_call x1, Pallas kernels, attn_forward(): pl.pallas_call(attn_fwd_kernel, grid=(blocks,), in_specs=[scalar, three,...  32 us
    pallas_call x1, Pallas kernels, project_back(): pl.pallas_call(project_back_kernel, grid=(3,), in_specs=[pl.BlockSpec(mem...  30.2 us
    ppermute x24, starting transfers between devices, dp_swap(): return lax.ppermute(value, ('dp', 'fsdp'), pairs)  30 us
    pallas_call x1, Pallas kernels, text_fwd(): pl.pallas_call(text_fwd_kernel, grid=(depth // bk,), in_specs=[pl.BlockSp...  16.3 us
  transfers between devices with their start and end apart: 47, of which 14 were waited for; matrix products, arithmetic and copies ran while one was open for 24% of the time, Pallas kernels for 39%

profile of v4, /device:TPU:0, one launch (start us, length us, event | category | flops | bytes accessed | tf_op | source)
XLA Modules:
  0.0 642.8 jit_solution(6789445639803899952)
XLA Ops:
  18.2 4.6 fusion.2
  23.4 16.3 %shard_map.222 = f32[2,256,1536]{2,1,0:T(8,128)} custom-call(bf16[256,2048]{1,0:T(8,128)(2,1)} %pad_maximum_fusion.2.x_ref, bf16[2048,2,1536]{2,1,0:T(2,128)(2,1)} %w_ref.5), custom_call_target="tpu_custom_call" | custom-call | tf_op jit(solution)/shard_map/pallas_call | solution.py:424
  53.5 14.4 %shard_map.221 = (bf16[1024,1536]{1,0:T(8,128)(2,1)}, f32[3,1024,768]{2,1,0:T(8,128)}, f32[8,1024]{1,0:T(8,128)}) custom-call(s32[2]{0:T(128)} %pad_add_fusion.1.id_ref, bf16[512,1536]{1,0:T(8,128)(2,1)} %bitcast.223, bf16[512,1536]{1,0:T(8,128)(2,1)} %collective-permute-done.1.xp_ref, f32[1,1536]{1,0:T(1,128)} %get-tuple-element.215.front_ref, ...), custom_call_target="tpu_custom_call" | custom-call | tf_op jit(solution)/shard_map/pallas_call | solution.py:581
  70.7 32.0 %shard_map.223 = (bf16[1024,768]{1,0:T(8,128)(2,1)}, bf16[1024,768]{1,0:T(8,128)(2,1)}, bf16[1024,768]{1,0:T(8,128)(2,1)}, bf16[1024,768]{1,0:T(8,128)(2,1)}, f3...) custom-call(s32[1]{0:T(128)S(6)} %copy.122.len_ref, ...), custom_call_target="tpu_custom_call" | custom-call | tf_op jit(solution)/shard_map/pallas_call | solution.py:367
  121.1 90.3 %shard_map.224 = (bf16[8,2,96,2048]{3,2,1,0:T(8,128)(2,1)}, bf16[8,2,96,2048]{3,2,1,0:T(8,128)(2,1)}, bf16[8,96,2048]{2,1,0:T(8,128)(2,1)}, bf16[8,96,2048]{2,1,...) custom-call(s32[2]{0:T(128)} %pad_add_fusion.1.id_ref, ...), custom_call_target="tpu_custom_call" | custom-call | tf_op jit(solution)/shard_map/pallas_call | solution.py:524
  222.5 5.9 fusion.7
  239.6 9.5 %shard_map.225 = (f32[1024,768]{1,0:T(8,128)}, bf16[8,96,768]{2,1,0:T(8,128)(2,1)}, bf16[8,96,768]{2,1,0:T(8,128)(2,1)}) custom-call(s32[2]{0:T(128)} %pad_add_fusion.1.id_ref, bf16[512,1536]{1,0:T(8,128)(2,1)} %multiply_convert_fusion.1.refs_0_, bf16[512,1536]{1,0:T(8,128)(2,1)} %collective-permute-done.13.refs_1_, bf16[768,1536]{1,0:T(8,128)(2,1)} %refs_2_.1, ...), custom_call_target="tpu_custom_call" | custom-call | tf_op jit(solution)/shard_map/pallas_call | solution.py:692
  249.1 44.7 %shard_map.226 = (f32[3,1024,512]{2,1,0:T(8,128)}, f32[256,512]{1,0:T(8,128)}, f32[256,512]{1,0:T(8,128)}, f32[8,1024]{1,0:T(8,128)}, f32[1,512]{1,0:T(1,128)}, /*index=5*/f32[1,512]{1,0:T(1,128)}, f32[1,512]{1,0:T(1,128)}) custom-call(s32[1]{0:T(128)S(6)} %copy.122.len_ref, bf16[1024,768]{1,0:T(8,128)(2,1)} %get-tuple-element.100.q_ref, ...), custom_call_target="tpu_custom_call" | custom-call | tf_op jit(solution)/shard_map/pallas_call | solution.py:382
  293.8 6.1 add_convert_fusion.1
  303.9 24.5 %shard_map.227 = (f32[3,1024,256]{2,1,0:T(8,128)}, f32[256,256]{1,0:T(8,128)}, f32[256,256]{1,0:T(8,128)}, f32[8,1024]{1,0:T(8,128)}, f32[1,256]{1,0:T(1,128)}, /*index=5*/f32[1,256]{1,0:T(1,128)}, f32[1,256]{1,0:T(1,128)}) custom-call(s32[1]{0:T(128)S(6)} %copy.122.len_ref, bf16[1024,768]{1,0:T(8,128)(2,1)} %get-tuple-element.100.q_ref, ...), custom_call_target="tpu_custom_call" | custom-call | tf_op jit(solution)/shard_map/pallas_call | solution.py:382
  329.6 6.9 %copy.79 = bf16[4,2,96,2048]{3,1,2,0:T(2,128)(2,1)} copy(bf16[4,2,96,2048]{3,2,1,0:T(8,128)(2,1)} %bitcast.225) | data formatting | bytes 6291456 | tf_op jit(solution)/shard_map/convert_element_type | solution.py:142
  338.1 5.1 add_convert_fusion.5
  346.4 14.0 %fusion.14 = bf16[2,2,2,96,2048]{4,2,3,1,0:T(2,128)(2,1)} fusion(bf16[2,2,1,2,96,2048]{5,4,3,2,1,0:T(8,128)(2,1)S(1)} %copy-done.10, bf16[2,2,1,2,96,2048]{5,4,3,2,1,0:T(8,128)(2,1)S(1)} %copy-done.9), kind=kLoop, calls=%fused_computation.27 | loop fusion | flops 6291456 | bytes 9437184 | tf_op jit(solution)/shard_map/convert_element_type | solution.py:142
  375.7 30.2 %shard_map.228 = (bf16[4,3,96,1536]{3,2,1,0:T(8,128)(2,1)}, bf16[4,3,96,1536]{3,2,1,0:T(8,128)(2,1)}, f32[512,1536]{1,0:T(8,128)}, bf16[512,1536]{1,0:T(8,128)(2,1)}) custom-call(s32[2]{0:T(128)} %pad_add_fusion.1.id_ref, f32[3,1024,512]{2,1,0:T(8,128)} %get-tuple-element.115.da_ref, f32[3,1024,256]{2,1,0:T(8,128)} %get-tuple-element.120.db_ref, ...), custom_call_target="tpu_custom_call" | custom-call | tf_op jit(solution)/shard_map/pallas_call | solution.py:647
  409.0 14.6 %shard_map.229 = bf16[256,2048]{1,0:T(8,128)(2,1)} custom-call(bf16[2,256,1536]{2,1,0:T(8,128)(2,1)} %pad_maximum_fusion.1.g_ref, bf16[2048,2,1536]{2,1,0:T(2,128)(2,1)} %w_ref.5), custom_call_target="tpu_custom_call" | custom-call | tf_op jit(solution)/shard_map/pallas_call | solution.py:443
  423.7 6.5 %add_convert_fusion.4 = (bf16[2,1,2,96,2048]{4,2,3,1,0:T(2,128)(2,1)}, bf16[2,2,96,2048]{3,1,2,0:T(2,128)(2,1)S(1)}) fusion(bf16[2,2,2,96,2048]{4,2,3,1,0:T(2,128)(2,1)} %bitcast.36, bf16[2,2,2,96,2048]{4,2,3,1,0:T(2,128)(2,1)} %fusion.14), kind=kLoop, calls=%fused_computation.29 | loop fusion | flops 6291456 | bytes 9437184 | tf_op jit(solution)/shard_map/convert_element_type | solution.py:142
  440.3 16.5 %collective-permute-done.28 = bf16[2,2,2,2,128,96]{4,5,3,2,1,0:T(8,128)(2,1)S(1)} collective-permute-done((bf16[2,2,2,2,128,96]{4,5,3,2,1,0:T(8,128)(2,1)S(1)}, bf16[2,2,2,2,128,96]{4,5,3,2,1,0:T(8,128)(2,1)S(1)}, u32[]{:S(2)}, u32[]{:S(2)}) %collective-permute-start.28) | collective-permute-done | bytes 393248 | tf_op jit(solution)/shard_map/ppermute | solution.py:104
  485.8 48.1 %collective-permute-done.34 = bf16[2,2,2,2,128,96]{4,5,3,2,1,0:T(8,128)(2,1)S(1)} collective-permute-done((bf16[2,2,2,2,128,96]{4,5,3,2,1,0:T(8,128)(2,1)S(1)}, bf16[2,2,2,2,128,96]{4,5,3,2,1,0:T(8,128)(2,1)S(1)}, u32[]{:S(2)}, u32[]{:S(2)}) %collective-permute-start.34) | collective-permute-done | bytes 393248 | tf_op jit(solution)/shard_map/ppermute | solution.py:104
  539.6 8.6 %collective-permute-done.45 = bf16[1,96,768]{2,1,0:T(8,128)(2,1)S(1)} collective-permute-done((bf16[1,96,768]{2,1,0:T(8,128)(2,1)S(1)}, bf16[1,96,768]{2,1,0:T(8,128)(2,1)S(1)}, u32[]{:S(2)}, u32[]{:S(2)}) %collective-permute-start.45) | collective-permute-done | bytes 147488 | tf_op jit(solution)/shard_map/ppermute | solution.py:104
  552.7 8.9 %fusion = f32[2,96,2048]{2,1,0:T(8,128)} fusion(bf16[2,96,4096]{2,1,0:T(8,128)(2,1)S(1)} %bitcast.240, bf16[4096,2048]{1,0:T(8,128)(2,1)} %all-gather.2.cloned.1.call-done), kind=kOutput, calls=%fused_computation.2 | convolution fusion | flops 3221225472 | bytes 19922944 | tf_op jit(solution)/shard_map/dot_general | solution.py:25
  567.3 6.7 %collective-permute-done.40 = f32[4,11,1536]{2,1,0:T(8,128)S(1)} collective-permute-done((f32[4,11,1536]{2,1,0:T(8,128)S(1)}, f32[4,11,1536]{2,1,0:T(8,128)S(1)}, u32[]{:S(2)}, u32[]{:S(2)}) %collective-permute-start.40) | collective-permute-done | bytes 270368 | tf_op jit(solution)/shard_map/ppermute | solution.py:104
  579.3 21.8 %collective-permute-done.41 = f32[8,11,1536]{2,0,1:T(8,128)} collective-permute-done((f32[8,11,1536]{2,0,1:T(8,128)S(1)}, f32[8,11,1536]{2,0,1:T(8,128)}, u32[]{:S(2)}, u32[]{:S(2)}) %collective-permute-start.41) | collective-permute-done | bytes 540704 | tf_op jit(solution)/shard_map/ppermute | solution.py:104
  601.1 4.3 concatenate.150
  616.3 18.4 %collective-permute-done.44 = bf16[3,96,768]{2,1,0:T(8,128)(2,1)S(1)} collective-permute-done((bf16[3,96,768]{2,1,0:T(8,128)(2,1)S(1)}, bf16[3,96,768]{2,1,0:T(8,128)(2,1)S(1)}, u32[]{:S(2)}, u32[]{:S(2)}) %collective-permute-start.44) | collective-permute-done | bytes 442400 | tf_op jit(solution)/shard_map/ppermute | solution.py:104
  (345 shorter events, 167.3 us)
Async XLA Ops:
  7.2 207.4 %all-gather.2.cloned.1.call-start = ((), (), s32[]{:S(2)}) async-start(), calls=%async_computation | async-start | bytes 17825792 | tf_op jit(solution)/shard_map/all_gather | solution.py:767
  12.9 40.6 %collective-permute-start.1 = (bf16[512,1536]{1,0:T(8,128)(2,1)S(1)}, bf16[512,1536]{1,0:T(8,128)(2,1)}, u32[]{:S(2)}, u32[]{:S(2)}) collective-permute-start(bf16[512,1536]{1,0:T(8,128)(2,1)S(1)} %bitcast.224), channel_id=1, source_target_pairs={{0,1},{1,0},{2,3},{3,2},{4,5},{5,4},{6,7},{7,6},{8,9},{9,8},{10,11... | collective-permute-start | bytes 4718600 | tf_op jit(solution)/shard_map/ppermute | solution.py:30
  17.3 36.2 %collective-permute-start.2 = (bf16[3,768,768]{2,1,0:T(8,128)(2,1)}, bf16[3,768,768]{2,1,0:T(8,128)(2,1)}, u32[]{:S(2)}, u32[]{:S(2)}) collective-permute-start(bf16[3,768,768]{2,1,0:T(8,128)(2,1)} %dynamic-slice_bitcast_fusion), channel_id=1, source_target_pairs={{0,1},{1,0},{2,3},{3,2},{4,5},{5,4},{6,7},{7,6},{8,9},{9,8},{10,11... | collective-permute-start | bytes 10616840 | tf_op jit(solution)/shard_map/ppermute | solution.py:30
  22.8 26.6 %collective-permute-start = (f32[4,1536]{1,0:T(4,128)S(1)}, f32[4,1536]{1,0:T(4,128)S(1)}, u32[]{:S(2)}, u32[]{:S(2)}) collective-permute-start(f32[4,1536]{1,0:T(4,128)S(1)} %bitcast.250), channel_id=1, source_target_pairs={{0,1},{1,0},{2,3},{3,2},{4,5},{5,4},{6,7},{7,6},{8,9},{9,8},{10,11... | collective-permute-start | bytes 73736 | tf_op jit(solution)/shard_map/ppermute | solution.py:30
  23.2 23.1 %collective-permute-start.4 = (s32[2,512]{1,0:T(2,128)S(1)}, s32[2,512]{1,0:T(2,128)S(1)}, u32[]{:S(2)}, u32[]{:S(2)}) collective-permute-start(s32[2,512]{1,0:T(2,128)S(1)} %bitcast.263), channel_id=1, source_target_pairs={{0,1},{1,0},{2,3},{3,2},{4,5},{5,4},{6,7},{7,6},{8,9},{9,8},{10,11... | collective-permute-start | bytes 12296 | tf_op jit(solution)/shard_map/ppermute | solution.py:30
  211.4 82.4 %collective-permute-start.14 = (bf16[8,2,96,2048]{3,2,1,0:T(8,128)(2,1)}, bf16[8,2,96,2048]{3,2,1,0:T(8,128)(2,1)}, u32[]{:S(2)}, u32[]{:S(2)}) collective-permute-start(bf16[8,2,96,2048]{3,2,1,0:T(8,128)(2,1)} %get-tuple-element.117), channel_id=1, source_target_pairs={{0,2},{1,5},{2,0},{3,7},{4,6},{5,1},{6,4},{7,3},{8,10},{9,13},{10,... | collective-permute-start | bytes 18874376 | tf_op jit(solution)/shard_map/ppermute | solution.py:104
  215.0 78.7 %collective-permute-start.15 = (bf16[8,96,2048]{2,1,0:T(8,128)(2,1)}, bf16[8,96,2048]{2,1,0:T(8,128)(2,1)}, u32[]{:S(2)}, u32[]{:S(2)}) collective-permute-start(bf16[8,96,2048]{2,1,0:T(8,128)(2,1)} %get-tuple-element.118), channel_id=1, source_target_pairs={{0,8},{1,9},{2,10},{3,11},{4,12},{5,13},{6,14},{7,15},{8,0},{9,1},... | collective-permute-start | bytes 9437192 | tf_op jit(solution)/shard_map/ppermute | solution.py:104
  329.2 35.2 %collective-permute-start.16 = (f32[8,1024]{1,0:T(8,128)S(1)}, f32[8,1024]{1,0:T(8,128)S(1)}, u32[]{:S(2)}, u32[]{:S(2)}) collective-permute-start(f32[8,1024]{1,0:T(8,128)S(1)} %add.324), channel_id=1, source_target_pairs={{0,1},{1,0},{2,3},{3,2},{4,5},{5,4},{6,7},{7,6},{8,9},{9,8},{10,11... | collective-permute-start | bytes 98312 | tf_op jit(solution)/shard_map/ppermute | solution.py:30
  336.6 87.1 %collective-permute-start.17 = (bf16[4,2,96,2048]{3,1,2,0:T(2,128)(2,1)}, bf16[4,2,96,2048]{3,1,2,0:T(2,128)(2,1)}, u32[]{:S(2)}, u32[]{:S(2)}) collective-permute-start(bf16[4,2,96,2048]{3,1,2,0:T(2,128)(2,1)} %copy.79), channel_id=1, source_target_pairs={{0,4},{1,3},{2,6},{3,1},{4,0},{5,7},{6,2},{7,5},{8,12},{9,11},{10,... | collective-permute-start | bytes 9437192 | tf_op jit(solution)/shard_map/ppermute | solution.py:104
  343.2 80.4 %collective-permute-start.18 = (bf16[4,96,2048]{2,1,0:T(8,128)(2,1)}, bf16[4,96,2048]{2,1,0:T(8,128)(2,1)}, u32[]{:S(2)}, u32[]{:S(2)}) collective-permute-start(bf16[4,96,2048]{2,1,0:T(8,128)(2,1)} %get-tuple-element.191), channel_id=1, source_target_pairs={{0,16},{1,17},{2,18},{3,19},{4,20},{5,21},{6,22},{7,23},{8,24},{9,... | collective-permute-start | bytes 4718600 | tf_op jit(solution)/shard_map/ppermute | solution.py:104
  345.7 77.9 %collective-permute-start.19 = (bf16[8,96,768]{2,1,0:T(8,128)(2,1)}, bf16[8,96,768]{2,1,0:T(8,128)(2,1)}, u32[]{:S(2)}, u32[]{:S(2)}) collective-permute-start(bf16[8,96,768]{2,1,0:T(8,128)(2,1)} %get-tuple-element.130), channel_id=1, source_target_pairs={{0,2},{1,5},{2,0},{3,7},{4,6},{5,1},{6,4},{7,3},{8,10},{9,13},{10,... | collective-permute-start | bytes 3538952 | tf_op jit(solution)/shard_map/ppermute | solution.py:104
  373.4 50.2 %collective-permute-start.22 = (bf16[2,2,2,2,128,96]{4,5,3,2,1,0:T(8,128)(2,1)}, bf16[2,2,2,2,128,96]{4,5,3,2,1,0:T(8,128)(2,1)}, u32[]{:S(2)}, u32[]{:S(2)}) collective-permute-start(bf16[2,2,2,2,128,96]{4,5,3,2,1,0:T(8,128)(2,1)} %get-tuple-element.214), channel_id=1, source_target_pairs={{0,2},{1,5},{2,0},{3,7},{4,6},{5,1},{6,4},{7,3},{8,10},{9,13},{10,... | collective-permute-start | bytes 1179656 | tf_op jit(solution)/shard_map/ppermute | solution.py:104
  405.9 63.0 %collective-permute-start.26 = (bf16[4,3,96,1536]{3,2,1,0:T(8,128)(2,1)}, bf16[4,3,96,1536]{3,2,1,0:T(8,128)(2,1)}, u32[]{:S(2)}, u32[]{:S(2)}) collective-permute-start(bf16[4,3,96,1536]{3,2,1,0:T(8,128)(2,1)} %get-tuple-element.139), channel_id=1, source_target_pairs={{0,2},{1,5},{2,0},{3,7},{4,6},{5,1},{6,4},{7,3},{8,10},{9,13},{10,... | collective-permute-start | bytes 10616840 | tf_op jit(solution)/shard_map/ppermute | solution.py:104
  423.6 40.0 %collective-permute-start.23 = (bf16[512,1536]{1,0:T(8,128)(2,1)}, bf16[512,1536]{1,0:T(8,128)(2,1)S(1)}, u32[]{:S(2)}, u32[]{:S(2)}) collective-permute-start(bf16[512,1536]{1,0:T(8,128)(2,1)} %get-tuple-element.136), channel_id=1, source_target_pairs={{0,1},{1,0},{2,3},{3,2},{4,5},{5,4},{6,7},{7,6},{8,9},{9,8},{10,11... | collective-permute-start | bytes 4718600 | tf_op jit(solution)/shard_map/ppermute | solution.py:54
  430.2 38.7 %collective-permute-start.24 = (bf16[2,2,96,2048]{3,1,2,0:T(2,128)(2,1)S(1)}, bf16[2,2,96,2048]{3,1,2,0:T(2,128)(2,1)S(1)}, u32[]{:S(2)}, u32[]{:S(2)}) collective-permute-start(bf16[2,2,96,2048]{3,1,2,0:T(2,128)(2,1)S(1)} %get-tuple-element.189), channel_id=1, source_target_pairs={{0,8},{1,9},{2,10},{3,11},{4,12},{5,13},{6,14},{7,15},{8,0},{9,1},... | collective-permute-start | bytes 4718600 | tf_op jit(solution)/shard_map/ppermute | solution.py:104
  433.1 24.6 %collective-permute-start.27 = (bf16[4,96,768]{2,1,0:T(8,128)(2,1)S(1)}, bf16[4,96,768]{2,1,0:T(8,128)(2,1)S(1)}, u32[]{:S(2)}, u32[]{:S(2)}) collective-permute-start(bf16[4,96,768]{2,1,0:T(8,128)(2,1)S(1)} %bitcast.245), channel_id=1, source_target_pairs={{0,4},{1,3},{2,6},{3,1},{4,0},{5,7},{6,2},{7,5},{8,12},{9,11},{10,... | collective-permute-start | bytes 1769480 | tf_op jit(solution)/shard_map/ppermute | solution.py:104
  435.3 21.5 %collective-permute-start.28 = (bf16[2,2,2,2,128,96]{4,5,3,2,1,0:T(8,128)(2,1)S(1)}, bf16[2,2,2,2,128,96]{4,5,3,2,1,0:T(8,128)(2,1)S(1)}, u32[]{:S(2)}, u32[]{:S(2)}) collective-permute-start(bf16[2,2,2,2,128,96]{4,5,3,2,1,0:T(8,128)(2,1)S(1)} %fusion.42), channel_id=1, source_target_pairs={{0,4},{1,3},{2,6},{3,1},{4,0},{5,7},{6,2},{7,5},{8,12},{9,11},{10,... | collective-permute-start | bytes 1179656 | tf_op jit(solution)/shard_map/ppermute | solution.py:104
  474.3 87.5 %collective-permute-start.36 = (bf16[2,3,96,1536]{3,2,1,0:T(8,128)(2,1)}, bf16[2,3,96,1536]{3,2,1,0:T(8,128)(2,1)}, u32[]{:S(2)}, u32[]{:S(2)}) collective-permute-start(bf16[2,3,96,1536]{3,2,1,0:T(8,128)(2,1)} %fusion.15), channel_id=1, source_target_pairs={{0,4},{1,3},{2,6},{3,1},{4,0},{5,7},{6,2},{7,5},{8,12},{9,11},{10,... | collective-permute-start | bytes 5308424 | tf_op jit(solution)/shard_map/ppermute | solution.py:104
  479.7 82.0 %collective-permute-start.38 = (bf16[1,2,96,2048]{3,1,2,0:T(2,128)(2,1)}, bf16[1,2,96,2048]{3,1,2,0:T(2,128)(2,1)}, u32[]{:S(2)}, u32[]{:S(2)}) collective-permute-start(bf16[1,2,96,2048]{3,1,2,0:T(2,128)(2,1)} %fusion.23), channel_id=1, source_target_pairs={{0,16},{1,17},{2,18},{3,19},{4,20},{5,21},{6,22},{7,23},{8,24},{9,... | collective-permute-start | bytes 2359304 | tf_op jit(solution)/shard_map/ppermute | solution.py:104
  483.0 50.9 %collective-permute-start.34 = (bf16[2,2,2,2,128,96]{4,5,3,2,1,0:T(8,128)(2,1)S(1)}, bf16[2,2,2,2,128,96]{4,5,3,2,1,0:T(8,128)(2,1)S(1)}, u32[]{:S(2)}, u32[]{:S(2)}) collective-permute-start(bf16[2,2,2,2,128,96]{4,5,3,2,1,0:T(8,128)(2,1)S(1)} %get-tuple-element.210), channel_id=1, source_target_pairs={{0,16},{1,17},{2,18},{3,19},{4,20},{5,21},{6,22},{7,23},{8,24},{9,... | collective-permute-start | bytes 1179656 | tf_op jit(solution)/shard_map/ppermute | solution.py:104
  536.3 25.4 %collective-permute-start.39 = (bf16[1,96,2048]{2,1,0:T(8,128)(2,1)S(1)}, bf16[1,96,2048]{2,1,0:T(8,128)(2,1)S(1)}, u32[]{:S(2)}, u32[]{:S(2)}) collective-permute-start(bf16[1,96,2048]{2,1,0:T(8,128)(2,1)S(1)} %fusion.32), channel_id=1, source_target_pairs={{0,4},{1,3},{2,6},{3,1},{4,0},{5,7},{6,2},{7,5},{8,12},{9,11},{10,... | collective-permute-start | bytes 1179656 | tf_op jit(solution)/shard_map/ppermute | solution.py:104
  564.4 42.3 %collective-permute-start.42 = (bf16[1,3,96,1536]{3,2,1,0:T(8,128)(2,1)}, bf16[1,3,96,1536]{3,2,1,0:T(8,128)(2,1)}, u32[]{:S(2)}, u32[]{:S(2)}) collective-permute-start(bf16[1,3,96,1536]{3,2,1,0:T(8,128)(2,1)} %fusion.16), channel_id=1, source_target_pairs={{0,8},{1,9},{2,10},{3,11},{4,12},{5,13},{6,14},{7,15},{8,0},{9,1},... | collective-permute-start | bytes 2654216 | tf_op jit(solution)/shard_map/ppermute | solution.py:104
  574.4 26.7 %collective-permute-start.41 = (f32[8,11,1536]{2,0,1:T(8,128)S(1)}, f32[8,11,1536]{2,0,1:T(8,128)}, u32[]{:S(2)}, u32[]{:S(2)}) collective-permute-start(f32[8,11,1536]{2,0,1:T(8,128)S(1)} %copy.91), channel_id=1, source_target_pairs={{0,16},{1,17},{2,18},{3,19},{4,20},{5,21},{6,22},{7,23},{8,24},{9,... | collective-permute-start | bytes 1622024 | tf_op jit(solution)/shard_map/ppermute | solution.py:104
  610.9 23.9 %collective-permute-start.44 = (bf16[3,96,768]{2,1,0:T(8,128)(2,1)S(1)}, bf16[3,96,768]{2,1,0:T(8,128)(2,1)S(1)}, u32[]{:S(2)}, u32[]{:S(2)}) collective-permute-start(bf16[3,96,768]{2,1,0:T(8,128)(2,1)S(1)} %bitcast_select_fusion.2), channel_id=1, source_target_pairs={{0,16},{1,17},{2,18},{3,19},{4,20},{5,21},{6,22},{7,23},{8,24},{9,... | collective-permute-start | bytes 1327112 | tf_op jit(solution)/shard_map/ppermute | solution.py:104
  (79 other events, 697.4 us)
Sparse Core Ops, SparseCore 0:
  13.0 194.2 all-gather.1

commit v5 on v4

--- a/solution.py
+++ b/solution.py
@@ -115,35 +115,29 @@
 
 
 class Halving:
-    def __init__(self, bits, order, pair):
-        self.labels, self.order = list(bits)[::-1], list(order)
-        bit = self.order.pop(0)
-        self.labels.remove(bit)
-        self.keep, self.got = pair[0], dp_swap(pair[1], bit)
+    def __init__(self, order, keep, send):
+        self.order = list(order)
+        self.keep, self.got = keep, dp_swap(send, self.order.pop(0))
 
     def step(self):
         if self.got is None:
             return
 
-        def add(keep, got):
-            return keep.astype(F32) + got.astype(F32)
+        def add(part):
+            return self.keep[part].astype(F32) + self.got[part].astype(F32)
 
         if not self.order:
-            self.last = add(self.keep, self.got)
+            self.last = add(slice(None))
             self.got = None
             return
-        bit = self.order.pop(0)
-        axis = self.labels.index(bit)
-        tail = self.keep.shape[1:]
-        parts = [v.reshape((2,) * len(self.labels) + tail) for v in (self.keep, self.got)]
-        self.labels.remove(bit)
-        self.keep, send = (
-            add(*(lax.index_in_dim(v, i, axis, keepdims=False) for v in parts))
-            .astype(BF16)
-            .reshape((-1,) + tail)
-            for i in range(2)
-        )
-        self.got = dp_swap(send, bit)
+        half = self.keep.shape[0] // 2
+        send = add(slice(half, None)).astype(BF16)
+        self.keep = add(slice(half)).astype(BF16)
+        self.got = dp_swap(send, self.order.pop(0))
+
+
+def place_of(p, order):
+    return sum((p >> bit & 1) << i for i, bit in enumerate(reversed(order)))
 
 
 class Exchange:
@@ -169,19 +163,29 @@
             self.start()
 
 
-class Gather:
-    def __init__(self, value):
-        self.bits, self.cur = list(range(dp_bits())), value[None]
+class Small:
+    def __init__(self, parts, total):
+        self.bits, self.shape, self.total = list(range(dp_bits())), parts.shape, total
+        self.cur = parts.reshape((2,) * dp_bits() + parts.shape[1:])
         self.got = None
         self.start()
 
     def start(self):
         if self.bits:
-            self.got = dp_swap(self.cur, self.bits.pop(0))
+            self.bit = self.bits.pop(0)
+            self.axis = dp_bits() - 1 - self.bit
+            self.keep, send = (
+                lax.index_in_dim(self.cur, i, self.axis, keepdims=False) for i in range(2)
+            )
+            flat = jnp.concatenate([send.reshape(-1, 128), self.total], axis=0)
+            self.got = dp_swap(flat, self.bit)
 
     def step(self):
         if self.got is not None:
-            self.cur = jnp.concatenate([self.cur, self.got], axis=0)
+            rows = self.keep.size // 128
+            self.total = self.total + self.got[rows:]
+            got = self.got[:rows].reshape(self.keep.shape)
+            self.cur = jnp.stack([self.keep, got], axis=self.axis)
             self.got = None
             self.start()
 
@@ -454,17 +458,16 @@
         dst[p * rows : (p + 1) * rows, :] = src[pl.ds(start, rows), :]
 
 
-def put_halves(keep, send, value, count, bit, slot=None):
+def put_halves(keep, send, value, count, order, slot=None):
     rows = value.shape[0] // count
-    low = (1 << bit) - 1
     for p in range(count):
-        place = (p & low) | (p >> (bit + 1) << bit)
+        place = place_of(p, order[1:])
         where = place if slot is None else (place, slot)
-        (send if p >> bit & 1 else keep)[where] = value[p * rows : (p + 1) * rows]
+        (send if p >> order[0] & 1 else keep)[where] = value[p * rows : (p + 1) * rows]
 
 
 def ffn_kernel(
-    bits, id_ref, s_ref, b_ref, w_ref, d_ref,
+    orders, id_ref, s_ref, b_ref, w_ref, d_ref,
     wk_ref, ws_ref, dk_ref, ds_ref, fo_ref, fp_ref, so_ref, sp_ref,
     st, bt, tmp, wg, wu, facc, sacc,
 ):
@@ -497,9 +500,9 @@
     hidden = (silu * up).astype(BF16)
     g_gate = (back * up * (sig + silu * (1.0 - sig))).astype(BF16)
     g_up = (back * silu).astype(BF16)
-    put_halves(wk_ref, ws_ref, dot(st[...], g_gate).astype(BF16), count, bits[0], 0)
-    put_halves(wk_ref, ws_ref, dot(st[...], g_up).astype(BF16), count, bits[0], 1)
-    put_halves(dk_ref, ds_ref, dot(bt[...], hidden).astype(BF16), count, bits[1])
+    put_halves(wk_ref, ws_ref, dot(st[...], g_gate).astype(BF16), count, orders[0], 0)
+    put_halves(wk_ref, ws_ref, dot(st[...], g_up).astype(BF16), count, orders[0], 1)
+    put_halves(dk_ref, ds_ref, dot(bt[...], hidden).astype(BF16), count, orders[1])
     facc[...] += dot(hidden, d_ref[...])
     sacc[...] += dot(g_gate, wg[...], 1, 1) + dot(g_up, wu[...], 1, 1)
 
@@ -511,7 +514,7 @@
         sp_ref[...] = sacc[own:].astype(BF16)
 
 
-def ffn(ids, s, b, w, d, local, dp, bits):
+def ffn(ids, s, b, w, d, local, dp, orders):
     tokens, depth = s.shape
     hid = d.shape[0]
     bc = min(256, hid)
@@ -522,7 +525,7 @@
     half = pl.BlockSpec((dp // 2, share, bc), lambda i: (0, 0, i))
     halves = pl.BlockSpec((dp // 2, 2, share, bc), lambda i: (0, 0, 0, i))
     return pl.pallas_call(
-        functools.partial(ffn_kernel, bits),
+        functools.partial(ffn_kernel, orders),
         grid=(hid // bc,),
         in_specs=[
             pl.BlockSpec(memory_space=pltpu.SMEM),
@@ -597,55 +600,46 @@
     )(ids, xo, xp, front, w, got)
 
 
-def project_back_kernel(
-    id_ref, da_ref, db_ref, pre_ref, stat_ref, gain_ref, first_ref, w_ref, got_ref,
-    keep_ref, send_ref, own_ref, peer_ref, gt, tmp, acc,
+def project_grad_kernel(
+    orders, id_ref, da_ref, db_ref, pre_ref, stat_ref, gain_ref, first_ref,
+    keep_ref, send_ref, vkeep_ref, vsend_ref, g_ref, gt, tmp,
 ):
+    order, late = orders
     j = pl.program_id(0)
-    tokens, own = pre_ref.shape[1:]
+    own = pre_ref.shape[2]
     cut = da_ref.shape[2]
-    local = own_ref.shape[0]
-    f = id_ref[1]
     count = 2 * keep_ref.shape[0]
     inv, mean = column(stat_ref, j, 128), column(stat_ref, j + 3, 128)
-    grads = []
     for c in range(own // 128):
         part = slice(c * 128, (c + 1) * 128)
         here = slice(c * 128 - cut, (c + 1) * 128 - cut) if c * 128 >= cut else part
         d = (db_ref if c * 128 >= cut else da_ref)[0, :, here]
         g = inv * (d * gain_ref[0, :, part] - pre_ref[0, :, part] * inv * mean)
         tmp[part, :] = g.T.astype(BF16)
-        grads.append(g.astype(BF16))
-    g = jnp.concatenate(grads, axis=1)
-    put_relative(gt, tmp, id_ref[0] % count, f, count)
-    put_halves(keep_ref, send_ref, dot(gt[...], first_ref[...]).astype(BF16), count, 0, j)
-
-    @pl.when(j == 0)
+        g_ref[0, :, part] = g.astype(BF16)
+    put_relative(gt, tmp, id_ref[0] % count, id_ref[1], count)
+    wide = dot(gt[...], first_ref[...]).astype(BF16)
+
+    @pl.when(j < 2)
     def _():
-        acc[...] = jnp.zeros_like(acc)
-
-    mine = pl.ds(pl.multiple_of(f * own, 128), own)
-    other = pl.ds(pl.multiple_of((1 - f) * own, 128), own)
-    acc[:, mine] += dot(g, w_ref[0, :, mine], 1, 1)
-    acc[:, other] += dot(g, got_ref[0], 1, 1)
+        put_halves(keep_ref, send_ref, wide, count, order, j)
 
     @pl.when(j == 2)
     def _():
-        own_ref[...] = acc[:local]
-        peer_ref[...] = acc[local:].astype(BF16)
-
-
-def project_back(ids, da, db, pre, stats, gain, first, w, got, dp):
+        put_halves(vkeep_ref, vsend_ref, wide, count, late)
+
+
+def project_grad(ids, da, db, pre, stats, gain, first, dp, orders):
     _, tokens, own = pre.shape
     depth = first.shape[1]
-    local = tokens // 2
     share = depth // dp
     const = lambda j: (0, 0)
     block = lambda j: (j, 0, 0)
     once = functools.partial(pl.BlockSpec, pipeline_mode=pl.Buffered(1))
-    half = once((dp // 4, 3, share, depth), lambda j: (0, 0, 0, 0))
+    half = once((dp // 4, 2, share, depth), lambda j: (0, 0, 0, 0))
+    vhalf = once((dp // 4, share, depth), lambda j: (0, 0, 0))
     return pl.pallas_call(
-        project_back_kernel,
+        functools.partial(project_grad_kernel, orders),
         grid=(3,),
         in_specs=[
             pl.BlockSpec(memory_space=pltpu.SMEM),
@@ -654,21 +648,58 @@
             pl.BlockSpec((8, tokens), const),
             pl.BlockSpec((1, 1, own), block),
             once((tokens, depth), const),
+        ],
+        out_specs=[half, half, vhalf, vhalf, pl.BlockSpec((1, tokens, own), block)],
+        out_shape=[sds((dp // 4, 2, share, depth), BF16)] * 2
+        + [sds((dp // 4, share, depth), BF16)] * 2
+        + [sds((3, tokens, own), BF16)],
+        scratch_shapes=[pltpu.VMEM((own, tokens), BF16), pltpu.VMEM((own, tokens), BF16)],
+    )(ids, da, db, pre, stats, gain, first)
+
+
+def project_back_kernel(id_ref, g_ref, w_ref, got_ref, own_ref, peer_ref, acc):
+    j = pl.program_id(0)
+    own = g_ref.shape[2]
+    local = own_ref.shape[0]
+    f = id_ref[1]
+    mine = pl.ds(pl.multiple_of(f * own, 128), own)
+    other = pl.ds(pl.multiple_of((1 - f) * own, 128), own)
+
+    @pl.when(j == 0)
+    def _():
+        acc[...] = jnp.zeros_like(acc)
+
+    acc[:, mine] += dot(g_ref[0], w_ref[0, :, mine], 1, 1)
+    acc[:, other] += dot(g_ref[0], got_ref[0], 1, 1)
+
+    @pl.when(j == 2)
+    def _():
+        own_ref[...] = acc[:local]
+        peer_ref[...] = acc[local:].astype(BF16)
+
+
+def project_back(ids, g, w, got):
+    _, tokens, own = g.shape
+    depth = w.shape[2]
+    local = tokens // 2
+    const = lambda j: (0, 0)
+    block = lambda j: (j, 0, 0)
+    once = functools.partial(pl.BlockSpec, pipeline_mode=pl.Buffered(1))
+    return pl.pallas_call(
+        project_back_kernel,
+        grid=(3,),
+        in_specs=[
+            pl.BlockSpec(memory_space=pltpu.SMEM),
+            pl.BlockSpec((1, tokens, own), block),
             pl.BlockSpec((1, own, depth), block), pl.BlockSpec((1, own, own), block),
         ],
-        out_specs=[half, half, once((local, depth), const), once((local, depth), const)],
-        out_shape=[sds((dp // 4, 3, share, depth), BF16)] * 2 + [
-            sds((local, depth)), sds((local, depth), BF16),
-        ],
-        scratch_shapes=[
-            pltpu.VMEM((own, tokens), BF16), pltpu.VMEM((own, tokens), BF16),
-            pltpu.VMEM((tokens, depth), F32),
-        ],
-        compiler_params=pltpu.CompilerParams(vmem_limit_bytes=62 << 20),
-    )(ids, da, db, pre, stats, gain, first, w, got)
-
-
-def out_back_kernel(id_ref, *refs):
+        out_specs=[once((local, depth), const), once((local, depth), const)],
+        out_shape=[sds((local, depth)), sds((local, depth), BF16)],
+        scratch_shapes=[pltpu.VMEM((tokens, depth), F32)],
+    )(ids, g, w, got)
+
+
+def out_back_kernel(order, id_ref, *refs):
     n = len(refs) - 8
     blocks, (w_ref, mixed_ref, g_ref, keep_ref, send_ref, all_ref, gt, tmp) = refs[:n], refs[n:]
     local = blocks[0].shape[0]
@@ -681,16 +712,16 @@
         tmp[part, :] = grad[:, part].astype(F32).T.astype(BF16)
     count = 2 * keep_ref.shape[0]
     put_relative(gt, tmp, id_ref[0], id_ref[1], count)
-    put_halves(keep_ref, send_ref, dot(gt[...], mixed_ref[...]).astype(BF16), count, 0)
-
-
-def out_back(ids, blocks, w, mixed, dp):
+    put_halves(keep_ref, send_ref, dot(gt[...], mixed_ref[...]).astype(BF16), count, order)
+
+
+def out_back(ids, blocks, w, mixed, dp, order):
     tokens, own = mixed.shape
     depth = w.shape[1]
     vmem = pl.BlockSpec(memory_space=pltpu.VMEM)
     half = sds((dp // 2, depth // dp, own), BF16)
     return pl.pallas_call(
-        out_back_kernel,
+        functools.partial(out_back_kernel, order),
         in_specs=[pl.BlockSpec(memory_space=pltpu.SMEM)] + [vmem] * (len(blocks) + 2),
         out_specs=[vmem] * 3,
         out_shape=[sds((tokens, own)), half, half],
@@ -739,7 +770,7 @@
     dpn, me = lax.axis_size("dp"), lax.axis_index("dp")
     bits = list(range(dp_bits()))
     low_bits = bits[:-1]
-    late = bits[2:] + bits[:2]
+    late = bits[2:3] + bits[:2] + bits[3:]
     own_d = D // n
     local = hidden_in.shape[1]
     tokens = n * local
@@ -812,13 +843,13 @@
     second_all = jnp.concatenate(gather_rot(second), axis=0)
     branch_all = (gate_ffn * dy_all.astype(F32)).astype(BF16)
     wide_keep, wide_send, down_keep, down_send, ffn_own, ffn_rest, back_own, back_rest = ffn(
-        ids, second_all, branch_all, w_gate_up, w_down, local, dpn, (bits[0], late[0])
+        ids, second_all, branch_all, w_gate_up, w_down, local, dpn, (bits, late)
     )
     (ffn_own, ffn_rest, back_own, back_rest), text_all = lax.optimization_barrier(
         ((ffn_own, ffn_rest, back_own, back_rest), text_all)
     )
-    wide_chain = Halving(bits, bits, (wide_keep, wide_send))
-    down_chain = Halving(bits, late, (down_keep, down_send))
+    wide_chain = Halving(bits, wide_keep, wide_send)
+    down_chain = Halving(late, down_keep, down_send)
     grad_second = scatter_rot([back_own] + [rows(back_rest, r) for r in range(n - 1)])
     ffn_branch = scatter_rot([ffn_own] + [rows(ffn_rest, r) for r in range(n - 1)])
     output = (after_attn + gate_ffn * ffn_branch).astype(BF16)
@@ -833,8 +864,8 @@
     )
     d_gate_attn = jnp.sum(grad_after * attn_branch, axis=0) * (1.0 - gate_attn[0] * gate_attn[0])
     grad_attn = (gate_attn * grad_after).astype(BF16)
-    grad_mixed, *halves = out_back(ids, gather_rot(grad_attn), w_out, mixed, dpn)
-    out_chain = Halving(bits, bits, halves)
+    grad_mixed, *halves = out_back(ids, gather_rot(grad_attn), w_out, mixed, dpn, bits)
+    out_chain = Halving(bits, *halves)
     blocks = pre_p.shape[2] // width
     cut = max(1, 2 * blocks // 3)
     grad_mixed = pad_cols(grad_mixed, width)
@@ -866,11 +897,15 @@
     if paired:
         stats = jnp.concatenate([inverse[:2], ones, means, zeros, zeros, zeros], axis=0)
         gain3 = jnp.stack([gain_own[2:3], gain_own[3:4], jnp.ones_like(gain_own[2:3])])
-        *halves, own_part, peer_part = project_back(
-            ids, part_a[0], part_b[0], pre, stats, gain3, first_all, w_flat, w_parts[1], dpn
+        *halves, grads = project_grad(
+            ids, part_a[0], part_b[0], pre, stats, gain3, first_all, dpn,
+            (low_bits, low_bits[2:] + low_bits[:2]),
         )
-        qkv_chain = Halving(low_bits, low_bits, halves)
-        parts = [own_part, peer_part]
+        qkv_chains = [
+            Halving(low_bits, *halves[:2]), Halving(low_bits[2:] + low_bits[:2], *halves[2:]),
+        ]
+        grads = advance([wide_chain, down_chain, out_chain, pair_chain], grads)
+        parts = project_back(ids, grads, w_flat, w_parts[1])
     else:
         d = jnp.concatenate([part_a[0], part_b[0]], axis=2)[:, :, :own_d]
         inv, mean = inverse[:2, :, None], means[:, :, None]
@@ -879,18 +914,17 @@
         wide = [dot(g, first_all, 0, 0).astype(BF16) for g in grads]
         wide = [jnp.concatenate(natural(exchange_rot(w_, 1)), axis=0) for w_ in wide]
         wide = relative(jnp.stack([w_.reshape(dpn, share, own_d) for w_ in wide], axis=1))
-        wide = wide.reshape((dpn // 2, 2) + wide.shape[1:])
-        qkv_chain = Halving(bits, bits, (wide[:, 0], wide[:, 1]))
+        wide = jnp.stack([wide[p] for p in sorted(range(dpn), key=lambda p: place_of(p, bits))])
+        qkv_chains = [Halving(bits, wide[: dpn // 2], wide[dpn // 2 :])]
         parts = [
             sum(dot(rows(g, r), w_heads[j], 1, 1) for j, g in enumerate(grads)) for r in range(n)
         ]
         parts = [parts[0]] + [p.astype(BF16) for p in parts[1:]]
-    chains = [wide_chain, down_chain, out_chain]
-    parts = advance([wide_chain, down_chain, out_chain, pair_chain], parts)
+    parts = advance([out_chain, pair_chain], parts)
     grad_first = scatter_rot(parts)
 
     text_in = text_bwd(pair_all, w_text)
-    text_in = advance([out_chain, pair_chain], text_in)
+    text_in = advance([wide_chain, down_chain, *qkv_chains, out_chain, pair_chain], text_in)
     text_in = jnp.concatenate(natural(exchange_rot(text_in, 0)), axis=1)
 
     inverse_one = inverse_rms(x_own)
@@ -903,40 +937,39 @@
         + rms_back(grad_first * gain_full[0] * (1.0 + scale_attn), normed_one, inverse_one)
     ).astype(BF16)
 
-    grad_input = advance([wide_chain, down_chain, qkv_chain], grad_input)
 
     sums = [d_scale_attn, d_gate_attn, d_scale_ffn, d_gate_ffn, gain_one, gain_two]
     sums = pair_sum(jnp.stack(sums))
     stamp = jnp.full((1, D), timesteps[0].astype(F32))
     gate_pad = jnp.pad(gate_total, (0, own_d - gate_total.shape[0]))[None]
     small = jnp.concatenate([block_of(sums[4:], f, 1), gain_q, gain_k, gain_text, gate_pad], axis=0)
-    small_chain = Gather(
-        jnp.concatenate([sums[:4], stamp, jnp.pad(small, ((0, 0), (0, D - own_d)))], axis=0)
-    )
+    mods = jnp.concatenate([sums[:4], stamp], axis=0).reshape(5, dpn, share).transpose(1, 0, 2)
+    mods = jnp.pad(mods, ((0, 0), (0, 3), (0, -share % 128)))
+    small_chain = Small(relative(mods), small.reshape(-1, 128))
 
     def rest(chain):
         while chain.got is not None:
             chain.step()
 
-    advance([pair_chain, out_chain, small_chain], ())
+    grad_input = advance([*qkv_chains, small_chain, pair_chain], grad_input)
     rest(pair_chain)
     pair_cols = absolute(pair_chain.cur.reshape(pair_chain.shape))
     pair_cols = jnp.concatenate(natural(gather_rot(pair_cols)), axis=2)
     pair_cols = pair_cols.transpose(0, 2, 1, 3).reshape(dpn * TEXT, 2 * share)
     text_grad = dot(pair_cols, text_all, 0, 0).reshape(2, share, TW // n)
-    text_grad = advance([qkv_chain, small_chain, wide_chain, down_chain], text_grad)
-    for chain in (small_chain, qkv_chain, out_chain, wide_chain, down_chain):
+    for chain in (*qkv_chains, small_chain, out_chain, wide_chain, down_chain):
         rest(chain)
-    total = jnp.sum(small_chain.cur[:, 5:, :own_d], axis=0)
-    mods = lax.dynamic_slice_in_dim(small_chain.cur[:, :4], me * share, share, 2)
-    times = time_embed(small_chain.cur[:, 4, 0])
+    total = small_chain.total.reshape(6, own_d)
+    mods = small_chain.cur.reshape(small_chain.shape)
+    times = time_embed(mods[:, 4, 0])
     times = lax.dynamic_slice_in_dim(times, f * own_te, own_te, 1).astype(F32)
     ada_grad = lax.dot_general(
-        mods.reshape(dpn, 4 * share), times, (((0,), (0,)), ((), ())),
+        mods[:, :4, :share].reshape(dpn, 4 * share), times, (((0,), (0,)), ((), ())),
         precision=lax.Precision.HIGHEST,
     ).reshape(4, share, own_te)
-    qkv_grad = qkv_chain.last[0]
+    qkv_grad = qkv_chains[0].last[0]
     if paired:
+        qkv_grad = jnp.concatenate([qkv_grad, qkv_chains[1].last])
         own_side = f == (me >> low_bits[-1] + 1)
         mine, got = exchange_rot(qkv_grad.astype(BF16), 2)
         keep, send = jnp.where(own_side, mine, got), jnp.where(own_side, got, mine)

time: 648 us -> 634 us (0.978)
  waiting for transfers between devices: 131 us -> 113 us
  local copies, waits for them, and re-layouts: 50.3 us -> 37 us
  other arithmetic: 108 us -> 118 us
    pallas_call x2 -> x3, Pallas kernels: 99.8 us -> 120 us  [the longest x1 90.2 us: ffn(): pl.pallas_call(functools.partial(ffn_kernel, orders), grid=(hid // bc,),...]
    ppermute x24 -> x27, waiting for transfers between devices: 122 us -> 104 us  [dp_swap(): return lax.ppermute(value, ('dp', 'fsdp'), pairs)]
    pallas_call x1, Pallas kernels: 30.2 us -> 13.7 us  [project_back(): pl.pallas_call(project_back_kernel, grid=(3,), in_specs=[pl.BlockSpec(mem...]
    convert_element_type x15 -> x13, other arithmetic: 52.9 us -> 41.6 us  [the longest x8 33.6 us: step(): self.keep = add(slice(half)).astype(BF16)]
    slice x5 -> x8, local copies, waits for them, and re-layouts: 9.9 us -> 1.6 us  [the longest x4 0.77 us: step(): got = self.got[:rows].reshape(self.keep.shape)]
    convert_element_type x1 -> x0, local copies, waits for them, and re-layouts: 6.95 us -> none  [step(): self.keep, send = (add(*(lax.index_in_dim(v, i, axis, keepdims=False) for...]
    ppermute x24 -> x27, starting transfers between devices: 30 us -> 34.9 us  [dp_swap(): return lax.ppermute(value, ('dp', 'fsdp'), pairs)]
  transfers between devices with their start and end apart: 47 -> 50, of which waited for: 14 -> 16; matrix products, arithmetic and copies ran while one was open for 24% -> 27% of each run, Pallas kernels for 39% -> 41%
where the time goes in v5:
time: 634 us; the launch traced here: 628 us
  Pallas kernels  280 us (44%)
  other arithmetic  118 us (19%)
  waiting for transfers between devices  113 us (18%)
  starting transfers between devices  39.5 us (6%)
  local copies, waits for them, and re-layouts  37 us (6%)
  matrix products  21.3 us (3%)
  between operations  16.6 us (3%)
    ppermute x27, waiting for transfers between devices, dp_swap(): return lax.ppermute(value, ('dp', 'fsdp'), pairs)  104 us
    pallas_call x1, Pallas kernels, ffn(): pl.pallas_call(functools.partial(ffn_kernel, orders), grid=(hid // bc,),...  90.2 us
    pallas_call x2, Pallas kernels, attn_backward(): pl.pallas_call(attn_bwd_kernel, grid=(blocks,), in_specs=[scalar, col, co...  68.9 us
    ppermute x27, starting transfers between devices, dp_swap(): return lax.ppermute(value, ('dp', 'fsdp'), pairs)  34.9 us
    convert_element_type x8, other arithmetic, step(): self.keep = add(slice(half)).astype(BF16)  33.6 us
    pallas_call x1, Pallas kernels, attn_forward(): pl.pallas_call(attn_fwd_kernel, grid=(blocks,), in_specs=[scalar, three,...  32.1 us
    pallas_call x1, Pallas kernels, project_grad(): pl.pallas_call(functools.partial(project_grad_kernel, orders), grid=(3,),...  19.9 us
    pallas_call x1, Pallas kernels, text_fwd(): pl.pallas_call(text_fwd_kernel, grid=(depth // bk,), in_specs=[pl.BlockSp...  16.2 us
  transfers between devices with their start and end apart: 50, of which 16 were waited for; matrix products, arithmetic and copies ran while one was open for 27% of the time, Pallas kernels for 41%

profile of v5, /device:TPU:0, one launch (start us, length us, event | category | flops | bytes accessed | tf_op | source)
XLA Modules:
  0.0 627.7 jit_solution(7392873004097976870)
XLA Ops:
  18.1 4.6 fusion.2
  23.3 16.2 %shard_map.222 = f32[2,256,1536]{2,1,0:T(8,128)} custom-call(bf16[256,2048]{1,0:T(8,128)(2,1)} %pad_maximum_fusion.2.x_ref, bf16[2048,2,1536]{2,1,0:T(2,128)(2,1)} %w_ref.5), custom_call_target="tpu_custom_call" | custom-call | tf_op jit(solution)/shard_map/pallas_call | solution.py:428
  53.9 14.9 %shard_map.221 = (bf16[1024,1536]{1,0:T(8,128)(2,1)}, f32[3,1024,768]{2,1,0:T(8,128)}, f32[8,1024]{1,0:T(8,128)}) custom-call(s32[2]{0:T(128)} %pad_add_fusion.1.id_ref, bf16[512,1536]{1,0:T(8,128)(2,1)} %bitcast.149, bf16[512,1536]{1,0:T(8,128)(2,1)} %collective-permute-done.1.xp_ref, f32[1,1536]{1,0:T(1,128)} %get-tuple-element.268.front_ref, ...), custom_call_target="tpu_custom_call" | custom-call | tf_op jit(solution)/shard_map/pallas_call | solution.py:584
  71.6 32.1 %shard_map.223 = (bf16[1024,768]{1,0:T(8,128)(2,1)}, bf16[1024,768]{1,0:T(8,128)(2,1)}, bf16[1024,768]{1,0:T(8,128)(2,1)}, bf16[1024,768]{1,0:T(8,128)(2,1)}, f3...) custom-call(s32[1]{0:T(128)S(6)} %copy.73.len_ref, ...), custom_call_target="tpu_custom_call" | custom-call | tf_op jit(solution)/shard_map/pallas_call | solution.py:371
  120.7 90.2 %shard_map.224 = (bf16[8,2,96,2048]{3,2,1,0:T(8,128)(2,1)}, bf16[8,2,96,2048]{3,2,1,0:T(8,128)(2,1)}, bf16[8,96,2048]{2,1,0:T(8,128)(2,1)}, bf16[8,96,2048]{2,1,...) custom-call(s32[2]{0:T(128)} %pad_add_fusion.1.id_ref, ...), custom_call_target="tpu_custom_call" | custom-call | tf_op jit(solution)/shard_map/pallas_call | solution.py:527
  221.5 5.8 fusion.7
  235.8 9.6 %shard_map.225 = (f32[1024,768]{1,0:T(8,128)}, bf16[8,96,768]{2,1,0:T(8,128)(2,1)}, bf16[8,96,768]{2,1,0:T(8,128)(2,1)}) custom-call(s32[2]{0:T(128)} %pad_add_fusion.1.id_ref, bf16[512,1536]{1,0:T(8,128)(2,1)} %multiply_convert_fusion.1.refs_0_, bf16[512,1536]{1,0:T(8,128)(2,1)} %collective-permute-done.13.refs_1_, bf16[768,1536]{1,0:T(8,128)(2,1)} %refs_2_.1, ...), custom_call_target="tpu_custom_call" | custom-call | tf_op jit(solution)/shard_map/pallas_call | solution.py:723
  245.4 44.4 %shard_map.226 = (f32[3,1024,512]{2,1,0:T(8,128)}, f32[256,512]{1,0:T(8,128)}, f32[256,512]{1,0:T(8,128)}, f32[8,1024]{1,0:T(8,128)}, f32[1,512]{1,0:T(1,128)}, /*index=5*/f32[1,512]{1,0:T(1,128)}, f32[1,512]{1,0:T(1,128)}) custom-call(s32[1]{0:T(128)S(6)} %copy.73.len_ref, bf16[1024,768]{1,0:T(8,128)(2,1)} %get-tuple-element.103.q_ref, ...), custom_call_target="tpu_custom_call" | custom-call | tf_op jit(solution)/shard_map/pallas_call | solution.py:386
  289.8 24.5 %shard_map.227 = (f32[3,1024,256]{2,1,0:T(8,128)}, f32[256,256]{1,0:T(8,128)}, f32[256,256]{1,0:T(8,128)}, f32[8,1024]{1,0:T(8,128)}, f32[1,256]{1,0:T(1,128)}, /*index=5*/f32[1,256]{1,0:T(1,128)}, f32[1,256]{1,0:T(1,128)}) custom-call(s32[1]{0:T(128)S(6)} %copy.73.len_ref, bf16[1024,768]{1,0:T(8,128)(2,1)} %get-tuple-element.103.q_ref, ...), custom_call_target="tpu_custom_call" | custom-call | tf_op jit(solution)/shard_map/pallas_call | solution.py:386
  316.1 8.0 %add_convert_fusion = (bf16[4,2,96,2048]{3,2,1,0:T(8,128)(2,1)}, bf16[4,2,96,2048]{3,2,1,0:T(8,128)(2,1)}) fusion(bf16[8,2,96,2048]{3,2,1,0:T(8,128)(2,1)} %collective-permute-done.14, bf16[8,2,96,2048]{3,2,1,0:T(8,128)(2,1)} %get-tuple-element.128), kind=kLoop, calls=%fused_computation.7 | loop fusion | flops 12582912 | bytes 18874368 | tf_op jit(solution)/shard_map/convert_element_type | solution.py:135
  329.8 4.9 add_convert_fusion.3
  357.9 19.9 %shard_map.228 = (bf16[4,2,96,1536]{3,2,1,0:T(8,128)(2,1)}, bf16[4,2,96,1536]{3,2,1,0:T(8,128)(2,1)}, bf16[4,96,1536]{2,1,0:T(8,128)(2,1)}, bf16[4,96,1536]{2,1,0:T(8,128)(2,1)}, bf16[3,1024,768]{2,1,0:T(8,128)(2,1)}) custom-call(s32[2]{0:T(128)} %pad_add_fusion.1.id_ref, f32[3,1024,512]{2,1,0:T(8,128)} %get-tuple-element.118.da_ref, ...), custom_call_target="tpu_custom_call" | custom-call | tf_op jit(solution)/shard_map/pallas_call | solution.py:641
  379.0 11.4 %collective-permute-done.19 = bf16[8,96,768]{2,1,0:T(8,128)(2,1)} collective-permute-done((bf16[8,96,768]{2,1,0:T(8,128)(2,1)}, bf16[8,96,768]{2,1,0:T(8,128)(2,1)}, u32[]{:S(2)}, u32[]{:S(2)}) %collective-permute-start.19) | collective-permute-done | bytes 1179680 | tf_op jit(solution)/shard_map/ppermute | solution.py:104
  399.0 4.9 add_convert_fusion.2
  407.7 13.7 %shard_map.229 = (f32[512,1536]{1,0:T(8,128)}, bf16[512,1536]{1,0:T(8,128)(2,1)}) custom-call(s32[2]{0:T(128)} %pad_add_fusion.1.id_ref, bf16[3,1024,768]{2,1,0:T(8,128)(2,1)} %get-tuple-element.137.g_ref, bf16[3,768,1536]{2,1,0:T(8,128)(2,1)} %bitcast.148, bf16[3,768,768]{2,1,0:T(8,128)(2,1)} %collective-permute-done.2.got_ref), custom_call_target="tpu_custom_call" | custom-call | tf_op jit(solution)/shard_map/pallas_call | solution.py:688
  435.9 14.7 %shard_map.230 = bf16[256,2048]{1,0:T(8,128)(2,1)} custom-call(bf16[2,256,1536]{2,1,0:T(8,128)(2,1)} %pad_maximum_fusion.1.g_ref, bf16[2048,2,1536]{2,1,0:T(2,128)(2,1)} %w_ref.5), custom_call_target="tpu_custom_call" | custom-call | tf_op jit(solution)/shard_map/pallas_call | solution.py:447
  450.7 17.3 %collective-permute-done.30 = bf16[2,96,768]{2,1,0:T(8,128)(2,1)} collective-permute-done((bf16[2,96,768]{2,1,0:T(8,128)(2,1)}, bf16[2,96,768]{2,1,0:T(8,128)(2,1)}, u32[]{:S(2)}, u32[]{:S(2)}) %collective-permute-start.30) | collective-permute-done | bytes 294944 | tf_op jit(solution)/shard_map/ppermute | solution.py:104
  486.4 10.7 %collective-permute-done.46 = bf16[1,96,768]{2,1,0:T(8,128)(2,1)S(1)} collective-permute-done((bf16[1,96,768]{2,1,0:T(8,128)(2,1)S(1)}, bf16[1,96,768]{2,1,0:T(8,128)(2,1)S(1)}, u32[]{:S(2)}, u32[]{:S(2)}) %collective-permute-start.46) | collective-permute-done | bytes 147488 | tf_op jit(solution)/shard_map/ppermute | solution.py:104
  498.8 5.7 collective-permute-done.48
  515.7 5.2 fusion.12
  524.8 33.0 %collective-permute-done.47 = bf16[1,2,96,2048]{3,2,1,0:T(8,128)(2,1)} collective-permute-done((bf16[1,2,96,2048]{3,2,1,0:T(8,128)(2,1)}, bf16[1,2,96,2048]{3,2,1,0:T(8,128)(2,1)}, u32[]{:S(2)}, u32[]{:S(2)}) %collective-permute-start.47) | collective-permute-done | bytes 786464 | tf_op jit(solution)/shard_map/ppermute | solution.py:104
  576.3 10.4 %collective-permute-done.40 = f32[100,128]{1,0:T(8,128)S(1)} collective-permute-done((f32[100,128]{1,0:T(8,128)S(1)}, f32[100,128]{1,0:T(8,128)S(1)}, u32[]{:S(2)}, u32[]{:S(2)}) %collective-permute-start.40) | collective-permute-done | bytes 51232 | tf_op jit(solution)/shard_map/ppermute | solution.py:104
  599.3 8.7 %fusion = f32[2048,2,96]{0,2,1:T(8,128)} fusion(bf16[2,96,4096]{2,1,0:T(8,128)(2,1)S(1)} %bitcast.160, bf16[4096,2048]{1,0:T(8,128)(2,1)} %all-gather.2.cloned.1.call-done), kind=kOutput, calls=%fused_computation.3 | convolution fusion | flops 3221225472 | bytes 19922944 | tf_op jit(solution)/shard_map/dot_general | solution.py:25
  608.1 11.6 %collective-permute-done.45 = bf16[3,96,768]{2,1,0:T(8,128)(2,1)S(1)} collective-permute-done((bf16[3,96,768]{2,1,0:T(8,128)(2,1)S(1)}, bf16[3,96,768]{2,1,0:T(8,128)(2,1)S(1)}, u32[]{:S(2)}, u32[]{:S(2)}) %collective-permute-start.45) | collective-permute-done | bytes 442400 | tf_op jit(solution)/shard_map/ppermute | solution.py:104
  (371 shorter events, 188.7 us)
Async XLA Ops:
  7.2 206.3 %all-gather.2.cloned.1.call-start = ((), (), s32[]{:S(2)}) async-start(), calls=%async_computation | async-start | bytes 17825792 | tf_op jit(solution)/shard_map/all_gather | solution.py:798
  12.8 41.1 %collective-permute-start.1 = (bf16[512,1536]{1,0:T(8,128)(2,1)S(1)}, bf16[512,1536]{1,0:T(8,128)(2,1)}, u32[]{:S(2)}, u32[]{:S(2)}) collective-permute-start(bf16[512,1536]{1,0:T(8,128)(2,1)S(1)} %bitcast.150), channel_id=1, source_target_pairs={{0,1},{1,0},{2,3},{3,2},{4,5},{5,4},{6,7},{7,6},{8,9},{9,8},{10,11... | collective-permute-start | bytes 4718600 | tf_op jit(solution)/shard_map/ppermute | solution.py:30
  17.2 36.7 %collective-permute-start.2 = (bf16[3,768,768]{2,1,0:T(8,128)(2,1)}, bf16[3,768,768]{2,1,0:T(8,128)(2,1)}, u32[]{:S(2)}, u32[]{:S(2)}) collective-permute-start(bf16[3,768,768]{2,1,0:T(8,128)(2,1)} %dynamic-slice_bitcast_fusion), channel_id=1, source_target_pairs={{0,1},{1,0},{2,3},{3,2},{4,5},{5,4},{6,7},{7,6},{8,9},{9,8},{10,11... | collective-permute-start | bytes 10616840 | tf_op jit(solution)/shard_map/ppermute | solution.py:30
  22.7 26.5 %collective-permute-start = (f32[4,1536]{1,0:T(4,128)S(1)}, f32[4,1536]{1,0:T(4,128)S(1)}, u32[]{:S(2)}, u32[]{:S(2)}) collective-permute-start(f32[4,1536]{1,0:T(4,128)S(1)} %bitcast.175), channel_id=1, source_target_pairs={{0,1},{1,0},{2,3},{3,2},{4,5},{5,4},{6,7},{7,6},{8,9},{9,8},{10,11... | collective-permute-start | bytes 73736 | tf_op jit(solution)/shard_map/ppermute | solution.py:30
  211.0 78.8 %collective-permute-start.14 = (bf16[8,2,96,2048]{3,2,1,0:T(8,128)(2,1)}, bf16[8,2,96,2048]{3,2,1,0:T(8,128)(2,1)}, u32[]{:S(2)}, u32[]{:S(2)}) collective-permute-start(bf16[8,2,96,2048]{3,2,1,0:T(8,128)(2,1)} %get-tuple-element.120), channel_id=1, source_target_pairs={{0,2},{1,5},{2,0},{3,7},{4,6},{5,1},{6,4},{7,3},{8,10},{9,13},{10,... | collective-permute-start | bytes 18874376 | tf_op jit(solution)/shard_map/ppermute | solution.py:104
  214.0 75.7 %collective-permute-start.15 = (bf16[8,96,2048]{2,1,0:T(8,128)(2,1)}, bf16[8,96,2048]{2,1,0:T(8,128)(2,1)}, u32[]{:S(2)}, u32[]{:S(2)}) collective-permute-start(bf16[8,96,2048]{2,1,0:T(8,128)(2,1)} %get-tuple-element.121), channel_id=1, source_target_pairs={{0,8},{1,9},{2,10},{3,11},{4,12},{5,13},{6,14},{7,15},{8,0},{9,1},... | collective-permute-start | bytes 9437192 | tf_op jit(solution)/shard_map/ppermute | solution.py:104
  324.1 70.5 %collective-permute-start.17 = (bf16[4,2,96,2048]{3,2,1,0:T(8,128)(2,1)}, bf16[4,2,96,2048]{3,2,1,0:T(8,128)(2,1)}, u32[]{:S(2)}, u32[]{:S(2)}) collective-permute-start(bf16[4,2,96,2048]{3,2,1,0:T(8,128)(2,1)} %get-tuple-element.228), channel_id=1, source_target_pairs={{0,4},{1,3},{2,6},{3,1},{4,0},{5,7},{6,2},{7,5},{8,12},{9,11},{10,... | collective-permute-start | bytes 9437192 | tf_op jit(solution)/shard_map/ppermute | solution.py:104
  334.8 59.9 %collective-permute-start.18 = (bf16[4,96,2048]{2,1,0:T(8,128)(2,1)}, bf16[4,96,2048]{2,1,0:T(8,128)(2,1)}, u32[]{:S(2)}, u32[]{:S(2)}) collective-permute-start(bf16[4,96,2048]{2,1,0:T(8,128)(2,1)} %get-tuple-element.232), channel_id=1, source_target_pairs={{0,2},{1,5},{2,0},{3,7},{4,6},{5,1},{6,4},{7,3},{8,10},{9,13},{10,... | collective-permute-start | bytes 4718600 | tf_op jit(solution)/shard_map/ppermute | solution.py:104
  335.7 54.7 %collective-permute-start.19 = (bf16[8,96,768]{2,1,0:T(8,128)(2,1)}, bf16[8,96,768]{2,1,0:T(8,128)(2,1)}, u32[]{:S(2)}, u32[]{:S(2)}) collective-permute-start(bf16[8,96,768]{2,1,0:T(8,128)(2,1)} %get-tuple-element.132), channel_id=1, source_target_pairs={{0,2},{1,5},{2,0},{3,7},{4,6},{5,1},{6,4},{7,3},{8,10},{9,13},{10,... | collective-permute-start | bytes 3538952 | tf_op jit(solution)/shard_map/ppermute | solution.py:104
  355.5 39.1 %collective-permute-start.22 = (bf16[2,2,2,2,128,96]{4,5,3,2,1,0:T(8,128)(2,1)}, bf16[2,2,2,2,128,96]{4,5,3,2,1,0:T(8,128)(2,1)}, u32[]{:S(2)}, u32[]{:S(2)}) collective-permute-start(bf16[2,2,2,2,128,96]{4,5,3,2,1,0:T(8,128)(2,1)} %get-tuple-element.259), channel_id=1, source_target_pairs={{0,2},{1,5},{2,0},{3,7},{4,6},{5,1},{6,4},{7,3},{8,10},{9,13},{10,... | collective-permute-start | bytes 1179656 | tf_op jit(solution)/shard_map/ppermute | solution.py:104
  377.8 72.8 %collective-permute-start.28 = (bf16[4,2,96,1536]{3,2,1,0:T(8,128)(2,1)}, bf16[4,2,96,1536]{3,2,1,0:T(8,128)(2,1)}, u32[]{:S(2)}, u32[]{:S(2)}) collective-permute-start(bf16[4,2,96,1536]{3,2,1,0:T(8,128)(2,1)} %get-tuple-element.148), channel_id=1, source_target_pairs={{0,2},{1,5},{2,0},{3,7},{4,6},{5,1},{6,4},{7,3},{8,10},{9,13},{10,... | collective-permute-start | bytes 7077896 | tf_op jit(solution)/shard_map/ppermute | solution.py:104
  390.4 40.9 %collective-permute-start.29 = (bf16[4,96,1536]{2,1,0:T(8,128)(2,1)}, bf16[4,96,1536]{2,1,0:T(8,128)(2,1)}, u32[]{:S(2)}, u32[]{:S(2)}) collective-permute-start(bf16[4,96,1536]{2,1,0:T(8,128)(2,1)} %get-tuple-element.149), channel_id=1, source_target_pairs={{0,8},{1,9},{2,10},{3,11},{4,12},{5,13},{6,14},{7,15},{8,0},{9,1},... | collective-permute-start | bytes 3538952 | tf_op jit(solution)/shard_map/ppermute | solution.py:104
  397.5 29.1 %collective-permute-start.23 = (bf16[4,96,768]{2,1,0:T(8,128)(2,1)}, bf16[4,96,768]{2,1,0:T(8,128)(2,1)}, u32[]{:S(2)}, u32[]{:S(2)}) collective-permute-start(bf16[4,96,768]{2,1,0:T(8,128)(2,1)} %get-tuple-element.244), channel_id=1, source_target_pairs={{0,4},{1,3},{2,6},{3,1},{4,0},{5,7},{6,2},{7,5},{8,12},{9,11},{10,... | collective-permute-start | bytes 1769480 | tf_op jit(solution)/shard_map/ppermute | solution.py:104
  403.9 64.1 %collective-permute-start.26 = (bf16[2,2,96,2048]{3,2,1,0:T(8,128)(2,1)}, bf16[2,2,96,2048]{3,2,1,0:T(8,128)(2,1)}, u32[]{:S(2)}, u32[]{:S(2)}) collective-permute-start(bf16[2,2,96,2048]{3,2,1,0:T(8,128)(2,1)} %get-tuple-element.230), channel_id=1, source_target_pairs={{0,8},{1,9},{2,10},{3,11},{4,12},{5,13},{6,14},{7,15},{8,0},{9,1},... | collective-permute-start | bytes 4718600 | tf_op jit(solution)/shard_map/ppermute | solution.py:104
  425.1 25.6 %collective-permute-start.27 = (bf16[2,96,2048]{2,1,0:T(8,128)(2,1)}, bf16[2,96,2048]{2,1,0:T(8,128)(2,1)}, u32[]{:S(2)}, u32[]{:S(2)}) collective-permute-start(bf16[2,96,2048]{2,1,0:T(8,128)(2,1)} %get-tuple-element.240), channel_id=1, source_target_pairs={{0,4},{1,3},{2,6},{3,1},{4,0},{5,7},{6,2},{7,5},{8,12},{9,11},{10,... | collective-permute-start | bytes 2359304 | tf_op jit(solution)/shard_map/ppermute | solution.py:104
  428.7 39.3 %collective-permute-start.31 = (bf16[2,2,2,2,128,96]{4,5,3,2,1,0:T(8,128)(2,1)}, bf16[2,2,2,2,128,96]{4,5,3,2,1,0:T(8,128)(2,1)}, u32[]{:S(2)}, u32[]{:S(2)}) collective-permute-start(bf16[2,2,2,2,128,96]{4,5,3,2,1,0:T(8,128)(2,1)} %get-tuple-element.257), channel_id=1, source_target_pairs={{0,8},{1,9},{2,10},{3,11},{4,12},{5,13},{6,14},{7,15},{8,0},{9,1},... | collective-permute-start | bytes 1179656 | tf_op jit(solution)/shard_map/ppermute | solution.py:104
  431.3 36.7 %collective-permute-start.30 = (bf16[2,96,768]{2,1,0:T(8,128)(2,1)}, bf16[2,96,768]{2,1,0:T(8,128)(2,1)}, u32[]{:S(2)}, u32[]{:S(2)}) collective-permute-start(bf16[2,96,768]{2,1,0:T(8,128)(2,1)} %get-tuple-element.255), channel_id=1, source_target_pairs={{0,8},{1,9},{2,10},{3,11},{4,12},{5,13},{6,14},{7,15},{8,0},{9,1},... | collective-permute-start | bytes 884744 | tf_op jit(solution)/shard_map/ppermute | solution.py:104
  450.6 60.3 %collective-permute-start.25 = (bf16[512,1536]{1,0:T(8,128)(2,1)}, bf16[512,1536]{1,0:T(8,128)(2,1)S(1)}, u32[]{:S(2)}, u32[]{:S(2)}) collective-permute-start(bf16[512,1536]{1,0:T(8,128)(2,1)} %get-tuple-element.144), channel_id=1, source_target_pairs={{0,1},{1,0},{2,3},{3,2},{4,5},{5,4},{6,7},{7,6},{8,9},{9,8},{10,11... | collective-permute-start | bytes 4718600 | tf_op jit(solution)/shard_map/ppermute | solution.py:54
  472.5 89.7 %collective-permute-start.32 = (bf16[2,2,96,1536]{3,2,1,0:T(8,128)(2,1)}, bf16[2,2,96,1536]{3,2,1,0:T(8,128)(2,1)}, u32[]{:S(2)}, u32[]{:S(2)}) collective-permute-start(bf16[2,2,96,1536]{3,2,1,0:T(8,128)(2,1)} %get-tuple-element.234), channel_id=1, source_target_pairs={{0,4},{1,3},{2,6},{3,1},{4,0},{5,7},{6,2},{7,5},{8,12},{9,11},{10,... | collective-permute-start | bytes 3538952 | tf_op jit(solution)/shard_map/ppermute | solution.py:104
  476.7 85.5 %collective-permute-start.33 = (bf16[2,96,1536]{2,1,0:T(8,128)(2,1)}, bf16[2,96,1536]{2,1,0:T(8,128)(2,1)}, u32[]{:S(2)}, u32[]{:S(2)}) collective-permute-start(bf16[2,96,1536]{2,1,0:T(8,128)(2,1)} %get-tuple-element.242), channel_id=1, source_target_pairs={{0,2},{1,5},{2,0},{3,7},{4,6},{5,1},{6,4},{7,3},{8,10},{9,13},{10,... | collective-permute-start | bytes 1769480 | tf_op jit(solution)/shard_map/ppermute | solution.py:104
  504.5 57.8 %collective-permute-start.36 = (bf16[2,2,2,2,128,96]{4,5,3,2,1,0:T(8,128)(2,1)}, bf16[2,2,2,2,128,96]{4,5,3,2,1,0:T(8,128)(2,1)}, u32[]{:S(2)}, u32[]{:S(2)}) collective-permute-start(bf16[2,2,2,2,128,96]{4,5,3,2,1,0:T(8,128)(2,1)} %fusion.37), channel_id=1, source_target_pairs={{0,16},{1,17},{2,18},{3,19},{4,20},{5,21},{6,22},{7,23},{8,24},{9,... | collective-permute-start | bytes 1179656 | tf_op jit(solution)/shard_map/ppermute | solution.py:104
  506.7 51.2 %collective-permute-start.47 = (bf16[1,2,96,2048]{3,2,1,0:T(8,128)(2,1)}, bf16[1,2,96,2048]{3,2,1,0:T(8,128)(2,1)}, u32[]{:S(2)}, u32[]{:S(2)}) collective-permute-start(bf16[1,2,96,2048]{3,2,1,0:T(8,128)(2,1)} %add_convert_fusion.10), channel_id=1, source_target_pairs={{0,16},{1,17},{2,18},{3,19},{4,20},{5,21},{6,22},{7,23},{8,24},{9,... | collective-permute-start | bytes 2359304 | tf_op jit(solution)/shard_map/ppermute | solution.py:104
  523.2 39.0 %collective-permute-start.35 = (f32[100,128]{1,0:T(8,128)S(1)}, f32[100,128]{1,0:T(8,128)S(1)}, u32[]{:S(2)}, u32[]{:S(2)}) collective-permute-start(f32[100,128]{1,0:T(8,128)S(1)} %pad_maximum_fusion.4), channel_id=1, source_target_pairs={{0,2},{1,5},{2,0},{3,7},{4,6},{5,1},{6,4},{7,3},{8,10},{9,13},{10,... | collective-permute-start | bytes 153608 | tf_op jit(solution)/shard_map/ppermute | solution.py:104
  566.6 26.0 %collective-permute-start.41 = (bf16[16,2,128,96]{2,3,1,0:T(8,128)(2,1)S(1)}, bf16[16,2,128,96]{2,3,1,0:T(8,128)(2,1)}, u32[]{:S(2)}, u32[]{:S(2)}) collective-permute-start(bf16[16,2,128,96]{2,3,1,0:T(8,128)(2,1)S(1)} %broadcast_select_fusion), channel_id=1, source_target_pairs={{0,1},{1,0},{2,3},{3,2},{4,5},{5,4},{6,7},{7,6},{8,9},{9,8},{10,11... | collective-permute-start | bytes 2359304 | tf_op jit(solution)/shard_map/ppermute | solution.py:30
  (86 other events, 937.6 us)
Sparse Core Ops, SparseCore 0:
  12.9 194.2 all-gather.1

commit v6 on v5

--- a/solution.py
+++ b/solution.py
@@ -601,7 +601,7 @@
 
 
 def project_grad_kernel(
-    orders, id_ref, da_ref, db_ref, pre_ref, stat_ref, gain_ref, first_ref,
+    orders, id_ref, da_ref, db_ref, pre_ref, stat_ref, gain_ref, first_ref, okeep_ref, osend_ref,
     keep_ref, send_ref, vkeep_ref, vsend_ref, g_ref, gt, tmp,
 ):
     order, late = orders
@@ -620,23 +620,29 @@
     put_relative(gt, tmp, id_ref[0] % count, id_ref[1], count)
     wide = dot(gt[...], first_ref[...]).astype(BF16)
 
+    depth = first_ref.shape[1]
+
     @pl.when(j < 2)
     def _():
-        put_halves(keep_ref, send_ref, wide, count, order, j)
+        put_halves(keep_ref.at[..., :depth], send_ref.at[..., :depth], wide, count, order, j)
+        for src, dst in ((okeep_ref, keep_ref), (osend_ref, send_ref)):
+            for p in range(dst.shape[0]):
+                dst[p, j, :, depth:] = src[2 * p + j]
 
     @pl.when(j == 2)
     def _():
         put_halves(vkeep_ref, vsend_ref, wide, count, late)
 
 
-def project_grad(ids, da, db, pre, stats, gain, first, dp, orders):
+def project_grad(ids, da, db, pre, stats, gain, first, okeep, osend, dp, orders):
     _, tokens, own = pre.shape
     depth = first.shape[1]
     share = depth // dp
     const = lambda j: (0, 0)
     block = lambda j: (j, 0, 0)
     once = functools.partial(pl.BlockSpec, pipeline_mode=pl.Buffered(1))
-    half = once((dp // 4, 2, share, depth), lambda j: (0, 0, 0, 0))
+    half = once((dp // 4, 2, share, depth + own), lambda j: (0, 0, 0, 0))
+    whole = once(okeep.shape, lambda j: (0, 0, 0))
     vhalf = once((dp // 4, share, depth), lambda j: (0, 0, 0))
     return pl.pallas_call(
         functools.partial(project_grad_kernel, orders),
@@ -647,14 +653,14 @@
             pl.BlockSpec((1, tokens, own), block),
             pl.BlockSpec((8, tokens), const),
             pl.BlockSpec((1, 1, own), block),
-            once((tokens, depth), const),
+            once((tokens, depth), const), whole, whole,
         ],
         out_specs=[half, half, vhalf, vhalf, pl.BlockSpec((1, tokens, own), block)],
-        out_shape=[sds((dp // 4, 2, share, depth), BF16)] * 2
+        out_shape=[sds((dp // 4, 2, share, depth + own), BF16)] * 2
         + [sds((dp // 4, share, depth), BF16)] * 2
         + [sds((3, tokens, own), BF16)],
         scratch_shapes=[pltpu.VMEM((own, tokens), BF16), pltpu.VMEM((own, tokens), BF16)],
-    )(ids, da, db, pre, stats, gain, first)
+    )(ids, da, db, pre, stats, gain, first, okeep, osend)
 
 
 def project_back_kernel(id_ref, g_ref, w_ref, got_ref, own_ref, peer_ref, acc):
@@ -770,7 +776,7 @@
     dpn, me = lax.axis_size("dp"), lax.axis_index("dp")
     bits = list(range(dp_bits()))
     low_bits = bits[:-1]
-    late = bits[2:3] + bits[:2] + bits[3:]
+    late = bits[2:] + bits[:2]
     own_d = D // n
     local = hidden_in.shape[1]
     tokens = n * local
@@ -864,8 +870,7 @@
     )
     d_gate_attn = jnp.sum(grad_after * attn_branch, axis=0) * (1.0 - gate_attn[0] * gate_attn[0])
     grad_attn = (gate_attn * grad_after).astype(BF16)
-    grad_mixed, *halves = out_back(ids, gather_rot(grad_attn), w_out, mixed, dpn, bits)
-    out_chain = Halving(bits, *halves)
+    grad_mixed, *out_halves = out_back(ids, gather_rot(grad_attn), w_out, mixed, dpn, bits)
     blocks = pre_p.shape[2] // width
     cut = max(1, 2 * blocks // 3)
     grad_mixed = pad_cols(grad_mixed, width)
@@ -876,38 +881,23 @@
     part_b = attn_backward(
         cut, blocks - cut, caption_lengths, q, k, v, tkp, tvp, grad_mixed, *inputs
     )
-    dtk, dtv, gain_q, gain_k, gate_g = (
-        jnp.concatenate([part_a[i], part_b[i]], axis=1)[:, :own_d] for i in (1, 2, 4, 5, 6)
-    )
     means = row_sum(part_a[3] + part_b[3])[:2] / D
-    gate_total = jnp.sum(gate_g[0].reshape(HEADS // n, HD), axis=1) * (
-        1.0 - head_tanh * head_tanh
-    )
-    text_hat = dtk * gain_own[4]
-    gain_text = jnp.sum(dtk * normed_t, axis=0, keepdims=True)
-    mean_t = pair_sum(jnp.sum(text_hat * normed_t, -1, keepdims=True)) / D
-
-    grad_tk = (inv_t * (text_hat - normed_t * mean_t)).astype(BF16)
-    text_pair = jnp.stack([grad_tk, dtv.astype(BF16)])
-    pair_all = jnp.concatenate(natural(gather_rot(text_pair)), axis=-1)
-    outgoing = block_of(pair_all, f, 1).reshape(2, TEXT // n, dpn, share).transpose(2, 0, 1, 3)
-    pair_chain = Exchange(relative(outgoing))
 
     ones, zeros = jnp.ones((1, tokens), F32), jnp.zeros((1, tokens), F32)
     if paired:
         stats = jnp.concatenate([inverse[:2], ones, means, zeros, zeros, zeros], axis=0)
         gain3 = jnp.stack([gain_own[2:3], gain_own[3:4], jnp.ones_like(gain_own[2:3])])
-        *halves, grads = project_grad(
-            ids, part_a[0], part_b[0], pre, stats, gain3, first_all, dpn,
-            (low_bits, low_bits[2:] + low_bits[:2]),
+        low_late = low_bits[2:] + low_bits[:2]
+        keep, send, v_keep, v_send, grads = project_grad(
+            ids, part_a[0], part_b[0], pre, stats, gain3, first_all, *out_halves, dpn,
+            (low_bits, low_late),
         )
-        qkv_chains = [
-            Halving(low_bits, *halves[:2]), Halving(low_bits[2:] + low_bits[:2], *halves[2:]),
-        ]
-        grads = advance([wide_chain, down_chain, out_chain, pair_chain], grads)
+        part_a, part_b, grads = advance([wide_chain], (part_a[1:], part_b[1:], grads))
+        qkv_chains = [Halving(low_bits, keep, send), Halving(low_late, v_keep, v_send)]
         parts = project_back(ids, grads, w_flat, w_parts[1])
     else:
         d = jnp.concatenate([part_a[0], part_b[0]], axis=2)[:, :, :own_d]
+        part_a, part_b = part_a[1:], part_b[1:]
         inv, mean = inverse[:2, :, None], means[:, :, None]
         hat = d[:2] * gain_own[2:4][:, None] - pre[:2] * inv * mean
         grads = [(inv[0] * hat[0]).astype(BF16), (inv[1] * hat[1]).astype(BF16), d[2].astype(BF16)]
@@ -915,16 +905,33 @@
         wide = [jnp.concatenate(natural(exchange_rot(w_, 1)), axis=0) for w_ in wide]
         wide = relative(jnp.stack([w_.reshape(dpn, share, own_d) for w_ in wide], axis=1))
         wide = jnp.stack([wide[p] for p in sorted(range(dpn), key=lambda p: place_of(p, bits))])
-        qkv_chains = [Halving(bits, wide[: dpn // 2], wide[dpn // 2 :])]
+        qkv_chains = [
+            Halving(bits, wide[: dpn // 2], wide[dpn // 2 :]), Halving(bits, *out_halves),
+        ]
         parts = [
             sum(dot(rows(g, r), w_heads[j], 1, 1) for j, g in enumerate(grads)) for r in range(n)
         ]
         parts = [parts[0]] + [p.astype(BF16) for p in parts[1:]]
-    parts = advance([out_chain, pair_chain], parts)
     grad_first = scatter_rot(parts)
 
+    dtk, dtv, gain_q, gain_k, gate_g = (
+        jnp.concatenate([part_a[i], part_b[i]], axis=1)[:, :own_d] for i in (0, 1, 3, 4, 5)
+    )
+    gate_total = jnp.sum(gate_g[0].reshape(HEADS // n, HD), axis=1) * (
+        1.0 - head_tanh * head_tanh
+    )
+    text_hat = dtk * gain_own[4]
+    gain_text = jnp.sum(dtk * normed_t, axis=0, keepdims=True)
+    mean_t = pair_sum(jnp.sum(text_hat * normed_t, -1, keepdims=True)) / D
+    grad_tk = (inv_t * (text_hat - normed_t * mean_t)).astype(BF16)
+    text_pair = jnp.stack([grad_tk, dtv.astype(BF16)])
+    pair_all = jnp.concatenate(natural(gather_rot(text_pair)), axis=-1)
+    outgoing = block_of(pair_all, f, 1).reshape(2, TEXT // n, dpn, share).transpose(2, 0, 1, 3)
+    pair_chain = Exchange(relative(outgoing))
     text_in = text_bwd(pair_all, w_text)
-    text_in = advance([wide_chain, down_chain, *qkv_chains, out_chain, pair_chain], text_in)
+    text_in, grad_first = advance(
+        [*qkv_chains, wide_chain, pair_chain], (text_in, grad_first)
+    )
     text_in = jnp.concatenate(natural(exchange_rot(text_in, 0)), axis=1)
 
     inverse_one = inverse_rms(x_own)
@@ -947,18 +954,34 @@
     mods = jnp.pad(mods, ((0, 0), (0, 3), (0, -share % 128)))
     small_chain = Small(relative(mods), small.reshape(-1, 128))
 
-    def rest(chain):
-        while chain.got is not None:
-            chain.step()
-
-    grad_input = advance([*qkv_chains, small_chain, pair_chain], grad_input)
-    rest(pair_chain)
+    grad_input = advance([*qkv_chains, small_chain, pair_chain, down_chain], grad_input)
+    advance([small_chain, pair_chain], ())
+    advance([*qkv_chains, small_chain, pair_chain, down_chain], ())
+    if paired:
+        last, v_last = (c.last[0].astype(BF16) for c in qkv_chains)
+        own_side = f == (me >> low_bits[-1] + 1)
+        side = jnp.concatenate([last[:, :, :D], v_last[None]])
+        mine, got = exchange_rot(side, 2)
+        keep = jnp.concatenate([jnp.where(own_side, mine, got), last[:1, :, D:]])
+        send = jnp.concatenate([jnp.where(own_side, got, mine), last[1:, :, D:]])
+        final_chain = Halving(bits[-1:], keep, send)
+    else:
+        final_chain = qkv_chains[0]
     pair_cols = absolute(pair_chain.cur.reshape(pair_chain.shape))
     pair_cols = jnp.concatenate(natural(gather_rot(pair_cols)), axis=2)
     pair_cols = pair_cols.transpose(0, 2, 1, 3).reshape(dpn * TEXT, 2 * share)
     text_grad = dot(pair_cols, text_all, 0, 0).reshape(2, share, TW // n)
-    for chain in (*qkv_chains, small_chain, out_chain, wide_chain, down_chain):
+
+    def rest(chain):
+        while chain.got is not None:
+            chain.step()
+
+    for chain in (pair_chain, small_chain, wide_chain, down_chain, *qkv_chains, final_chain):
         rest(chain)
+    if paired:
+        qkv_grad, out_grad = final_chain.last[:3], final_chain.last[3]
+    else:
+        qkv_grad, out_grad = qkv_chains[0].last[0], qkv_chains[1].last[0]
     total = small_chain.total.reshape(6, own_d)
     mods = small_chain.cur.reshape(small_chain.shape)
     times = time_embed(mods[:, 4, 0])
@@ -967,13 +990,6 @@
         mods[:, :4, :share].reshape(dpn, 4 * share), times, (((0,), (0,)), ((), ())),
         precision=lax.Precision.HIGHEST,
     ).reshape(4, share, own_te)
-    qkv_grad = qkv_chains[0].last[0]
-    if paired:
-        qkv_grad = jnp.concatenate([qkv_grad, qkv_chains[1].last])
-        own_side = f == (me >> low_bits[-1] + 1)
-        mine, got = exchange_rot(qkv_grad.astype(BF16), 2)
-        keep, send = jnp.where(own_side, mine, got), jnp.where(own_side, got, mine)
-        qkv_grad = keep.astype(F32) + dp_swap(send, bits[-1]).astype(F32)
     return (
         output[None],
         grad_input[None],
@@ -981,7 +997,7 @@
         ada_grad.transpose(2, 0, 1),
         text_grad.transpose(2, 0, 1),
         qkv_grad.transpose(2, 0, 1),
-        out_chain.last[0].T,
+        out_grad.T,
         total[:5],
         total[5, : HEADS // n],
         wide_chain.last[0].transpose(1, 0, 2),

time: 634 us -> 624 us (0.984)
  local copies, waits for them, and re-layouts: 37 us -> 51.1 us
  waiting for transfers between devices: 113 us -> 101 us
  other arithmetic: 118 us -> 109 us
    ppermute x27 -> x23, waiting for transfers between devices: 104 us -> 90.1 us  [dp_swap(): return lax.ppermute(value, ('dp', 'fsdp'), pairs)]
    ppermute x27 -> x23, starting transfers between devices: 34.9 us -> 29.9 us  [dp_swap(): return lax.ppermute(value, ('dp', 'fsdp'), pairs)]
    convert_element_type x8 -> x6, other arithmetic: 33.6 us -> 29.4 us  [step(): self.keep = add(slice(half)).astype(BF16)]
  transfers between devices with their start and end apart: 50 -> 46, of which waited for: 16 -> 15; matrix products, arithmetic and copies ran while one was open for 27% -> 26% of each run, Pallas kernels for 41% -> 45%
where the time goes in v6:
time: 624 us; the launch traced here: 618 us
  Pallas kernels  281 us (45%)
  other arithmetic  109 us (17%)
  waiting for transfers between devices  101 us (16%)
  local copies, waits for them, and re-layouts  51.1 us (8%)
  starting transfers between devices  35 us (6%)
  matrix products  22.9 us (4%)
  between operations  16.7 us (3%)
    pallas_call x1, Pallas kernels, ffn(): pl.pallas_call(functools.partial(ffn_kernel, orders), grid=(hid // bc,),...  90.3 us
    ppermute x23, waiting for transfers between devices, dp_swap(): return lax.ppermute(value, ('dp', 'fsdp'), pairs)  90.1 us
    pallas_call x2, Pallas kernels, attn_backward(): pl.pallas_call(attn_bwd_kernel, grid=(blocks,), in_specs=[scalar, col, co...  68.8 us
    pallas_call x1, Pallas kernels, attn_forward(): pl.pallas_call(attn_fwd_kernel, grid=(blocks,), in_specs=[scalar, three,...  32 us
    ppermute x23, starting transfers between devices, dp_swap(): return lax.ppermute(value, ('dp', 'fsdp'), pairs)  29.9 us
    convert_element_type x6, other arithmetic, step(): self.keep = add(slice(half)).astype(BF16)  29.4 us
    pallas_call x1, Pallas kernels, project_grad(): pl.pallas_call(functools.partial(project_grad_kernel, orders), grid=(3,),...  21 us
    pallas_call x1, Pallas kernels, text_fwd(): pl.pallas_call(text_fwd_kernel, grid=(depth // bk,), in_specs=[pl.BlockSp...  16.2 us
  transfers between devices with their start and end apart: 46, of which 15 were waited for; matrix products, arithmetic and copies ran while one was open for 26% of the time, Pallas kernels for 45%

profile of v6, /device:TPU:0, one launch (start us, length us, event | category | flops | bytes accessed | tf_op | source)
XLA Modules:
  0.0 618.1 jit_solution(13928142441905116964)
XLA Ops:
  12.8 4.0 dynamic-slice_bitcast_fusion
  17.9 4.7 fusion.2
  23.3 16.2 %shard_map.222 = f32[2,256,1536]{2,1,0:T(8,128)} custom-call(bf16[256,2048]{1,0:T(8,128)(2,1)} %pad_maximum_fusion.2.x_ref, bf16[2048,2,1536]{2,1,0:T(2,128)(2,1)} %w_ref.5), custom_call_target="tpu_custom_call" | custom-call | tf_op jit(solution)/shard_map/pallas_call | solution.py:428
  53.4 14.4 %shard_map.221 = (bf16[1024,1536]{1,0:T(8,128)(2,1)}, f32[3,1024,768]{2,1,0:T(8,128)}, f32[8,1024]{1,0:T(8,128)}) custom-call(s32[2]{0:T(128)} %pad_add_fusion.1.id_ref, bf16[512,1536]{1,0:T(8,128)(2,1)} %bitcast.149, bf16[512,1536]{1,0:T(8,128)(2,1)} %collective-permute-done.1.xp_ref, f32[1,1536]{1,0:T(1,128)} %get-tuple-element.288.front_ref, ...), custom_call_target="tpu_custom_call" | custom-call | tf_op jit(solution)/shard_map/pallas_call | solution.py:584
  70.6 32.0 %shard_map.223 = (bf16[1024,768]{1,0:T(8,128)(2,1)}, bf16[1024,768]{1,0:T(8,128)(2,1)}, bf16[1024,768]{1,0:T(8,128)(2,1)}, bf16[1024,768]{1,0:T(8,128)(2,1)}, f3...) custom-call(s32[1]{0:T(128)S(6)} %copy.73.len_ref, ...), custom_call_target="tpu_custom_call" | custom-call | tf_op jit(solution)/shard_map/pallas_call | solution.py:371
  120.8 90.3 %shard_map.224 = (bf16[8,2,96,2048]{3,2,1,0:T(8,128)(2,1)}, bf16[8,2,96,2048]{3,2,1,0:T(8,128)(2,1)}, bf16[8,96,2048]{2,1,0:T(8,128)(2,1)}, bf16[8,96,2048]{2,1,...) custom-call(s32[2]{0:T(128)} %pad_add_fusion.1.id_ref, ...), custom_call_target="tpu_custom_call" | custom-call | tf_op jit(solution)/shard_map/pallas_call | solution.py:527
  217.9 4.3 multiply_reduce_fusion
  222.2 5.9 fusion.7
  233.2 9.6 %shard_map.225 = (f32[1024,768]{1,0:T(8,128)}, bf16[8,96,768]{2,1,0:T(8,128)(2,1)}, bf16[8,96,768]{2,1,0:T(8,128)(2,1)}) custom-call(s32[2]{0:T(128)} %pad_add_fusion.1.id_ref, bf16[512,1536]{1,0:T(8,128)(2,1)} %copy-done.19, bf16[512,1536]{1,0:T(8,128)(2,1)} %collective-permute-done.13.refs_1_, bf16[768,1536]{1,0:T(8,128)(2,1)} %refs_2_.1, ...), custom_call_target="tpu_custom_call" | custom-call | tf_op jit(solution)/shard_map/pallas_call | solution.py:729
  242.8 44.5 %shard_map.226 = (f32[3,1024,512]{2,1,0:T(8,128)}, f32[256,512]{1,0:T(8,128)}, f32[256,512]{1,0:T(8,128)}, f32[8,1024]{1,0:T(8,128)}, f32[1,512]{1,0:T(1,128)}, /*index=5*/f32[1,512]{1,0:T(1,128)}, f32[1,512]{1,0:T(1,128)}) custom-call(s32[1]{0:T(128)S(6)} %copy.73.len_ref, bf16[1024,768]{1,0:T(8,128)(2,1)} %get-tuple-element.113.q_ref, ...), custom_call_target="tpu_custom_call" | custom-call | tf_op jit(solution)/shard_map/pallas_call | solution.py:386
  287.3 8.3 %add_convert_fusion = (bf16[4,2,96,2048]{3,2,1,0:T(8,128)(2,1)}, bf16[4,2,96,2048]{3,2,1,0:T(8,128)(2,1)}) fusion(bf16[8,2,96,2048]{3,2,1,0:T(8,128)(2,1)} %collective-permute-done.14, bf16[8,2,96,2048]{3,2,1,0:T(8,128)(2,1)} %get-tuple-element.150), kind=kLoop, calls=%fused_computation.7 | loop fusion | flops 12582912 | bytes 18874368 | tf_op jit(solution)/shard_map/convert_element_type | solution.py:135
  303.1 24.3 %shard_map.227 = (f32[3,1024,256]{2,1,0:T(8,128)}, f32[256,256]{1,0:T(8,128)}, f32[256,256]{1,0:T(8,128)}, f32[8,1024]{1,0:T(8,128)}, f32[1,256]{1,0:T(1,128)}, /*index=5*/f32[1,256]{1,0:T(1,128)}, f32[1,256]{1,0:T(1,128)}) custom-call(s32[1]{0:T(128)S(6)} %copy.73.len_ref, bf16[1024,768]{1,0:T(8,128)(2,1)} %get-tuple-element.113.q_ref, ...), custom_call_target="tpu_custom_call" | custom-call | tf_op jit(solution)/shard_map/pallas_call | solution.py:386
  328.2 6.2 %add_convert_fusion.5 = (bf16[4,96,2048]{2,1,0:T(8,128)(2,1)}, bf16[4,96,2048]{2,1,0:T(8,128)(2,1)}) fusion(bf16[8,96,2048]{2,1,0:T(8,128)(2,1)} %collective-permute-done.15, bf16[8,96,2048]{2,1,0:T(8,128)(2,1)} %get-tuple-element.174), kind=kLoop, calls=%fused_computation.30 | loop fusion | flops 6291456 | bytes 9437184 | tf_op jit(solution)/shard_map/convert_element_type | solution.py:135
  337.7 21.0 %shard_map.228 = (bf16[4,2,96,2304]{3,2,1,0:T(8,128)(2,1)}, bf16[4,2,96,2304]{3,2,1,0:T(8,128)(2,1)}, bf16[4,96,1536]{2,1,0:T(8,128)(2,1)}, bf16[4,96,1536]{2,1,0:T(8,128)(2,1)}, bf16[3,1024,768]{2,1,0:T(8,128)(2,1)}) custom-call(s32[2]{0:T(128)} %pad_add_fusion.1.id_ref, f32[3,1024,512]{2,1,0:T(8,128)} %get-tuple-element.144.da_ref, ...), custom_call_target="tpu_custom_call" | custom-call | tf_op jit(solution)/shard_map/pallas_call | solution.py:647
  364.2 13.7 %shard_map.230 = (f32[512,1536]{1,0:T(8,128)}, bf16[512,1536]{1,0:T(8,128)(2,1)}) custom-call(s32[2]{0:T(128)} %pad_add_fusion.1.id_ref, bf16[3,1024,768]{2,1,0:T(8,128)(2,1)} %get-tuple-element.156.g_ref, bf16[3,768,1536]{2,1,0:T(8,128)(2,1)} %bitcast.148, bf16[3,768,768]{2,1,0:T(8,128)(2,1)} %collective-permute-done.2.got_ref), custom_call_target="tpu_custom_call" | custom-call | tf_op jit(solution)/shard_map/pallas_call | solution.py:694
  385.3 4.9 add_convert_fusion.4
  402.3 14.7 %shard_map.229 = bf16[256,2048]{1,0:T(8,128)(2,1)} custom-call(bf16[2,256,1536]{2,1,0:T(8,128)(2,1)} %pad_maximum_fusion.1.g_ref, bf16[2048,2,1536]{2,1,0:T(2,128)(2,1)} %w_ref.5), custom_call_target="tpu_custom_call" | custom-call | tf_op jit(solution)/shard_map/pallas_call | solution.py:447
  425.0 4.2 collective-permute-done.24
  429.2 24.6 %collective-permute-done.23 = bf16[2,2,96,2048]{3,2,1,0:T(8,128)(2,1)} collective-permute-done((bf16[2,2,96,2048]{3,2,1,0:T(8,128)(2,1)}, bf16[2,2,96,2048]{3,2,1,0:T(8,128)(2,1)}, u32[]{:S(2)}, u32[]{:S(2)}) %collective-permute-start.23) | collective-permute-done | bytes 1572896 | tf_op jit(solution)/shard_map/ppermute | solution.py:104
  464.2 4.9 add_convert_fusion.2
  504.4 26.1 %collective-permute-done.33 = bf16[2,2,2,2,128,96]{4,5,3,2,1,0:T(8,128)(2,1)S(1)} collective-permute-done((bf16[2,2,2,2,128,96]{4,5,3,2,1,0:T(8,128)(2,1)S(1)}, bf16[2,2,2,2,128,96]{4,5,3,2,1,0:T(8,128)(2,1)S(1)}, u32[]{:S(2)}, u32[]{:S(2)}) %collective-permute-start.33) | collective-permute-done | bytes 393248 | tf_op jit(solution)/shard_map/ppermute | solution.py:104
  537.4 15.9 %collective-permute-done.36 = f32[100,128]{1,0:T(8,128)S(1)} collective-permute-done((f32[100,128]{1,0:T(8,128)S(1)}, f32[100,128]{1,0:T(8,128)S(1)}, u32[]{:S(2)}, u32[]{:S(2)}) %collective-permute-start.36) | collective-permute-done | bytes 51232 | tf_op jit(solution)/shard_map/ppermute | solution.py:104
  586.1 8.7 %fusion = f32[2048,2,96]{0,2,1:T(8,128)} fusion(bf16[2,96,4096]{2,1,0:T(8,128)(2,1)S(1)} %bitcast.159, bf16[4096,2048]{1,0:T(8,128)(2,1)} %all-gather.2.cloned.1.call-done), kind=kOutput, calls=%fused_computation.3 | convolution fusion | flops 3221225472 | bytes 19922944 | tf_op jit(solution)/shard_map/dot_general | solution.py:25
  594.9 14.3 %collective-permute-done.42 = bf16[4,96,768]{2,1,0:T(8,128)(2,1)S(1)} collective-permute-done((bf16[4,96,768]{2,1,0:T(8,128)(2,1)S(1)}, bf16[4,96,768]{2,1,0:T(8,128)(2,1)S(1)}, u32[]{:S(2)}, u32[]{:S(2)}) %collective-permute-start.42) | collective-permute-done | bytes 589856 | tf_op jit(solution)/shard_map/ppermute | solution.py:104
  (371 shorter events, 183.6 us)
Async XLA Ops:
  7.2 207.1 %all-gather.2.cloned.1.call-start = ((), (), s32[]{:S(2)}) async-start(), calls=%async_computation | async-start | bytes 17825792 | tf_op jit(solution)/shard_map/all_gather | solution.py:804
  16.8 36.6 %collective-permute-start.2 = (bf16[3,768,768]{2,1,0:T(8,128)(2,1)}, bf16[3,768,768]{2,1,0:T(8,128)(2,1)}, u32[]{:S(2)}, u32[]{:S(2)}) collective-permute-start(bf16[3,768,768]{2,1,0:T(8,128)(2,1)} %dynamic-slice_bitcast_fusion), channel_id=1, source_target_pairs={{0,1},{1,0},{2,3},{3,2},{4,5},{5,4},{6,7},{7,6},{8,9},{9,8},{10,11... | collective-permute-start | bytes 10616840 | tf_op jit(solution)/shard_map/ppermute | solution.py:30
  22.6 26.7 %collective-permute-start = (f32[4,1536]{1,0:T(4,128)S(1)}, f32[4,1536]{1,0:T(4,128)S(1)}, u32[]{:S(2)}, u32[]{:S(2)}) collective-permute-start(f32[4,1536]{1,0:T(4,128)S(1)} %bitcast.180), channel_id=1, source_target_pairs={{0,1},{1,0},{2,3},{3,2},{4,5},{5,4},{6,7},{7,6},{8,9},{9,8},{10,11... | collective-permute-start | bytes 73736 | tf_op jit(solution)/shard_map/ppermute | solution.py:30
  22.8 30.6 %collective-permute-start.1 = (bf16[512,1536]{1,0:T(8,128)(2,1)S(1)}, bf16[512,1536]{1,0:T(8,128)(2,1)}, u32[]{:S(2)}, u32[]{:S(2)}) collective-permute-start(bf16[512,1536]{1,0:T(8,128)(2,1)S(1)} %bitcast.150), channel_id=1, source_target_pairs={{0,1},{1,0},{2,3},{3,2},{4,5},{5,4},{6,7},{7,6},{8,9},{9,8},{10,11... | collective-permute-start | bytes 4718600 | tf_op jit(solution)/shard_map/ppermute | solution.py:30
  23.2 23.0 %collective-permute-start.4 = (s32[2,512]{1,0:T(2,128)S(1)}, s32[2,512]{1,0:T(2,128)S(1)}, u32[]{:S(2)}, u32[]{:S(2)}) collective-permute-start(s32[2,512]{1,0:T(2,128)S(1)} %bitcast.191), channel_id=1, source_target_pairs={{0,1},{1,0},{2,3},{3,2},{4,5},{5,4},{6,7},{7,6},{8,9},{9,8},{10,11... | collective-permute-start | bytes 12296 | tf_op jit(solution)/shard_map/ppermute | solution.py:30
  211.1 76.2 %collective-permute-start.14 = (bf16[8,2,96,2048]{3,2,1,0:T(8,128)(2,1)}, bf16[8,2,96,2048]{3,2,1,0:T(8,128)(2,1)}, u32[]{:S(2)}, u32[]{:S(2)}) collective-permute-start(bf16[8,2,96,2048]{3,2,1,0:T(8,128)(2,1)} %get-tuple-element.135), channel_id=1, source_target_pairs={{0,2},{1,5},{2,0},{3,7},{4,6},{5,1},{6,4},{7,3},{8,10},{9,13},{10,... | collective-permute-start | bytes 18874376 | tf_op jit(solution)/shard_map/ppermute | solution.py:104
  214.8 72.5 %collective-permute-start.15 = (bf16[8,96,2048]{2,1,0:T(8,128)(2,1)}, bf16[8,96,2048]{2,1,0:T(8,128)(2,1)}, u32[]{:S(2)}, u32[]{:S(2)}) collective-permute-start(bf16[8,96,2048]{2,1,0:T(8,128)(2,1)} %get-tuple-element.136), channel_id=1, source_target_pairs={{0,8},{1,9},{2,10},{3,11},{4,12},{5,13},{6,14},{7,15},{8,0},{9,1},... | collective-permute-start | bytes 9437192 | tf_op jit(solution)/shard_map/ppermute | solution.py:104
  295.6 65.3 %collective-permute-start.17 = (bf16[4,2,96,2048]{3,2,1,0:T(8,128)(2,1)}, bf16[4,2,96,2048]{3,2,1,0:T(8,128)(2,1)}, u32[]{:S(2)}, u32[]{:S(2)}) collective-permute-start(bf16[4,2,96,2048]{3,2,1,0:T(8,128)(2,1)} %get-tuple-element.248), channel_id=1, source_target_pairs={{0,4},{1,3},{2,6},{3,1},{4,0},{5,7},{6,2},{7,5},{8,12},{9,11},{10,... | collective-permute-start | bytes 9437192 | tf_op jit(solution)/shard_map/ppermute | solution.py:104
  334.5 154.1 %collective-permute-start.30 = (bf16[4,96,2048]{2,1,0:T(8,128)(2,1)}, bf16[4,96,2048]{2,1,0:T(8,128)(2,1)}, u32[]{:S(2)}, u32[]{:S(2)}) collective-permute-start(bf16[4,96,2048]{2,1,0:T(8,128)(2,1)} %get-tuple-element.254), channel_id=1, source_target_pairs={{0,16},{1,17},{2,18},{3,19},{4,20},{5,21},{6,22},{7,23},{8,24},{9,... | collective-permute-start | bytes 4718600 | tf_op jit(solution)/shard_map/ppermute | solution.py:104
  358.8 66.2 %collective-permute-start.21 = (bf16[4,2,96,2304]{3,2,1,0:T(8,128)(2,1)}, bf16[4,2,96,2304]{3,2,1,0:T(8,128)(2,1)}, u32[]{:S(2)}, u32[]{:S(2)}) collective-permute-start(bf16[4,2,96,2304]{3,2,1,0:T(8,128)(2,1)} %get-tuple-element.159), channel_id=1, source_target_pairs={{0,2},{1,5},{2,0},{3,7},{4,6},{5,1},{6,4},{7,3},{8,10},{9,13},{10,... | collective-permute-start | bytes 10616840 | tf_op jit(solution)/shard_map/ppermute | solution.py:104
  359.4 65.7 %collective-permute-start.22 = (bf16[4,96,1536]{2,1,0:T(8,128)(2,1)}, bf16[4,96,1536]{2,1,0:T(8,128)(2,1)}, u32[]{:S(2)}, u32[]{:S(2)}) collective-permute-start(bf16[4,96,1536]{2,1,0:T(8,128)(2,1)} %get-tuple-element.160), channel_id=1, source_target_pairs={{0,8},{1,9},{2,10},{3,11},{4,12},{5,13},{6,14},{7,15},{8,0},{9,1},... | collective-permute-start | bytes 3538952 | tf_op jit(solution)/shard_map/ppermute | solution.py:104
  378.0 43.4 %collective-permute-start.20 = (bf16[512,1536]{1,0:T(8,128)(2,1)}, bf16[512,1536]{1,0:T(8,128)(2,1)}, u32[]{:S(2)}, u32[]{:S(2)}) collective-permute-start(bf16[512,1536]{1,0:T(8,128)(2,1)} %get-tuple-element.158), channel_id=1, source_target_pairs={{0,1},{1,0},{2,3},{3,2},{4,5},{5,4},{6,7},{7,6},{8,9},{9,8},{10,11... | collective-permute-start | bytes 4718600 | tf_op jit(solution)/shard_map/ppermute | solution.py:54
  392.5 61.3 %collective-permute-start.23 = (bf16[2,2,96,2048]{3,2,1,0:T(8,128)(2,1)}, bf16[2,2,96,2048]{3,2,1,0:T(8,128)(2,1)}, u32[]{:S(2)}, u32[]{:S(2)}) collective-permute-start(bf16[2,2,96,2048]{3,2,1,0:T(8,128)(2,1)} %get-tuple-element.252), channel_id=1, source_target_pairs={{0,8},{1,9},{2,10},{3,11},{4,12},{5,13},{6,14},{7,15},{8,0},{9,1},... | collective-permute-start | bytes 4718600 | tf_op jit(solution)/shard_map/ppermute | solution.py:104
  454.6 35.6 %collective-permute-start.29 = (bf16[2,2,2,2,128,96]{4,5,3,2,1,0:T(8,128)(2,1)}, bf16[2,2,2,2,128,96]{4,5,3,2,1,0:T(8,128)(2,1)}, u32[]{:S(2)}, u32[]{:S(2)}) collective-permute-start(bf16[2,2,2,2,128,96]{4,5,3,2,1,0:T(8,128)(2,1)} %fusion.39), channel_id=1, source_target_pairs={{0,4},{1,3},{2,6},{3,1},{4,0},{5,7},{6,2},{7,5},{8,12},{9,11},{10,... | collective-permute-start | bytes 1179656 | tf_op jit(solution)/shard_map/ppermute | solution.py:104
  463.8 26.4 %collective-permute-start.26 = (bf16[2,96,1536]{2,1,0:T(8,128)(2,1)}, bf16[2,96,1536]{2,1,0:T(8,128)(2,1)}, u32[]{:S(2)}, u32[]{:S(2)}) collective-permute-start(bf16[2,96,1536]{2,1,0:T(8,128)(2,1)} %get-tuple-element.262), channel_id=1, source_target_pairs={{0,2},{1,5},{2,0},{3,7},{4,6},{5,1},{6,4},{7,3},{8,10},{9,13},{10,... | collective-permute-start | bytes 1769480 | tf_op jit(solution)/shard_map/ppermute | solution.py:104
  469.2 23.7 %collective-permute-start.25 = (bf16[2,2,96,2304]{3,2,1,0:T(8,128)(2,1)}, bf16[2,2,96,2304]{3,2,1,0:T(8,128)(2,1)}, u32[]{:S(2)}, u32[]{:S(2)}) collective-permute-start(bf16[2,2,96,2304]{3,2,1,0:T(8,128)(2,1)} %get-tuple-element.250), channel_id=1, source_target_pairs={{0,4},{1,3},{2,6},{3,1},{4,0},{5,7},{6,2},{7,5},{8,12},{9,11},{10,... | collective-permute-start | bytes 5308424 | tf_op jit(solution)/shard_map/ppermute | solution.py:104
  488.5 42.5 %collective-permute-start.43 = (bf16[1,2,96,2048]{3,2,1,0:T(8,128)(2,1)S(1)}, bf16[1,2,96,2048]{3,2,1,0:T(8,128)(2,1)S(1)}, u32[]{:S(2)}, u32[]{:S(2)}) collective-permute-start(bf16[1,2,96,2048]{3,2,1,0:T(8,128)(2,1)S(1)} %copy-done.31), channel_id=1, source_target_pairs={{0,16},{1,17},{2,18},{3,19},{4,20},{5,21},{6,22},{7,23},{8,24},{9,... | collective-permute-start | bytes 2359304 | tf_op jit(solution)/shard_map/ppermute | solution.py:104
  494.9 58.4 %collective-permute-start.38 = (bf16[2,96,2048]{2,1,0:T(8,128)(2,1)S(1)}, bf16[2,96,2048]{2,1,0:T(8,128)(2,1)S(1)}, u32[]{:S(2)}, u32[]{:S(2)}) collective-permute-start(bf16[2,96,2048]{2,1,0:T(8,128)(2,1)S(1)} %get-tuple-element.260), channel_id=1, source_target_pairs={{0,2},{1,5},{2,0},{3,7},{4,6},{5,1},{6,4},{7,3},{8,10},{9,13},{10,... | collective-permute-start | bytes 2359304 | tf_op jit(solution)/shard_map/ppermute | solution.py:104
  497.4 33.1 %collective-permute-start.33 = (bf16[2,2,2,2,128,96]{4,5,3,2,1,0:T(8,128)(2,1)S(1)}, bf16[2,2,2,2,128,96]{4,5,3,2,1,0:T(8,128)(2,1)S(1)}, u32[]{:S(2)}, u32[]{:S(2)}) collective-permute-start(bf16[2,2,2,2,128,96]{4,5,3,2,1,0:T(8,128)(2,1)S(1)} %get-tuple-element.277), channel_id=1, source_target_pairs={{0,8},{1,9},{2,10},{3,11},{4,12},{5,13},{6,14},{7,15},{8,0},{9,1},... | collective-permute-start | bytes 1179656 | tf_op jit(solution)/shard_map/ppermute | solution.py:104
  499.1 38.3 %collective-permute-start.35 = (bf16[1,96,1536]{2,1,0:T(8,128)(2,1)S(1)}, bf16[1,96,1536]{2,1,0:T(8,128)(2,1)S(1)}, u32[]{:S(2)}, u32[]{:S(2)}) collective-permute-start(bf16[1,96,1536]{2,1,0:T(8,128)(2,1)S(1)} %add_convert_fusion.22), channel_id=1, source_target_pairs={{0,4},{1,3},{2,6},{3,1},{4,0},{5,7},{6,2},{7,5},{8,12},{9,11},{10,... | collective-permute-start | bytes 884744 | tf_op jit(solution)/shard_map/ppermute | solution.py:104
  502.4 51.0 %collective-permute-start.34 = (bf16[1,2,96,2304]{3,2,1,0:T(8,128)(2,1)S(1)}, bf16[1,2,96,2304]{3,2,1,0:T(8,128)(2,1)S(1)}, u32[]{:S(2)}, u32[]{:S(2)}) collective-permute-start(bf16[1,2,96,2304]{3,2,1,0:T(8,128)(2,1)S(1)} %add_convert_fusion.11), channel_id=1, source_target_pairs={{0,8},{1,9},{2,10},{3,11},{4,12},{5,13},{6,14},{7,15},{8,0},{9,1},... | collective-permute-start | bytes 2654216 | tf_op jit(solution)/shard_map/ppermute | solution.py:104
  530.6 22.8 %collective-permute-start.37 = (bf16[2,2,2,2,128,96]{4,5,3,2,1,0:T(8,128)(2,1)S(1)}, bf16[2,2,2,2,128,96]{4,5,3,2,1,0:T(8,128)(2,1)S(1)}, u32[]{:S(2)}, u32[]{:S(2)}) collective-permute-start(bf16[2,2,2,2,128,96]{4,5,3,2,1,0:T(8,128)(2,1)S(1)} %fusion.37), channel_id=1, source_target_pairs={{0,16},{1,17},{2,18},{3,19},{4,20},{5,21},{6,22},{7,23},{8,24},{9,... | collective-permute-start | bytes 1179656 | tf_op jit(solution)/shard_map/ppermute | solution.py:104
  531.0 22.4 %collective-permute-start.36 = (f32[100,128]{1,0:T(8,128)S(1)}, f32[100,128]{1,0:T(8,128)S(1)}, u32[]{:S(2)}, u32[]{:S(2)}) collective-permute-start(f32[100,128]{1,0:T(8,128)S(1)} %pad_maximum_fusion.7), channel_id=1, source_target_pairs={{0,8},{1,9},{2,10},{3,11},{4,12},{5,13},{6,14},{7,15},{8,0},{9,1},... | collective-permute-start | bytes 153608 | tf_op jit(solution)/shard_map/ppermute | solution.py:104
  580.8 28.4 %collective-permute-start.42 = (bf16[4,96,768]{2,1,0:T(8,128)(2,1)S(1)}, bf16[4,96,768]{2,1,0:T(8,128)(2,1)S(1)}, u32[]{:S(2)}, u32[]{:S(2)}) collective-permute-start(bf16[4,96,768]{2,1,0:T(8,128)(2,1)S(1)} %pad_maximum_fusion.3), channel_id=1, source_target_pairs={{0,16},{1,17},{2,18},{3,19},{4,20},{5,21},{6,22},{7,23},{8,24},{9,... | collective-permute-start | bytes 1769480 | tf_op jit(solution)/shard_map/ppermute | solution.py:104
  (85 other events, 1392.3 us)
Sparse Core Ops, SparseCore 0:
  12.9 194.2 all-gather.1

commit v7 on v6

--- a/solution.py
+++ b/solution.py
@@ -109,11 +109,6 @@
     return jnp.take(value, lax.axis_index("dp") ^ places, axis=0)
 
 
-def absolute(value):
-    places = lax.axis_index("dp") ^ jnp.arange(lax.axis_size("dp"))
-    return jnp.take(value, turned(places, lax.axis_index("fsdp")), axis=0)
-
-
 class Halving:
     def __init__(self, order, keep, send):
         self.order = list(order)
@@ -140,54 +135,53 @@
     return sum((p >> bit & 1) << i for i, bit in enumerate(reversed(order)))
 
 
-class Exchange:
-    def __init__(self, value):
-        self.bits, self.shape = list(range(dp_bits())), value.shape
-        self.cur = value.reshape((2,) * dp_bits() + value.shape[1:])
-        self.keep = self.got = None
-        self.start()
-
-    def start(self):
-        if self.bits:
-            self.bit = self.bits.pop(0)
-            self.axis = dp_bits() - 1 - self.bit
-            self.keep, send = (
-                lax.index_in_dim(self.cur, i, self.axis, keepdims=False) for i in range(2)
+def swap_all_kernel(text_ref, mod_ref, small_ref, text_out, mod_out, small_out, sends, gets, own):
+    dpn, me = lax.axis_size("dp"), lax.axis_index("dp")
+    copies = []
+    for r in range(1, dpn):
+        peer = me ^ r
+        moves = (
+            (text_ref.at[peer], text_out.at[me]),
+            (mod_ref.at[peer], mod_out.at[me]),
+            (small_ref, small_out.at[me]),
+        )
+        for i, (src, dst) in enumerate(moves):
+            copies.append(
+                pltpu.make_async_remote_copy(
+                    src_ref=src, dst_ref=dst, send_sem=sends.at[i, r], recv_sem=gets.at[i, r],
+                    device_id={"dp": peer}, device_id_type=pl.DeviceIdType.MESH,
+                )
             )
-            self.got = dp_swap(send, self.bit)
-
-    def step(self):
-        if self.got is not None:
-            self.cur = jnp.stack([self.keep, self.got], axis=self.axis)
-            self.got = None
-            self.start()
-
-
-class Small:
-    def __init__(self, parts, total):
-        self.bits, self.shape, self.total = list(range(dp_bits())), parts.shape, total
-        self.cur = parts.reshape((2,) * dp_bits() + parts.shape[1:])
-        self.got = None
-        self.start()
-
-    def start(self):
-        if self.bits:
-            self.bit = self.bits.pop(0)
-            self.axis = dp_bits() - 1 - self.bit
-            self.keep, send = (
-                lax.index_in_dim(self.cur, i, self.axis, keepdims=False) for i in range(2)
-            )
-            flat = jnp.concatenate([send.reshape(-1, 128), self.total], axis=0)
-            self.got = dp_swap(flat, self.bit)
-
-    def step(self):
-        if self.got is not None:
-            rows = self.keep.size // 128
-            self.total = self.total + self.got[rows:]
-            got = self.got[:rows].reshape(self.keep.shape)
-            self.cur = jnp.stack([self.keep, got], axis=self.axis)
-            self.got = None
-            self.start()
+            copies[-1].start()
+    local = (
+        pltpu.make_async_copy(text_ref.at[me], text_out.at[me], own.at[0]),
+        pltpu.make_async_copy(mod_ref.at[me], mod_out.at[me], own.at[1]),
+        pltpu.make_async_copy(small_ref, small_out.at[me], own.at[2]),
+    )
+    for copy in local:
+        copy.start()
+    for copy in (*local, *copies):
+        copy.wait()
+
+
+def swap_all(text, mods, small):
+    vmem = pl.BlockSpec(memory_space=pltpu.VMEM)
+    count = text.shape[0]
+    return pl.pallas_call(
+        swap_all_kernel,
+        in_specs=[vmem] * 3,
+        out_specs=[vmem] * 3,
+        out_shape=[
+            jax.ShapeDtypeStruct(text.shape, text.dtype),
+            jax.ShapeDtypeStruct(mods.shape, mods.dtype),
+            jax.ShapeDtypeStruct((count,) + small.shape, small.dtype),
+        ],
+        scratch_shapes=[
+            pltpu.SemaphoreType.DMA((3, count)), pltpu.SemaphoreType.DMA((3, count)),
+            pltpu.SemaphoreType.DMA((3,)),
+        ],
+        compiler_params=pltpu.CompilerParams(has_side_effects=True),
+    )(text, mods, small)
 
 
 def advance(chains, value):
@@ -601,10 +595,9 @@
 
 
 def project_grad_kernel(
-    orders, id_ref, da_ref, db_ref, pre_ref, stat_ref, gain_ref, first_ref, okeep_ref, osend_ref,
-    keep_ref, send_ref, vkeep_ref, vsend_ref, g_ref, gt, tmp,
+    order, id_ref, da_ref, db_ref, pre_ref, stat_ref, gain_ref, first_ref,
+    keep_ref, send_ref, g_ref, gt, tmp,
 ):
-    order, late = orders
     j = pl.program_id(0)
     own = pre_ref.shape[2]
     cut = da_ref.shape[2]
@@ -618,34 +611,19 @@
         tmp[part, :] = g.T.astype(BF16)
         g_ref[0, :, part] = g.astype(BF16)
     put_relative(gt, tmp, id_ref[0] % count, id_ref[1], count)
-    wide = dot(gt[...], first_ref[...]).astype(BF16)
-
-    depth = first_ref.shape[1]
-
-    @pl.when(j < 2)
-    def _():
-        put_halves(keep_ref.at[..., :depth], send_ref.at[..., :depth], wide, count, order, j)
-        for src, dst in ((okeep_ref, keep_ref), (osend_ref, send_ref)):
-            for p in range(dst.shape[0]):
-                dst[p, j, :, depth:] = src[2 * p + j]
-
-    @pl.when(j == 2)
-    def _():
-        put_halves(vkeep_ref, vsend_ref, wide, count, late)
-
-
-def project_grad(ids, da, db, pre, stats, gain, first, okeep, osend, dp, orders):
+    put_halves(keep_ref, send_ref, dot(gt[...], first_ref[...]).astype(BF16), count, order, j)
+
+
+def project_grad(ids, da, db, pre, stats, gain, first, dp, order):
     _, tokens, own = pre.shape
     depth = first.shape[1]
     share = depth // dp
     const = lambda j: (0, 0)
     block = lambda j: (j, 0, 0)
     once = functools.partial(pl.BlockSpec, pipeline_mode=pl.Buffered(1))
-    half = once((dp // 4, 2, share, depth + own), lambda j: (0, 0, 0, 0))
-    whole = once(okeep.shape, lambda j: (0, 0, 0))
-    vhalf = once((dp // 4, share, depth), lambda j: (0, 0, 0))
+    half = once((dp // 4, 3, share, depth), lambda j: (0, 0, 0, 0))
     return pl.pallas_call(
-        functools.partial(project_grad_kernel, orders),
+        functools.partial(project_grad_kernel, order),
         grid=(3,),
         in_specs=[
             pl.BlockSpec(memory_space=pltpu.SMEM),
@@ -653,14 +631,13 @@
             pl.BlockSpec((1, tokens, own), block),
             pl.BlockSpec((8, tokens), const),
             pl.BlockSpec((1, 1, own), block),
-            once((tokens, depth), const), whole, whole,
-        ],
-        out_specs=[half, half, vhalf, vhalf, pl.BlockSpec((1, tokens, own), block)],
-        out_shape=[sds((dp // 4, 2, share, depth + own), BF16)] * 2
-        + [sds((dp // 4, share, depth), BF16)] * 2
+            once((tokens, depth), const),
+        ],
+        out_specs=[half, half, pl.BlockSpec((1, tokens, own), block)],
+        out_shape=[sds((dp // 4, 3, share, depth), BF16)] * 2
         + [sds((3, tokens, own), BF16)],
         scratch_shapes=[pltpu.VMEM((own, tokens), BF16), pltpu.VMEM((own, tokens), BF16)],
-    )(ids, da, db, pre, stats, gain, first, okeep, osend)
+    )(ids, da, db, pre, stats, gain, first)
 
 
 def project_back_kernel(id_ref, g_ref, w_ref, got_ref, own_ref, peer_ref, acc):
@@ -871,6 +848,7 @@
     d_gate_attn = jnp.sum(grad_after * attn_branch, axis=0) * (1.0 - gate_attn[0] * gate_attn[0])
     grad_attn = (gate_attn * grad_after).astype(BF16)
     grad_mixed, *out_halves = out_back(ids, gather_rot(grad_attn), w_out, mixed, dpn, bits)
+    out_chain = Halving(bits, *out_halves)
     blocks = pre_p.shape[2] // width
     cut = max(1, 2 * blocks // 3)
     grad_mixed = pad_cols(grad_mixed, width)
@@ -887,13 +865,11 @@
     if paired:
         stats = jnp.concatenate([inverse[:2], ones, means, zeros, zeros, zeros], axis=0)
         gain3 = jnp.stack([gain_own[2:3], gain_own[3:4], jnp.ones_like(gain_own[2:3])])
-        low_late = low_bits[2:] + low_bits[:2]
-        keep, send, v_keep, v_send, grads = project_grad(
-            ids, part_a[0], part_b[0], pre, stats, gain3, first_all, *out_halves, dpn,
-            (low_bits, low_late),
+        keep, send, grads = project_grad(
+            ids, part_a[0], part_b[0], pre, stats, gain3, first_all, dpn, low_bits
         )
-        part_a, part_b, grads = advance([wide_chain], (part_a[1:], part_b[1:], grads))
-        qkv_chains = [Halving(low_bits, keep, send), Halving(low_late, v_keep, v_send)]
+        part_a, part_b, grads = advance([wide_chain, out_chain], (part_a[1:], part_b[1:], grads))
+        qkv_chain = Halving(low_bits, keep, send)
         parts = project_back(ids, grads, w_flat, w_parts[1])
     else:
         d = jnp.concatenate([part_a[0], part_b[0]], axis=2)[:, :, :own_d]
@@ -905,9 +881,7 @@
         wide = [jnp.concatenate(natural(exchange_rot(w_, 1)), axis=0) for w_ in wide]
         wide = relative(jnp.stack([w_.reshape(dpn, share, own_d) for w_ in wide], axis=1))
         wide = jnp.stack([wide[p] for p in sorted(range(dpn), key=lambda p: place_of(p, bits))])
-        qkv_chains = [
-            Halving(bits, wide[: dpn // 2], wide[dpn // 2 :]), Halving(bits, *out_halves),
-        ]
+        qkv_chain = Halving(bits, wide[: dpn // 2], wide[dpn // 2 :])
         parts = [
             sum(dot(rows(g, r), w_heads[j], 1, 1) for j, g in enumerate(grads)) for r in range(n)
         ]
@@ -926,12 +900,8 @@
     grad_tk = (inv_t * (text_hat - normed_t * mean_t)).astype(BF16)
     text_pair = jnp.stack([grad_tk, dtv.astype(BF16)])
     pair_all = jnp.concatenate(natural(gather_rot(text_pair)), axis=-1)
-    outgoing = block_of(pair_all, f, 1).reshape(2, TEXT // n, dpn, share).transpose(2, 0, 1, 3)
-    pair_chain = Exchange(relative(outgoing))
+    pair_all = advance([qkv_chain, out_chain], pair_all)
     text_in = text_bwd(pair_all, w_text)
-    text_in, grad_first = advance(
-        [*qkv_chains, wide_chain, pair_chain], (text_in, grad_first)
-    )
     text_in = jnp.concatenate(natural(exchange_rot(text_in, 0)), axis=1)
 
     inverse_one = inverse_rms(x_own)
@@ -952,52 +922,39 @@
     small = jnp.concatenate([block_of(sums[4:], f, 1), gain_q, gain_k, gain_text, gate_pad], axis=0)
     mods = jnp.concatenate([sums[:4], stamp], axis=0).reshape(5, dpn, share).transpose(1, 0, 2)
     mods = jnp.pad(mods, ((0, 0), (0, 3), (0, -share % 128)))
-    small_chain = Small(relative(mods), small.reshape(-1, 128))
-
-    grad_input = advance([*qkv_chains, small_chain, pair_chain, down_chain], grad_input)
-    advance([small_chain, pair_chain], ())
-    advance([*qkv_chains, small_chain, pair_chain, down_chain], ())
-    if paired:
-        last, v_last = (c.last[0].astype(BF16) for c in qkv_chains)
-        own_side = f == (me >> low_bits[-1] + 1)
-        side = jnp.concatenate([last[:, :, :D], v_last[None]])
-        mine, got = exchange_rot(side, 2)
-        keep = jnp.concatenate([jnp.where(own_side, mine, got), last[:1, :, D:]])
-        send = jnp.concatenate([jnp.where(own_side, got, mine), last[1:, :, D:]])
-        final_chain = Halving(bits[-1:], keep, send)
-    else:
-        final_chain = qkv_chains[0]
-    pair_cols = absolute(pair_chain.cur.reshape(pair_chain.shape))
+    small = jnp.pad(small.reshape(-1, 128), ((0, -small.size // 128 % 8), (0, 0)))
+    outgoing = block_of(pair_all, f, 1).reshape(2, TEXT // n, dpn, share).transpose(2, 0, 1, 3)
+    mods = advance([wide_chain, down_chain, qkv_chain, out_chain], mods)
+    pair_cols, mods, small = swap_all(outgoing, mods, small)
     pair_cols = jnp.concatenate(natural(gather_rot(pair_cols)), axis=2)
     pair_cols = pair_cols.transpose(0, 2, 1, 3).reshape(dpn * TEXT, 2 * share)
     text_grad = dot(pair_cols, text_all, 0, 0).reshape(2, share, TW // n)
-
-    def rest(chain):
-        while chain.got is not None:
-            chain.step()
-
-    for chain in (pair_chain, small_chain, wide_chain, down_chain, *qkv_chains, final_chain):
-        rest(chain)
-    if paired:
-        qkv_grad, out_grad = final_chain.last[:3], final_chain.last[3]
-    else:
-        qkv_grad, out_grad = qkv_chains[0].last[0], qkv_chains[1].last[0]
-    total = small_chain.total.reshape(6, own_d)
-    mods = small_chain.cur.reshape(small_chain.shape)
+    total = jnp.sum(small, axis=0)[: 6 * own_d // 128].reshape(6, own_d)
     times = time_embed(mods[:, 4, 0])
     times = lax.dynamic_slice_in_dim(times, f * own_te, own_te, 1).astype(F32)
     ada_grad = lax.dot_general(
         mods[:, :4, :share].reshape(dpn, 4 * share), times, (((0,), (0,)), ((), ())),
         precision=lax.Precision.HIGHEST,
     ).reshape(4, share, own_te)
+
+    text_grad = advance([qkv_chain, down_chain], text_grad)
+    if paired:
+        own_side = f == (me >> low_bits[-1] + 1)
+        mine, got = exchange_rot(qkv_chain.last[0].astype(BF16), 2)
+        qkv_chain = Halving(
+            bits[-1:], jnp.where(own_side, mine, got)[None], jnp.where(own_side, got, mine)[None]
+        )
+    for chain in (out_chain, down_chain, wide_chain, qkv_chain):
+        while chain.got is not None:
+            chain.step()
     return (
         output[None],
         grad_input[None],
         text_in[None],
         ada_grad.transpose(2, 0, 1),
         text_grad.transpose(2, 0, 1),
-        qkv_grad.transpose(2, 0, 1),
-        out_grad.T,
+        qkv_chain.last[0].transpose(2, 0, 1),
+        out_chain.last[0].T,
         total[:5],
         total[5, : HEADS // n],
         wide_chain.last[0].transpose(1, 0, 2),

time: 624 us -> 597 us (0.957)
  Pallas kernels: 281 us -> 315 us
  waiting for transfers between devices: 101 us -> 72.5 us
  local copies, waits for them, and re-layouts: 51.1 us -> 36.6 us
  other arithmetic: 109 us -> 96.6 us
    pallas_call x1 -> x2, Pallas kernels: 21 us -> 55.2 us  [the longest x1 36.9 us: swap_all(): pl.pallas_call(swap_all_kernel, in_specs=[vmem] * 3, out_specs=[vmem] * 3...]
    ppermute x23 -> x16, waiting for transfers between devices: 90.1 us -> 61.4 us  [dp_swap(): return lax.ppermute(value, ('dp', 'fsdp'), pairs)]
    convert_element_type x6 -> x7, other arithmetic: 29.4 us -> 33.3 us  [step(): self.keep = add(slice(half)).astype(BF16)]
    ppermute x23 -> x16, starting transfers between devices: 29.9 us -> 26 us  [dp_swap(): return lax.ppermute(value, ('dp', 'fsdp'), pairs)]
  transfers between devices with their start and end apart: 46 -> 39, of which waited for: 15 -> 12; matrix products, arithmetic and copies ran while one was open for 26% -> 23% of each run, Pallas kernels for 45% -> 47%
where the time goes in v7:
time: 597 us; the launch traced here: 592 us
  Pallas kernels  315 us (53%)
  other arithmetic  96.6 us (16%)
  waiting for transfers between devices  72.5 us (12%)
  local copies, waits for them, and re-layouts  36.6 us (6%)
  starting transfers between devices  31.1 us (5%)
  matrix products  21.4 us (4%)
  between operations  16.3 us (3%)
    pallas_call x1, Pallas kernels, ffn(): pl.pallas_call(functools.partial(ffn_kernel, orders), grid=(hid // bc,),...  90.3 us
    pallas_call x2, Pallas kernels, attn_backward(): pl.pallas_call(attn_bwd_kernel, grid=(blocks,), in_specs=[scalar, col, co...  68.7 us
    ppermute x16, waiting for transfers between devices, dp_swap(): return lax.ppermute(value, ('dp', 'fsdp'), pairs)  61.4 us
    pallas_call x1, Pallas kernels, swap_all(): pl.pallas_call(swap_all_kernel, in_specs=[vmem] * 3, out_specs=[vmem] * 3...  36.9 us
    convert_element_type x7, other arithmetic, step(): self.keep = add(slice(half)).astype(BF16)  33.3 us
    pallas_call x1, Pallas kernels, attn_forward(): pl.pallas_call(attn_fwd_kernel, grid=(blocks,), in_specs=[scalar, three,...  32.1 us
    ppermute x16, starting transfers between devices, dp_swap(): return lax.ppermute(value, ('dp', 'fsdp'), pairs)  26 us
    pallas_call x1, Pallas kernels, project_grad(): pl.pallas_call(functools.partial(project_grad_kernel, order), grid=(3,),...  18.3 us
  transfers between devices with their start and end apart: 39, of which 12 were waited for; matrix products, arithmetic and copies ran while one was open for 23% of the time, Pallas kernels for 47%

profile of v7, /device:TPU:0, one launch (start us, length us, event | category | flops | bytes accessed | tf_op | source)
XLA Modules:
  0.0 591.7 jit_solution(16150664724456126272)
XLA Ops:
  23.4 16.2 %shard_map.222 = f32[2,256,1536]{2,1,0:T(8,128)} custom-call(bf16[256,2048]{1,0:T(8,128)(2,1)} %pad_maximum_fusion.2.x_ref, bf16[2048,2,1536]{2,1,0:T(2,128)(2,1)} %w_ref.5), custom_call_target="tpu_custom_call" | custom-call | tf_op jit(solution)/shard_map/pallas_call | solution.py:422
  53.4 14.3 %shard_map.221 = (bf16[1024,1536]{1,0:T(8,128)(2,1)}, f32[3,1024,768]{2,1,0:T(8,128)}, f32[8,1024]{1,0:T(8,128)}) custom-call(s32[2]{0:T(128)} %pad_add_fusion.1.id_ref, bf16[512,1536]{1,0:T(8,128)(2,1)} %bitcast.134, bf16[512,1536]{1,0:T(8,128)(2,1)} %collective-permute-done.1.xp_ref, f32[1,1536]{1,0:T(1,128)} %get-tuple-element.257.front_ref, ...), custom_call_target="tpu_custom_call" | custom-call | tf_op jit(solution)/shard_map/pallas_call | solution.py:578
  70.4 32.1 %shard_map.223 = (bf16[1024,768]{1,0:T(8,128)(2,1)}, bf16[1024,768]{1,0:T(8,128)(2,1)}, bf16[1024,768]{1,0:T(8,128)(2,1)}, bf16[1024,768]{1,0:T(8,128)(2,1)}, f3...) custom-call(s32[1]{0:T(128)S(6)} %copy.55.len_ref, ...), custom_call_target="tpu_custom_call" | custom-call | tf_op jit(solution)/shard_map/pallas_call | solution.py:365
  120.5 90.3 %shard_map.224 = (bf16[8,2,96,2048]{3,2,1,0:T(8,128)(2,1)}, bf16[8,2,96,2048]{3,2,1,0:T(8,128)(2,1)}, bf16[8,96,2048]{2,1,0:T(8,128)(2,1)}, bf16[8,96,2048]{2,1,...) custom-call(s32[2]{0:T(128)} %pad_add_fusion.1.id_ref, ...), custom_call_target="tpu_custom_call" | custom-call | tf_op jit(solution)/shard_map/pallas_call | solution.py:521
  221.7 5.8 fusion.7
  232.6 9.6 %shard_map.225 = (f32[1024,768]{1,0:T(8,128)}, bf16[8,96,768]{2,1,0:T(8,128)(2,1)}, bf16[8,96,768]{2,1,0:T(8,128)(2,1)}) custom-call(s32[2]{0:T(128)} %pad_add_fusion.1.id_ref, bf16[512,1536]{1,0:T(8,128)(2,1)} %copy-done.17, bf16[512,1536]{1,0:T(8,128)(2,1)} %collective-permute-done.13.refs_1_, bf16[768,1536]{1,0:T(8,128)(2,1)} %refs_2_.1, ...), custom_call_target="tpu_custom_call" | custom-call | tf_op jit(solution)/shard_map/pallas_call | solution.py:706
  242.1 44.4 %shard_map.226 = (f32[3,1024,512]{2,1,0:T(8,128)}, f32[256,512]{1,0:T(8,128)}, f32[256,512]{1,0:T(8,128)}, f32[8,1024]{1,0:T(8,128)}, f32[1,512]{1,0:T(1,128)}, /*index=5*/f32[1,512]{1,0:T(1,128)}, f32[1,512]{1,0:T(1,128)}) custom-call(s32[1]{0:T(128)S(6)} %copy.55.len_ref, bf16[1024,768]{1,0:T(8,128)(2,1)} %get-tuple-element.106.q_ref, ...), custom_call_target="tpu_custom_call" | custom-call | tf_op jit(solution)/shard_map/pallas_call | solution.py:380
  286.6 8.1 %add_convert_fusion = (bf16[4,2,96,2048]{3,2,1,0:T(8,128)(2,1)}, bf16[4,2,96,2048]{3,2,1,0:T(8,128)(2,1)}) fusion(bf16[8,2,96,2048]{3,2,1,0:T(8,128)(2,1)} %collective-permute-done.14, bf16[8,2,96,2048]{3,2,1,0:T(8,128)(2,1)} %get-tuple-element.141), kind=kLoop, calls=%fused_computation.4 | loop fusion | flops 12582912 | bytes 18874368 | tf_op jit(solution)/shard_map/convert_element_type | solution.py:130
  297.1 24.3 %shard_map.227 = (f32[3,1024,256]{2,1,0:T(8,128)}, f32[256,256]{1,0:T(8,128)}, f32[256,256]{1,0:T(8,128)}, f32[8,1024]{1,0:T(8,128)}, f32[1,256]{1,0:T(1,128)}, /*index=5*/f32[1,256]{1,0:T(1,128)}, f32[1,256]{1,0:T(1,128)}) custom-call(s32[1]{0:T(128)S(6)} %copy.55.len_ref, bf16[1024,768]{1,0:T(8,128)(2,1)} %get-tuple-element.106.q_ref, ...), custom_call_target="tpu_custom_call" | custom-call | tf_op jit(solution)/shard_map/pallas_call | solution.py:380
  324.1 18.3 %shard_map.228 = (bf16[4,3,96,1536]{3,2,1,0:T(8,128)(2,1)}, bf16[4,3,96,1536]{3,2,1,0:T(8,128)(2,1)}, bf16[3,1024,768]{2,1,0:T(8,128)(2,1)}) custom-call(s32[2]{0:T(128)} %pad_add_fusion.1.id_ref, f32[3,1024,512]{2,1,0:T(8,128)} %get-tuple-element.137.da_ref, f32[3,1024,256]{2,1,0:T(8,128)} %get-tuple-element.138.db_ref, ...), custom_call_target="tpu_custom_call" | custom-call | tf_op jit(solution)/shard_map/pallas_call | solution.py:625
  343.4 6.1 %add_convert_fusion.5 = (bf16[4,96,2048]{2,1,0:T(8,128)(2,1)}, bf16[4,96,2048]{2,1,0:T(8,128)(2,1)}) fusion(bf16[8,96,2048]{2,1,0:T(8,128)(2,1)} %collective-permute-done.15, bf16[8,96,2048]{2,1,0:T(8,128)(2,1)} %get-tuple-element.156), kind=kLoop, calls=%fused_computation.27 | loop fusion | flops 6291456 | bytes 9437184 | tf_op jit(solution)/shard_map/convert_element_type | solution.py:130
  352.0 14.1 %shard_map.229 = (f32[512,1536]{1,0:T(8,128)}, bf16[512,1536]{1,0:T(8,128)(2,1)}) custom-call(s32[2]{0:T(128)} %pad_add_fusion.1.id_ref, bf16[3,1024,768]{2,1,0:T(8,128)(2,1)} %get-tuple-element.144.g_ref, bf16[3,768,1536]{2,1,0:T(8,128)(2,1)} %bitcast.133, bf16[3,768,768]{2,1,0:T(8,128)(2,1)} %collective-permute-done.2.got_ref), custom_call_target="tpu_custom_call" | custom-call | tf_op jit(solution)/shard_map/pallas_call | solution.py:671
  376.9 4.9 add_convert_fusion.4
  385.0 5.6 collective-permute-done.22
  390.6 14.6 %shard_map.230 = bf16[256,2048]{1,0:T(8,128)(2,1)} custom-call(bf16[2,256,1536]{2,1,0:T(8,128)(2,1)} %pad_maximum_fusion.1.g_ref, bf16[2048,2,1536]{2,1,0:T(2,128)(2,1)} %w_ref.5), custom_call_target="tpu_custom_call" | custom-call | tf_op jit(solution)/shard_map/pallas_call | solution.py:441
  407.1 6.0 %add_convert_fusion.2 = (bf16[2,3,96,1536]{3,2,1,0:T(8,128)(2,1)}, bf16[2,3,96,1536]{3,2,1,0:T(8,128)(2,1)}) fusion(bf16[4,3,96,1536]{3,2,1,0:T(8,128)(2,1)} %collective-permute-done.22, bf16[4,3,96,1536]{3,2,1,0:T(8,128)(2,1)} %get-tuple-element.158), kind=kLoop, calls=%fused_computation.15 | loop fusion | flops 7077888 | bytes 10616832 | tf_op jit(solution)/shard_map/convert_element_type | solution.py:130
  429.0 5.1 fusion.15
  435.7 22.1 %collective-permute-done.29 = bf16[2,96,768]{2,1,0:T(8,128)(2,1)} collective-permute-done((bf16[2,96,768]{2,1,0:T(8,128)(2,1)}, bf16[2,96,768]{2,1,0:T(8,128)(2,1)}, u32[]{:S(2)}, u32[]{:S(2)}) %collective-permute-start.29) | collective-permute-done | bytes 294944 | tf_op jit(solution)/shard_map/ppermute | solution.py:104
  457.8 36.9 %shard_map.231 = (bf16[16,2,128,96]{3,2,1,0:T(8,128)(2,1)}, f32[16,8,128]{2,1,0:T(8,128)}, f32[16,40,128]{2,1,0:T(8,128)}) custom-call(bf16[16,2,128,96]{3,2,1,0:T(8,128)(2,1)} %bitcast.139, f32[16,8,128]{2,1,0:T(8,128)} %pad.13.mod_ref, f32[40,128]{1,0:T(8,128)} %pad.15.small_ref), custom_call_target="tpu_custom_call" | custom-call | tf_op jit(solution)/shard_map/pallas_call | solution.py:170
  501.3 7.2 %collective-permute-start.31 = (bf16[1,3,96,1536]{3,2,1,0:T(8,128)(2,1)}, bf16[1,3,96,1536]{3,2,1,0:T(8,128)(2,1)}, u32[]{:S(2)}, u32[]{:S(2)}) collective-permute-start(bf16[1,3,96,1536]{3,2,1,0:T(8,128)(2,1)} %add_convert_fusion.11), channel_id=1, source_target_pairs={{0,8},{1,9},{2,10},{3,11},{4,12},{5,13},{6,14},{7,15},{8,0},{9,1},... | collective-permute-start | bytes 2654216 | tf_op jit(solution)/shard_map/ppermute | solution.py:104
  522.3 9.6 %collective-permute-done.35 = bf16[1,96,768]{2,1,0:T(8,128)(2,1)S(1)} collective-permute-done((bf16[1,96,768]{2,1,0:T(8,128)(2,1)S(1)}, bf16[1,96,768]{2,1,0:T(8,128)(2,1)S(1)}, u32[]{:S(2)}, u32[]{:S(2)}) %collective-permute-start.35) | collective-permute-done | bytes 147488 | tf_op jit(solution)/shard_map/ppermute | solution.py:104
  540.6 8.9 %fusion = f32[2,96,2048]{2,1,0:T(8,128)} fusion(bf16[2,96,4096]{2,1,0:T(8,128)(2,1)S(1)} %bitcast.142, bf16[4096,2048]{1,0:T(8,128)(2,1)} %all-gather.2.cloned.1.call-done), kind=kOutput, calls=%fused_computation | convolution fusion | flops 3221225472 | bytes 19922944 | tf_op jit(solution)/shard_map/dot_general | solution.py:25
  553.3 4.8 collective-permute-done.36
  564.4 19.2 %collective-permute-done.34 = bf16[1,3,96,768]{3,2,1,0:T(8,128)(2,1)S(1)} collective-permute-done((bf16[1,3,96,768]{3,2,1,0:T(8,128)(2,1)S(1)}, bf16[1,3,96,768]{3,2,1,0:T(8,128)(2,1)S(1)}, u32[]{:S(2)}, u32[]{:S(2)}) %collective-permute-start.34) | collective-permute-done | bytes 442400 | tf_op jit(solution)/shard_map/ppermute | solution.py:104
  (276 shorter events, 146.8 us)
Async XLA Ops:
  7.2 206.5 %all-gather.2.cloned.1.call-start = ((), (), s32[]{:S(2)}) async-start(), calls=%async_computation | async-start | bytes 17825792 | tf_op jit(solution)/shard_map/all_gather | solution.py:781
  12.9 40.4 %collective-permute-start.1 = (bf16[512,1536]{1,0:T(8,128)(2,1)S(1)}, bf16[512,1536]{1,0:T(8,128)(2,1)}, u32[]{:S(2)}, u32[]{:S(2)}) collective-permute-start(bf16[512,1536]{1,0:T(8,128)(2,1)S(1)} %bitcast.135), channel_id=1, source_target_pairs={{0,1},{1,0},{2,3},{3,2},{4,5},{5,4},{6,7},{7,6},{8,9},{9,8},{10,11... | collective-permute-start | bytes 4718600 | tf_op jit(solution)/shard_map/ppermute | solution.py:30
  17.3 36.0 %collective-permute-start.2 = (bf16[3,768,768]{2,1,0:T(8,128)(2,1)}, bf16[3,768,768]{2,1,0:T(8,128)(2,1)}, u32[]{:S(2)}, u32[]{:S(2)}) collective-permute-start(bf16[3,768,768]{2,1,0:T(8,128)(2,1)} %dynamic-slice_bitcast_fusion), channel_id=1, source_target_pairs={{0,1},{1,0},{2,3},{3,2},{4,5},{5,4},{6,7},{7,6},{8,9},{9,8},{10,11... | collective-permute-start | bytes 10616840 | tf_op jit(solution)/shard_map/ppermute | solution.py:30
  22.8 26.5 %collective-permute-start = (f32[4,1536]{1,0:T(4,128)S(1)}, f32[4,1536]{1,0:T(4,128)S(1)}, u32[]{:S(2)}, u32[]{:S(2)}) collective-permute-start(f32[4,1536]{1,0:T(4,128)S(1)} %bitcast.147), channel_id=1, source_target_pairs={{0,1},{1,0},{2,3},{3,2},{4,5},{5,4},{6,7},{7,6},{8,9},{9,8},{10,11... | collective-permute-start | bytes 73736 | tf_op jit(solution)/shard_map/ppermute | solution.py:30
  23.2 22.9 %collective-permute-start.4 = (s32[2,512]{1,0:T(2,128)S(1)}, s32[2,512]{1,0:T(2,128)S(1)}, u32[]{:S(2)}, u32[]{:S(2)}) collective-permute-start(s32[2,512]{1,0:T(2,128)S(1)} %bitcast.160), channel_id=1, source_target_pairs={{0,1},{1,0},{2,3},{3,2},{4,5},{5,4},{6,7},{7,6},{8,9},{9,8},{10,11... | collective-permute-start | bytes 12296 | tf_op jit(solution)/shard_map/ppermute | solution.py:30
  210.7 75.9 %collective-permute-start.14 = (bf16[8,2,96,2048]{3,2,1,0:T(8,128)(2,1)}, bf16[8,2,96,2048]{3,2,1,0:T(8,128)(2,1)}, u32[]{:S(2)}, u32[]{:S(2)}) collective-permute-start(bf16[8,2,96,2048]{3,2,1,0:T(8,128)(2,1)} %get-tuple-element.128), channel_id=1, source_target_pairs={{0,2},{1,5},{2,0},{3,7},{4,6},{5,1},{6,4},{7,3},{8,10},{9,13},{10,... | collective-permute-start | bytes 18874376 | tf_op jit(solution)/shard_map/ppermute | solution.py:104
  214.2 72.4 %collective-permute-start.15 = (bf16[8,96,2048]{2,1,0:T(8,128)(2,1)}, bf16[8,96,2048]{2,1,0:T(8,128)(2,1)}, u32[]{:S(2)}, u32[]{:S(2)}) collective-permute-start(bf16[8,96,2048]{2,1,0:T(8,128)(2,1)} %get-tuple-element.129), channel_id=1, source_target_pairs={{0,8},{1,9},{2,10},{3,11},{4,12},{5,13},{6,14},{7,15},{8,0},{9,1},... | collective-permute-start | bytes 9437192 | tf_op jit(solution)/shard_map/ppermute | solution.py:104
  294.8 57.2 %collective-permute-start.17 = (bf16[4,2,96,2048]{3,2,1,0:T(8,128)(2,1)}, bf16[4,2,96,2048]{3,2,1,0:T(8,128)(2,1)}, u32[]{:S(2)}, u32[]{:S(2)}) collective-permute-start(bf16[4,2,96,2048]{3,2,1,0:T(8,128)(2,1)} %get-tuple-element.231), channel_id=1, source_target_pairs={{0,4},{1,3},{2,6},{3,1},{4,0},{5,7},{6,2},{7,5},{8,12},{9,11},{10,... | collective-permute-start | bytes 9437192 | tf_op jit(solution)/shard_map/ppermute | solution.py:104
  322.2 29.7 %collective-permute-start.18 = (bf16[8,96,768]{2,1,0:T(8,128)(2,1)}, bf16[8,96,768]{2,1,0:T(8,128)(2,1)}, u32[]{:S(2)}, u32[]{:S(2)}) collective-permute-start(bf16[8,96,768]{2,1,0:T(8,128)(2,1)} %get-tuple-element.143), channel_id=1, source_target_pairs={{0,2},{1,5},{2,0},{3,7},{4,6},{5,1},{6,4},{7,3},{8,10},{9,13},{10,... | collective-permute-start | bytes 3538952 | tf_op jit(solution)/shard_map/ppermute | solution.py:104
  342.4 48.2 %collective-permute-start.22 = (bf16[4,3,96,1536]{3,2,1,0:T(8,128)(2,1)}, bf16[4,3,96,1536]{3,2,1,0:T(8,128)(2,1)}, u32[]{:S(2)}, u32[]{:S(2)}) collective-permute-start(bf16[4,3,96,1536]{3,2,1,0:T(8,128)(2,1)} %get-tuple-element.151), channel_id=1, source_target_pairs={{0,2},{1,5},{2,0},{3,7},{4,6},{5,1},{6,4},{7,3},{8,10},{9,13},{10,... | collective-permute-start | bytes 10616840 | tf_op jit(solution)/shard_map/ppermute | solution.py:104
  349.5 86.3 %collective-permute-start.27 = (bf16[4,96,2048]{2,1,0:T(8,128)(2,1)}, bf16[4,96,2048]{2,1,0:T(8,128)(2,1)}, u32[]{:S(2)}, u32[]{:S(2)}) collective-permute-start(bf16[4,96,2048]{2,1,0:T(8,128)(2,1)} %get-tuple-element.237), channel_id=1, source_target_pairs={{0,16},{1,17},{2,18},{3,19},{4,20},{5,21},{6,22},{7,23},{8,24},{9,... | collective-permute-start | bytes 4718600 | tf_op jit(solution)/shard_map/ppermute | solution.py:104
  366.1 59.8 %collective-permute-start.19 = (bf16[512,1536]{1,0:T(8,128)(2,1)}, bf16[512,1536]{1,0:T(8,128)(2,1)}, u32[]{:S(2)}, u32[]{:S(2)}) collective-permute-start(bf16[512,1536]{1,0:T(8,128)(2,1)} %get-tuple-element.146), channel_id=1, source_target_pairs={{0,1},{1,0},{2,3},{3,2},{4,5},{5,4},{6,7},{7,6},{8,9},{9,8},{10,11... | collective-permute-start | bytes 4718600 | tf_op jit(solution)/shard_map/ppermute | solution.py:54
  371.9 18.7 %collective-permute-start.23 = (bf16[4,96,768]{2,1,0:T(8,128)(2,1)}, bf16[4,96,768]{2,1,0:T(8,128)(2,1)}, u32[]{:S(2)}, u32[]{:S(2)}) collective-permute-start(bf16[4,96,768]{2,1,0:T(8,128)(2,1)} %get-tuple-element.245), channel_id=1, source_target_pairs={{0,4},{1,3},{2,6},{3,1},{4,0},{5,7},{6,2},{7,5},{8,12},{9,11},{10,... | collective-permute-start | bytes 1769480 | tf_op jit(solution)/shard_map/ppermute | solution.py:104
  381.8 76.0 %collective-permute-start.26 = (bf16[2,2,96,2048]{3,2,1,0:T(8,128)(2,1)}, bf16[2,2,96,2048]{3,2,1,0:T(8,128)(2,1)}, u32[]{:S(2)}, u32[]{:S(2)}) collective-permute-start(bf16[2,2,96,2048]{3,2,1,0:T(8,128)(2,1)} %get-tuple-element.235), channel_id=1, source_target_pairs={{0,8},{1,9},{2,10},{3,11},{4,12},{5,13},{6,14},{7,15},{8,0},{9,1},... | collective-permute-start | bytes 4718600 | tf_op jit(solution)/shard_map/ppermute | solution.py:104
  407.1 14.9 %collective-permute-start.24 = (bf16[128,2048]{1,0:T(8,128)(2,1)}, bf16[128,2048]{1,0:T(8,128)(2,1)}, u32[]{:S(2)}, u32[]{:S(2)}) collective-permute-start(bf16[128,2048]{1,0:T(8,128)(2,1)} %constant_dynamic-slice_fusion.2), channel_id=1, source_target_pairs={{0,1},{1,0},{2,3},{3,2},{4,5},{5,4},{6,7},{7,6},{8,9},{9,8},{10,11... | collective-permute-start | bytes 1572872 | tf_op jit(solution)/shard_map/ppermute | solution.py:30
  418.5 39.3 %collective-permute-start.28 = (bf16[2,3,96,1536]{3,2,1,0:T(8,128)(2,1)}, bf16[2,3,96,1536]{3,2,1,0:T(8,128)(2,1)}, u32[]{:S(2)}, u32[]{:S(2)}) collective-permute-start(bf16[2,3,96,1536]{3,2,1,0:T(8,128)(2,1)} %get-tuple-element.233), channel_id=1, source_target_pairs={{0,4},{1,3},{2,6},{3,1},{4,0},{5,7},{6,2},{7,5},{8,12},{9,11},{10,... | collective-permute-start | bytes 5308424 | tf_op jit(solution)/shard_map/ppermute | solution.py:104
  421.9 35.9 %collective-permute-start.29 = (bf16[2,96,768]{2,1,0:T(8,128)(2,1)}, bf16[2,96,768]{2,1,0:T(8,128)(2,1)}, u32[]{:S(2)}, u32[]{:S(2)}) collective-permute-start(bf16[2,96,768]{2,1,0:T(8,128)(2,1)} %get-tuple-element.256), channel_id=1, source_target_pairs={{0,8},{1,9},{2,10},{3,11},{4,12},{5,13},{6,14},{7,15},{8,0},{9,1},... | collective-permute-start | bytes 884744 | tf_op jit(solution)/shard_map/ppermute | solution.py:104
  499.0 34.6 %collective-permute-start.30 = (bf16[16,2,128,96]{2,3,1,0:T(8,128)(2,1)}, bf16[16,2,128,96]{2,3,1,0:T(8,128)(2,1)}, u32[]{:S(2)}, u32[]{:S(2)}) collective-permute-start(bf16[16,2,128,96]{2,3,1,0:T(8,128)(2,1)} %copy.36), channel_id=1, source_target_pairs={{0,1},{1,0},{2,3},{3,2},{4,5},{5,4},{6,7},{7,6},{8,9},{9,8},{10,11... | collective-permute-start | bytes 2359304 | tf_op jit(solution)/shard_map/ppermute | solution.py:30
  501.3 48.1 %collective-permute-start.31 = (bf16[1,3,96,1536]{3,2,1,0:T(8,128)(2,1)}, bf16[1,3,96,1536]{3,2,1,0:T(8,128)(2,1)}, u32[]{:S(2)}, u32[]{:S(2)}) collective-permute-start(bf16[1,3,96,1536]{3,2,1,0:T(8,128)(2,1)} %add_convert_fusion.11), channel_id=1, source_target_pairs={{0,8},{1,9},{2,10},{3,11},{4,12},{5,13},{6,14},{7,15},{8,0},{9,1},... | collective-permute-start | bytes 2654216 | tf_op jit(solution)/shard_map/ppermute | solution.py:104
  511.7 37.8 %collective-permute-start.32 = (bf16[2,96,2048]{2,1,0:T(8,128)(2,1)}, bf16[2,96,2048]{2,1,0:T(8,128)(2,1)}, u32[]{:S(2)}, u32[]{:S(2)}) collective-permute-start(bf16[2,96,2048]{2,1,0:T(8,128)(2,1)} %get-tuple-element.243), channel_id=1, source_target_pairs={{0,2},{1,5},{2,0},{3,7},{4,6},{5,1},{6,4},{7,3},{8,10},{9,13},{10,... | collective-permute-start | bytes 2359304 | tf_op jit(solution)/shard_map/ppermute | solution.py:104
  513.2 18.8 %collective-permute-start.35 = (bf16[1,96,768]{2,1,0:T(8,128)(2,1)S(1)}, bf16[1,96,768]{2,1,0:T(8,128)(2,1)S(1)}, u32[]{:S(2)}, u32[]{:S(2)}) collective-permute-start(bf16[1,96,768]{2,1,0:T(8,128)(2,1)S(1)} %add_convert_fusion.22), channel_id=1, source_target_pairs={{0,16},{1,17},{2,18},{3,19},{4,20},{5,21},{6,22},{7,23},{8,24},{9,... | collective-permute-start | bytes 442376 | tf_op jit(solution)/shard_map/ppermute | solution.py:104
  517.4 40.7 %collective-permute-start.36 = (bf16[1,2,96,2048]{3,2,1,0:T(8,128)(2,1)}, bf16[1,2,96,2048]{3,2,1,0:T(8,128)(2,1)}, u32[]{:S(2)}, u32[]{:S(2)}) collective-permute-start(bf16[1,2,96,2048]{3,2,1,0:T(8,128)(2,1)} %add_convert_fusion.13), channel_id=1, source_target_pairs={{0,16},{1,17},{2,18},{3,19},{4,20},{5,21},{6,22},{7,23},{8,24},{9,... | collective-permute-start | bytes 2359304 | tf_op jit(solution)/shard_map/ppermute | solution.py:104
  551.5 10.7 %collective-permute-start.33 = (bf16[3,96,768]{2,1,0:T(8,128)(2,1)S(1)}, bf16[3,96,768]{2,1,0:T(8,128)(2,1)S(1)}, u32[]{:S(2)}, u32[]{:S(2)}) collective-permute-start(bf16[3,96,768]{2,1,0:T(8,128)(2,1)S(1)} %dynamic-slice_bitcast_fusion.2), channel_id=1, source_target_pairs={{0,1},{1,0},{2,3},{3,2},{4,5},{5,4},{6,7},{7,6},{8,9},{9,8},{10,11... | collective-permute-start | bytes 1327112 | tf_op jit(solution)/shard_map/ppermute | solution.py:30
  562.3 21.3 %collective-permute-start.34 = (bf16[1,3,96,768]{3,2,1,0:T(8,128)(2,1)S(1)}, bf16[1,3,96,768]{3,2,1,0:T(8,128)(2,1)S(1)}, u32[]{:S(2)}, u32[]{:S(2)}) collective-permute-start(bf16[1,3,96,768]{3,2,1,0:T(8,128)(2,1)S(1)} %fusion.25), channel_id=1, source_target_pairs={{0,16},{1,17},{2,18},{3,19},{4,20},{5,21},{6,22},{7,23},{8,24},{9,... | collective-permute-start | bytes 1327112 | tf_op jit(solution)/shard_map/ppermute | solution.py:104
  (54 other events, 546.5 us)
Sparse Core Ops, SparseCore 0:
  13.0 194.2 all-gather.1

commit v8 on v7

--- a/solution.py
+++ b/solution.py
@@ -135,53 +135,61 @@
     return sum((p >> bit & 1) << i for i, bit in enumerate(reversed(order)))
 
 
-def swap_all_kernel(text_ref, mod_ref, small_ref, text_out, mod_out, small_out, sends, gets, own):
+SUMS = 3
+
+
+def swap_all_kernel(text_ref, mod_ref, text_out, mod_out, sum_out, part, sends, gets, own):
     dpn, me = lax.axis_size("dp"), lax.axis_index("dp")
-    copies = []
-    for r in range(1, dpn):
-        peer = me ^ r
-        moves = (
-            (text_ref.at[peer], text_out.at[me]),
-            (mod_ref.at[peer], mod_out.at[me]),
-            (small_ref, small_out.at[me]),
-        )
-        for i, (src, dst) in enumerate(moves):
+
+    def to_all(kind, source, target):
+        copies = []
+        for r in range(1, dpn):
+            peer = me ^ r
             copies.append(
                 pltpu.make_async_remote_copy(
-                    src_ref=src, dst_ref=dst, send_sem=sends.at[i, r], recv_sem=gets.at[i, r],
+                    src_ref=source(peer), dst_ref=target,
+                    send_sem=sends.at[kind, r], recv_sem=gets.at[kind, r],
                     device_id={"dp": peer}, device_id_type=pl.DeviceIdType.MESH,
                 )
             )
             copies[-1].start()
+        return copies
+
+    mods = to_all(0, lambda peer: mod_ref.at[peer], mod_out.at[me])
+    texts = to_all(1, lambda peer: text_ref.at[peer], text_out.at[me])
     local = (
         pltpu.make_async_copy(text_ref.at[me], text_out.at[me], own.at[0]),
         pltpu.make_async_copy(mod_ref.at[me], mod_out.at[me], own.at[1]),
-        pltpu.make_async_copy(small_ref, small_out.at[me], own.at[2]),
     )
     for copy in local:
         copy.start()
-    for copy in (*local, *copies):
+    for copy in (*local, *mods):
         copy.wait()
-
-
-def swap_all(text, mods, small):
+    part[...] = jnp.sum(mod_out[...], axis=0)
+    sums = to_all(2, lambda peer: part, sum_out.at[me])
+    mine = pltpu.make_async_copy(part, sum_out.at[me], own.at[2])
+    mine.start()
+    for copy in (mine, *sums, *texts):
+        copy.wait()
+
+
+def swap_all(text, mods):
     vmem = pl.BlockSpec(memory_space=pltpu.VMEM)
     count = text.shape[0]
     return pl.pallas_call(
         swap_all_kernel,
-        in_specs=[vmem] * 3,
+        in_specs=[vmem] * 2,
         out_specs=[vmem] * 3,
         out_shape=[
-            jax.ShapeDtypeStruct(text.shape, text.dtype),
-            jax.ShapeDtypeStruct(mods.shape, mods.dtype),
-            jax.ShapeDtypeStruct((count,) + small.shape, small.dtype),
+            jax.ShapeDtypeStruct(v.shape, v.dtype) for v in (text, mods, mods)
         ],
         scratch_shapes=[
+            pltpu.VMEM(mods.shape[1:], mods.dtype),
             pltpu.SemaphoreType.DMA((3, count)), pltpu.SemaphoreType.DMA((3, count)),
             pltpu.SemaphoreType.DMA((3,)),
         ],
         compiler_params=pltpu.CompilerParams(has_side_effects=True),
-    )(text, mods, small)
+    )(text, mods)
 
 
 def advance(chains, value):
@@ -900,8 +908,9 @@
     grad_tk = (inv_t * (text_hat - normed_t * mean_t)).astype(BF16)
     text_pair = jnp.stack([grad_tk, dtv.astype(BF16)])
     pair_all = jnp.concatenate(natural(gather_rot(text_pair)), axis=-1)
-    pair_all = advance([qkv_chain, out_chain], pair_all)
+    pair_all = advance([qkv_chain], pair_all)
     text_in = text_bwd(pair_all, w_text)
+    text_in, grad_first = advance([qkv_chain], (text_in, grad_first))
     text_in = jnp.concatenate(natural(exchange_rot(text_in, 0)), axis=1)
 
     inverse_one = inverse_rms(x_own)
@@ -920,16 +929,32 @@
     stamp = jnp.full((1, D), timesteps[0].astype(F32))
     gate_pad = jnp.pad(gate_total, (0, own_d - gate_total.shape[0]))[None]
     small = jnp.concatenate([block_of(sums[4:], f, 1), gain_q, gain_k, gain_text, gate_pad], axis=0)
+    small = jnp.pad(small.reshape(-1), (0, dpn * SUMS * 128 - small.size))
     mods = jnp.concatenate([sums[:4], stamp], axis=0).reshape(5, dpn, share).transpose(1, 0, 2)
-    mods = jnp.pad(mods, ((0, 0), (0, 3), (0, -share % 128)))
-    small = jnp.pad(small.reshape(-1, 128), ((0, -small.size // 128 % 8), (0, 0)))
-    outgoing = block_of(pair_all, f, 1).reshape(2, TEXT // n, dpn, share).transpose(2, 0, 1, 3)
-    mods = advance([wide_chain, down_chain, qkv_chain, out_chain], mods)
-    pair_cols, mods, small = swap_all(outgoing, mods, small)
-    pair_cols = jnp.concatenate(natural(gather_rot(pair_cols)), axis=2)
-    pair_cols = pair_cols.transpose(0, 2, 1, 3).reshape(dpn * TEXT, 2 * share)
-    text_grad = dot(pair_cols, text_all, 0, 0).reshape(2, share, TW // n)
-    total = jnp.sum(small, axis=0)[: 6 * own_d // 128].reshape(6, own_d)
+    mods = jnp.pad(mods, ((0, 0), (0, 0), (0, -share % 128)))
+    mods = jnp.concatenate([mods, small.reshape(dpn, SUMS, 128)], axis=1)
+    outgoing = block_of(pair_all.transpose(0, 2, 1), f, 2)
+    outgoing = outgoing.reshape(2, dpn, share, TEXT // n).transpose(1, 0, 2, 3)
+    mods = advance([wide_chain, down_chain, out_chain], mods)
+    pair_cols, mods, small = swap_all(outgoing, mods)
+    chains = [out_chain, down_chain] if paired else [qkv_chain, out_chain, down_chain]
+    if paired:
+        qkv_got = qkv_chain.got
+        (pair_cols, mods, small), qkv_chain.got = lax.optimization_barrier(
+            ((pair_cols, mods, small), qkv_got)
+        )
+        qkv_chain.step()
+        own_side = f == (me >> low_bits[-1] + 1)
+        mine, got = exchange_rot(qkv_chain.last[0].astype(BF16), 2)
+        got, wide_chain.keep = lax.optimization_barrier((got, wide_chain.keep))
+        qkv_chain = Halving(
+            bits[-1:], jnp.where(own_side, mine, got)[None], jnp.where(own_side, got, mine)[None]
+        )
+    pair_cols = advance(chains, pair_cols)
+    pair_cols = jnp.concatenate(natural(gather_rot(pair_cols)), axis=3)
+    pair_cols = pair_cols.transpose(1, 2, 0, 3).reshape(2 * share, dpn * TEXT)
+    text_grad = dot(pair_cols, text_all).reshape(2, share, TW // n)
+    total = small[:, 5 : 5 + SUMS].reshape(-1)[: 6 * own_d].reshape(6, own_d)
     times = time_embed(mods[:, 4, 0])
     times = lax.dynamic_slice_in_dim(times, f * own_te, own_te, 1).astype(F32)
     ada_grad = lax.dot_general(
@@ -937,13 +962,6 @@
         precision=lax.Precision.HIGHEST,
     ).reshape(4, share, own_te)
 
-    text_grad = advance([qkv_chain, down_chain], text_grad)
-    if paired:
-        own_side = f == (me >> low_bits[-1] + 1)
-        mine, got = exchange_rot(qkv_chain.last[0].astype(BF16), 2)
-        qkv_chain = Halving(
-            bits[-1:], jnp.where(own_side, mine, got)[None], jnp.where(own_side, got, mine)[None]
-        )
     for chain in (out_chain, down_chain, wide_chain, qkv_chain):
         while chain.got is not None:
             chain.step()

time: 597 us -> 597 us (level)
  Pallas kernels: 315 us -> 335 us
  local copies, waits for them, and re-layouts: 36.6 us -> 27.2 us
  waiting for transfers between devices: 72.5 us -> 66 us
    pallas_call x1, Pallas kernels: 36.9 us -> 56.4 us  [swap_all(): pl.pallas_call(swap_all_kernel, in_specs=[vmem] * 2, out_specs=[vmem] * 3...]
    ppermute x16, waiting for transfers between devices: 61.4 us -> 54 us  [dp_swap(): return lax.ppermute(value, ('dp', 'fsdp'), pairs)]
  transfers between devices with their start and end apart: 39 -> 39, of which waited for: 12 -> 12; matrix products, arithmetic and copies ran while one was open for 23% -> 22% of each run, Pallas kernels for 47% -> 57%
where the time goes in v8:
time: 597 us; the launch traced here: 592 us
  Pallas kernels  335 us (56%)
  other arithmetic  101 us (17%)
  waiting for transfers between devices  66 us (11%)
  local copies, waits for them, and re-layouts  27.2 us (5%)
  starting transfers between devices  26.6 us (4%)
  matrix products  17.8 us (3%)
  between operations  16.6 us (3%)
    pallas_call x1, Pallas kernels, ffn(): pl.pallas_call(functools.partial(ffn_kernel, orders), grid=(hid // bc,),...  90.2 us
    pallas_call x2, Pallas kernels, attn_backward(): pl.pallas_call(attn_bwd_kernel, grid=(blocks,), in_specs=[scalar, col, co...  68.8 us
    pallas_call x1, Pallas kernels, swap_all(): pl.pallas_call(swap_all_kernel, in_specs=[vmem] * 2, out_specs=[vmem] * 3...  56.4 us
    ppermute x16, waiting for transfers between devices, dp_swap(): return lax.ppermute(value, ('dp', 'fsdp'), pairs)  54 us
    pallas_call x1, Pallas kernels, attn_forward(): pl.pallas_call(attn_fwd_kernel, grid=(blocks,), in_specs=[scalar, three,...  32.1 us
    convert_element_type x7, other arithmetic, step(): self.keep = add(slice(half)).astype(BF16)  31.4 us
    ppermute x16, starting transfers between devices, dp_swap(): return lax.ppermute(value, ('dp', 'fsdp'), pairs)  22.1 us
    pallas_call x1, Pallas kernels, project_grad(): pl.pallas_call(functools.partial(project_grad_kernel, order), grid=(3,),...  18.3 us
  transfers between devices with their start and end apart: 39, of which 12 were waited for; matrix products, arithmetic and copies ran while one was open for 22% of the time, Pallas kernels for 57%

profile of v8, /device:TPU:0, one launch (start us, length us, event | category | flops | bytes accessed | tf_op | source)
XLA Modules:
  0.0 592.0 jit_solution(18299278790252109078)
XLA Ops:
  17.9 4.7 fusion.2
  23.3 16.2 %shard_map.222 = f32[2,256,1536]{2,1,0:T(8,128)} custom-call(bf16[256,2048]{1,0:T(8,128)(2,1)} %pad_maximum_fusion.2.x_ref, bf16[2048,2,1536]{2,1,0:T(2,128)(2,1)} %w_ref.5), custom_call_target="tpu_custom_call" | custom-call | tf_op jit(solution)/shard_map/pallas_call | solution.py:430
  53.5 14.4 %shard_map.221 = (bf16[1024,1536]{1,0:T(8,128)(2,1)}, f32[3,1024,768]{2,1,0:T(8,128)}, f32[8,1024]{1,0:T(8,128)}) custom-call(s32[2]{0:T(128)} %pad_add_fusion.1.id_ref, bf16[512,1536]{1,0:T(8,128)(2,1)} %bitcast.129, bf16[512,1536]{1,0:T(8,128)(2,1)} %collective-permute-done.1.xp_ref, f32[1,1536]{1,0:T(1,128)} %get-tuple-element.262.front_ref, ...), custom_call_target="tpu_custom_call" | custom-call | tf_op jit(solution)/shard_map/pallas_call | solution.py:586
  70.7 32.1 %shard_map.223 = (bf16[1024,768]{1,0:T(8,128)(2,1)}, bf16[1024,768]{1,0:T(8,128)(2,1)}, bf16[1024,768]{1,0:T(8,128)(2,1)}, bf16[1024,768]{1,0:T(8,128)(2,1)}, f3...) custom-call(s32[1]{0:T(128)S(6)} %copy.48.len_ref, ...), custom_call_target="tpu_custom_call" | custom-call | tf_op jit(solution)/shard_map/pallas_call | solution.py:373
  109.0 4.5 multiply_reduce_fusion.6
  121.0 90.2 %shard_map.224 = (bf16[8,2,96,2048]{3,2,1,0:T(8,128)(2,1)}, bf16[8,2,96,2048]{3,2,1,0:T(8,128)(2,1)}, bf16[8,96,2048]{2,1,0:T(8,128)(2,1)}, bf16[8,96,2048]{2,1,...) custom-call(s32[2]{0:T(128)} %pad_add_fusion.1.id_ref, ...), custom_call_target="tpu_custom_call" | custom-call | tf_op jit(solution)/shard_map/pallas_call | solution.py:529
  217.9 4.3 multiply_reduce_fusion
  222.2 5.9 fusion.7
  233.2 9.6 %shard_map.225 = (f32[1024,768]{1,0:T(8,128)}, bf16[8,96,768]{2,1,0:T(8,128)(2,1)}, bf16[8,96,768]{2,1,0:T(8,128)(2,1)}) custom-call(s32[2]{0:T(128)} %pad_add_fusion.1.id_ref, bf16[512,1536]{1,0:T(8,128)(2,1)} %copy-done.17, bf16[512,1536]{1,0:T(8,128)(2,1)} %collective-permute-done.13.refs_1_, bf16[768,1536]{1,0:T(8,128)(2,1)} %refs_2_.1, ...), custom_call_target="tpu_custom_call" | custom-call | tf_op jit(solution)/shard_map/pallas_call | solution.py:714
  242.8 44.5 %shard_map.226 = (f32[3,1024,512]{2,1,0:T(8,128)}, f32[256,512]{1,0:T(8,128)}, f32[256,512]{1,0:T(8,128)}, f32[8,1024]{1,0:T(8,128)}, f32[1,512]{1,0:T(1,128)}, /*index=5*/f32[1,512]{1,0:T(1,128)}, f32[1,512]{1,0:T(1,128)}) custom-call(s32[1]{0:T(128)S(6)} %copy.48.len_ref, bf16[1024,768]{1,0:T(8,128)(2,1)} %get-tuple-element.113.q_ref, ...), custom_call_target="tpu_custom_call" | custom-call | tf_op jit(solution)/shard_map/pallas_call | solution.py:388
  287.3 8.1 %add_convert_fusion = (bf16[4,2,96,2048]{3,2,1,0:T(8,128)(2,1)}, bf16[4,2,96,2048]{3,2,1,0:T(8,128)(2,1)}) fusion(bf16[8,2,96,2048]{3,2,1,0:T(8,128)(2,1)} %collective-permute-done.14, bf16[8,2,96,2048]{3,2,1,0:T(8,128)(2,1)} %get-tuple-element.148), kind=kLoop, calls=%fused_computation.4 | loop fusion | flops 12582912 | bytes 18874368 | tf_op jit(solution)/shard_map/convert_element_type | solution.py:130
  297.6 24.3 %shard_map.227 = (f32[3,1024,256]{2,1,0:T(8,128)}, f32[256,256]{1,0:T(8,128)}, f32[256,256]{1,0:T(8,128)}, f32[8,1024]{1,0:T(8,128)}, f32[1,256]{1,0:T(1,128)}, /*index=5*/f32[1,256]{1,0:T(1,128)}, f32[1,256]{1,0:T(1,128)}) custom-call(s32[1]{0:T(128)S(6)} %copy.48.len_ref, bf16[1024,768]{1,0:T(8,128)(2,1)} %get-tuple-element.113.q_ref, ...), custom_call_target="tpu_custom_call" | custom-call | tf_op jit(solution)/shard_map/pallas_call | solution.py:388
  324.6 18.3 %shard_map.228 = (bf16[4,3,96,1536]{3,2,1,0:T(8,128)(2,1)}, bf16[4,3,96,1536]{3,2,1,0:T(8,128)(2,1)}, bf16[3,1024,768]{2,1,0:T(8,128)(2,1)}) custom-call(s32[2]{0:T(128)} %pad_add_fusion.1.id_ref, f32[3,1024,512]{2,1,0:T(8,128)} %get-tuple-element.144.da_ref, f32[3,1024,256]{2,1,0:T(8,128)} %get-tuple-element.145.db_ref, ...), custom_call_target="tpu_custom_call" | custom-call | tf_op jit(solution)/shard_map/pallas_call | solution.py:633
  353.4 5.0 add_convert_fusion.5
  364.1 14.1 %shard_map.230 = (f32[512,1536]{1,0:T(8,128)}, bf16[512,1536]{1,0:T(8,128)(2,1)}) custom-call(s32[2]{0:T(128)} %pad_add_fusion.1.id_ref, bf16[3,1024,768]{2,1,0:T(8,128)(2,1)} %get-tuple-element.157.g_ref, bf16[3,768,1536]{2,1,0:T(8,128)(2,1)} %bitcast.128, bf16[3,768,768]{2,1,0:T(8,128)(2,1)} %collective-permute-done.2.got_ref), custom_call_target="tpu_custom_call" | custom-call | tf_op jit(solution)/shard_map/pallas_call | solution.py:679
  381.1 10.0 %collective-permute-done.21 = bf16[4,3,96,1536]{3,2,1,0:T(8,128)(2,1)} collective-permute-done((bf16[4,3,96,1536]{3,2,1,0:T(8,128)(2,1)}, bf16[4,3,96,1536]{3,2,1,0:T(8,128)(2,1)}, u32[]{:S(2)}, u32[]{:S(2)}) %collective-permute-start.21) | collective-permute-done | bytes 3538976 | tf_op jit(solution)/shard_map/ppermute | solution.py:104
  391.1 5.0 add_convert_fusion.2
  397.6 4.9 add_convert_fusion.4
  404.3 14.6 %shard_map.229 = bf16[256,2048]{1,0:T(8,128)(2,1)} custom-call(bf16[2,256,1536]{2,1,0:T(8,128)(2,1)} %pad_maximum_fusion.1.g_ref, bf16[2048,2,1536]{2,1,0:T(2,128)(2,1)} %w_ref.5), custom_call_target="tpu_custom_call" | custom-call | tf_op jit(solution)/shard_map/pallas_call | solution.py:449
  440.1 23.7 %collective-permute-done.26 = bf16[2,2,96,2048]{3,2,1,0:T(8,128)(2,1)} collective-permute-done((bf16[2,2,96,2048]{3,2,1,0:T(8,128)(2,1)}, bf16[2,2,96,2048]{3,2,1,0:T(8,128)(2,1)}, u32[]{:S(2)}, u32[]{:S(2)}) %collective-permute-start.26) | collective-permute-done | bytes 1572896 | tf_op jit(solution)/shard_map/ppermute | solution.py:104
  477.2 56.4 %shard_map.231 = (bf16[16,2,96,128]{3,2,1,0:T(8,128)(2,1)}, f32[16,8,128]{2,1,0:T(8,128)}, f32[16,8,128]{2,1,0:T(8,128)}) custom-call(bf16[16,2,96,128]{3,2,1,0:T(8,128)(2,1)} %bitcast.133, f32[16,8,128]{2,1,0:T(8,128)} %select_maximum_fusion.mod_ref), custom_call_target="tpu_custom_call" | custom-call | tf_op jit(solution)/shard_map/pallas_call | solution.py:179
  548.0 5.7 collective-permute-done.35
  564.7 4.6 fusion
  569.3 14.6 %collective-permute-done.34 = bf16[1,3,96,768]{3,2,1,0:T(8,128)(2,1)S(1)} collective-permute-done((bf16[1,3,96,768]{3,2,1,0:T(8,128)(2,1)S(1)}, bf16[1,3,96,768]{3,2,1,0:T(8,128)(2,1)S(1)}, u32[]{:S(2)}, u32[]{:S(2)}) %collective-permute-start.34) | collective-permute-done | bytes 442400 | tf_op jit(solution)/shard_map/ppermute | solution.py:104
  (325 shorter events, 139.6 us)
Async XLA Ops:
  7.2 207.1 %all-gather.2.cloned.1.call-start = ((), (), s32[]{:S(2)}) async-start(), calls=%async_computation | async-start | bytes 17825792 | tf_op jit(solution)/shard_map/all_gather | solution.py:789
  16.8 36.7 %collective-permute-start.2 = (bf16[3,768,768]{2,1,0:T(8,128)(2,1)}, bf16[3,768,768]{2,1,0:T(8,128)(2,1)}, u32[]{:S(2)}, u32[]{:S(2)}) collective-permute-start(bf16[3,768,768]{2,1,0:T(8,128)(2,1)} %dynamic-slice_bitcast_fusion), channel_id=1, source_target_pairs={{0,1},{1,0},{2,3},{3,2},{4,5},{5,4},{6,7},{7,6},{8,9},{9,8},{10,11... | collective-permute-start | bytes 10616840 | tf_op jit(solution)/shard_map/ppermute | solution.py:30
  22.6 26.8 %collective-permute-start = (f32[4,1536]{1,0:T(4,128)S(1)}, f32[4,1536]{1,0:T(4,128)S(1)}, u32[]{:S(2)}, u32[]{:S(2)}) collective-permute-start(f32[4,1536]{1,0:T(4,128)S(1)} %bitcast.140), channel_id=1, source_target_pairs={{0,1},{1,0},{2,3},{3,2},{4,5},{5,4},{6,7},{7,6},{8,9},{9,8},{10,11... | collective-permute-start | bytes 73736 | tf_op jit(solution)/shard_map/ppermute | solution.py:30
  22.8 30.7 %collective-permute-start.1 = (bf16[512,1536]{1,0:T(8,128)(2,1)S(1)}, bf16[512,1536]{1,0:T(8,128)(2,1)}, u32[]{:S(2)}, u32[]{:S(2)}) collective-permute-start(bf16[512,1536]{1,0:T(8,128)(2,1)S(1)} %bitcast.130), channel_id=1, source_target_pairs={{0,1},{1,0},{2,3},{3,2},{4,5},{5,4},{6,7},{7,6},{8,9},{9,8},{10,11... | collective-permute-start | bytes 4718600 | tf_op jit(solution)/shard_map/ppermute | solution.py:30
  23.2 23.1 %collective-permute-start.4 = (s32[2,512]{1,0:T(2,128)S(1)}, s32[2,512]{1,0:T(2,128)S(1)}, u32[]{:S(2)}, u32[]{:S(2)}) collective-permute-start(s32[2,512]{1,0:T(2,128)S(1)} %bitcast.153), channel_id=1, source_target_pairs={{0,1},{1,0},{2,3},{3,2},{4,5},{5,4},{6,7},{7,6},{8,9},{9,8},{10,11... | collective-permute-start | bytes 12296 | tf_op jit(solution)/shard_map/ppermute | solution.py:30
  211.2 76.0 %collective-permute-start.14 = (bf16[8,2,96,2048]{3,2,1,0:T(8,128)(2,1)}, bf16[8,2,96,2048]{3,2,1,0:T(8,128)(2,1)}, u32[]{:S(2)}, u32[]{:S(2)}) collective-permute-start(bf16[8,2,96,2048]{3,2,1,0:T(8,128)(2,1)} %get-tuple-element.135), channel_id=1, source_target_pairs={{0,2},{1,5},{2,0},{3,7},{4,6},{5,1},{6,4},{7,3},{8,10},{9,13},{10,... | collective-permute-start | bytes 18874376 | tf_op jit(solution)/shard_map/ppermute | solution.py:104
  214.8 72.5 %collective-permute-start.15 = (bf16[8,96,2048]{2,1,0:T(8,128)(2,1)}, bf16[8,96,2048]{2,1,0:T(8,128)(2,1)}, u32[]{:S(2)}, u32[]{:S(2)}) collective-permute-start(bf16[8,96,2048]{2,1,0:T(8,128)(2,1)} %get-tuple-element.136), channel_id=1, source_target_pairs={{0,8},{1,9},{2,10},{3,11},{4,12},{5,13},{6,14},{7,15},{8,0},{9,1},... | collective-permute-start | bytes 9437192 | tf_op jit(solution)/shard_map/ppermute | solution.py:104
  295.4 51.6 %collective-permute-start.17 = (bf16[4,2,96,2048]{3,2,1,0:T(8,128)(2,1)}, bf16[4,2,96,2048]{3,2,1,0:T(8,128)(2,1)}, u32[]{:S(2)}, u32[]{:S(2)}) collective-permute-start(bf16[4,2,96,2048]{3,2,1,0:T(8,128)(2,1)} %get-tuple-element.234), channel_id=1, source_target_pairs={{0,4},{1,3},{2,6},{3,1},{4,0},{5,7},{6,2},{7,5},{8,12},{9,11},{10,... | collective-permute-start | bytes 9437192 | tf_op jit(solution)/shard_map/ppermute | solution.py:104
  323.3 23.6 %collective-permute-start.18 = (bf16[8,96,768]{2,1,0:T(8,128)(2,1)}, bf16[8,96,768]{2,1,0:T(8,128)(2,1)}, u32[]{:S(2)}, u32[]{:S(2)}) collective-permute-start(bf16[8,96,768]{2,1,0:T(8,128)(2,1)} %get-tuple-element.150), channel_id=1, source_target_pairs={{0,2},{1,5},{2,0},{3,7},{4,6},{5,1},{6,4},{7,3},{8,10},{9,13},{10,... | collective-permute-start | bytes 3538952 | tf_op jit(solution)/shard_map/ppermute | solution.py:104
  343.0 48.2 %collective-permute-start.21 = (bf16[4,3,96,1536]{3,2,1,0:T(8,128)(2,1)}, bf16[4,3,96,1536]{3,2,1,0:T(8,128)(2,1)}, u32[]{:S(2)}, u32[]{:S(2)}) collective-permute-start(bf16[4,3,96,1536]{3,2,1,0:T(8,128)(2,1)} %get-tuple-element.155), channel_id=1, source_target_pairs={{0,2},{1,5},{2,0},{3,7},{4,6},{5,1},{6,4},{7,3},{8,10},{9,13},{10,... | collective-permute-start | bytes 10616840 | tf_op jit(solution)/shard_map/ppermute | solution.py:104
  353.2 24.9 %collective-permute-start.20 = (bf16[2,256,768]{2,1,0:T(8,128)(2,1)}, bf16[2,256,768]{2,1,0:T(8,128)(2,1)}, u32[]{:S(2)}, u32[]{:S(2)}) collective-permute-start(bf16[2,256,768]{2,1,0:T(8,128)(2,1)} %maximum_maximum_fusion), channel_id=1, source_target_pairs={{0,1},{1,0},{2,3},{3,2},{4,5},{5,4},{6,7},{7,6},{8,9},{9,8},{10,11... | collective-permute-start | bytes 2359304 | tf_op jit(solution)/shard_map/ppermute | solution.py:30
  358.4 81.6 %collective-permute-start.27 = (bf16[4,96,2048]{2,1,0:T(8,128)(2,1)}, bf16[4,96,2048]{2,1,0:T(8,128)(2,1)}, u32[]{:S(2)}, u32[]{:S(2)}) collective-permute-start(bf16[4,96,2048]{2,1,0:T(8,128)(2,1)} %get-tuple-element.240), channel_id=1, source_target_pairs={{0,16},{1,17},{2,18},{3,19},{4,20},{5,21},{6,22},{7,23},{8,24},{9,... | collective-permute-start | bytes 4718600 | tf_op jit(solution)/shard_map/ppermute | solution.py:104
  363.6 76.5 %collective-permute-start.28 = (bf16[4,96,768]{2,1,0:T(8,128)(2,1)}, bf16[4,96,768]{2,1,0:T(8,128)(2,1)}, u32[]{:S(2)}, u32[]{:S(2)}) collective-permute-start(bf16[4,96,768]{2,1,0:T(8,128)(2,1)} %get-tuple-element.250), channel_id=1, source_target_pairs={{0,4},{1,3},{2,6},{3,1},{4,0},{5,7},{6,2},{7,5},{8,12},{9,11},{10,... | collective-permute-start | bytes 1769480 | tf_op jit(solution)/shard_map/ppermute | solution.py:104
  378.2 47.2 %collective-permute-start.22 = (bf16[512,1536]{1,0:T(8,128)(2,1)}, bf16[512,1536]{1,0:T(8,128)(2,1)}, u32[]{:S(2)}, u32[]{:S(2)}) collective-permute-start(bf16[512,1536]{1,0:T(8,128)(2,1)} %get-tuple-element.159), channel_id=1, source_target_pairs={{0,1},{1,0},{2,3},{3,2},{4,5},{5,4},{6,7},{7,6},{8,9},{9,8},{10,11... | collective-permute-start | bytes 4718600 | tf_op jit(solution)/shard_map/ppermute | solution.py:54
  396.2 32.2 %collective-permute-start.23 = (bf16[2,3,96,1536]{3,2,1,0:T(8,128)(2,1)}, bf16[2,3,96,1536]{3,2,1,0:T(8,128)(2,1)}, u32[]{:S(2)}, u32[]{:S(2)}) collective-permute-start(bf16[2,3,96,1536]{3,2,1,0:T(8,128)(2,1)} %get-tuple-element.236), channel_id=1, source_target_pairs={{0,4},{1,3},{2,6},{3,1},{4,0},{5,7},{6,2},{7,5},{8,12},{9,11},{10,... | collective-permute-start | bytes 5308424 | tf_op jit(solution)/shard_map/ppermute | solution.py:104
  402.5 61.3 %collective-permute-start.26 = (bf16[2,2,96,2048]{3,2,1,0:T(8,128)(2,1)}, bf16[2,2,96,2048]{3,2,1,0:T(8,128)(2,1)}, u32[]{:S(2)}, u32[]{:S(2)}) collective-permute-start(bf16[2,2,96,2048]{3,2,1,0:T(8,128)(2,1)} %get-tuple-element.238), channel_id=1, source_target_pairs={{0,8},{1,9},{2,10},{3,11},{4,12},{5,13},{6,14},{7,15},{8,0},{9,1},... | collective-permute-start | bytes 4718600 | tf_op jit(solution)/shard_map/ppermute | solution.py:104
  434.2 101.9 %collective-permute-start.29 = (bf16[1,3,96,1536]{3,2,1,0:T(8,128)(2,1)}, bf16[1,3,96,1536]{3,2,1,0:T(8,128)(2,1)}, u32[]{:S(2)}, u32[]{:S(2)}) collective-permute-start(bf16[1,3,96,1536]{3,2,1,0:T(8,128)(2,1)} %add_convert_fusion.11), channel_id=1, source_target_pairs={{0,8},{1,9},{2,10},{3,11},{4,12},{5,13},{6,14},{7,15},{8,0},{9,1},... | collective-permute-start | bytes 2654216 | tf_op jit(solution)/shard_map/ppermute | solution.py:104
  439.0 94.7 %collective-permute-start.24 = (bf16[128,2048]{1,0:T(8,128)(2,1)S(1)}, bf16[128,2048]{1,0:T(8,128)(2,1)}, u32[]{:S(2)}, u32[]{:S(2)}) collective-permute-start(bf16[128,2048]{1,0:T(8,128)(2,1)S(1)} %constant_dynamic-slice_fusion.1), channel_id=1, source_target_pairs={{0,1},{1,0},{2,3},{3,2},{4,5},{5,4},{6,7},{7,6},{8,9},{9,8},{10,11... | collective-permute-start | bytes 1572872 | tf_op jit(solution)/shard_map/ppermute | solution.py:30
  467.5 68.8 %collective-permute-start.31 = (bf16[2,96,2048]{2,1,0:T(8,128)(2,1)}, bf16[2,96,2048]{2,1,0:T(8,128)(2,1)}, u32[]{:S(2)}, u32[]{:S(2)}) collective-permute-start(bf16[2,96,2048]{2,1,0:T(8,128)(2,1)} %get-tuple-element.246), channel_id=1, source_target_pairs={{0,2},{1,5},{2,0},{3,7},{4,6},{5,1},{6,4},{7,3},{8,10},{9,13},{10,... | collective-permute-start | bytes 2359304 | tf_op jit(solution)/shard_map/ppermute | solution.py:104
  470.1 66.3 %collective-permute-start.30 = (bf16[2,96,768]{2,1,0:T(8,128)(2,1)}, bf16[2,96,768]{2,1,0:T(8,128)(2,1)}, u32[]{:S(2)}, u32[]{:S(2)}) collective-permute-start(bf16[2,96,768]{2,1,0:T(8,128)(2,1)} %get-tuple-element.261), channel_id=1, source_target_pairs={{0,8},{1,9},{2,10},{3,11},{4,12},{5,13},{6,14},{7,15},{8,0},{9,1},... | collective-permute-start | bytes 884744 | tf_op jit(solution)/shard_map/ppermute | solution.py:104
  473.3 84.4 %collective-permute-start.36 = (bf16[1,2,96,2048]{3,2,1,0:T(8,128)(2,1)}, bf16[1,2,96,2048]{3,2,1,0:T(8,128)(2,1)}, u32[]{:S(2)}, u32[]{:S(2)}) collective-permute-start(bf16[1,2,96,2048]{3,2,1,0:T(8,128)(2,1)} %get-tuple-element.247), channel_id=1, source_target_pairs={{0,16},{1,17},{2,18},{3,19},{4,20},{5,21},{6,22},{7,23},{8,24},{9,... | collective-permute-start | bytes 2359304 | tf_op jit(solution)/shard_map/ppermute | solution.py:104
  538.2 17.3 %collective-permute-start.37 = (bf16[1,96,2048]{2,1,0:T(8,128)(2,1)}, bf16[1,96,2048]{2,1,0:T(8,128)(2,1)}, u32[]{:S(2)}, u32[]{:S(2)}) collective-permute-start(bf16[1,96,2048]{2,1,0:T(8,128)(2,1)} %add_convert_fusion.18), channel_id=1, source_target_pairs={{0,4},{1,3},{2,6},{3,1},{4,0},{5,7},{6,2},{7,5},{8,12},{9,11},{10,... | collective-permute-start | bytes 1179656 | tf_op jit(solution)/shard_map/ppermute | solution.py:104
  544.9 16.9 %collective-permute-start.32 = (bf16[16,2,96,128]{3,2,1,0:T(8,128)(2,1)}, bf16[16,2,96,128]{3,2,1,0:T(8,128)(2,1)}, u32[]{:S(2)}, u32[]{:S(2)}) collective-permute-start(bf16[16,2,96,128]{3,2,1,0:T(8,128)(2,1)} %get-tuple-element.185), channel_id=1, source_target_pairs={{0,1},{1,0},{2,3},{3,2},{4,5},{5,4},{6,7},{7,6},{8,9},{9,8},{10,11... | collective-permute-start | bytes 2359304 | tf_op jit(solution)/shard_map/ppermute | solution.py:30
  561.7 22.2 %collective-permute-start.34 = (bf16[1,3,96,768]{3,2,1,0:T(8,128)(2,1)S(1)}, bf16[1,3,96,768]{3,2,1,0:T(8,128)(2,1)S(1)}, u32[]{:S(2)}, u32[]{:S(2)}) collective-permute-start(bf16[1,3,96,768]{3,2,1,0:T(8,128)(2,1)S(1)} %fusion.25), channel_id=1, source_target_pairs={{0,16},{1,17},{2,18},{3,19},{4,20},{5,21},{6,22},{7,23},{8,24},{9,... | collective-permute-start | bytes 1327112 | tf_op jit(solution)/shard_map/ppermute | solution.py:104
  (79 other events, 1038.3 us)
Sparse Core Ops, SparseCore 0:
  12.9 194.2 all-gather.1

commit v9 on v8

--- a/solution.py
+++ b/solution.py
@@ -761,7 +761,7 @@
     dpn, me = lax.axis_size("dp"), lax.axis_index("dp")
     bits = list(range(dp_bits()))
     low_bits = bits[:-1]
-    late = bits[2:] + bits[:2]
+    late = bits[2:3] + bits[:2] + bits[3:]
     own_d = D // n
     local = hidden_in.shape[1]
     tokens = n * local
@@ -876,7 +876,9 @@
         keep, send, grads = project_grad(
             ids, part_a[0], part_b[0], pre, stats, gain3, first_all, dpn, low_bits
         )
-        part_a, part_b, grads = advance([wide_chain, out_chain], (part_a[1:], part_b[1:], grads))
+        part_a, part_b, grads = advance(
+            [wide_chain, down_chain, out_chain], (part_a[1:], part_b[1:], grads)
+        )
         qkv_chain = Halving(low_bits, keep, send)
         parts = project_back(ids, grads, w_flat, w_parts[1])
     else:
@@ -908,7 +910,7 @@
     grad_tk = (inv_t * (text_hat - normed_t * mean_t)).astype(BF16)
     text_pair = jnp.stack([grad_tk, dtv.astype(BF16)])
     pair_all = jnp.concatenate(natural(gather_rot(text_pair)), axis=-1)
-    pair_all = advance([qkv_chain], pair_all)
+    pair_all = advance([qkv_chain, wide_chain, down_chain, out_chain], pair_all)
     text_in = text_bwd(pair_all, w_text)
     text_in, grad_first = advance([qkv_chain], (text_in, grad_first))
     text_in = jnp.concatenate(natural(exchange_rot(text_in, 0)), axis=1)
@@ -935,7 +937,7 @@
     mods = jnp.concatenate([mods, small.reshape(dpn, SUMS, 128)], axis=1)
     outgoing = block_of(pair_all.transpose(0, 2, 1), f, 2)
     outgoing = outgoing.reshape(2, dpn, share, TEXT // n).transpose(1, 0, 2, 3)
-    mods = advance([wide_chain, down_chain, out_chain], mods)
+    mods = advance([down_chain, out_chain], mods)
     pair_cols, mods, small = swap_all(outgoing, mods)
     chains = [out_chain, down_chain] if paired else [qkv_chain, out_chain, down_chain]
     if paired:

time: 597 us -> 572 us (0.958)
  waiting for transfers between devices: 66 us -> 38.8 us
  Pallas kernels: 335 us -> 327 us
    ppermute x16, waiting for transfers between devices: 54 us -> 27 us  [dp_swap(): return lax.ppermute(value, ('dp', 'fsdp'), pairs)]
    pallas_call x1, Pallas kernels: 56.4 us -> 48.5 us  [swap_all(): pl.pallas_call(swap_all_kernel, in_specs=[vmem] * 2, out_specs=[vmem] * 3...]
  transfers between devices with their start and end apart: 39 -> 39, of which waited for: 12 -> 11; matrix products, arithmetic and copies ran while one was open for 22% -> 24% of each run, Pallas kernels for 57% -> 58%
where the time goes in v9:
time: 572 us; the launch traced here: 567 us
  Pallas kernels  327 us (57%)
  other arithmetic  104 us (18%)
  waiting for transfers between devices  38.8 us (7%)
  local copies, waits for them, and re-layouts  29.5 us (5%)
  starting transfers between devices  27.6 us (5%)
  matrix products  21.4 us (4%)
  between operations  16.4 us (3%)
    pallas_call x1, Pallas kernels, ffn(): pl.pallas_call(functools.partial(ffn_kernel, orders), grid=(hid // bc,),...  90.3 us
    pallas_call x2, Pallas kernels, attn_backward(): pl.pallas_call(attn_bwd_kernel, grid=(blocks,), in_specs=[scalar, col, co...  68.8 us
    pallas_call x1, Pallas kernels, swap_all(): pl.pallas_call(swap_all_kernel, in_specs=[vmem] * 2, out_specs=[vmem] * 3...  48.5 us
    pallas_call x1, Pallas kernels, attn_forward(): pl.pallas_call(attn_fwd_kernel, grid=(blocks,), in_specs=[scalar, three,...  32.1 us
    convert_element_type x7, other arithmetic, step(): self.keep = add(slice(half)).astype(BF16)  32.1 us
    ppermute x16, waiting for transfers between devices, dp_swap(): return lax.ppermute(value, ('dp', 'fsdp'), pairs)  27 us
    ppermute x16, starting transfers between devices, dp_swap(): return lax.ppermute(value, ('dp', 'fsdp'), pairs)  22.6 us
    pallas_call x1, Pallas kernels, project_grad(): pl.pallas_call(functools.partial(project_grad_kernel, order), grid=(3,),...  18.7 us
  transfers between devices with their start and end apart: 39, of which 11 were waited for; matrix products, arithmetic and copies ran while one was open for 24% of the time, Pallas kernels for 58%

profile of v9, /device:TPU:0, one launch (start us, length us, event | category | flops | bytes accessed | tf_op | source)
XLA Modules:
  0.0 567.1 jit_solution(1516275251983162819)
XLA Ops:
  12.8 4.0 dynamic-slice_bitcast_fusion
  17.9 4.7 fusion.2
  23.3 16.2 %shard_map.222 = f32[2,256,1536]{2,1,0:T(8,128)} custom-call(bf16[256,2048]{1,0:T(8,128)(2,1)} %pad_maximum_fusion.2.x_ref, bf16[2048,2,1536]{2,1,0:T(2,128)(2,1)} %w_ref.5), custom_call_target="tpu_custom_call" | custom-call | tf_op jit(solution)/shard_map/pallas_call | solution.py:430
  53.4 14.4 %shard_map.221 = (bf16[1024,1536]{1,0:T(8,128)(2,1)}, f32[3,1024,768]{2,1,0:T(8,128)}, f32[8,1024]{1,0:T(8,128)}) custom-call(s32[2]{0:T(128)} %pad_add_fusion.1.id_ref, bf16[512,1536]{1,0:T(8,128)(2,1)} %bitcast.129, bf16[512,1536]{1,0:T(8,128)(2,1)} %collective-permute-done.1.xp_ref, f32[1,1536]{1,0:T(1,128)} %get-tuple-element.266.front_ref, ...), custom_call_target="tpu_custom_call" | custom-call | tf_op jit(solution)/shard_map/pallas_call | solution.py:586
  70.6 32.1 %shard_map.223 = (bf16[1024,768]{1,0:T(8,128)(2,1)}, bf16[1024,768]{1,0:T(8,128)(2,1)}, bf16[1024,768]{1,0:T(8,128)(2,1)}, bf16[1024,768]{1,0:T(8,128)(2,1)}, f3...) custom-call(s32[1]{0:T(128)S(6)} %copy.48.len_ref, ...), custom_call_target="tpu_custom_call" | custom-call | tf_op jit(solution)/shard_map/pallas_call | solution.py:373
  120.4 90.3 %shard_map.224 = (bf16[8,2,96,2048]{3,2,1,0:T(8,128)(2,1)}, bf16[8,2,96,2048]{3,2,1,0:T(8,128)(2,1)}, bf16[8,96,2048]{2,1,0:T(8,128)(2,1)}, bf16[8,96,2048]{2,1,...) custom-call(s32[2]{0:T(128)} %pad_add_fusion.1.id_ref, ...), custom_call_target="tpu_custom_call" | custom-call | tf_op jit(solution)/shard_map/pallas_call | solution.py:529
  217.3 4.3 multiply_reduce_fusion
  221.6 5.8 %fusion.7 = (f32[1536]{0:T(1024)S(1)}, bf16[1,512,1536]{2,1,0:T(8,128)(2,1)}, f32[1536]{0:T(1024)S(1)}, f32[512,1536]{1,0:T(8,128)S(1)}) fusion(f32[512,1536]{1,0:T(8,128)} %get-tuple-element.111, bf16[512,1536]{1,0:T(8,128)(2,1)S(1)} %collective-permute-done.11, bf16[1,512,1536]{2,1,0:T(8,128)(2,1)} %param.19, f32[512,1536]{1,0:T(8,128)S(1)} %copy-done.1, ...), kind=kLoop, calls=%fused_computation.18 | loop fusion | flops 16512000 | bytes 23627776 | tf_op jit(solution)/shard_map/reduce_sum | solution.py:848
  232.5 9.6 %shard_map.225 = (f32[1024,768]{1,0:T(8,128)}, bf16[8,96,768]{2,1,0:T(8,128)(2,1)}, bf16[8,96,768]{2,1,0:T(8,128)(2,1)}) custom-call(s32[2]{0:T(128)} %pad_add_fusion.1.id_ref, bf16[512,1536]{1,0:T(8,128)(2,1)} %copy-done.18, bf16[512,1536]{1,0:T(8,128)(2,1)} %collective-permute-done.13.refs_1_, bf16[768,1536]{1,0:T(8,128)(2,1)} %refs_2_.1, ...), custom_call_target="tpu_custom_call" | custom-call | tf_op jit(solution)/shard_map/pallas_call | solution.py:714
  242.1 44.5 %shard_map.226 = (f32[3,1024,512]{2,1,0:T(8,128)}, f32[256,512]{1,0:T(8,128)}, f32[256,512]{1,0:T(8,128)}, f32[8,1024]{1,0:T(8,128)}, f32[1,512]{1,0:T(1,128)}, /*index=5*/f32[1,512]{1,0:T(1,128)}, f32[1,512]{1,0:T(1,128)}) custom-call(s32[1]{0:T(128)S(6)} %copy.48.len_ref, bf16[1024,768]{1,0:T(8,128)(2,1)} %get-tuple-element.115.q_ref, ...), custom_call_target="tpu_custom_call" | custom-call | tf_op jit(solution)/shard_map/pallas_call | solution.py:388
  286.7 8.1 %add_convert_fusion = (bf16[4,2,96,2048]{3,2,1,0:T(8,128)(2,1)}, bf16[4,2,96,2048]{3,2,1,0:T(8,128)(2,1)}) fusion(bf16[8,2,96,2048]{3,2,1,0:T(8,128)(2,1)} %collective-permute-done.14, bf16[8,2,96,2048]{3,2,1,0:T(8,128)(2,1)} %get-tuple-element.150), kind=kLoop, calls=%fused_computation.4 | loop fusion | flops 12582912 | bytes 18874368 | tf_op jit(solution)/shard_map/convert_element_type | solution.py:130
  297.0 6.1 %add_convert_fusion.5 = (bf16[4,96,2048]{2,1,0:T(8,128)(2,1)}, bf16[4,96,2048]{2,1,0:T(8,128)(2,1)}) fusion(bf16[8,96,2048]{2,1,0:T(8,128)(2,1)} %collective-permute-done.15, bf16[8,96,2048]{2,1,0:T(8,128)(2,1)} %get-tuple-element.152), kind=kLoop, calls=%fused_computation.34 | loop fusion | flops 6291456 | bytes 9437184 | tf_op jit(solution)/shard_map/convert_element_type | solution.py:130
  306.4 24.3 %shard_map.227 = (f32[3,1024,256]{2,1,0:T(8,128)}, f32[256,256]{1,0:T(8,128)}, f32[256,256]{1,0:T(8,128)}, f32[8,1024]{1,0:T(8,128)}, f32[1,256]{1,0:T(1,128)}, /*index=5*/f32[1,256]{1,0:T(1,128)}, f32[1,256]{1,0:T(1,128)}) custom-call(s32[1]{0:T(128)S(6)} %copy.48.len_ref, bf16[1024,768]{1,0:T(8,128)(2,1)} %get-tuple-element.115.q_ref, ...), custom_call_target="tpu_custom_call" | custom-call | tf_op jit(solution)/shard_map/pallas_call | solution.py:388
  334.0 18.7 %shard_map.228 = (bf16[4,3,96,1536]{3,2,1,0:T(8,128)(2,1)}, bf16[4,3,96,1536]{3,2,1,0:T(8,128)(2,1)}, bf16[3,1024,768]{2,1,0:T(8,128)(2,1)}) custom-call(s32[2]{0:T(128)} %pad_add_fusion.1.id_ref, f32[3,1024,512]{2,1,0:T(8,128)} %get-tuple-element.146.da_ref, f32[3,1024,256]{2,1,0:T(8,128)} %get-tuple-element.147.db_ref, ...), custom_call_target="tpu_custom_call" | custom-call | tf_op jit(solution)/shard_map/pallas_call | solution.py:633
  353.3 7.7 %collective-permute-done.19 = bf16[8,96,768]{2,1,0:T(8,128)(2,1)} collective-permute-done((bf16[8,96,768]{2,1,0:T(8,128)(2,1)}, bf16[8,96,768]{2,1,0:T(8,128)(2,1)}, u32[]{:S(2)}, u32[]{:S(2)}) %collective-permute-start.19) | collective-permute-done | bytes 1179680 | tf_op jit(solution)/shard_map/ppermute | solution.py:104
  365.4 5.0 add_convert_fusion.4
  388.3 13.7 %shard_map.230 = (f32[512,1536]{1,0:T(8,128)}, bf16[512,1536]{1,0:T(8,128)(2,1)}) custom-call(s32[2]{0:T(128)} %pad_add_fusion.1.id_ref, bf16[3,1024,768]{2,1,0:T(8,128)(2,1)} %get-tuple-element.165.g_ref, bf16[3,768,1536]{2,1,0:T(8,128)(2,1)} %bitcast.128, bf16[3,768,768]{2,1,0:T(8,128)(2,1)} %collective-permute-done.2.got_ref), custom_call_target="tpu_custom_call" | custom-call | tf_op jit(solution)/shard_map/pallas_call | solution.py:679
  404.9 8.7 %collective-permute-done.22 = bf16[4,3,96,1536]{3,2,1,0:T(8,128)(2,1)} collective-permute-done((bf16[4,3,96,1536]{3,2,1,0:T(8,128)(2,1)}, bf16[4,3,96,1536]{3,2,1,0:T(8,128)(2,1)}, u32[]{:S(2)}, u32[]{:S(2)}) %collective-permute-start.22) | collective-permute-done | bytes 3538976 | tf_op jit(solution)/shard_map/ppermute | solution.py:104
  417.1 4.9 add_convert_fusion.2
  427.9 14.7 %shard_map.229 = bf16[256,2048]{1,0:T(8,128)(2,1)} custom-call(bf16[2,256,1536]{2,1,0:T(8,128)(2,1)} %pad_maximum_fusion.1.g_ref, bf16[2048,2,1536]{2,1,0:T(2,128)(2,1)} %w_ref.5), custom_call_target="tpu_custom_call" | custom-call | tf_op jit(solution)/shard_map/pallas_call | solution.py:449
  462.8 4.2 fusion.15
  472.5 48.5 %shard_map.231 = (bf16[16,2,96,128]{3,2,1,0:T(8,128)(2,1)}, f32[16,8,128]{2,1,0:T(8,128)}, f32[16,8,128]{2,1,0:T(8,128)}) custom-call(bf16[16,2,96,128]{3,2,1,0:T(8,128)(2,1)} %bitcast.133, f32[16,8,128]{2,1,0:T(8,128)} %select_maximum_fusion.mod_ref), custom_call_target="tpu_custom_call" | custom-call | tf_op jit(solution)/shard_map/pallas_call | solution.py:179
  539.7 8.7 %fusion = f32[2048,2,96]{0,2,1:T(8,128)} fusion(bf16[2,96,4096]{2,1,0:T(8,128)(2,1)S(1)} %bitcast.136, bf16[4096,2048]{1,0:T(8,128)(2,1)} %all-gather.2.cloned.1.call-done), kind=kOutput, calls=%fused_computation | convolution fusion | flops 3221225472 | bytes 19922944 | tf_op jit(solution)/shard_map/dot_general | solution.py:25
  548.4 10.6 %collective-permute-done.36 = bf16[1,3,96,768]{3,2,1,0:T(8,128)(2,1)S(1)} collective-permute-done((bf16[1,3,96,768]{3,2,1,0:T(8,128)(2,1)S(1)}, bf16[1,3,96,768]{3,2,1,0:T(8,128)(2,1)S(1)}, u32[]{:S(2)}, u32[]{:S(2)}) %collective-permute-start.36) | collective-permute-done | bytes 442400 | tf_op jit(solution)/shard_map/ppermute | solution.py:104
  (301 shorter events, 140.7 us)
Async XLA Ops:
  7.2 206.5 %all-gather.2.cloned.1.call-start = ((), (), s32[]{:S(2)}) async-start(), calls=%async_computation | async-start | bytes 17825792 | tf_op jit(solution)/shard_map/all_gather | solution.py:789
  16.7 36.6 %collective-permute-start.2 = (bf16[3,768,768]{2,1,0:T(8,128)(2,1)}, bf16[3,768,768]{2,1,0:T(8,128)(2,1)}, u32[]{:S(2)}, u32[]{:S(2)}) collective-permute-start(bf16[3,768,768]{2,1,0:T(8,128)(2,1)} %dynamic-slice_bitcast_fusion), channel_id=1, source_target_pairs={{0,1},{1,0},{2,3},{3,2},{4,5},{5,4},{6,7},{7,6},{8,9},{9,8},{10,11... | collective-permute-start | bytes 10616840 | tf_op jit(solution)/shard_map/ppermute | solution.py:30
  22.5 26.8 %collective-permute-start = (f32[4,1536]{1,0:T(4,128)S(1)}, f32[4,1536]{1,0:T(4,128)S(1)}, u32[]{:S(2)}, u32[]{:S(2)}) collective-permute-start(f32[4,1536]{1,0:T(4,128)S(1)} %bitcast.140), channel_id=1, source_target_pairs={{0,1},{1,0},{2,3},{3,2},{4,5},{5,4},{6,7},{7,6},{8,9},{9,8},{10,11... | collective-permute-start | bytes 73736 | tf_op jit(solution)/shard_map/ppermute | solution.py:30
  22.8 30.6 %collective-permute-start.1 = (bf16[512,1536]{1,0:T(8,128)(2,1)S(1)}, bf16[512,1536]{1,0:T(8,128)(2,1)}, u32[]{:S(2)}, u32[]{:S(2)}) collective-permute-start(bf16[512,1536]{1,0:T(8,128)(2,1)S(1)} %bitcast.130), channel_id=1, source_target_pairs={{0,1},{1,0},{2,3},{3,2},{4,5},{5,4},{6,7},{7,6},{8,9},{9,8},{10,11... | collective-permute-start | bytes 4718600 | tf_op jit(solution)/shard_map/ppermute | solution.py:30
  23.1 23.0 %collective-permute-start.4 = (s32[2,512]{1,0:T(2,128)S(1)}, s32[2,512]{1,0:T(2,128)S(1)}, u32[]{:S(2)}, u32[]{:S(2)}) collective-permute-start(s32[2,512]{1,0:T(2,128)S(1)} %bitcast.153), channel_id=1, source_target_pairs={{0,1},{1,0},{2,3},{3,2},{4,5},{5,4},{6,7},{7,6},{8,9},{9,8},{10,11... | collective-permute-start | bytes 12296 | tf_op jit(solution)/shard_map/ppermute | solution.py:30
  210.6 76.0 %collective-permute-start.14 = (bf16[8,2,96,2048]{3,2,1,0:T(8,128)(2,1)}, bf16[8,2,96,2048]{3,2,1,0:T(8,128)(2,1)}, u32[]{:S(2)}, u32[]{:S(2)}) collective-permute-start(bf16[8,2,96,2048]{3,2,1,0:T(8,128)(2,1)} %get-tuple-element.137), channel_id=1, source_target_pairs={{0,2},{1,5},{2,0},{3,7},{4,6},{5,1},{6,4},{7,3},{8,10},{9,13},{10,... | collective-permute-start | bytes 18874376 | tf_op jit(solution)/shard_map/ppermute | solution.py:104
  214.2 72.5 %collective-permute-start.15 = (bf16[8,96,2048]{2,1,0:T(8,128)(2,1)}, bf16[8,96,2048]{2,1,0:T(8,128)(2,1)}, u32[]{:S(2)}, u32[]{:S(2)}) collective-permute-start(bf16[8,96,2048]{2,1,0:T(8,128)(2,1)} %get-tuple-element.138), channel_id=1, source_target_pairs={{0,8},{1,9},{2,10},{3,11},{4,12},{5,13},{6,14},{7,15},{8,0},{9,1},... | collective-permute-start | bytes 9437192 | tf_op jit(solution)/shard_map/ppermute | solution.py:104
  294.8 66.2 %collective-permute-start.17 = (bf16[4,2,96,2048]{3,2,1,0:T(8,128)(2,1)}, bf16[4,2,96,2048]{3,2,1,0:T(8,128)(2,1)}, u32[]{:S(2)}, u32[]{:S(2)}) collective-permute-start(bf16[4,2,96,2048]{3,2,1,0:T(8,128)(2,1)} %get-tuple-element.238), channel_id=1, source_target_pairs={{0,4},{1,3},{2,6},{3,1},{4,0},{5,7},{6,2},{7,5},{8,12},{9,11},{10,... | collective-permute-start | bytes 9437192 | tf_op jit(solution)/shard_map/ppermute | solution.py:104
  303.1 57.9 %collective-permute-start.18 = (bf16[4,96,2048]{2,1,0:T(8,128)(2,1)}, bf16[4,96,2048]{2,1,0:T(8,128)(2,1)}, u32[]{:S(2)}, u32[]{:S(2)}) collective-permute-start(bf16[4,96,2048]{2,1,0:T(8,128)(2,1)} %get-tuple-element.244), channel_id=1, source_target_pairs={{0,2},{1,5},{2,0},{3,7},{4,6},{5,1},{6,4},{7,3},{8,10},{9,13},{10,... | collective-permute-start | bytes 4718600 | tf_op jit(solution)/shard_map/ppermute | solution.py:104
  304.3 56.7 %collective-permute-start.19 = (bf16[8,96,768]{2,1,0:T(8,128)(2,1)}, bf16[8,96,768]{2,1,0:T(8,128)(2,1)}, u32[]{:S(2)}, u32[]{:S(2)}) collective-permute-start(bf16[8,96,768]{2,1,0:T(8,128)(2,1)} %get-tuple-element.154), channel_id=1, source_target_pairs={{0,2},{1,5},{2,0},{3,7},{4,6},{5,1},{6,4},{7,3},{8,10},{9,13},{10,... | collective-permute-start | bytes 3538952 | tf_op jit(solution)/shard_map/ppermute | solution.py:104
  352.7 60.9 %collective-permute-start.22 = (bf16[4,3,96,1536]{3,2,1,0:T(8,128)(2,1)}, bf16[4,3,96,1536]{3,2,1,0:T(8,128)(2,1)}, u32[]{:S(2)}, u32[]{:S(2)}) collective-permute-start(bf16[4,3,96,1536]{3,2,1,0:T(8,128)(2,1)} %get-tuple-element.159), channel_id=1, source_target_pairs={{0,2},{1,5},{2,0},{3,7},{4,6},{5,1},{6,4},{7,3},{8,10},{9,13},{10,... | collective-permute-start | bytes 10616840 | tf_op jit(solution)/shard_map/ppermute | solution.py:104
  363.9 49.8 %collective-permute-start.25 = (bf16[4,96,768]{2,1,0:T(8,128)(2,1)}, bf16[4,96,768]{2,1,0:T(8,128)(2,1)}, u32[]{:S(2)}, u32[]{:S(2)}) collective-permute-start(bf16[4,96,768]{2,1,0:T(8,128)(2,1)} %get-tuple-element.254), channel_id=1, source_target_pairs={{0,4},{1,3},{2,6},{3,1},{4,0},{5,7},{6,2},{7,5},{8,12},{9,11},{10,... | collective-permute-start | bytes 1769480 | tf_op jit(solution)/shard_map/ppermute | solution.py:104
  370.4 43.2 %collective-permute-start.23 = (bf16[2,2,96,2048]{3,2,1,0:T(8,128)(2,1)}, bf16[2,2,96,2048]{3,2,1,0:T(8,128)(2,1)}, u32[]{:S(2)}, u32[]{:S(2)}) collective-permute-start(bf16[2,2,96,2048]{3,2,1,0:T(8,128)(2,1)} %get-tuple-element.242), channel_id=1, source_target_pairs={{0,8},{1,9},{2,10},{3,11},{4,12},{5,13},{6,14},{7,15},{8,0},{9,1},... | collective-permute-start | bytes 4718600 | tf_op jit(solution)/shard_map/ppermute | solution.py:104
  375.9 26.1 %collective-permute-start.21 = (bf16[2,256,768]{2,1,0:T(8,128)(2,1)}, bf16[2,256,768]{2,1,0:T(8,128)(2,1)}, u32[]{:S(2)}, u32[]{:S(2)}) collective-permute-start(bf16[2,256,768]{2,1,0:T(8,128)(2,1)} %maximum_maximum_fusion), channel_id=1, source_target_pairs={{0,1},{1,0},{2,3},{3,2},{4,5},{5,4},{6,7},{7,6},{8,9},{9,8},{10,11... | collective-permute-start | bytes 2359304 | tf_op jit(solution)/shard_map/ppermute | solution.py:30
  379.2 34.5 %collective-permute-start.24 = (bf16[2,96,2048]{2,1,0:T(8,128)(2,1)}, bf16[2,96,2048]{2,1,0:T(8,128)(2,1)}, u32[]{:S(2)}, u32[]{:S(2)}) collective-permute-start(bf16[2,96,2048]{2,1,0:T(8,128)(2,1)} %get-tuple-element.252), channel_id=1, source_target_pairs={{0,4},{1,3},{2,6},{3,1},{4,0},{5,7},{6,2},{7,5},{8,12},{9,11},{10,... | collective-permute-start | bytes 2359304 | tf_op jit(solution)/shard_map/ppermute | solution.py:104
  402.0 50.2 %collective-permute-start.26 = (bf16[512,1536]{1,0:T(8,128)(2,1)}, bf16[512,1536]{1,0:T(8,128)(2,1)}, u32[]{:S(2)}, u32[]{:S(2)}) collective-permute-start(bf16[512,1536]{1,0:T(8,128)(2,1)} %get-tuple-element.167), channel_id=1, source_target_pairs={{0,1},{1,0},{2,3},{3,2},{4,5},{5,4},{6,7},{7,6},{8,9},{9,8},{10,11... | collective-permute-start | bytes 4718600 | tf_op jit(solution)/shard_map/ppermute | solution.py:54
  415.6 53.4 %collective-permute-start.31 = (bf16[2,96,768]{2,1,0:T(8,128)(2,1)}, bf16[2,96,768]{2,1,0:T(8,128)(2,1)}, u32[]{:S(2)}, u32[]{:S(2)}) collective-permute-start(bf16[2,96,768]{2,1,0:T(8,128)(2,1)} %get-tuple-element.265), channel_id=1, source_target_pairs={{0,8},{1,9},{2,10},{3,11},{4,12},{5,13},{6,14},{7,15},{8,0},{9,1},... | collective-permute-start | bytes 884744 | tf_op jit(solution)/shard_map/ppermute | solution.py:104
  422.0 33.2 %collective-permute-start.27 = (bf16[2,3,96,1536]{3,2,1,0:T(8,128)(2,1)}, bf16[2,3,96,1536]{3,2,1,0:T(8,128)(2,1)}, u32[]{:S(2)}, u32[]{:S(2)}) collective-permute-start(bf16[2,3,96,1536]{3,2,1,0:T(8,128)(2,1)} %get-tuple-element.240), channel_id=1, source_target_pairs={{0,4},{1,3},{2,6},{3,1},{4,0},{5,7},{6,2},{7,5},{8,12},{9,11},{10,... | collective-permute-start | bytes 5308424 | tf_op jit(solution)/shard_map/ppermute | solution.py:104
  425.3 43.7 %collective-permute-start.30 = (bf16[1,96,2048]{2,1,0:T(8,128)(2,1)}, bf16[1,96,2048]{2,1,0:T(8,128)(2,1)}, u32[]{:S(2)}, u32[]{:S(2)}) collective-permute-start(bf16[1,96,2048]{2,1,0:T(8,128)(2,1)} %add_convert_fusion.19), channel_id=1, source_target_pairs={{0,16},{1,17},{2,18},{3,19},{4,20},{5,21},{6,22},{7,23},{8,24},{9,... | collective-permute-start | bytes 1179656 | tf_op jit(solution)/shard_map/ppermute | solution.py:104
  446.6 86.2 %collective-permute-start.37 = (bf16[1,2,96,2048]{3,2,1,0:T(8,128)(2,1)}, bf16[1,2,96,2048]{3,2,1,0:T(8,128)(2,1)}, u32[]{:S(2)}, u32[]{:S(2)}) collective-permute-start(bf16[1,2,96,2048]{3,2,1,0:T(8,128)(2,1)} %get-tuple-element.249), channel_id=1, source_target_pairs={{0,16},{1,17},{2,18},{3,19},{4,20},{5,21},{6,22},{7,23},{8,24},{9,... | collective-permute-start | bytes 2359304 | tf_op jit(solution)/shard_map/ppermute | solution.py:104
  461.6 63.1 %collective-permute-start.32 = (bf16[1,3,96,1536]{3,2,1,0:T(8,128)(2,1)}, bf16[1,3,96,1536]{3,2,1,0:T(8,128)(2,1)}, u32[]{:S(2)}, u32[]{:S(2)}) collective-permute-start(bf16[1,3,96,1536]{3,2,1,0:T(8,128)(2,1)} %add_convert_fusion.11), channel_id=1, source_target_pairs={{0,8},{1,9},{2,10},{3,11},{4,12},{5,13},{6,14},{7,15},{8,0},{9,1},... | collective-permute-start | bytes 2654216 | tf_op jit(solution)/shard_map/ppermute | solution.py:104
  467.1 56.3 %collective-permute-start.28 = (bf16[128,2048]{1,0:T(8,128)(2,1)S(1)}, bf16[128,2048]{1,0:T(8,128)(2,1)S(1)}, u32[]{:S(2)}, u32[]{:S(2)}) collective-permute-start(bf16[128,2048]{1,0:T(8,128)(2,1)S(1)} %constant_dynamic-slice_fusion.1), channel_id=1, source_target_pairs={{0,1},{1,0},{2,3},{3,2},{4,5},{5,4},{6,7},{7,6},{8,9},{9,8},{10,11... | collective-permute-start | bytes 1572872 | tf_op jit(solution)/shard_map/ppermute | solution.py:30
  470.0 57.3 %collective-permute-start.33 = (bf16[1,96,768]{2,1,0:T(8,128)(2,1)S(1)}, bf16[1,96,768]{2,1,0:T(8,128)(2,1)}, u32[]{:S(2)}, u32[]{:S(2)}) collective-permute-start(bf16[1,96,768]{2,1,0:T(8,128)(2,1)S(1)} %add_convert_fusion.23), channel_id=1, source_target_pairs={{0,16},{1,17},{2,18},{3,19},{4,20},{5,21},{6,22},{7,23},{8,24},{9,... | collective-permute-start | bytes 442376 | tf_op jit(solution)/shard_map/ppermute | solution.py:104
  536.6 22.3 %collective-permute-start.36 = (bf16[1,3,96,768]{3,2,1,0:T(8,128)(2,1)S(1)}, bf16[1,3,96,768]{3,2,1,0:T(8,128)(2,1)S(1)}, u32[]{:S(2)}, u32[]{:S(2)}) collective-permute-start(bf16[1,3,96,768]{3,2,1,0:T(8,128)(2,1)S(1)} %fusion.25), channel_id=1, source_target_pairs={{0,16},{1,17},{2,18},{3,19},{4,20},{5,21},{6,22},{7,23},{8,24},{9,... | collective-permute-start | bytes 1327112 | tf_op jit(solution)/shard_map/ppermute | solution.py:104
  (67 other events, 1157.4 us)
Sparse Core Ops, SparseCore 0:
  12.9 194.2 all-gather.1

commit v10 on v9

--- a/solution.py
+++ b/solution.py
@@ -138,58 +138,49 @@
 SUMS = 3
 
 
-def swap_all_kernel(text_ref, mod_ref, text_out, mod_out, sum_out, part, sends, gets, own):
-    dpn, me = lax.axis_size("dp"), lax.axis_index("dp")
-
-    def to_all(kind, source, target):
-        copies = []
-        for r in range(1, dpn):
-            peer = me ^ r
-            copies.append(
-                pltpu.make_async_remote_copy(
-                    src_ref=source(peer), dst_ref=target,
-                    send_sem=sends.at[kind, r], recv_sem=gets.at[kind, r],
-                    device_id={"dp": peer}, device_id_type=pl.DeviceIdType.MESH,
-                )
-            )
-            copies[-1].start()
-        return copies
-
-    mods = to_all(0, lambda peer: mod_ref.at[peer], mod_out.at[me])
-    texts = to_all(1, lambda peer: text_ref.at[peer], text_out.at[me])
-    local = (
-        pltpu.make_async_copy(text_ref.at[me], text_out.at[me], own.at[0]),
-        pltpu.make_async_copy(mod_ref.at[me], mod_out.at[me], own.at[1]),
-    )
-    for copy in local:
-        copy.start()
-    for copy in (*local, *mods):
-        copy.wait()
-    part[...] = jnp.sum(mod_out[...], axis=0)
-    sums = to_all(2, lambda peer: part, sum_out.at[me])
-    mine = pltpu.make_async_copy(part, sum_out.at[me], own.at[2])
-    mine.start()
-    for copy in (mine, *sums, *texts):
-        copy.wait()
-
-
-def swap_all(text, mods):
+def to_all(source, target, sends, gets):
+    me = lax.axis_index("dp")
+    return [
+        pltpu.make_async_remote_copy(
+            src_ref=source(me ^ r), dst_ref=target, send_sem=sends.at[r], recv_sem=gets.at[r],
+            device_id={"dp": me ^ r}, device_id_type=pl.DeviceIdType.MESH,
+        )
+        for r in range(1, lax.axis_size("dp"))
+    ]
+
+
+def small_kernel(mod_ref, mod_out, sum_out, part, sends, gets, own):
+    me = lax.axis_index("dp")
+    steps = (
+        to_all(lambda peer: mod_ref.at[peer], mod_out.at[me], sends.at[0], gets.at[0])
+        + [pltpu.make_async_copy(mod_ref.at[me], mod_out.at[me], own.at[0])],
+        to_all(lambda peer: part, sum_out.at[me], sends.at[1], gets.at[1])
+        + [pltpu.make_async_copy(part, sum_out.at[me], own.at[1])],
+    )
+    for i, copies in enumerate(steps):
+        if i == 1:
+            part[...] = jnp.sum(mod_out[...], axis=0)
+        for copy in copies:
+            copy.start()
+        for copy in copies:
+            copy.wait()
+
+
+def small_exchange(mods):
     vmem = pl.BlockSpec(memory_space=pltpu.VMEM)
-    count = text.shape[0]
+    count = mods.shape[0]
     return pl.pallas_call(
-        swap_all_kernel,
-        in_specs=[vmem] * 2,
-        out_specs=[vmem] * 3,
-        out_shape=[
-            jax.ShapeDtypeStruct(v.shape, v.dtype) for v in (text, mods, mods)
-        ],
+        small_kernel,
+        in_specs=[vmem],
+        out_specs=[vmem] * 2,
+        out_shape=[jax.ShapeDtypeStruct(mods.shape, mods.dtype)] * 2,
         scratch_shapes=[
             pltpu.VMEM(mods.shape[1:], mods.dtype),
-            pltpu.SemaphoreType.DMA((3, count)), pltpu.SemaphoreType.DMA((3, count)),
-            pltpu.SemaphoreType.DMA((3,)),
+            pltpu.SemaphoreType.DMA((2, count)), pltpu.SemaphoreType.DMA((2, count)),
+            pltpu.SemaphoreType.DMA((2,)),
         ],
         compiler_params=pltpu.CompilerParams(has_side_effects=True),
-    )(text, mods)
+    )(mods)
 
 
 def advance(chains, value):
@@ -434,7 +425,17 @@
         out_shape=sds((2, x.shape[0], cols)),
     )(x, w)
 
-def text_bwd_kernel(g_ref, w_ref, o_ref):
+def text_bwd_kernel(g_ref, w_ref, pair_ref, o_ref, pair_out, sends, gets, own):
+    me = lax.axis_index("dp")
+    step = pl.program_id(0)
+    copies = to_all(lambda peer: pair_ref.at[peer], pair_out.at[me], sends, gets)
+    copies.append(pltpu.make_async_copy(pair_ref.at[me], pair_out.at[me], own))
+
+    @pl.when(step == 0)
+    def _():
+        for copy in copies:
+            copy.start()
+
     for b in range(w_ref.shape[0] // 128):
         rows = slice(b * 128, (b + 1) * 128)
         w = w_ref[rows].reshape(256, w_ref.shape[2])
@@ -443,15 +444,37 @@
             total = total + dot(g_ref[j], dot(pick(128, 256, 2, j), w).astype(BF16), 1, 1)
         o_ref[:, rows] = total.astype(BF16)
 
-def text_bwd(g, w):
+    @pl.when(step == pl.num_programs(0) - 1)
+    def _():
+        for copy in copies:
+            copy.wait()
+
+
+def text_bwd(g, w, pair):
     depth, _, cols = w.shape
     bk = 256
+    count = pair.shape[0]
     return pl.pallas_call(
-        text_bwd_kernel, grid=(depth // bk,),
-        in_specs=[pl.BlockSpec(g.shape, lambda i: (0, 0, 0)), pl.BlockSpec((bk, 2, cols), lambda i: (i, 0, 0))],
-        out_specs=pl.BlockSpec((g.shape[1], bk), lambda i: (0, i)),
-        out_shape=sds((g.shape[1], depth), BF16),
-    )(g, w)
+        text_bwd_kernel,
+        grid=(depth // bk,),
+        in_specs=[
+            pl.BlockSpec(g.shape, lambda i: (0, 0, 0)),
+            pl.BlockSpec((bk, 2, cols), lambda i: (i, 0, 0)),
+            pl.BlockSpec(memory_space=pl.ANY),
+        ],
+        out_specs=[
+            pl.BlockSpec((g.shape[1], bk), lambda i: (0, i)), pl.BlockSpec(memory_space=pl.ANY),
+        ],
+        out_shape=[
+            sds((g.shape[1], depth), BF16), jax.ShapeDtypeStruct(pair.shape, pair.dtype),
+        ],
+        scratch_shapes=[
+            pltpu.SemaphoreType.DMA((count,)), pltpu.SemaphoreType.DMA((count,)),
+            pltpu.SemaphoreType.DMA,
+        ],
+        compiler_params=pltpu.CompilerParams(has_side_effects=True),
+    )(g, w, pair)
+
 
 def put_relative(dst, src, me, f, count):
     rows = dst.shape[0] // count
@@ -901,9 +924,6 @@
     dtk, dtv, gain_q, gain_k, gate_g = (
         jnp.concatenate([part_a[i], part_b[i]], axis=1)[:, :own_d] for i in (0, 1, 3, 4, 5)
     )
-    gate_total = jnp.sum(gate_g[0].reshape(HEADS // n, HD), axis=1) * (
-        1.0 - head_tanh * head_tanh
-    )
     text_hat = dtk * gain_own[4]
     gain_text = jnp.sum(dtk * normed_t, axis=0, keepdims=True)
     mean_t = pair_sum(jnp.sum(text_hat * normed_t, -1, keepdims=True)) / D
@@ -911,7 +931,9 @@
     text_pair = jnp.stack([grad_tk, dtv.astype(BF16)])
     pair_all = jnp.concatenate(natural(gather_rot(text_pair)), axis=-1)
     pair_all = advance([qkv_chain, wide_chain, down_chain, out_chain], pair_all)
-    text_in = text_bwd(pair_all, w_text)
+    outgoing = block_of(pair_all.transpose(0, 2, 1), f, 2)
+    outgoing = outgoing.reshape(2, dpn, share, TEXT // n).transpose(1, 0, 2, 3)
+    text_in, pair_cols = text_bwd(pair_all, w_text, outgoing)
     text_in, grad_first = advance([qkv_chain], (text_in, grad_first))
     text_in = jnp.concatenate(natural(exchange_rot(text_in, 0)), axis=1)
 
@@ -929,22 +951,17 @@
     sums = [d_scale_attn, d_gate_attn, d_scale_ffn, d_gate_ffn, gain_one, gain_two]
     sums = pair_sum(jnp.stack(sums))
     stamp = jnp.full((1, D), timesteps[0].astype(F32))
-    gate_pad = jnp.pad(gate_total, (0, own_d - gate_total.shape[0]))[None]
-    small = jnp.concatenate([block_of(sums[4:], f, 1), gain_q, gain_k, gain_text, gate_pad], axis=0)
+    small = jnp.concatenate([block_of(sums[4:], f, 1), gain_q, gain_k, gain_text, gate_g], axis=0)
     small = jnp.pad(small.reshape(-1), (0, dpn * SUMS * 128 - small.size))
     mods = jnp.concatenate([sums[:4], stamp], axis=0).reshape(5, dpn, share).transpose(1, 0, 2)
     mods = jnp.pad(mods, ((0, 0), (0, 0), (0, -share % 128)))
     mods = jnp.concatenate([mods, small.reshape(dpn, SUMS, 128)], axis=1)
-    outgoing = block_of(pair_all.transpose(0, 2, 1), f, 2)
-    outgoing = outgoing.reshape(2, dpn, share, TEXT // n).transpose(1, 0, 2, 3)
     mods = advance([down_chain, out_chain], mods)
-    pair_cols, mods, small = swap_all(outgoing, mods)
+    mods, small = small_exchange(mods)
     chains = [out_chain, down_chain] if paired else [qkv_chain, out_chain, down_chain]
     if paired:
         qkv_got = qkv_chain.got
-        (pair_cols, mods, small), qkv_chain.got = lax.optimization_barrier(
-            ((pair_cols, mods, small), qkv_got)
-        )
+        (mods, small), qkv_chain.got = lax.optimization_barrier(((mods, small), qkv_got))
         qkv_chain.step()
         own_side = f == (me >> low_bits[-1] + 1)
         mine, got = exchange_rot(qkv_chain.last[0].astype(BF16), 2)
@@ -952,11 +969,14 @@
         qkv_chain = Halving(
             bits[-1:], jnp.where(own_side, mine, got)[None], jnp.where(own_side, got, mine)[None]
         )
-    pair_cols = advance(chains, pair_cols)
+    mods = advance(chains, mods)
     pair_cols = jnp.concatenate(natural(gather_rot(pair_cols)), axis=3)
     pair_cols = pair_cols.transpose(1, 2, 0, 3).reshape(2 * share, dpn * TEXT)
     text_grad = dot(pair_cols, text_all).reshape(2, share, TW // n)
     total = small[:, 5 : 5 + SUMS].reshape(-1)[: 6 * own_d].reshape(6, own_d)
+    gate_total = jnp.sum(total[5].reshape(HEADS // n, HD), axis=1) * (
+        1.0 - head_tanh * head_tanh
+    )
     times = time_embed(mods[:, 4, 0])
     times = lax.dynamic_slice_in_dim(times, f * own_te, own_te, 1).astype(F32)
     ada_grad = lax.dot_general(
@@ -976,7 +996,7 @@
         qkv_chain.last[0].transpose(2, 0, 1),
         out_chain.last[0].T,
         total[:5],
-        total[5, : HEADS // n],
+        gate_total,
         wide_chain.last[0].transpose(1, 0, 2),
         down_chain.last[0].T,
     )

time: 572 us -> 579 us (1.012)
  waiting for transfers between devices: 38.8 us -> 54.8 us
    ppermute x16, waiting for transfers between devices: 27 us -> 43.1 us  [dp_swap(): return lax.ppermute(value, ('dp', 'fsdp'), pairs)]
    pallas_call x1, Pallas kernels: 48.5 us -> 36.7 us  [small_exchange(): pl.pallas_call(small_kernel, in_specs=[vmem], out_specs=[vmem] * 2, out_s...]
    pallas_call x1, Pallas kernels: 14.7 us -> 24.9 us  [text_bwd(): pl.pallas_call(text_bwd_kernel, grid=(depth // bk,), in_specs=[pl.BlockSp...]
  transfers between devices with their start and end apart: 39 -> 39, of which waited for: 11 -> 12; matrix products, arithmetic and copies ran while one was open for 24% -> 23% of each run, Pallas kernels for 58% -> 57%
where the time goes in v10:
time: 579 us; the launch traced here: 573 us
  Pallas kernels  325 us (56%)
  other arithmetic  99.3 us (17%)
  waiting for transfers between devices  54.8 us (9%)
  starting transfers between devices  27.1 us (5%)
  local copies, waits for them, and re-layouts  26.3 us (5%)
  matrix products  21.9 us (4%)
  between operations  16.5 us (3%)
    pallas_call x1, Pallas kernels, ffn(): pl.pallas_call(functools.partial(ffn_kernel, orders), grid=(hid // bc,),...  90.2 us
    pallas_call x2, Pallas kernels, attn_backward(): pl.pallas_call(attn_bwd_kernel, grid=(blocks,), in_specs=[scalar, col, co...  68.8 us
    ppermute x16, waiting for transfers between devices, dp_swap(): return lax.ppermute(value, ('dp', 'fsdp'), pairs)  43.1 us
    pallas_call x1, Pallas kernels, small_exchange(): pl.pallas_call(small_kernel, in_specs=[vmem], out_specs=[vmem] * 2, out_s...  36.7 us
    pallas_call x1, Pallas kernels, attn_forward(): pl.pallas_call(attn_fwd_kernel, grid=(blocks,), in_specs=[scalar, three,...  32.1 us
    convert_element_type x7, other arithmetic, step(): self.keep = add(slice(half)).astype(BF16)  32.1 us
    pallas_call x1, Pallas kernels, text_bwd(): pl.pallas_call(text_bwd_kernel, grid=(depth // bk,), in_specs=[pl.BlockSp...  24.9 us
    ppermute x16, starting transfers between devices, dp_swap(): return lax.ppermute(value, ('dp', 'fsdp'), pairs)  21.8 us
  transfers between devices with their start and end apart: 39, of which 12 were waited for; matrix products, arithmetic and copies ran while one was open for 23% of the time, Pallas kernels for 57%

profile of v10, /device:TPU:0, one launch (start us, length us, event | category | flops | bytes accessed | tf_op | source)
XLA Modules:
  0.0 573.4 jit_solution(14316945491684180479)
XLA Ops:
  12.8 4.0 dynamic-slice_bitcast_fusion
  17.9 4.7 fusion.2
  23.3 16.2 %shard_map.222 = f32[2,256,1536]{2,1,0:T(8,128)} custom-call(bf16[256,2048]{1,0:T(8,128)(2,1)} %pad_maximum_fusion.2.x_ref, bf16[2048,2,1536]{2,1,0:T(2,128)(2,1)} %w_ref.5), custom_call_target="tpu_custom_call" | custom-call | tf_op jit(solution)/shard_map/pallas_call | solution.py:421
  53.3 14.3 %shard_map.221 = (bf16[1024,1536]{1,0:T(8,128)(2,1)}, f32[3,1024,768]{2,1,0:T(8,128)}, f32[8,1024]{1,0:T(8,128)}) custom-call(s32[2]{0:T(128)} %pad_add_fusion.1.id_ref, bf16[512,1536]{1,0:T(8,128)(2,1)} %bitcast.127, bf16[512,1536]{1,0:T(8,128)(2,1)} %collective-permute-done.1.xp_ref, f32[1,1536]{1,0:T(1,128)} %get-tuple-element.266.front_ref, ...), custom_call_target="tpu_custom_call" | custom-call | tf_op jit(solution)/shard_map/pallas_call | solution.py:609
  70.4 32.1 %shard_map.223 = (bf16[1024,768]{1,0:T(8,128)(2,1)}, bf16[1024,768]{1,0:T(8,128)(2,1)}, bf16[1024,768]{1,0:T(8,128)(2,1)}, bf16[1024,768]{1,0:T(8,128)(2,1)}, f3...) custom-call(s32[1]{0:T(128)S(6)} %copy.48.len_ref, ...), custom_call_target="tpu_custom_call" | custom-call | tf_op jit(solution)/shard_map/pallas_call | solution.py:364
  120.3 90.2 %shard_map.224 = (bf16[8,2,96,2048]{3,2,1,0:T(8,128)(2,1)}, bf16[8,2,96,2048]{3,2,1,0:T(8,128)(2,1)}, bf16[8,96,2048]{2,1,0:T(8,128)(2,1)}, bf16[8,96,2048]{2,1,...) custom-call(s32[2]{0:T(128)} %pad_add_fusion.1.id_ref, ...), custom_call_target="tpu_custom_call" | custom-call | tf_op jit(solution)/shard_map/pallas_call | solution.py:552
  217.1 4.3 multiply_reduce_fusion
  221.5 5.8 %fusion.7 = (f32[1536]{0:T(1024)S(1)}, bf16[1,512,1536]{2,1,0:T(8,128)(2,1)}, f32[1536]{0:T(1024)S(1)}, f32[512,1536]{1,0:T(8,128)S(1)}) fusion(f32[512,1536]{1,0:T(8,128)} %get-tuple-element.111, bf16[512,1536]{1,0:T(8,128)(2,1)S(1)} %collective-permute-done.11, bf16[1,512,1536]{2,1,0:T(8,128)(2,1)} %param.19, f32[512,1536]{1,0:T(8,128)S(1)} %copy-done.1, ...), kind=kLoop, calls=%fused_computation.18 | loop fusion | flops 16512000 | bytes 23627776 | tf_op jit(solution)/shard_map/reduce_sum | solution.py:871
  232.4 9.6 %shard_map.225 = (f32[1024,768]{1,0:T(8,128)}, bf16[8,96,768]{2,1,0:T(8,128)(2,1)}, bf16[8,96,768]{2,1,0:T(8,128)(2,1)}) custom-call(s32[2]{0:T(128)} %pad_add_fusion.1.id_ref, bf16[512,1536]{1,0:T(8,128)(2,1)} %copy-done.18, bf16[512,1536]{1,0:T(8,128)(2,1)} %collective-permute-done.13.refs_1_, bf16[768,1536]{1,0:T(8,128)(2,1)} %refs_2_.1, ...), custom_call_target="tpu_custom_call" | custom-call | tf_op jit(solution)/shard_map/pallas_call | solution.py:737
  242.0 44.5 %shard_map.226 = (f32[3,1024,512]{2,1,0:T(8,128)}, f32[256,512]{1,0:T(8,128)}, f32[256,512]{1,0:T(8,128)}, f32[8,1024]{1,0:T(8,128)}, f32[1,512]{1,0:T(1,128)}, /*index=5*/f32[1,512]{1,0:T(1,128)}, f32[1,512]{1,0:T(1,128)}) custom-call(s32[1]{0:T(128)S(6)} %copy.48.len_ref, bf16[1024,768]{1,0:T(8,128)(2,1)} %get-tuple-element.115.q_ref, ...), custom_call_target="tpu_custom_call" | custom-call | tf_op jit(solution)/shard_map/pallas_call | solution.py:379
  286.5 8.2 %add_convert_fusion = (bf16[4,2,96,2048]{3,2,1,0:T(8,128)(2,1)}, bf16[4,2,96,2048]{3,2,1,0:T(8,128)(2,1)}) fusion(bf16[8,2,96,2048]{3,2,1,0:T(8,128)(2,1)} %collective-permute-done.14, bf16[8,2,96,2048]{3,2,1,0:T(8,128)(2,1)} %get-tuple-element.150), kind=kLoop, calls=%fused_computation.4 | loop fusion | flops 12582912 | bytes 18874368 | tf_op jit(solution)/shard_map/convert_element_type | solution.py:130
  296.9 6.1 %add_convert_fusion.5 = (bf16[4,96,2048]{2,1,0:T(8,128)(2,1)}, bf16[4,96,2048]{2,1,0:T(8,128)(2,1)}) fusion(bf16[8,96,2048]{2,1,0:T(8,128)(2,1)} %collective-permute-done.15, bf16[8,96,2048]{2,1,0:T(8,128)(2,1)} %get-tuple-element.152), kind=kLoop, calls=%fused_computation.34 | loop fusion | flops 6291456 | bytes 9437184 | tf_op jit(solution)/shard_map/convert_element_type | solution.py:130
  306.3 24.3 %shard_map.227 = (f32[3,1024,256]{2,1,0:T(8,128)}, f32[256,256]{1,0:T(8,128)}, f32[256,256]{1,0:T(8,128)}, f32[8,1024]{1,0:T(8,128)}, f32[1,256]{1,0:T(1,128)}, /*index=5*/f32[1,256]{1,0:T(1,128)}, f32[1,256]{1,0:T(1,128)}) custom-call(s32[1]{0:T(128)S(6)} %copy.48.len_ref, bf16[1024,768]{1,0:T(8,128)(2,1)} %get-tuple-element.115.q_ref, ...), custom_call_target="tpu_custom_call" | custom-call | tf_op jit(solution)/shard_map/pallas_call | solution.py:379
  333.9 18.8 %shard_map.228 = (bf16[4,3,96,1536]{3,2,1,0:T(8,128)(2,1)}, bf16[4,3,96,1536]{3,2,1,0:T(8,128)(2,1)}, bf16[3,1024,768]{2,1,0:T(8,128)(2,1)}) custom-call(s32[2]{0:T(128)} %pad_add_fusion.1.id_ref, f32[3,1024,512]{2,1,0:T(8,128)} %get-tuple-element.146.da_ref, f32[3,1024,256]{2,1,0:T(8,128)} %get-tuple-element.147.db_ref, ...), custom_call_target="tpu_custom_call" | custom-call | tf_op jit(solution)/shard_map/pallas_call | solution.py:656
  353.3 7.6 %collective-permute-done.19 = bf16[8,96,768]{2,1,0:T(8,128)(2,1)} collective-permute-done((bf16[8,96,768]{2,1,0:T(8,128)(2,1)}, bf16[8,96,768]{2,1,0:T(8,128)(2,1)}, u32[]{:S(2)}, u32[]{:S(2)}) %collective-permute-start.19) | collective-permute-done | bytes 1179680 | tf_op jit(solution)/shard_map/ppermute | solution.py:104
  365.3 5.1 add_convert_fusion.4
  381.8 13.7 %shard_map.230 = (f32[512,1536]{1,0:T(8,128)}, bf16[512,1536]{1,0:T(8,128)(2,1)}) custom-call(s32[2]{0:T(128)} %pad_add_fusion.1.id_ref, bf16[3,1024,768]{2,1,0:T(8,128)(2,1)} %get-tuple-element.166.g_ref, bf16[3,768,1536]{2,1,0:T(8,128)(2,1)} %bitcast.126, bf16[3,768,768]{2,1,0:T(8,128)(2,1)} %collective-permute-done.2.got_ref), custom_call_target="tpu_custom_call" | custom-call | tf_op jit(solution)/shard_map/pallas_call | solution.py:702
  397.3 16.2 %collective-permute-done.22 = bf16[4,3,96,1536]{3,2,1,0:T(8,128)(2,1)} collective-permute-done((bf16[4,3,96,1536]{3,2,1,0:T(8,128)(2,1)}, bf16[4,3,96,1536]{3,2,1,0:T(8,128)(2,1)}, u32[]{:S(2)}, u32[]{:S(2)}) %collective-permute-start.22) | collective-permute-done | bytes 3538976 | tf_op jit(solution)/shard_map/ppermute | solution.py:104
  421.4 4.8 add_convert_fusion.2
  433.1 24.9 %shard_map.229 = (bf16[256,2048]{1,0:T(8,128)(2,1)}, bf16[16,2,96,128]{3,2,1,0:T(8,128)(2,1)}) custom-call(bf16[2,256,1536]{2,1,0:T(8,128)(2,1)} %copy-done.11, bf16[2048,2,1536]{2,1,0:T(2,128)(2,1)} %w_ref.5, bf16[16,2,96,128]{3,2,1,0:T(8,128)(2,1)} %bitcast.131), custom_call_target="tpu_custom_call" | custom-call | tf_op jit(solution)/shard_map/pallas_call | solution.py:457
  467.5 9.3 %fusion = f32[2048,2,96]{0,2,1:T(8,128)} fusion(bf16[2,96,4096]{2,1,0:T(8,128)(2,1)S(1)} %bitcast.134, bf16[4096,2048]{1,0:T(8,128)(2,1)} %all-gather.2.cloned.1.call-done), kind=kOutput, calls=%fused_computation | convolution fusion | flops 3221225472 | bytes 19922944 | tf_op jit(solution)/shard_map/dot_general | solution.py:25
  482.6 4.2 fusion.15
  491.0 36.7 %shard_map.231 = (f32[16,8,128]{2,1,0:T(8,128)}, f32[16,8,128]{2,1,0:T(8,128)}) custom-call(f32[16,8,128]{2,1,0:T(8,128)} %select_maximum_fusion.mod_ref), custom_call_target="tpu_custom_call" | custom-call | tf_op jit(solution)/shard_map/pallas_call | solution.py:172
  547.8 17.5 %collective-permute-done.36 = bf16[1,3,96,768]{3,2,1,0:T(8,128)(2,1)S(1)} collective-permute-done((bf16[1,3,96,768]{3,2,1,0:T(8,128)(2,1)S(1)}, bf16[1,3,96,768]{3,2,1,0:T(8,128)(2,1)S(1)}, u32[]{:S(2)}, u32[]{:S(2)}) %collective-permute-start.36) | collective-permute-done | bytes 442400 | tf_op jit(solution)/shard_map/ppermute | solution.py:104
  (309 shorter events, 133.8 us)
Async XLA Ops:
  7.2 206.3 %all-gather.2.cloned.1.call-start = ((), (), s32[]{:S(2)}) async-start(), calls=%async_computation | async-start | bytes 17825792 | tf_op jit(solution)/shard_map/all_gather | solution.py:812
  16.8 36.5 %collective-permute-start.2 = (bf16[3,768,768]{2,1,0:T(8,128)(2,1)}, bf16[3,768,768]{2,1,0:T(8,128)(2,1)}, u32[]{:S(2)}, u32[]{:S(2)}) collective-permute-start(bf16[3,768,768]{2,1,0:T(8,128)(2,1)} %dynamic-slice_bitcast_fusion), channel_id=1, source_target_pairs={{0,1},{1,0},{2,3},{3,2},{4,5},{5,4},{6,7},{7,6},{8,9},{9,8},{10,11... | collective-permute-start | bytes 10616840 | tf_op jit(solution)/shard_map/ppermute | solution.py:30
  22.6 26.7 %collective-permute-start = (f32[4,1536]{1,0:T(4,128)S(1)}, f32[4,1536]{1,0:T(4,128)S(1)}, u32[]{:S(2)}, u32[]{:S(2)}) collective-permute-start(f32[4,1536]{1,0:T(4,128)S(1)} %bitcast.138), channel_id=1, source_target_pairs={{0,1},{1,0},{2,3},{3,2},{4,5},{5,4},{6,7},{7,6},{8,9},{9,8},{10,11... | collective-permute-start | bytes 73736 | tf_op jit(solution)/shard_map/ppermute | solution.py:30
  22.8 30.5 %collective-permute-start.1 = (bf16[512,1536]{1,0:T(8,128)(2,1)S(1)}, bf16[512,1536]{1,0:T(8,128)(2,1)}, u32[]{:S(2)}, u32[]{:S(2)}) collective-permute-start(bf16[512,1536]{1,0:T(8,128)(2,1)S(1)} %bitcast.128), channel_id=1, source_target_pairs={{0,1},{1,0},{2,3},{3,2},{4,5},{5,4},{6,7},{7,6},{8,9},{9,8},{10,11... | collective-permute-start | bytes 4718600 | tf_op jit(solution)/shard_map/ppermute | solution.py:30
  23.1 22.9 %collective-permute-start.4 = (s32[2,512]{1,0:T(2,128)S(1)}, s32[2,512]{1,0:T(2,128)S(1)}, u32[]{:S(2)}, u32[]{:S(2)}) collective-permute-start(s32[2,512]{1,0:T(2,128)S(1)} %bitcast.151), channel_id=1, source_target_pairs={{0,1},{1,0},{2,3},{3,2},{4,5},{5,4},{6,7},{7,6},{8,9},{9,8},{10,11... | collective-permute-start | bytes 12296 | tf_op jit(solution)/shard_map/ppermute | solution.py:30
  105.5 9.8 %collective-permute-start.10 = (bf16[512,1536]{1,0:T(8,128)(2,1)S(1)}, bf16[512,1536]{1,0:T(8,128)(2,1)S(1)}, u32[]{:S(2)}, u32[]{:S(2)}) collective-permute-start(bf16[512,1536]{1,0:T(8,128)(2,1)S(1)} %bitcast.129), channel_id=1, source_target_pairs={{0,1},{1,0},{2,3},{3,2},{4,5},{5,4},{6,7},{7,6},{8,9},{9,8},{10,11... | collective-permute-start | bytes 4718600 | tf_op jit(solution)/shard_map/ppermute | solution.py:30
  210.5 75.9 %collective-permute-start.14 = (bf16[8,2,96,2048]{3,2,1,0:T(8,128)(2,1)}, bf16[8,2,96,2048]{3,2,1,0:T(8,128)(2,1)}, u32[]{:S(2)}, u32[]{:S(2)}) collective-permute-start(bf16[8,2,96,2048]{3,2,1,0:T(8,128)(2,1)} %get-tuple-element.137), channel_id=1, source_target_pairs={{0,2},{1,5},{2,0},{3,7},{4,6},{5,1},{6,4},{7,3},{8,10},{9,13},{10,... | collective-permute-start | bytes 18874376 | tf_op jit(solution)/shard_map/ppermute | solution.py:104
  214.0 72.5 %collective-permute-start.15 = (bf16[8,96,2048]{2,1,0:T(8,128)(2,1)}, bf16[8,96,2048]{2,1,0:T(8,128)(2,1)}, u32[]{:S(2)}, u32[]{:S(2)}) collective-permute-start(bf16[8,96,2048]{2,1,0:T(8,128)(2,1)} %get-tuple-element.138), channel_id=1, source_target_pairs={{0,8},{1,9},{2,10},{3,11},{4,12},{5,13},{6,14},{7,15},{8,0},{9,1},... | collective-permute-start | bytes 9437192 | tf_op jit(solution)/shard_map/ppermute | solution.py:104
  294.6 66.2 %collective-permute-start.17 = (bf16[4,2,96,2048]{3,2,1,0:T(8,128)(2,1)}, bf16[4,2,96,2048]{3,2,1,0:T(8,128)(2,1)}, u32[]{:S(2)}, u32[]{:S(2)}) collective-permute-start(bf16[4,2,96,2048]{3,2,1,0:T(8,128)(2,1)} %get-tuple-element.238), channel_id=1, source_target_pairs={{0,4},{1,3},{2,6},{3,1},{4,0},{5,7},{6,2},{7,5},{8,12},{9,11},{10,... | collective-permute-start | bytes 9437192 | tf_op jit(solution)/shard_map/ppermute | solution.py:104
  303.0 57.8 %collective-permute-start.18 = (bf16[4,96,2048]{2,1,0:T(8,128)(2,1)}, bf16[4,96,2048]{2,1,0:T(8,128)(2,1)}, u32[]{:S(2)}, u32[]{:S(2)}) collective-permute-start(bf16[4,96,2048]{2,1,0:T(8,128)(2,1)} %get-tuple-element.244), channel_id=1, source_target_pairs={{0,2},{1,5},{2,0},{3,7},{4,6},{5,1},{6,4},{7,3},{8,10},{9,13},{10,... | collective-permute-start | bytes 4718600 | tf_op jit(solution)/shard_map/ppermute | solution.py:104
  304.2 56.7 %collective-permute-start.19 = (bf16[8,96,768]{2,1,0:T(8,128)(2,1)}, bf16[8,96,768]{2,1,0:T(8,128)(2,1)}, u32[]{:S(2)}, u32[]{:S(2)}) collective-permute-start(bf16[8,96,768]{2,1,0:T(8,128)(2,1)} %get-tuple-element.154), channel_id=1, source_target_pairs={{0,2},{1,5},{2,0},{3,7},{4,6},{5,1},{6,4},{7,3},{8,10},{9,13},{10,... | collective-permute-start | bytes 3538952 | tf_op jit(solution)/shard_map/ppermute | solution.py:104
  352.7 60.8 %collective-permute-start.22 = (bf16[4,3,96,1536]{3,2,1,0:T(8,128)(2,1)}, bf16[4,3,96,1536]{3,2,1,0:T(8,128)(2,1)}, u32[]{:S(2)}, u32[]{:S(2)}) collective-permute-start(bf16[4,3,96,1536]{3,2,1,0:T(8,128)(2,1)} %get-tuple-element.159), channel_id=1, source_target_pairs={{0,2},{1,5},{2,0},{3,7},{4,6},{5,1},{6,4},{7,3},{8,10},{9,13},{10,... | collective-permute-start | bytes 10616840 | tf_op jit(solution)/shard_map/ppermute | solution.py:104
  363.8 49.8 %collective-permute-start.25 = (bf16[4,96,768]{2,1,0:T(8,128)(2,1)}, bf16[4,96,768]{2,1,0:T(8,128)(2,1)}, u32[]{:S(2)}, u32[]{:S(2)}) collective-permute-start(bf16[4,96,768]{2,1,0:T(8,128)(2,1)} %get-tuple-element.254), channel_id=1, source_target_pairs={{0,4},{1,3},{2,6},{3,1},{4,0},{5,7},{6,2},{7,5},{8,12},{9,11},{10,... | collective-permute-start | bytes 1769480 | tf_op jit(solution)/shard_map/ppermute | solution.py:104
  370.4 43.1 %collective-permute-start.23 = (bf16[2,2,96,2048]{3,2,1,0:T(8,128)(2,1)}, bf16[2,2,96,2048]{3,2,1,0:T(8,128)(2,1)}, u32[]{:S(2)}, u32[]{:S(2)}) collective-permute-start(bf16[2,2,96,2048]{3,2,1,0:T(8,128)(2,1)} %get-tuple-element.242), channel_id=1, source_target_pairs={{0,8},{1,9},{2,10},{3,11},{4,12},{5,13},{6,14},{7,15},{8,0},{9,1},... | collective-permute-start | bytes 4718600 | tf_op jit(solution)/shard_map/ppermute | solution.py:104
  375.4 20.1 %collective-permute-start.21 = (bf16[2,256,768]{2,1,0:T(8,128)(2,1)}, bf16[2,256,768]{2,1,0:T(8,128)(2,1)}, u32[]{:S(2)}, u32[]{:S(2)}) collective-permute-start(bf16[2,256,768]{2,1,0:T(8,128)(2,1)} %maximum_maximum_fusion), channel_id=1, source_target_pairs={{0,1},{1,0},{2,3},{3,2},{4,5},{5,4},{6,7},{7,6},{8,9},{9,8},{10,11... | collective-permute-start | bytes 2359304 | tf_op jit(solution)/shard_map/ppermute | solution.py:30
  378.7 34.8 %collective-permute-start.24 = (bf16[2,96,2048]{2,1,0:T(8,128)(2,1)}, bf16[2,96,2048]{2,1,0:T(8,128)(2,1)}, u32[]{:S(2)}, u32[]{:S(2)}) collective-permute-start(bf16[2,96,2048]{2,1,0:T(8,128)(2,1)} %get-tuple-element.252), channel_id=1, source_target_pairs={{0,4},{1,3},{2,6},{3,1},{4,0},{5,7},{6,2},{7,5},{8,12},{9,11},{10,... | collective-permute-start | bytes 2359304 | tf_op jit(solution)/shard_map/ppermute | solution.py:104
  395.5 67.0 %collective-permute-start.26 = (bf16[512,1536]{1,0:T(8,128)(2,1)}, bf16[512,1536]{1,0:T(8,128)(2,1)}, u32[]{:S(2)}, u32[]{:S(2)}) collective-permute-start(bf16[512,1536]{1,0:T(8,128)(2,1)} %get-tuple-element.168), channel_id=1, source_target_pairs={{0,1},{1,0},{2,3},{3,2},{4,5},{5,4},{6,7},{7,6},{8,9},{9,8},{10,11... | collective-permute-start | bytes 4718600 | tf_op jit(solution)/shard_map/ppermute | solution.py:54
  415.5 73.9 %collective-permute-start.31 = (bf16[2,96,768]{2,1,0:T(8,128)(2,1)}, bf16[2,96,768]{2,1,0:T(8,128)(2,1)}, u32[]{:S(2)}, u32[]{:S(2)}) collective-permute-start(bf16[2,96,768]{2,1,0:T(8,128)(2,1)} %get-tuple-element.265), channel_id=1, source_target_pairs={{0,8},{1,9},{2,10},{3,11},{4,12},{5,13},{6,14},{7,15},{8,0},{9,1},... | collective-permute-start | bytes 884744 | tf_op jit(solution)/shard_map/ppermute | solution.py:104
  418.8 70.6 %collective-permute-start.30 = (bf16[1,96,2048]{2,1,0:T(8,128)(2,1)}, bf16[1,96,2048]{2,1,0:T(8,128)(2,1)}, u32[]{:S(2)}, u32[]{:S(2)}) collective-permute-start(bf16[1,96,2048]{2,1,0:T(8,128)(2,1)} %add_convert_fusion.19), channel_id=1, source_target_pairs={{0,16},{1,17},{2,18},{3,19},{4,20},{5,21},{6,22},{7,23},{8,24},{9,... | collective-permute-start | bytes 1179656 | tf_op jit(solution)/shard_map/ppermute | solution.py:104
  426.2 50.5 %collective-permute-start.27 = (bf16[2,3,96,1536]{3,2,1,0:T(8,128)(2,1)}, bf16[2,3,96,1536]{3,2,1,0:T(8,128)(2,1)}, u32[]{:S(2)}, u32[]{:S(2)}) collective-permute-start(bf16[2,3,96,1536]{3,2,1,0:T(8,128)(2,1)} %get-tuple-element.240), channel_id=1, source_target_pairs={{0,4},{1,3},{2,6},{3,1},{4,0},{5,7},{6,2},{7,5},{8,12},{9,11},{10,... | collective-permute-start | bytes 5308424 | tf_op jit(solution)/shard_map/ppermute | solution.py:104
  462.5 81.5 %collective-permute-start.37 = (bf16[1,2,96,2048]{3,2,1,0:T(8,128)(2,1)}, bf16[1,2,96,2048]{3,2,1,0:T(8,128)(2,1)}, u32[]{:S(2)}, u32[]{:S(2)}) collective-permute-start(bf16[1,2,96,2048]{3,2,1,0:T(8,128)(2,1)} %get-tuple-element.249), channel_id=1, source_target_pairs={{0,16},{1,17},{2,18},{3,19},{4,20},{5,21},{6,22},{7,23},{8,24},{9,... | collective-permute-start | bytes 2359304 | tf_op jit(solution)/shard_map/ppermute | solution.py:104
  481.6 51.1 %collective-permute-start.32 = (bf16[1,3,96,1536]{3,2,1,0:T(8,128)(2,1)}, bf16[1,3,96,1536]{3,2,1,0:T(8,128)(2,1)}, u32[]{:S(2)}, u32[]{:S(2)}) collective-permute-start(bf16[1,3,96,1536]{3,2,1,0:T(8,128)(2,1)} %add_convert_fusion.11), channel_id=1, source_target_pairs={{0,8},{1,9},{2,10},{3,11},{4,12},{5,13},{6,14},{7,15},{8,0},{9,1},... | collective-permute-start | bytes 2654216 | tf_op jit(solution)/shard_map/ppermute | solution.py:104
  487.6 42.7 %collective-permute-start.28 = (bf16[128,2048]{1,0:T(8,128)(2,1)}, bf16[128,2048]{1,0:T(8,128)(2,1)}, u32[]{:S(2)}, u32[]{:S(2)}) collective-permute-start(bf16[128,2048]{1,0:T(8,128)(2,1)} %constant_dynamic-slice_fusion.1), channel_id=1, source_target_pairs={{0,1},{1,0},{2,3},{3,2},{4,5},{5,4},{6,7},{7,6},{8,9},{9,8},{10,11... | collective-permute-start | bytes 1572872 | tf_op jit(solution)/shard_map/ppermute | solution.py:30
  543.2 22.1 %collective-permute-start.36 = (bf16[1,3,96,768]{3,2,1,0:T(8,128)(2,1)S(1)}, bf16[1,3,96,768]{3,2,1,0:T(8,128)(2,1)S(1)}, u32[]{:S(2)}, u32[]{:S(2)}) collective-permute-start(bf16[1,3,96,768]{3,2,1,0:T(8,128)(2,1)S(1)} %fusion.25), channel_id=1, source_target_pairs={{0,16},{1,17},{2,18},{3,19},{4,20},{5,21},{6,22},{7,23},{8,24},{9,... | collective-permute-start | bytes 1327112 | tf_op jit(solution)/shard_map/ppermute | solution.py:104
  (73 other events, 1316.2 us)
Sparse Core Ops, SparseCore 0:
  12.9 194.2 all-gather.1

commit v11 on v10

--- a/solution.py
+++ b/solution.py
@@ -183,11 +183,17 @@
     )(mods)
 
 
-def advance(chains, value):
+def settle(chains, value):
     live = [c for c in chains if c.got is not None]
     value, got = lax.optimization_barrier((value, [c.got for c in live]))
     for c, g in zip(live, got):
         c.got = g
+    return value
+
+
+def advance(chains, value):
+    value = settle(chains, value)
+    for c in chains:
         c.step()
     return value
 
@@ -930,11 +936,11 @@
     grad_tk = (inv_t * (text_hat - normed_t * mean_t)).astype(BF16)
     text_pair = jnp.stack([grad_tk, dtv.astype(BF16)])
     pair_all = jnp.concatenate(natural(gather_rot(text_pair)), axis=-1)
-    pair_all = advance([qkv_chain, wide_chain, down_chain, out_chain], pair_all)
+    pair_all = settle([wide_chain], pair_all)
     outgoing = block_of(pair_all.transpose(0, 2, 1), f, 2)
     outgoing = outgoing.reshape(2, dpn, share, TEXT // n).transpose(1, 0, 2, 3)
     text_in, pair_cols = text_bwd(pair_all, w_text, outgoing)
-    text_in, grad_first = advance([qkv_chain], (text_in, grad_first))
+    text_in, grad_first = advance([qkv_chain, down_chain, out_chain], (text_in, grad_first))
     text_in = jnp.concatenate(natural(exchange_rot(text_in, 0)), axis=1)
 
     inverse_one = inverse_rms(x_own)
@@ -956,34 +962,30 @@
     mods = jnp.concatenate([sums[:4], stamp], axis=0).reshape(5, dpn, share).transpose(1, 0, 2)
     mods = jnp.pad(mods, ((0, 0), (0, 0), (0, -share % 128)))
     mods = jnp.concatenate([mods, small.reshape(dpn, SUMS, 128)], axis=1)
-    mods = advance([down_chain, out_chain], mods)
     mods, small = small_exchange(mods)
-    chains = [out_chain, down_chain] if paired else [qkv_chain, out_chain, down_chain]
+    mods = advance([qkv_chain, wide_chain, out_chain, down_chain], mods)
+    pair_cols = jnp.concatenate(natural(gather_rot(pair_cols)), axis=3)
+    pair_cols = pair_cols.transpose(1, 2, 0, 3).reshape(2 * share, dpn * TEXT)
+    text_grad = dot(pair_cols, text_all).reshape(2, share, TW // n)
+    total = small[:, 5 : 5 + SUMS].reshape(-1)[: 6 * own_d].reshape(6, own_d)
+    gate_total = jnp.sum(total[5].reshape(HEADS // n, HD), axis=1) * (
+        1.0 - head_tanh * head_tanh
+    )
+    times = time_embed(mods[:, 4, 0])
+    times = lax.dynamic_slice_in_dim(times, f * own_te, own_te, 1).astype(F32)
+    ada_grad = lax.dot_general(
+        mods[:, :4, :share].reshape(dpn, 4 * share), times, (((0,), (0,)), ((), ())),
+        precision=lax.Precision.HIGHEST,
+    ).reshape(4, share, own_te)
+
     if paired:
-        qkv_got = qkv_chain.got
-        (mods, small), qkv_chain.got = lax.optimization_barrier(((mods, small), qkv_got))
-        qkv_chain.step()
+        text_grad = advance([qkv_chain], text_grad)
         own_side = f == (me >> low_bits[-1] + 1)
         mine, got = exchange_rot(qkv_chain.last[0].astype(BF16), 2)
         got, wide_chain.keep = lax.optimization_barrier((got, wide_chain.keep))
         qkv_chain = Halving(
             bits[-1:], jnp.where(own_side, mine, got)[None], jnp.where(own_side, got, mine)[None]
         )
-    mods = advance(chains, mods)
-    pair_cols = jnp.concatenate(natural(gather_rot(pair_cols)), axis=3)
-    pair_cols = pair_cols.transpose(1, 2, 0, 3).reshape(2 * share, dpn * TEXT)
-    text_grad = dot(pair_cols, text_all).reshape(2, share, TW // n)
-    total = small[:, 5 : 5 + SUMS].reshape(-1)[: 6 * own_d].reshape(6, own_d)
-    gate_total = jnp.sum(total[5].reshape(HEADS // n, HD), axis=1) * (
-        1.0 - head_tanh * head_tanh
-    )
-    times = time_embed(mods[:, 4, 0])
-    times = lax.dynamic_slice_in_dim(times, f * own_te, own_te, 1).astype(F32)
-    ada_grad = lax.dot_general(
-        mods[:, :4, :share].reshape(dpn, 4 * share), times, (((0,), (0,)), ((), ())),
-        precision=lax.Precision.HIGHEST,
-    ).reshape(4, share, own_te)
-
     for chain in (out_chain, down_chain, wide_chain, qkv_chain):
         while chain.got is not None:
             chain.step()

time: 579 us -> 603 us (1.041)
  waiting for transfers between devices: 54.8 us -> 97.5 us
  Pallas kernels: 325 us -> 308 us
    ppermute x16, waiting for transfers between devices: 43.1 us -> 85.7 us  [dp_swap(): return lax.ppermute(value, ('dp', 'fsdp'), pairs)]
    pallas_call x1, Pallas kernels: 36.7 us -> 16.7 us  [small_exchange(): pl.pallas_call(small_kernel, in_specs=[vmem], out_specs=[vmem] * 2, out_s...]
  transfers between devices with their start and end apart: 39 -> 39, of which waited for: 12 -> 12; matrix products, arithmetic and copies ran while one was open for 23% -> 21% of each run, Pallas kernels for 57% -> 52%
where the time goes in v11:
time: 603 us; the launch traced here: 598 us
  Pallas kernels  308 us (51%)
  waiting for transfers between devices  97.5 us (16%)
  other arithmetic  96.3 us (16%)
  local copies, waits for them, and re-layouts  30 us (5%)
  starting transfers between devices  26 us (4%)
  matrix products  21.5 us (4%)
  between operations  16.4 us (3%)
    pallas_call x1, Pallas kernels, ffn(): pl.pallas_call(functools.partial(ffn_kernel, orders), grid=(hid // bc,),...  90.3 us
    ppermute x16, waiting for transfers between devices, dp_swap(): return lax.ppermute(value, ('dp', 'fsdp'), pairs)  85.7 us
    pallas_call x2, Pallas kernels, attn_backward(): pl.pallas_call(attn_bwd_kernel, grid=(blocks,), in_specs=[scalar, col, co...  68.8 us
    convert_element_type x7, other arithmetic, step(): self.keep = add(slice(half)).astype(BF16)  32.7 us
    pallas_call x1, Pallas kernels, attn_forward(): pl.pallas_call(attn_fwd_kernel, grid=(blocks,), in_specs=[scalar, three,...  32.1 us
    pallas_call x1, Pallas kernels, text_bwd(): pl.pallas_call(text_bwd_kernel, grid=(depth // bk,), in_specs=[pl.BlockSp...  27.7 us
    ppermute x16, starting transfers between devices, dp_swap(): return lax.ppermute(value, ('dp', 'fsdp'), pairs)  20.7 us
    pallas_call x1, Pallas kernels, project_grad(): pl.pallas_call(functools.partial(project_grad_kernel, order), grid=(3,),...  18.4 us
  transfers between devices with their start and end apart: 39, of which 12 were waited for; matrix products, arithmetic and copies ran while one was open for 21% of the time, Pallas kernels for 52%

profile of v11, /device:TPU:0, one launch (start us, length us, event | category | flops | bytes accessed | tf_op | source)
XLA Modules:
  0.0 597.8 jit_solution(1696474901173606732)
XLA Ops:
  17.9 4.7 fusion.2
  23.3 16.2 %shard_map.222 = f32[2,256,1536]{2,1,0:T(8,128)} custom-call(bf16[256,2048]{1,0:T(8,128)(2,1)} %pad_maximum_fusion.2.x_ref, bf16[2048,2,1536]{2,1,0:T(2,128)(2,1)} %w_ref.5), custom_call_target="tpu_custom_call" | custom-call | tf_op jit(solution)/shard_map/pallas_call | solution.py:427
  53.4 14.4 %shard_map.221 = (bf16[1024,1536]{1,0:T(8,128)(2,1)}, f32[3,1024,768]{2,1,0:T(8,128)}, f32[8,1024]{1,0:T(8,128)}) custom-call(s32[2]{0:T(128)} %pad_add_fusion.1.id_ref, bf16[512,1536]{1,0:T(8,128)(2,1)} %bitcast.128, bf16[512,1536]{1,0:T(8,128)(2,1)} %collective-permute-done.1.xp_ref, f32[1,1536]{1,0:T(1,128)} %get-tuple-element.262.front_ref, ...), custom_call_target="tpu_custom_call" | custom-call | tf_op jit(solution)/shard_map/pallas_call | solution.py:615
  70.6 32.1 %shard_map.223 = (bf16[1024,768]{1,0:T(8,128)(2,1)}, bf16[1024,768]{1,0:T(8,128)(2,1)}, bf16[1024,768]{1,0:T(8,128)(2,1)}, bf16[1024,768]{1,0:T(8,128)(2,1)}, f3...) custom-call(s32[1]{0:T(128)S(6)} %copy.48.len_ref, ...), custom_call_target="tpu_custom_call" | custom-call | tf_op jit(solution)/shard_map/pallas_call | solution.py:370
  120.4 90.3 %shard_map.224 = (bf16[8,2,96,2048]{3,2,1,0:T(8,128)(2,1)}, bf16[8,2,96,2048]{3,2,1,0:T(8,128)(2,1)}, bf16[8,96,2048]{2,1,0:T(8,128)(2,1)}, bf16[8,96,2048]{2,1,...) custom-call(s32[2]{0:T(128)} %pad_add_fusion.1.id_ref, ...), custom_call_target="tpu_custom_call" | custom-call | tf_op jit(solution)/shard_map/pallas_call | solution.py:558
  217.3 4.3 multiply_reduce_fusion
  221.6 5.8 fusion.7
  232.5 9.6 %shard_map.225 = (f32[1024,768]{1,0:T(8,128)}, bf16[8,96,768]{2,1,0:T(8,128)(2,1)}, bf16[8,96,768]{2,1,0:T(8,128)(2,1)}) custom-call(s32[2]{0:T(128)} %pad_add_fusion.1.id_ref, bf16[512,1536]{1,0:T(8,128)(2,1)} %copy-done.17, bf16[512,1536]{1,0:T(8,128)(2,1)} %collective-permute-done.13.refs_1_, bf16[768,1536]{1,0:T(8,128)(2,1)} %refs_2_.1, ...), custom_call_target="tpu_custom_call" | custom-call | tf_op jit(solution)/shard_map/pallas_call | solution.py:743
  242.1 44.5 %shard_map.226 = (f32[3,1024,512]{2,1,0:T(8,128)}, f32[256,512]{1,0:T(8,128)}, f32[256,512]{1,0:T(8,128)}, f32[8,1024]{1,0:T(8,128)}, f32[1,512]{1,0:T(1,128)}, /*index=5*/f32[1,512]{1,0:T(1,128)}, f32[1,512]{1,0:T(1,128)}) custom-call(s32[1]{0:T(128)S(6)} %copy.48.len_ref, bf16[1024,768]{1,0:T(8,128)(2,1)} %get-tuple-element.113.q_ref, ...), custom_call_target="tpu_custom_call" | custom-call | tf_op jit(solution)/shard_map/pallas_call | solution.py:385
  286.6 8.1 %add_convert_fusion = (bf16[4,2,96,2048]{3,2,1,0:T(8,128)(2,1)}, bf16[4,2,96,2048]{3,2,1,0:T(8,128)(2,1)}) fusion(bf16[8,2,96,2048]{3,2,1,0:T(8,128)(2,1)} %collective-permute-done.14, bf16[8,2,96,2048]{3,2,1,0:T(8,128)(2,1)} %get-tuple-element.148), kind=kLoop, calls=%fused_computation.4 | loop fusion | flops 12582912 | bytes 18874368 | tf_op jit(solution)/shard_map/convert_element_type | solution.py:130
  296.9 6.1 %add_convert_fusion.5 = (bf16[4,96,2048]{2,1,0:T(8,128)(2,1)}, bf16[4,96,2048]{2,1,0:T(8,128)(2,1)}) fusion(bf16[8,96,2048]{2,1,0:T(8,128)(2,1)} %collective-permute-done.15, bf16[8,96,2048]{2,1,0:T(8,128)(2,1)} %get-tuple-element.150), kind=kLoop, calls=%fused_computation.33 | loop fusion | flops 6291456 | bytes 9437184 | tf_op jit(solution)/shard_map/convert_element_type | solution.py:130
  306.3 24.3 %shard_map.227 = (f32[3,1024,256]{2,1,0:T(8,128)}, f32[256,256]{1,0:T(8,128)}, f32[256,256]{1,0:T(8,128)}, f32[8,1024]{1,0:T(8,128)}, f32[1,256]{1,0:T(1,128)}, /*index=5*/f32[1,256]{1,0:T(1,128)}, f32[1,256]{1,0:T(1,128)}) custom-call(s32[1]{0:T(128)S(6)} %copy.48.len_ref, bf16[1024,768]{1,0:T(8,128)(2,1)} %get-tuple-element.113.q_ref, ...), custom_call_target="tpu_custom_call" | custom-call | tf_op jit(solution)/shard_map/pallas_call | solution.py:385
  334.0 18.4 %shard_map.228 = (bf16[4,3,96,1536]{3,2,1,0:T(8,128)(2,1)}, bf16[4,3,96,1536]{3,2,1,0:T(8,128)(2,1)}, bf16[3,1024,768]{2,1,0:T(8,128)(2,1)}) custom-call(s32[2]{0:T(128)} %pad_add_fusion.1.id_ref, f32[3,1024,512]{2,1,0:T(8,128)} %get-tuple-element.144.da_ref, f32[3,1024,256]{2,1,0:T(8,128)} %get-tuple-element.145.db_ref, ...), custom_call_target="tpu_custom_call" | custom-call | tf_op jit(solution)/shard_map/pallas_call | solution.py:662
  352.9 8.0 %collective-permute-done.19 = bf16[8,96,768]{2,1,0:T(8,128)(2,1)} collective-permute-done((bf16[8,96,768]{2,1,0:T(8,128)(2,1)}, bf16[8,96,768]{2,1,0:T(8,128)(2,1)}, u32[]{:S(2)}, u32[]{:S(2)}) %collective-permute-start.19) | collective-permute-done | bytes 1179680 | tf_op jit(solution)/shard_map/ppermute | solution.py:104
  365.3 14.0 %shard_map.230 = (f32[512,1536]{1,0:T(8,128)}, bf16[512,1536]{1,0:T(8,128)(2,1)}) custom-call(s32[2]{0:T(128)} %pad_add_fusion.1.id_ref, bf16[3,1024,768]{2,1,0:T(8,128)(2,1)} %get-tuple-element.160.g_ref, bf16[3,768,1536]{2,1,0:T(8,128)(2,1)} %bitcast.127, bf16[3,768,768]{2,1,0:T(8,128)(2,1)} %collective-permute-done.2.got_ref), custom_call_target="tpu_custom_call" | custom-call | tf_op jit(solution)/shard_map/pallas_call | solution.py:708
  379.6 5.5 add_convert_fusion.4
  395.7 25.9 %collective-permute-done.22 = bf16[2,2,96,2048]{3,2,1,0:T(8,128)(2,1)S(1)} collective-permute-done((bf16[2,2,96,2048]{3,2,1,0:T(8,128)(2,1)S(1)}, bf16[2,2,96,2048]{3,2,1,0:T(8,128)(2,1)S(1)}, u32[]{:S(2)}, u32[]{:S(2)}) %collective-permute-start.22) | collective-permute-done | bytes 1572896 | tf_op jit(solution)/shard_map/ppermute | solution.py:104
  428.1 27.7 %shard_map.229 = (bf16[256,2048]{1,0:T(8,128)(2,1)}, bf16[16,2,96,128]{3,2,1,0:T(8,128)(2,1)}) custom-call(bf16[2,256,1536]{2,1,0:T(8,128)(2,1)} %copy-done.9, bf16[2048,2,1536]{2,1,0:T(2,128)(2,1)} %w_ref.5, bf16[16,2,96,128]{3,2,1,0:T(8,128)(2,1)} %bitcast.132), custom_call_target="tpu_custom_call" | custom-call | tf_op jit(solution)/shard_map/pallas_call | solution.py:463
  466.1 5.0 add_convert_fusion.2
  477.4 4.6 fusion.15
  483.7 16.7 %shard_map.231 = (f32[16,8,128]{2,1,0:T(8,128)}, f32[16,8,128]{2,1,0:T(8,128)}) custom-call(f32[16,8,128]{2,1,0:T(8,128)} %select_maximum_fusion.mod_ref), custom_call_target="tpu_custom_call" | custom-call | tf_op jit(solution)/shard_map/pallas_call | solution.py:172
  508.0 8.9 %fusion = f32[2,96,2048]{2,1,0:T(8,128)} fusion(bf16[2,96,4096]{2,1,0:T(8,128)(2,1)S(1)} %bitcast.135, bf16[4096,2048]{1,0:T(8,128)(2,1)} %all-gather.2.cloned.1.call-done), kind=kOutput, calls=%fused_computation | convolution fusion | flops 3221225472 | bytes 19922944 | tf_op jit(solution)/shard_map/dot_general | solution.py:25
  529.1 33.2 %collective-permute-done.33 = bf16[1,3,96,1536]{3,2,1,0:T(8,128)(2,1)} collective-permute-done((bf16[1,3,96,1536]{3,2,1,0:T(8,128)(2,1)}, bf16[1,3,96,1536]{3,2,1,0:T(8,128)(2,1)}, u32[]{:S(2)}, u32[]{:S(2)}) %collective-permute-start.33) | collective-permute-done | bytes 884768 | tf_op jit(solution)/shard_map/ppermute | solution.py:104
  571.3 18.4 %collective-permute-done.35 = bf16[1,3,96,768]{3,2,1,0:T(8,128)(2,1)S(1)} collective-permute-done((bf16[1,3,96,768]{3,2,1,0:T(8,128)(2,1)S(1)}, bf16[1,3,96,768]{3,2,1,0:T(8,128)(2,1)S(1)}, u32[]{:S(2)}, u32[]{:S(2)}) %collective-permute-start.35) | collective-permute-done | bytes 442400 | tf_op jit(solution)/shard_map/ppermute | solution.py:104
  (291 shorter events, 134.7 us)
Async XLA Ops:
  7.2 206.5 %all-gather.2.cloned.1.call-start = ((), (), s32[]{:S(2)}) async-start(), calls=%async_computation | async-start | bytes 17825792 | tf_op jit(solution)/shard_map/all_gather | solution.py:818
  16.7 36.7 %collective-permute-start.2 = (bf16[3,768,768]{2,1,0:T(8,128)(2,1)}, bf16[3,768,768]{2,1,0:T(8,128)(2,1)}, u32[]{:S(2)}, u32[]{:S(2)}) collective-permute-start(bf16[3,768,768]{2,1,0:T(8,128)(2,1)} %dynamic-slice_bitcast_fusion), channel_id=1, source_target_pairs={{0,1},{1,0},{2,3},{3,2},{4,5},{5,4},{6,7},{7,6},{8,9},{9,8},{10,11... | collective-permute-start | bytes 10616840 | tf_op jit(solution)/shard_map/ppermute | solution.py:30
  22.5 26.8 %collective-permute-start = (f32[4,1536]{1,0:T(4,128)S(1)}, f32[4,1536]{1,0:T(4,128)S(1)}, u32[]{:S(2)}, u32[]{:S(2)}) collective-permute-start(f32[4,1536]{1,0:T(4,128)S(1)} %bitcast.139), channel_id=1, source_target_pairs={{0,1},{1,0},{2,3},{3,2},{4,5},{5,4},{6,7},{7,6},{8,9},{9,8},{10,11... | collective-permute-start | bytes 73736 | tf_op jit(solution)/shard_map/ppermute | solution.py:30
  22.7 30.7 %collective-permute-start.1 = (bf16[512,1536]{1,0:T(8,128)(2,1)S(1)}, bf16[512,1536]{1,0:T(8,128)(2,1)}, u32[]{:S(2)}, u32[]{:S(2)}) collective-permute-start(bf16[512,1536]{1,0:T(8,128)(2,1)S(1)} %bitcast.129), channel_id=1, source_target_pairs={{0,1},{1,0},{2,3},{3,2},{4,5},{5,4},{6,7},{7,6},{8,9},{9,8},{10,11... | collective-permute-start | bytes 4718600 | tf_op jit(solution)/shard_map/ppermute | solution.py:30
  23.1 23.1 %collective-permute-start.4 = (s32[2,512]{1,0:T(2,128)S(1)}, s32[2,512]{1,0:T(2,128)S(1)}, u32[]{:S(2)}, u32[]{:S(2)}) collective-permute-start(s32[2,512]{1,0:T(2,128)S(1)} %bitcast.152), channel_id=1, source_target_pairs={{0,1},{1,0},{2,3},{3,2},{4,5},{5,4},{6,7},{7,6},{8,9},{9,8},{10,11... | collective-permute-start | bytes 12296 | tf_op jit(solution)/shard_map/ppermute | solution.py:30
  210.6 76.0 %collective-permute-start.14 = (bf16[8,2,96,2048]{3,2,1,0:T(8,128)(2,1)}, bf16[8,2,96,2048]{3,2,1,0:T(8,128)(2,1)}, u32[]{:S(2)}, u32[]{:S(2)}) collective-permute-start(bf16[8,2,96,2048]{3,2,1,0:T(8,128)(2,1)} %get-tuple-element.135), channel_id=1, source_target_pairs={{0,2},{1,5},{2,0},{3,7},{4,6},{5,1},{6,4},{7,3},{8,10},{9,13},{10,... | collective-permute-start | bytes 18874376 | tf_op jit(solution)/shard_map/ppermute | solution.py:104
  214.2 72.4 %collective-permute-start.15 = (bf16[8,96,2048]{2,1,0:T(8,128)(2,1)}, bf16[8,96,2048]{2,1,0:T(8,128)(2,1)}, u32[]{:S(2)}, u32[]{:S(2)}) collective-permute-start(bf16[8,96,2048]{2,1,0:T(8,128)(2,1)} %get-tuple-element.136), channel_id=1, source_target_pairs={{0,8},{1,9},{2,10},{3,11},{4,12},{5,13},{6,14},{7,15},{8,0},{9,1},... | collective-permute-start | bytes 9437192 | tf_op jit(solution)/shard_map/ppermute | solution.py:104
  294.7 66.3 %collective-permute-start.17 = (bf16[4,2,96,2048]{3,2,1,0:T(8,128)(2,1)}, bf16[4,2,96,2048]{3,2,1,0:T(8,128)(2,1)}, u32[]{:S(2)}, u32[]{:S(2)}) collective-permute-start(bf16[4,2,96,2048]{3,2,1,0:T(8,128)(2,1)} %get-tuple-element.234), channel_id=1, source_target_pairs={{0,4},{1,3},{2,6},{3,1},{4,0},{5,7},{6,2},{7,5},{8,12},{9,11},{10,... | collective-permute-start | bytes 9437192 | tf_op jit(solution)/shard_map/ppermute | solution.py:104
  303.0 57.9 %collective-permute-start.18 = (bf16[4,96,2048]{2,1,0:T(8,128)(2,1)}, bf16[4,96,2048]{2,1,0:T(8,128)(2,1)}, u32[]{:S(2)}, u32[]{:S(2)}) collective-permute-start(bf16[4,96,2048]{2,1,0:T(8,128)(2,1)} %get-tuple-element.240), channel_id=1, source_target_pairs={{0,2},{1,5},{2,0},{3,7},{4,6},{5,1},{6,4},{7,3},{8,10},{9,13},{10,... | collective-permute-start | bytes 4718600 | tf_op jit(solution)/shard_map/ppermute | solution.py:104
  304.2 56.7 %collective-permute-start.19 = (bf16[8,96,768]{2,1,0:T(8,128)(2,1)}, bf16[8,96,768]{2,1,0:T(8,128)(2,1)}, u32[]{:S(2)}, u32[]{:S(2)}) collective-permute-start(bf16[8,96,768]{2,1,0:T(8,128)(2,1)} %get-tuple-element.152), channel_id=1, source_target_pairs={{0,2},{1,5},{2,0},{3,7},{4,6},{5,1},{6,4},{7,3},{8,10},{9,13},{10,... | collective-permute-start | bytes 3538952 | tf_op jit(solution)/shard_map/ppermute | solution.py:104
  352.3 106.5 %collective-permute-start.24 = (bf16[4,3,96,1536]{3,2,1,0:T(8,128)(2,1)}, bf16[4,3,96,1536]{3,2,1,0:T(8,128)(2,1)}, u32[]{:S(2)}, u32[]{:S(2)}) collective-permute-start(bf16[4,3,96,1536]{3,2,1,0:T(8,128)(2,1)} %get-tuple-element.163), channel_id=1, source_target_pairs={{0,2},{1,5},{2,0},{3,7},{4,6},{5,1},{6,4},{7,3},{8,10},{9,13},{10,... | collective-permute-start | bytes 10616840 | tf_op jit(solution)/shard_map/ppermute | solution.py:104
  363.8 95.0 %collective-permute-start.26 = (bf16[4,96,768]{2,1,0:T(8,128)(2,1)}, bf16[4,96,768]{2,1,0:T(8,128)(2,1)}, u32[]{:S(2)}, u32[]{:S(2)}) collective-permute-start(bf16[4,96,768]{2,1,0:T(8,128)(2,1)} %get-tuple-element.250), channel_id=1, source_target_pairs={{0,4},{1,3},{2,6},{3,1},{4,0},{5,7},{6,2},{7,5},{8,12},{9,11},{10,... | collective-permute-start | bytes 1769480 | tf_op jit(solution)/shard_map/ppermute | solution.py:104
  379.3 76.6 %collective-permute-start.23 = (bf16[512,1536]{1,0:T(8,128)(2,1)}, bf16[512,1536]{1,0:T(8,128)(2,1)}, u32[]{:S(2)}, u32[]{:S(2)}) collective-permute-start(bf16[512,1536]{1,0:T(8,128)(2,1)} %get-tuple-element.162), channel_id=1, source_target_pairs={{0,1},{1,0},{2,3},{3,2},{4,5},{5,4},{6,7},{7,6},{8,9},{9,8},{10,11... | collective-permute-start | bytes 4718600 | tf_op jit(solution)/shard_map/ppermute | solution.py:54
  385.1 36.5 %collective-permute-start.22 = (bf16[2,2,96,2048]{3,2,1,0:T(8,128)(2,1)S(1)}, bf16[2,2,96,2048]{3,2,1,0:T(8,128)(2,1)S(1)}, u32[]{:S(2)}, u32[]{:S(2)}) collective-permute-start(bf16[2,2,96,2048]{3,2,1,0:T(8,128)(2,1)S(1)} %get-tuple-element.238), channel_id=1, source_target_pairs={{0,8},{1,9},{2,10},{3,11},{4,12},{5,13},{6,14},{7,15},{8,0},{9,1},... | collective-permute-start | bytes 4718600 | tf_op jit(solution)/shard_map/ppermute | solution.py:104
  394.3 64.5 %collective-permute-start.25 = (bf16[2,96,2048]{2,1,0:T(8,128)(2,1)}, bf16[2,96,2048]{2,1,0:T(8,128)(2,1)}, u32[]{:S(2)}, u32[]{:S(2)}) collective-permute-start(bf16[2,96,2048]{2,1,0:T(8,128)(2,1)} %get-tuple-element.248), channel_id=1, source_target_pairs={{0,4},{1,3},{2,6},{3,1},{4,0},{5,7},{6,2},{7,5},{8,12},{9,11},{10,... | collective-permute-start | bytes 2359304 | tf_op jit(solution)/shard_map/ppermute | solution.py:104
  460.2 56.7 %collective-permute-start.31 = (bf16[1,96,2048]{2,1,0:T(8,128)(2,1)S(1)}, bf16[1,96,2048]{2,1,0:T(8,128)(2,1)}, u32[]{:S(2)}, u32[]{:S(2)}) collective-permute-start(bf16[1,96,2048]{2,1,0:T(8,128)(2,1)S(1)} %add_convert_fusion.19), channel_id=1, source_target_pairs={{0,16},{1,17},{2,18},{3,19},{4,20},{5,21},{6,22},{7,23},{8,24},{9,... | collective-permute-start | bytes 1179656 | tf_op jit(solution)/shard_map/ppermute | solution.py:104
  466.1 50.9 %collective-permute-start.30 = (bf16[2,96,768]{2,1,0:T(8,128)(2,1)}, bf16[2,96,768]{2,1,0:T(8,128)(2,1)}, u32[]{:S(2)}, u32[]{:S(2)}) collective-permute-start(bf16[2,96,768]{2,1,0:T(8,128)(2,1)} %get-tuple-element.261), channel_id=1, source_target_pairs={{0,8},{1,9},{2,10},{3,11},{4,12},{5,13},{6,14},{7,15},{8,0},{9,1},... | collective-permute-start | bytes 884744 | tf_op jit(solution)/shard_map/ppermute | solution.py:104
  471.1 45.8 %collective-permute-start.29 = (bf16[2,3,96,1536]{3,2,1,0:T(8,128)(2,1)}, bf16[2,3,96,1536]{3,2,1,0:T(8,128)(2,1)}, u32[]{:S(2)}, u32[]{:S(2)}) collective-permute-start(bf16[2,3,96,1536]{3,2,1,0:T(8,128)(2,1)} %get-tuple-element.236), channel_id=1, source_target_pairs={{0,4},{1,3},{2,6},{3,1},{4,0},{5,7},{6,2},{7,5},{8,12},{9,11},{10,... | collective-permute-start | bytes 5308424 | tf_op jit(solution)/shard_map/ppermute | solution.py:104
  476.2 30.1 %collective-permute-start.32 = (bf16[16,2,96,128]{3,2,1,0:T(8,128)(2,1)}, bf16[16,2,96,128]{3,2,1,0:T(8,128)(2,1)}, u32[]{:S(2)}, u32[]{:S(2)}) collective-permute-start(bf16[16,2,96,128]{3,2,1,0:T(8,128)(2,1)} %get-tuple-element.182), channel_id=1, source_target_pairs={{0,1},{1,0},{2,3},{3,2},{4,5},{5,4},{6,7},{7,6},{8,9},{9,8},{10,11... | collective-permute-start | bytes 2359304 | tf_op jit(solution)/shard_map/ppermute | solution.py:30
  482.0 22.0 %collective-permute-start.27 = (bf16[128,2048]{1,0:T(8,128)(2,1)S(1)}, bf16[128,2048]{1,0:T(8,128)(2,1)S(1)}, u32[]{:S(2)}, u32[]{:S(2)}) collective-permute-start(bf16[128,2048]{1,0:T(8,128)(2,1)S(1)} %constant_dynamic-slice_fusion.1), channel_id=1, source_target_pairs={{0,1},{1,0},{2,3},{3,2},{4,5},{5,4},{6,7},{7,6},{8,9},{9,8},{10,11... | collective-permute-start | bytes 1572872 | tf_op jit(solution)/shard_map/ppermute | solution.py:30
  518.5 49.1 %collective-permute-start.37 = (bf16[1,2,96,2048]{3,2,1,0:T(8,128)(2,1)}, bf16[1,2,96,2048]{3,2,1,0:T(8,128)(2,1)}, u32[]{:S(2)}, u32[]{:S(2)}) collective-permute-start(bf16[1,2,96,2048]{3,2,1,0:T(8,128)(2,1)} %get-tuple-element.245), channel_id=1, source_target_pairs={{0,16},{1,17},{2,18},{3,19},{4,20},{5,21},{6,22},{7,23},{8,24},{9,... | collective-permute-start | bytes 2359304 | tf_op jit(solution)/shard_map/ppermute | solution.py:104
  522.6 39.7 %collective-permute-start.33 = (bf16[1,3,96,1536]{3,2,1,0:T(8,128)(2,1)}, bf16[1,3,96,1536]{3,2,1,0:T(8,128)(2,1)}, u32[]{:S(2)}, u32[]{:S(2)}) collective-permute-start(bf16[1,3,96,1536]{3,2,1,0:T(8,128)(2,1)} %add_convert_fusion.11), channel_id=1, source_target_pairs={{0,8},{1,9},{2,10},{3,11},{4,12},{5,13},{6,14},{7,15},{8,0},{9,1},... | collective-permute-start | bytes 2654216 | tf_op jit(solution)/shard_map/ppermute | solution.py:104
  525.2 40.4 %collective-permute-start.36 = (bf16[1,96,768]{2,1,0:T(8,128)(2,1)S(1)}, bf16[1,96,768]{2,1,0:T(8,128)(2,1)}, u32[]{:S(2)}, u32[]{:S(2)}) collective-permute-start(bf16[1,96,768]{2,1,0:T(8,128)(2,1)S(1)} %add_convert_fusion.22), channel_id=1, source_target_pairs={{0,16},{1,17},{2,18},{3,19},{4,20},{5,21},{6,22},{7,23},{8,24},{9,... | collective-permute-start | bytes 442376 | tf_op jit(solution)/shard_map/ppermute | solution.py:104
  567.5 22.2 %collective-permute-start.35 = (bf16[1,3,96,768]{3,2,1,0:T(8,128)(2,1)S(1)}, bf16[1,3,96,768]{3,2,1,0:T(8,128)(2,1)S(1)}, u32[]{:S(2)}, u32[]{:S(2)}) collective-permute-start(bf16[1,3,96,768]{3,2,1,0:T(8,128)(2,1)S(1)} %fusion.25), channel_id=1, source_target_pairs={{0,16},{1,17},{2,18},{3,19},{4,20},{5,21},{6,22},{7,23},{8,24},{9,... | collective-permute-start | bytes 1327112 | tf_op jit(solution)/shard_map/ppermute | solution.py:104
  (64 other events, 480.9 us)
Sparse Core Ops, SparseCore 0:
  12.9 194.2 all-gather.1

commit v12 on v10

--- a/solution.py
+++ b/solution.py
@@ -183,11 +183,17 @@
     )(mods)
 
 
-def advance(chains, value):
+def settle(chains, value):
     live = [c for c in chains if c.got is not None]
     value, got = lax.optimization_barrier((value, [c.got for c in live]))
     for c, g in zip(live, got):
         c.got = g
+    return value
+
+
+def advance(chains, value):
+    value = settle(chains, value)
+    for c in chains:
         c.step()
     return value
 
@@ -935,6 +941,7 @@
     outgoing = outgoing.reshape(2, dpn, share, TEXT // n).transpose(1, 0, 2, 3)
     text_in, pair_cols = text_bwd(pair_all, w_text, outgoing)
     text_in, grad_first = advance([qkv_chain], (text_in, grad_first))
+    pair_cols, qkv_chain.keep = lax.optimization_barrier((pair_cols, qkv_chain.keep))
     text_in = jnp.concatenate(natural(exchange_rot(text_in, 0)), axis=1)
 
     inverse_one = inverse_rms(x_own)
@@ -956,7 +963,7 @@
     mods = jnp.concatenate([sums[:4], stamp], axis=0).reshape(5, dpn, share).transpose(1, 0, 2)
     mods = jnp.pad(mods, ((0, 0), (0, 0), (0, -share % 128)))
     mods = jnp.concatenate([mods, small.reshape(dpn, SUMS, 128)], axis=1)
-    mods = advance([down_chain, out_chain], mods)
+    mods = settle([wide_chain], advance([down_chain, out_chain], mods))
     mods, small = small_exchange(mods)
     chains = [out_chain, down_chain] if paired else [qkv_chain, out_chain, down_chain]
     if paired:

time: 579 us -> 585 us (1.010)
  waiting for transfers between devices: 54.8 us -> 70.6 us
  Pallas kernels: 325 us -> 312 us
    ppermute x16, waiting for transfers between devices: 43.1 us -> 59 us  [dp_swap(): return lax.ppermute(value, ('dp', 'fsdp'), pairs)]
    pallas_call x1, Pallas kernels: 36.7 us -> 20.9 us  [small_exchange(): pl.pallas_call(small_kernel, in_specs=[vmem], out_specs=[vmem] * 2, out_s...]
    convert_element_type x7 -> x9, other arithmetic: 32.1 us -> 39.8 us  [step(): self.keep = add(slice(half)).astype(BF16)]
    convert_element_type x4 -> x2, other arithmetic: 10.1 us -> 2.8 us  [step(): send = add(slice(half, None)).astype(BF16)]
  transfers between devices with their start and end apart: 39 -> 39, of which waited for: 12 -> 12; matrix products, arithmetic and copies ran while one was open for 23% -> 22% of each run, Pallas kernels for 57% -> 54%
where the time goes in v12:
time: 585 us; the launch traced here: 579 us
  Pallas kernels  312 us (53%)
  other arithmetic  97.5 us (17%)
  waiting for transfers between devices  70.6 us (12%)
  starting transfers between devices  31.9 us (5%)
  local copies, waits for them, and re-layouts  27.1 us (5%)
  matrix products  21.5 us (4%)
  between operations  16.6 us (3%)
    pallas_call x1, Pallas kernels, ffn(): pl.pallas_call(functools.partial(ffn_kernel, orders), grid=(hid // bc,),...  90.2 us
    pallas_call x2, Pallas kernels, attn_backward(): pl.pallas_call(attn_bwd_kernel, grid=(blocks,), in_specs=[scalar, col, co...  68.8 us
    ppermute x16, waiting for transfers between devices, dp_swap(): return lax.ppermute(value, ('dp', 'fsdp'), pairs)  59 us
    convert_element_type x9, other arithmetic, step(): self.keep = add(slice(half)).astype(BF16)  39.8 us
    pallas_call x1, Pallas kernels, attn_forward(): pl.pallas_call(attn_fwd_kernel, grid=(blocks,), in_specs=[scalar, three,...  32.1 us
    pallas_call x1, Pallas kernels, text_bwd(): pl.pallas_call(text_bwd_kernel, grid=(depth // bk,), in_specs=[pl.BlockSp...  27.5 us
    ppermute x16, starting transfers between devices, dp_swap(): return lax.ppermute(value, ('dp', 'fsdp'), pairs)  26.6 us
    pallas_call x1, Pallas kernels, small_exchange(): pl.pallas_call(small_kernel, in_specs=[vmem], out_specs=[vmem] * 2, out_s...  20.9 us
  transfers between devices with their start and end apart: 39, of which 12 were waited for; matrix products, arithmetic and copies ran while one was open for 22% of the time, Pallas kernels for 54%

profile of v12, /device:TPU:0, one launch (start us, length us, event | category | flops | bytes accessed | tf_op | source)
XLA Modules:
  0.0 579.4 jit_solution(9326394201258132635)
XLA Ops:
  17.9 4.7 fusion.2
  23.3 16.2 %shard_map.222 = f32[2,256,1536]{2,1,0:T(8,128)} custom-call(bf16[256,2048]{1,0:T(8,128)(2,1)} %pad_maximum_fusion.2.x_ref, bf16[2048,2,1536]{2,1,0:T(2,128)(2,1)} %w_ref.5), custom_call_target="tpu_custom_call" | custom-call | tf_op jit(solution)/shard_map/pallas_call | solution.py:427
  53.3 14.3 %shard_map.221 = (bf16[1024,1536]{1,0:T(8,128)(2,1)}, f32[3,1024,768]{2,1,0:T(8,128)}, f32[8,1024]{1,0:T(8,128)}) custom-call(s32[2]{0:T(128)} %pad_add_fusion.1.id_ref, bf16[512,1536]{1,0:T(8,128)(2,1)} %bitcast.127, bf16[512,1536]{1,0:T(8,128)(2,1)} %collective-permute-done.1.xp_ref, f32[1,1536]{1,0:T(1,128)} %get-tuple-element.276.front_ref, ...), custom_call_target="tpu_custom_call" | custom-call | tf_op jit(solution)/shard_map/pallas_call | solution.py:615
  70.4 32.1 %shard_map.223 = (bf16[1024,768]{1,0:T(8,128)(2,1)}, bf16[1024,768]{1,0:T(8,128)(2,1)}, bf16[1024,768]{1,0:T(8,128)(2,1)}, bf16[1024,768]{1,0:T(8,128)(2,1)}, f3...) custom-call(s32[1]{0:T(128)S(6)} %copy.48.len_ref, ...), custom_call_target="tpu_custom_call" | custom-call | tf_op jit(solution)/shard_map/pallas_call | solution.py:370
  120.3 90.2 %shard_map.224 = (bf16[8,2,96,2048]{3,2,1,0:T(8,128)(2,1)}, bf16[8,2,96,2048]{3,2,1,0:T(8,128)(2,1)}, bf16[8,96,2048]{2,1,0:T(8,128)(2,1)}, bf16[8,96,2048]{2,1,...) custom-call(s32[2]{0:T(128)} %pad_add_fusion.1.id_ref, ...), custom_call_target="tpu_custom_call" | custom-call | tf_op jit(solution)/shard_map/pallas_call | solution.py:558
  217.1 4.3 multiply_reduce_fusion
  221.5 5.8 %fusion.7 = (f32[1536]{0:T(1024)S(1)}, bf16[1,512,1536]{2,1,0:T(8,128)(2,1)}, f32[1536]{0:T(1024)S(1)}, f32[512,1536]{1,0:T(8,128)S(1)}) fusion(f32[512,1536]{1,0:T(8,128)} %get-tuple-element.115, bf16[512,1536]{1,0:T(8,128)(2,1)S(1)} %collective-permute-done.11, bf16[1,512,1536]{2,1,0:T(8,128)(2,1)} %param.19, f32[512,1536]{1,0:T(8,128)S(1)} %copy-done.1, ...), kind=kLoop, calls=%fused_computation.18 | loop fusion | flops 16512000 | bytes 23627776 | tf_op jit(solution)/shard_map/reduce_sum | solution.py:877
  232.4 9.6 %shard_map.225 = (f32[1024,768]{1,0:T(8,128)}, bf16[8,96,768]{2,1,0:T(8,128)(2,1)}, bf16[8,96,768]{2,1,0:T(8,128)(2,1)}) custom-call(s32[2]{0:T(128)} %pad_add_fusion.1.id_ref, bf16[512,1536]{1,0:T(8,128)(2,1)} %copy-done.18, bf16[512,1536]{1,0:T(8,128)(2,1)} %collective-permute-done.13.refs_1_, bf16[768,1536]{1,0:T(8,128)(2,1)} %refs_2_.1, ...), custom_call_target="tpu_custom_call" | custom-call | tf_op jit(solution)/shard_map/pallas_call | solution.py:743
  242.0 44.5 %shard_map.226 = (f32[3,1024,512]{2,1,0:T(8,128)}, f32[256,512]{1,0:T(8,128)}, f32[256,512]{1,0:T(8,128)}, f32[8,1024]{1,0:T(8,128)}, f32[1,512]{1,0:T(1,128)}, /*index=5*/f32[1,512]{1,0:T(1,128)}, f32[1,512]{1,0:T(1,128)}) custom-call(s32[1]{0:T(128)S(6)} %copy.48.len_ref, bf16[1024,768]{1,0:T(8,128)(2,1)} %get-tuple-element.119.q_ref, ...), custom_call_target="tpu_custom_call" | custom-call | tf_op jit(solution)/shard_map/pallas_call | solution.py:385
  286.5 8.2 %add_convert_fusion = (bf16[4,2,96,2048]{3,2,1,0:T(8,128)(2,1)}, bf16[4,2,96,2048]{3,2,1,0:T(8,128)(2,1)}) fusion(bf16[8,2,96,2048]{3,2,1,0:T(8,128)(2,1)} %collective-permute-done.14, bf16[8,2,96,2048]{3,2,1,0:T(8,128)(2,1)} %get-tuple-element.154), kind=kLoop, calls=%fused_computation.4 | loop fusion | flops 12582912 | bytes 18874368 | tf_op jit(solution)/shard_map/convert_element_type | solution.py:130
  296.9 6.1 %add_convert_fusion.5 = (bf16[4,96,2048]{2,1,0:T(8,128)(2,1)}, bf16[4,96,2048]{2,1,0:T(8,128)(2,1)}) fusion(bf16[8,96,2048]{2,1,0:T(8,128)(2,1)} %collective-permute-done.15, bf16[8,96,2048]{2,1,0:T(8,128)(2,1)} %get-tuple-element.156), kind=kLoop, calls=%fused_computation.34 | loop fusion | flops 6291456 | bytes 9437184 | tf_op jit(solution)/shard_map/convert_element_type | solution.py:130
  306.3 24.3 %shard_map.227 = (f32[3,1024,256]{2,1,0:T(8,128)}, f32[256,256]{1,0:T(8,128)}, f32[256,256]{1,0:T(8,128)}, f32[8,1024]{1,0:T(8,128)}, f32[1,256]{1,0:T(1,128)}, /*index=5*/f32[1,256]{1,0:T(1,128)}, f32[1,256]{1,0:T(1,128)}) custom-call(s32[1]{0:T(128)S(6)} %copy.48.len_ref, bf16[1024,768]{1,0:T(8,128)(2,1)} %get-tuple-element.119.q_ref, ...), custom_call_target="tpu_custom_call" | custom-call | tf_op jit(solution)/shard_map/pallas_call | solution.py:385
  333.9 18.8 %shard_map.228 = (bf16[4,3,96,1536]{3,2,1,0:T(8,128)(2,1)}, bf16[4,3,96,1536]{3,2,1,0:T(8,128)(2,1)}, bf16[3,1024,768]{2,1,0:T(8,128)(2,1)}) custom-call(s32[2]{0:T(128)} %pad_add_fusion.1.id_ref, f32[3,1024,512]{2,1,0:T(8,128)} %get-tuple-element.150.da_ref, f32[3,1024,256]{2,1,0:T(8,128)} %get-tuple-element.151.db_ref, ...), custom_call_target="tpu_custom_call" | custom-call | tf_op jit(solution)/shard_map/pallas_call | solution.py:662
  353.3 7.6 %collective-permute-done.19 = bf16[8,96,768]{2,1,0:T(8,128)(2,1)} collective-permute-done((bf16[8,96,768]{2,1,0:T(8,128)(2,1)}, bf16[8,96,768]{2,1,0:T(8,128)(2,1)}, u32[]{:S(2)}, u32[]{:S(2)}) %collective-permute-start.19) | collective-permute-done | bytes 1179680 | tf_op jit(solution)/shard_map/ppermute | solution.py:104
  365.3 5.1 add_convert_fusion.4
  381.8 13.7 %shard_map.230 = (f32[512,1536]{1,0:T(8,128)}, bf16[512,1536]{1,0:T(8,128)(2,1)}) custom-call(s32[2]{0:T(128)} %pad_add_fusion.1.id_ref, bf16[3,1024,768]{2,1,0:T(8,128)(2,1)} %get-tuple-element.170.g_ref, bf16[3,768,1536]{2,1,0:T(8,128)(2,1)} %bitcast.126, bf16[3,768,768]{2,1,0:T(8,128)(2,1)} %collective-permute-done.2.got_ref), custom_call_target="tpu_custom_call" | custom-call | tf_op jit(solution)/shard_map/pallas_call | solution.py:708
  397.3 16.2 %collective-permute-done.22 = bf16[4,3,96,1536]{3,2,1,0:T(8,128)(2,1)} collective-permute-done((bf16[4,3,96,1536]{3,2,1,0:T(8,128)(2,1)}, bf16[4,3,96,1536]{3,2,1,0:T(8,128)(2,1)}, u32[]{:S(2)}, u32[]{:S(2)}) %collective-permute-start.22) | collective-permute-done | bytes 3538976 | tf_op jit(solution)/shard_map/ppermute | solution.py:104
  417.0 4.9 add_convert_fusion.2
  433.2 27.5 %shard_map.229 = (bf16[256,2048]{1,0:T(8,128)(2,1)}, bf16[16,2,96,128]{3,2,1,0:T(8,128)(2,1)}) custom-call(bf16[2,256,1536]{2,1,0:T(8,128)(2,1)} %copy-done.12, bf16[2048,2,1536]{2,1,0:T(2,128)(2,1)} %w_ref.5, bf16[16,2,96,128]{3,2,1,0:T(8,128)(2,1)} %bitcast.131), custom_call_target="tpu_custom_call" | custom-call | tf_op jit(solution)/shard_map/pallas_call | solution.py:463
  464.5 5.7 collective-permute-start.32
  486.0 18.3 %collective-permute-done.32 = bf16[1,2,96,2048]{3,2,1,0:T(8,128)(2,1)} collective-permute-done((bf16[1,2,96,2048]{3,2,1,0:T(8,128)(2,1)}, bf16[1,2,96,2048]{3,2,1,0:T(8,128)(2,1)}, u32[]{:S(2)}, u32[]{:S(2)}) %collective-permute-start.32) | collective-permute-done | bytes 786464 | tf_op jit(solution)/shard_map/ppermute | solution.py:104
  504.4 20.9 %shard_map.231 = (f32[16,8,128]{2,1,0:T(8,128)}, f32[16,8,128]{2,1,0:T(8,128)}) custom-call(f32[16,8,128]{2,1,0:T(8,128)} %select_maximum_fusion.mod_ref), custom_call_target="tpu_custom_call" | custom-call | tf_op jit(solution)/shard_map/pallas_call | solution.py:172
  531.1 8.8 %fusion = f32[2048,2,96]{0,2,1:T(8,128)} fusion(bf16[2,96,4096]{2,1,0:T(8,128)(2,1)S(1)} %bitcast.134, bf16[4096,2048]{1,0:T(8,128)(2,1)} %all-gather.2.cloned.1.call-done), kind=kOutput, calls=%fused_computation | convolution fusion | flops 3221225472 | bytes 19922944 | tf_op jit(solution)/shard_map/dot_general | solution.py:25
  554.4 16.8 %collective-permute-done.37 = bf16[1,3,96,768]{3,2,1,0:T(8,128)(2,1)S(1)} collective-permute-done((bf16[1,3,96,768]{3,2,1,0:T(8,128)(2,1)S(1)}, bf16[1,3,96,768]{3,2,1,0:T(8,128)(2,1)S(1)}, u32[]{:S(2)}, u32[]{:S(2)}) %collective-permute-start.37) | collective-permute-done | bytes 442400 | tf_op jit(solution)/shard_map/ppermute | solution.py:104
  (307 shorter events, 138.1 us)
Async XLA Ops:
  7.2 206.3 %all-gather.2.cloned.1.call-start = ((), (), s32[]{:S(2)}) async-start(), calls=%async_computation | async-start | bytes 17825792 | tf_op jit(solution)/shard_map/all_gather | solution.py:818
  16.8 36.5 %collective-permute-start.2 = (bf16[3,768,768]{2,1,0:T(8,128)(2,1)}, bf16[3,768,768]{2,1,0:T(8,128)(2,1)}, u32[]{:S(2)}, u32[]{:S(2)}) collective-permute-start(bf16[3,768,768]{2,1,0:T(8,128)(2,1)} %dynamic-slice_bitcast_fusion), channel_id=1, source_target_pairs={{0,1},{1,0},{2,3},{3,2},{4,5},{5,4},{6,7},{7,6},{8,9},{9,8},{10,11... | collective-permute-start | bytes 10616840 | tf_op jit(solution)/shard_map/ppermute | solution.py:30
  22.6 26.7 %collective-permute-start = (f32[4,1536]{1,0:T(4,128)S(1)}, f32[4,1536]{1,0:T(4,128)S(1)}, u32[]{:S(2)}, u32[]{:S(2)}) collective-permute-start(f32[4,1536]{1,0:T(4,128)S(1)} %bitcast.138), channel_id=1, source_target_pairs={{0,1},{1,0},{2,3},{3,2},{4,5},{5,4},{6,7},{7,6},{8,9},{9,8},{10,11... | collective-permute-start | bytes 73736 | tf_op jit(solution)/shard_map/ppermute | solution.py:30
  22.8 30.5 %collective-permute-start.1 = (bf16[512,1536]{1,0:T(8,128)(2,1)S(1)}, bf16[512,1536]{1,0:T(8,128)(2,1)}, u32[]{:S(2)}, u32[]{:S(2)}) collective-permute-start(bf16[512,1536]{1,0:T(8,128)(2,1)S(1)} %bitcast.128), channel_id=1, source_target_pairs={{0,1},{1,0},{2,3},{3,2},{4,5},{5,4},{6,7},{7,6},{8,9},{9,8},{10,11... | collective-permute-start | bytes 4718600 | tf_op jit(solution)/shard_map/ppermute | solution.py:30
  23.1 22.9 %collective-permute-start.4 = (s32[2,512]{1,0:T(2,128)S(1)}, s32[2,512]{1,0:T(2,128)S(1)}, u32[]{:S(2)}, u32[]{:S(2)}) collective-permute-start(s32[2,512]{1,0:T(2,128)S(1)} %bitcast.151), channel_id=1, source_target_pairs={{0,1},{1,0},{2,3},{3,2},{4,5},{5,4},{6,7},{7,6},{8,9},{9,8},{10,11... | collective-permute-start | bytes 12296 | tf_op jit(solution)/shard_map/ppermute | solution.py:30
  210.5 75.9 %collective-permute-start.14 = (bf16[8,2,96,2048]{3,2,1,0:T(8,128)(2,1)}, bf16[8,2,96,2048]{3,2,1,0:T(8,128)(2,1)}, u32[]{:S(2)}, u32[]{:S(2)}) collective-permute-start(bf16[8,2,96,2048]{3,2,1,0:T(8,128)(2,1)} %get-tuple-element.141), channel_id=1, source_target_pairs={{0,2},{1,5},{2,0},{3,7},{4,6},{5,1},{6,4},{7,3},{8,10},{9,13},{10,... | collective-permute-start | bytes 18874376 | tf_op jit(solution)/shard_map/ppermute | solution.py:104
  214.0 72.5 %collective-permute-start.15 = (bf16[8,96,2048]{2,1,0:T(8,128)(2,1)}, bf16[8,96,2048]{2,1,0:T(8,128)(2,1)}, u32[]{:S(2)}, u32[]{:S(2)}) collective-permute-start(bf16[8,96,2048]{2,1,0:T(8,128)(2,1)} %get-tuple-element.142), channel_id=1, source_target_pairs={{0,8},{1,9},{2,10},{3,11},{4,12},{5,13},{6,14},{7,15},{8,0},{9,1},... | collective-permute-start | bytes 9437192 | tf_op jit(solution)/shard_map/ppermute | solution.py:104
  294.6 66.2 %collective-permute-start.17 = (bf16[4,2,96,2048]{3,2,1,0:T(8,128)(2,1)}, bf16[4,2,96,2048]{3,2,1,0:T(8,128)(2,1)}, u32[]{:S(2)}, u32[]{:S(2)}) collective-permute-start(bf16[4,2,96,2048]{3,2,1,0:T(8,128)(2,1)} %get-tuple-element.246), channel_id=1, source_target_pairs={{0,4},{1,3},{2,6},{3,1},{4,0},{5,7},{6,2},{7,5},{8,12},{9,11},{10,... | collective-permute-start | bytes 9437192 | tf_op jit(solution)/shard_map/ppermute | solution.py:104
  303.0 57.8 %collective-permute-start.18 = (bf16[4,96,2048]{2,1,0:T(8,128)(2,1)}, bf16[4,96,2048]{2,1,0:T(8,128)(2,1)}, u32[]{:S(2)}, u32[]{:S(2)}) collective-permute-start(bf16[4,96,2048]{2,1,0:T(8,128)(2,1)} %get-tuple-element.252), channel_id=1, source_target_pairs={{0,2},{1,5},{2,0},{3,7},{4,6},{5,1},{6,4},{7,3},{8,10},{9,13},{10,... | collective-permute-start | bytes 4718600 | tf_op jit(solution)/shard_map/ppermute | solution.py:104
  304.2 56.7 %collective-permute-start.19 = (bf16[8,96,768]{2,1,0:T(8,128)(2,1)}, bf16[8,96,768]{2,1,0:T(8,128)(2,1)}, u32[]{:S(2)}, u32[]{:S(2)}) collective-permute-start(bf16[8,96,768]{2,1,0:T(8,128)(2,1)} %get-tuple-element.158), channel_id=1, source_target_pairs={{0,2},{1,5},{2,0},{3,7},{4,6},{5,1},{6,4},{7,3},{8,10},{9,13},{10,... | collective-permute-start | bytes 3538952 | tf_op jit(solution)/shard_map/ppermute | solution.py:104
  352.7 60.8 %collective-permute-start.22 = (bf16[4,3,96,1536]{3,2,1,0:T(8,128)(2,1)}, bf16[4,3,96,1536]{3,2,1,0:T(8,128)(2,1)}, u32[]{:S(2)}, u32[]{:S(2)}) collective-permute-start(bf16[4,3,96,1536]{3,2,1,0:T(8,128)(2,1)} %get-tuple-element.163), channel_id=1, source_target_pairs={{0,2},{1,5},{2,0},{3,7},{4,6},{5,1},{6,4},{7,3},{8,10},{9,13},{10,... | collective-permute-start | bytes 10616840 | tf_op jit(solution)/shard_map/ppermute | solution.py:104
  363.8 49.8 %collective-permute-start.25 = (bf16[4,96,768]{2,1,0:T(8,128)(2,1)}, bf16[4,96,768]{2,1,0:T(8,128)(2,1)}, u32[]{:S(2)}, u32[]{:S(2)}) collective-permute-start(bf16[4,96,768]{2,1,0:T(8,128)(2,1)} %get-tuple-element.264), channel_id=1, source_target_pairs={{0,4},{1,3},{2,6},{3,1},{4,0},{5,7},{6,2},{7,5},{8,12},{9,11},{10,... | collective-permute-start | bytes 1769480 | tf_op jit(solution)/shard_map/ppermute | solution.py:104
  370.4 43.1 %collective-permute-start.23 = (bf16[2,2,96,2048]{3,2,1,0:T(8,128)(2,1)}, bf16[2,2,96,2048]{3,2,1,0:T(8,128)(2,1)}, u32[]{:S(2)}, u32[]{:S(2)}) collective-permute-start(bf16[2,2,96,2048]{3,2,1,0:T(8,128)(2,1)} %get-tuple-element.250), channel_id=1, source_target_pairs={{0,8},{1,9},{2,10},{3,11},{4,12},{5,13},{6,14},{7,15},{8,0},{9,1},... | collective-permute-start | bytes 4718600 | tf_op jit(solution)/shard_map/ppermute | solution.py:104
  375.4 20.1 %collective-permute-start.21 = (bf16[2,256,768]{2,1,0:T(8,128)(2,1)}, bf16[2,256,768]{2,1,0:T(8,128)(2,1)}, u32[]{:S(2)}, u32[]{:S(2)}) collective-permute-start(bf16[2,256,768]{2,1,0:T(8,128)(2,1)} %maximum_maximum_fusion), channel_id=1, source_target_pairs={{0,1},{1,0},{2,3},{3,2},{4,5},{5,4},{6,7},{7,6},{8,9},{9,8},{10,11... | collective-permute-start | bytes 2359304 | tf_op jit(solution)/shard_map/ppermute | solution.py:30
  378.7 34.8 %collective-permute-start.24 = (bf16[2,96,2048]{2,1,0:T(8,128)(2,1)}, bf16[2,96,2048]{2,1,0:T(8,128)(2,1)}, u32[]{:S(2)}, u32[]{:S(2)}) collective-permute-start(bf16[2,96,2048]{2,1,0:T(8,128)(2,1)} %get-tuple-element.262), channel_id=1, source_target_pairs={{0,4},{1,3},{2,6},{3,1},{4,0},{5,7},{6,2},{7,5},{8,12},{9,11},{10,... | collective-permute-start | bytes 2359304 | tf_op jit(solution)/shard_map/ppermute | solution.py:104
  395.5 74.7 %collective-permute-start.26 = (bf16[512,1536]{1,0:T(8,128)(2,1)}, bf16[512,1536]{1,0:T(8,128)(2,1)}, u32[]{:S(2)}, u32[]{:S(2)}) collective-permute-start(bf16[512,1536]{1,0:T(8,128)(2,1)} %get-tuple-element.172), channel_id=1, source_target_pairs={{0,1},{1,0},{2,3},{3,2},{4,5},{5,4},{6,7},{7,6},{8,9},{9,8},{10,11... | collective-permute-start | bytes 4718600 | tf_op jit(solution)/shard_map/ppermute | solution.py:54
  415.5 69.5 %collective-permute-start.31 = (bf16[2,96,768]{2,1,0:T(8,128)(2,1)}, bf16[2,96,768]{2,1,0:T(8,128)(2,1)}, u32[]{:S(2)}, u32[]{:S(2)}) collective-permute-start(bf16[2,96,768]{2,1,0:T(8,128)(2,1)} %get-tuple-element.275), channel_id=1, source_target_pairs={{0,8},{1,9},{2,10},{3,11},{4,12},{5,13},{6,14},{7,15},{8,0},{9,1},... | collective-permute-start | bytes 884744 | tf_op jit(solution)/shard_map/ppermute | solution.py:104
  421.8 50.5 %collective-permute-start.27 = (bf16[2,3,96,1536]{3,2,1,0:T(8,128)(2,1)}, bf16[2,3,96,1536]{3,2,1,0:T(8,128)(2,1)}, u32[]{:S(2)}, u32[]{:S(2)}) collective-permute-start(bf16[2,3,96,1536]{3,2,1,0:T(8,128)(2,1)} %get-tuple-element.248), channel_id=1, source_target_pairs={{0,4},{1,3},{2,6},{3,1},{4,0},{5,7},{6,2},{7,5},{8,12},{9,11},{10,... | collective-permute-start | bytes 5308424 | tf_op jit(solution)/shard_map/ppermute | solution.py:104
  425.2 59.9 %collective-permute-start.30 = (bf16[1,96,2048]{2,1,0:T(8,128)(2,1)}, bf16[1,96,2048]{2,1,0:T(8,128)(2,1)}, u32[]{:S(2)}, u32[]{:S(2)}) collective-permute-start(bf16[1,96,2048]{2,1,0:T(8,128)(2,1)} %add_convert_fusion.19), channel_id=1, source_target_pairs={{0,16},{1,17},{2,18},{3,19},{4,20},{5,21},{6,22},{7,23},{8,24},{9,... | collective-permute-start | bytes 1179656 | tf_op jit(solution)/shard_map/ppermute | solution.py:104
  464.5 39.8 %collective-permute-start.32 = (bf16[1,2,96,2048]{3,2,1,0:T(8,128)(2,1)}, bf16[1,2,96,2048]{3,2,1,0:T(8,128)(2,1)}, u32[]{:S(2)}, u32[]{:S(2)}) collective-permute-start(bf16[1,2,96,2048]{3,2,1,0:T(8,128)(2,1)} %get-tuple-element.260), channel_id=1, source_target_pairs={{0,16},{1,17},{2,18},{3,19},{4,20},{5,21},{6,22},{7,23},{8,24},{9,... | collective-permute-start | bytes 2359304 | tf_op jit(solution)/shard_map/ppermute | solution.py:104
  479.8 60.1 %collective-permute-start.33 = (bf16[1,3,96,1536]{3,2,1,0:T(8,128)(2,1)}, bf16[1,3,96,1536]{3,2,1,0:T(8,128)(2,1)}, u32[]{:S(2)}, u32[]{:S(2)}) collective-permute-start(bf16[1,3,96,1536]{3,2,1,0:T(8,128)(2,1)} %get-tuple-element.258), channel_id=1, source_target_pairs={{0,8},{1,9},{2,10},{3,11},{4,12},{5,13},{6,14},{7,15},{8,0},{9,1},... | collective-permute-start | bytes 2654216 | tf_op jit(solution)/shard_map/ppermute | solution.py:104
  482.8 46.6 %collective-permute-start.35 = (bf16[16,2,96,128]{3,2,1,0:T(8,128)(2,1)}, bf16[16,2,96,128]{3,2,1,0:T(8,128)(2,1)S(1)}, u32[]{:S(2)}, u32[]{:S(2)}) collective-permute-start(bf16[16,2,96,128]{3,2,1,0:T(8,128)(2,1)} %get-tuple-element.196), channel_id=1, source_target_pairs={{0,1},{1,0},{2,3},{3,2},{4,5},{5,4},{6,7},{7,6},{8,9},{9,8},{10,11... | collective-permute-start | bytes 2359304 | tf_op jit(solution)/shard_map/ppermute | solution.py:30
  484.9 43.2 %collective-permute-start.28 = (bf16[128,2048]{1,0:T(8,128)(2,1)S(1)}, bf16[128,2048]{1,0:T(8,128)(2,1)S(1)}, u32[]{:S(2)}, u32[]{:S(2)}) collective-permute-start(bf16[128,2048]{1,0:T(8,128)(2,1)S(1)} %constant_dynamic-slice_fusion.1), channel_id=1, source_target_pairs={{0,1},{1,0},{2,3},{3,2},{4,5},{5,4},{6,7},{7,6},{8,9},{9,8},{10,11... | collective-permute-start | bytes 1572872 | tf_op jit(solution)/shard_map/ppermute | solution.py:30
  548.2 23.0 %collective-permute-start.37 = (bf16[1,3,96,768]{3,2,1,0:T(8,128)(2,1)S(1)}, bf16[1,3,96,768]{3,2,1,0:T(8,128)(2,1)S(1)}, u32[]{:S(2)}, u32[]{:S(2)}) collective-permute-start(bf16[1,3,96,768]{3,2,1,0:T(8,128)(2,1)S(1)} %fusion.25), channel_id=1, source_target_pairs={{0,16},{1,17},{2,18},{3,19},{4,20},{5,21},{6,22},{7,23},{8,24},{9,... | collective-permute-start | bytes 1327112 | tf_op jit(solution)/shard_map/ppermute | solution.py:104
  (72 other events, 1180.8 us)
Sparse Core Ops, SparseCore 0:
  12.9 194.2 all-gather.1

commit v13 on v11

--- a/solution.py
+++ b/solution.py
@@ -936,11 +936,18 @@
     grad_tk = (inv_t * (text_hat - normed_t * mean_t)).astype(BF16)
     text_pair = jnp.stack([grad_tk, dtv.astype(BF16)])
     pair_all = jnp.concatenate(natural(gather_rot(text_pair)), axis=-1)
-    pair_all = settle([wide_chain], pair_all)
     outgoing = block_of(pair_all.transpose(0, 2, 1), f, 2)
     outgoing = outgoing.reshape(2, dpn, share, TEXT // n).transpose(1, 0, 2, 3)
+    pair_all, outgoing = settle(
+        [qkv_chain, wide_chain, down_chain, out_chain], (pair_all, outgoing)
+    )
+    for chain in (qkv_chain, down_chain, out_chain):
+        chain.step()
     text_in, pair_cols = text_bwd(pair_all, w_text, outgoing)
-    text_in, grad_first = advance([qkv_chain, down_chain, out_chain], (text_in, grad_first))
+    text_in, grad_first = advance(
+        [qkv_chain, wide_chain, down_chain, out_chain], (text_in, grad_first)
+    )
+    pair_cols, qkv_chain.keep = lax.optimization_barrier((pair_cols, qkv_chain.keep))
     text_in = jnp.concatenate(natural(exchange_rot(text_in, 0)), axis=1)
 
     inverse_one = inverse_rms(x_own)
@@ -962,11 +969,19 @@
     mods = jnp.concatenate([sums[:4], stamp], axis=0).reshape(5, dpn, share).transpose(1, 0, 2)
     mods = jnp.pad(mods, ((0, 0), (0, 0), (0, -share % 128)))
     mods = jnp.concatenate([mods, small.reshape(dpn, SUMS, 128)], axis=1)
-    mods, small = small_exchange(mods)
-    mods = advance([qkv_chain, wide_chain, out_chain, down_chain], mods)
     pair_cols = jnp.concatenate(natural(gather_rot(pair_cols)), axis=3)
     pair_cols = pair_cols.transpose(1, 2, 0, 3).reshape(2 * share, dpn * TEXT)
     text_grad = dot(pair_cols, text_all).reshape(2, share, TW // n)
+    mods, text_grad = settle([wide_chain], (mods, text_grad))
+    if paired:
+        mods = advance([qkv_chain], mods)
+        own_side = f == (me >> low_bits[-1] + 1)
+        mine, got = exchange_rot(qkv_chain.last[0].astype(BF16), 2)
+        keep, send = jnp.where(own_side, mine, got)[None], jnp.where(own_side, got, mine)[None]
+        mods, keep, send = lax.optimization_barrier((mods, keep, send))
+        qkv_chain = Halving(bits[-1:], keep, send)
+    mods, small = small_exchange(mods)
+    mods = settle([qkv_chain], mods)
     total = small[:, 5 : 5 + SUMS].reshape(-1)[: 6 * own_d].reshape(6, own_d)
     gate_total = jnp.sum(total[5].reshape(HEADS // n, HD), axis=1) * (
         1.0 - head_tanh * head_tanh
@@ -978,14 +993,6 @@
         precision=lax.Precision.HIGHEST,
     ).reshape(4, share, own_te)
 
-    if paired:
-        text_grad = advance([qkv_chain], text_grad)
-        own_side = f == (me >> low_bits[-1] + 1)
-        mine, got = exchange_rot(qkv_chain.last[0].astype(BF16), 2)
-        got, wide_chain.keep = lax.optimization_barrier((got, wide_chain.keep))
-        qkv_chain = Halving(
-            bits[-1:], jnp.where(own_side, mine, got)[None], jnp.where(own_side, got, mine)[None]
-        )
     for chain in (out_chain, down_chain, wide_chain, qkv_chain):
         while chain.got is not None:
             chain.step()

time: 603 us -> 581 us (0.964)
  waiting for transfers between devices: 97.5 us -> 51.9 us
  Pallas kernels: 308 us -> 320 us
  other arithmetic: 96.3 us -> 107 us
    ppermute x16, waiting for transfers between devices: 85.7 us -> 39.6 us  [dp_swap(): return lax.ppermute(value, ('dp', 'fsdp'), pairs)]
    pallas_call x1, Pallas kernels: 16.7 us -> 25.9 us  [small_exchange(): pl.pallas_call(small_kernel, in_specs=[vmem], out_specs=[vmem] * 2, out_s...]
  transfers between devices with their start and end apart: 39 -> 39, of which waited for: 12 -> 12; matrix products, arithmetic and copies ran while one was open for 21% -> 22% of each run, Pallas kernels for 52% -> 56%
where the time goes in v13:
time: 581 us; the launch traced here: 576 us
  Pallas kernels  320 us (55%)
  other arithmetic  107 us (18%)
  waiting for transfers between devices  51.9 us (9%)
  starting transfers between devices  30.4 us (5%)
  local copies, waits for them, and re-layouts  27.4 us (5%)
  matrix products  21.5 us (4%)
  between operations  16.5 us (3%)
    pallas_call x1, Pallas kernels, ffn(): pl.pallas_call(functools.partial(ffn_kernel, orders), grid=(hid // bc,),...  90.2 us
    pallas_call x2, Pallas kernels, attn_backward(): pl.pallas_call(attn_bwd_kernel, grid=(blocks,), in_specs=[scalar, col, co...  68.7 us
    ppermute x16, waiting for transfers between devices, dp_swap(): return lax.ppermute(value, ('dp', 'fsdp'), pairs)  39.6 us
    convert_element_type x7, other arithmetic, step(): self.keep = add(slice(half)).astype(BF16)  33.2 us
    pallas_call x1, Pallas kernels, attn_forward(): pl.pallas_call(attn_fwd_kernel, grid=(blocks,), in_specs=[scalar, three,...  32.1 us
    pallas_call x1, Pallas kernels, text_bwd(): pl.pallas_call(text_bwd_kernel, grid=(depth // bk,), in_specs=[pl.BlockSp...  30 us
    pallas_call x1, Pallas kernels, small_exchange(): pl.pallas_call(small_kernel, in_specs=[vmem], out_specs=[vmem] * 2, out_s...  25.9 us
    ppermute x16, starting transfers between devices, dp_swap(): return lax.ppermute(value, ('dp', 'fsdp'), pairs)  24.6 us
  transfers between devices with their start and end apart: 39, of which 12 were waited for; matrix products, arithmetic and copies ran while one was open for 22% of the time, Pallas kernels for 56%

profile of v13, /device:TPU:0, one launch (start us, length us, event | category | flops | bytes accessed | tf_op | source)
XLA Modules:
  0.0 575.9 jit_solution(2050667689114946942)
XLA Ops:
  17.9 4.7 fusion.2
  23.3 16.2 %shard_map.222 = f32[2,256,1536]{2,1,0:T(8,128)} custom-call(bf16[256,2048]{1,0:T(8,128)(2,1)} %pad_maximum_fusion.2.x_ref, bf16[2048,2,1536]{2,1,0:T(2,128)(2,1)} %w_ref.5), custom_call_target="tpu_custom_call" | custom-call | tf_op jit(solution)/shard_map/pallas_call | solution.py:427
  53.4 14.4 %shard_map.221 = (bf16[1024,1536]{1,0:T(8,128)(2,1)}, f32[3,1024,768]{2,1,0:T(8,128)}, f32[8,1024]{1,0:T(8,128)}) custom-call(s32[2]{0:T(128)} %pad_add_fusion.1.id_ref, bf16[512,1536]{1,0:T(8,128)(2,1)} %bitcast.127, bf16[512,1536]{1,0:T(8,128)(2,1)} %collective-permute-done.1.xp_ref, f32[1,1536]{1,0:T(1,128)} %get-tuple-element.280.front_ref, ...), custom_call_target="tpu_custom_call" | custom-call | tf_op jit(solution)/shard_map/pallas_call | solution.py:615
  70.7 32.1 %shard_map.223 = (bf16[1024,768]{1,0:T(8,128)(2,1)}, bf16[1024,768]{1,0:T(8,128)(2,1)}, bf16[1024,768]{1,0:T(8,128)(2,1)}, bf16[1024,768]{1,0:T(8,128)(2,1)}, f3...) custom-call(s32[1]{0:T(128)S(6)} %copy.48.len_ref, ...), custom_call_target="tpu_custom_call" | custom-call | tf_op jit(solution)/shard_map/pallas_call | solution.py:370
  120.4 90.2 %shard_map.224 = (bf16[8,2,96,2048]{3,2,1,0:T(8,128)(2,1)}, bf16[8,2,96,2048]{3,2,1,0:T(8,128)(2,1)}, bf16[8,96,2048]{2,1,0:T(8,128)(2,1)}, bf16[8,96,2048]{2,1,...) custom-call(s32[2]{0:T(128)} %pad_add_fusion.1.id_ref, ...), custom_call_target="tpu_custom_call" | custom-call | tf_op jit(solution)/shard_map/pallas_call | solution.py:558
  217.3 4.3 multiply_reduce_fusion
  221.6 5.8 %fusion.7 = (f32[1536]{0:T(1024)S(1)}, bf16[1,512,1536]{2,1,0:T(8,128)(2,1)}, f32[1536]{0:T(1024)S(1)}, f32[512,1536]{1,0:T(8,128)S(1)}) fusion(f32[512,1536]{1,0:T(8,128)} %get-tuple-element.117, bf16[512,1536]{1,0:T(8,128)(2,1)S(1)} %collective-permute-done.11, bf16[1,512,1536]{2,1,0:T(8,128)(2,1)} %param.19, f32[512,1536]{1,0:T(8,128)S(1)} %copy-done.1, ...), kind=kLoop, calls=%fused_computation.18 | loop fusion | flops 16512000 | bytes 23627776 | tf_op jit(solution)/shard_map/reduce_sum | solution.py:877
  232.5 9.6 %shard_map.225 = (f32[1024,768]{1,0:T(8,128)}, bf16[8,96,768]{2,1,0:T(8,128)(2,1)}, bf16[8,96,768]{2,1,0:T(8,128)(2,1)}) custom-call(s32[2]{0:T(128)} %pad_add_fusion.1.id_ref, bf16[512,1536]{1,0:T(8,128)(2,1)} %copy-done.17, bf16[512,1536]{1,0:T(8,128)(2,1)} %collective-permute-done.13.refs_1_, bf16[768,1536]{1,0:T(8,128)(2,1)} %refs_2_.1, ...), custom_call_target="tpu_custom_call" | custom-call | tf_op jit(solution)/shard_map/pallas_call | solution.py:743
  242.1 44.4 %shard_map.226 = (f32[3,1024,512]{2,1,0:T(8,128)}, f32[256,512]{1,0:T(8,128)}, f32[256,512]{1,0:T(8,128)}, f32[8,1024]{1,0:T(8,128)}, f32[1,512]{1,0:T(1,128)}, /*index=5*/f32[1,512]{1,0:T(1,128)}, f32[1,512]{1,0:T(1,128)}) custom-call(s32[1]{0:T(128)S(6)} %copy.48.len_ref, bf16[1024,768]{1,0:T(8,128)(2,1)} %get-tuple-element.121.q_ref, ...), custom_call_target="tpu_custom_call" | custom-call | tf_op jit(solution)/shard_map/pallas_call | solution.py:385
  286.6 8.1 %add_convert_fusion = (bf16[4,2,96,2048]{3,2,1,0:T(8,128)(2,1)}, bf16[4,2,96,2048]{3,2,1,0:T(8,128)(2,1)}) fusion(bf16[8,2,96,2048]{3,2,1,0:T(8,128)(2,1)} %collective-permute-done.14, bf16[8,2,96,2048]{3,2,1,0:T(8,128)(2,1)} %get-tuple-element.156), kind=kLoop, calls=%fused_computation.4 | loop fusion | flops 12582912 | bytes 18874368 | tf_op jit(solution)/shard_map/convert_element_type | solution.py:130
  296.9 6.1 %add_convert_fusion.5 = (bf16[4,96,2048]{2,1,0:T(8,128)(2,1)}, bf16[4,96,2048]{2,1,0:T(8,128)(2,1)}) fusion(bf16[8,96,2048]{2,1,0:T(8,128)(2,1)} %collective-permute-done.15, bf16[8,96,2048]{2,1,0:T(8,128)(2,1)} %get-tuple-element.158), kind=kLoop, calls=%fused_computation.34 | loop fusion | flops 6291456 | bytes 9437184 | tf_op jit(solution)/shard_map/convert_element_type | solution.py:130
  306.3 24.3 %shard_map.227 = (f32[3,1024,256]{2,1,0:T(8,128)}, f32[256,256]{1,0:T(8,128)}, f32[256,256]{1,0:T(8,128)}, f32[8,1024]{1,0:T(8,128)}, f32[1,256]{1,0:T(1,128)}, /*index=5*/f32[1,256]{1,0:T(1,128)}, f32[1,256]{1,0:T(1,128)}) custom-call(s32[1]{0:T(128)S(6)} %copy.48.len_ref, bf16[1024,768]{1,0:T(8,128)(2,1)} %get-tuple-element.121.q_ref, ...), custom_call_target="tpu_custom_call" | custom-call | tf_op jit(solution)/shard_map/pallas_call | solution.py:385
  334.0 18.6 %shard_map.228 = (bf16[4,3,96,1536]{3,2,1,0:T(8,128)(2,1)}, bf16[4,3,96,1536]{3,2,1,0:T(8,128)(2,1)}, bf16[3,1024,768]{2,1,0:T(8,128)(2,1)}) custom-call(s32[2]{0:T(128)} %pad_add_fusion.1.id_ref, f32[3,1024,512]{2,1,0:T(8,128)} %get-tuple-element.152.da_ref, f32[3,1024,256]{2,1,0:T(8,128)} %get-tuple-element.153.db_ref, ...), custom_call_target="tpu_custom_call" | custom-call | tf_op jit(solution)/shard_map/pallas_call | solution.py:662
  353.2 7.8 %collective-permute-done.19 = bf16[8,96,768]{2,1,0:T(8,128)(2,1)} collective-permute-done((bf16[8,96,768]{2,1,0:T(8,128)(2,1)}, bf16[8,96,768]{2,1,0:T(8,128)(2,1)}, u32[]{:S(2)}, u32[]{:S(2)}) %collective-permute-start.19) | collective-permute-done | bytes 1179680 | tf_op jit(solution)/shard_map/ppermute | solution.py:104
  361.0 6.2 %add_convert_fusion.4 = (bf16[2,2,96,2048]{3,2,1,0:T(8,128)(2,1)}, bf16[2,2,96,2048]{3,2,1,0:T(8,128)(2,1)}) fusion(bf16[4,2,96,2048]{3,2,1,0:T(8,128)(2,1)} %get-tuple-element.249, bf16[4,2,96,2048]{3,2,1,0:T(8,128)(2,1)} %collective-permute-done.17), kind=kLoop, calls=%fused_computation.26 | loop fusion | flops 6291456 | bytes 9437184 | tf_op jit(solution)/shard_map/convert_element_type | solution.py:130
  381.4 13.7 %shard_map.230 = (f32[512,1536]{1,0:T(8,128)}, bf16[512,1536]{1,0:T(8,128)(2,1)}) custom-call(s32[2]{0:T(128)} %pad_add_fusion.1.id_ref, bf16[3,1024,768]{2,1,0:T(8,128)(2,1)} %get-tuple-element.173.g_ref, bf16[3,768,1536]{2,1,0:T(8,128)(2,1)} %bitcast.126, bf16[3,768,768]{2,1,0:T(8,128)(2,1)} %collective-permute-done.2.got_ref), custom_call_target="tpu_custom_call" | custom-call | tf_op jit(solution)/shard_map/pallas_call | solution.py:708
  405.9 7.8 %collective-permute-done.22 = bf16[4,3,96,1536]{3,2,1,0:T(8,128)(2,1)} collective-permute-done((bf16[4,3,96,1536]{3,2,1,0:T(8,128)(2,1)}, bf16[4,3,96,1536]{3,2,1,0:T(8,128)(2,1)}, u32[]{:S(2)}, u32[]{:S(2)}) %collective-permute-start.22) | collective-permute-done | bytes 3538976 | tf_op jit(solution)/shard_map/ppermute | solution.py:104
  413.8 5.1 add_convert_fusion.2
  433.4 30.0 %shard_map.229 = (bf16[256,2048]{1,0:T(8,128)(2,1)}, bf16[16,2,96,128]{3,2,1,0:T(8,128)(2,1)}) custom-call(bf16[2,256,1536]{2,1,0:T(8,128)(2,1)} %pad_maximum_fusion.1.g_ref, bf16[2048,2,1536]{2,1,0:T(2,128)(2,1)} %w_ref.5, bf16[16,2,96,128]{3,2,1,0:T(8,128)(2,1)} %bitcast.131), custom_call_target="tpu_custom_call" | custom-call | tf_op jit(solution)/shard_map/pallas_call | solution.py:463
  468.4 5.0 collective-permute-start.33
  483.5 4.6 fusion.15
  489.8 24.0 %collective-permute-done.37 = bf16[1,96,768]{2,1,0:T(8,128)(2,1)} collective-permute-done((bf16[1,96,768]{2,1,0:T(8,128)(2,1)}, bf16[1,96,768]{2,1,0:T(8,128)(2,1)}, u32[]{:S(2)}, u32[]{:S(2)}) %collective-permute-start.37) | collective-permute-done | bytes 147488 | tf_op jit(solution)/shard_map/ppermute | solution.py:104
  518.8 8.8 %fusion = f32[2,96,2048]{2,1,0:T(8,128)} fusion(bf16[2,96,4096]{2,1,0:T(8,128)(2,1)S(1)} %bitcast.134, bf16[4096,2048]{1,0:T(8,128)(2,1)} %all-gather.2.cloned.1.call-done), kind=kOutput, calls=%fused_computation | convolution fusion | flops 3221225472 | bytes 19922944 | tf_op jit(solution)/shard_map/dot_general | solution.py:25
  535.5 25.9 %shard_map.231 = (f32[16,8,128]{2,1,0:T(8,128)}, f32[16,8,128]{2,1,0:T(8,128)}) custom-call(f32[16,8,128]{2,1,0:T(8,128)} %select_maximum_fusion.mod_ref), custom_call_target="tpu_custom_call" | custom-call | tf_op jit(solution)/shard_map/pallas_call | solution.py:172
  (301 shorter events, 141.4 us)
Async XLA Ops:
  7.2 206.5 %all-gather.2.cloned.1.call-start = ((), (), s32[]{:S(2)}) async-start(), calls=%async_computation | async-start | bytes 17825792 | tf_op jit(solution)/shard_map/all_gather | solution.py:818
  16.8 36.7 %collective-permute-start.2 = (bf16[3,768,768]{2,1,0:T(8,128)(2,1)}, bf16[3,768,768]{2,1,0:T(8,128)(2,1)}, u32[]{:S(2)}, u32[]{:S(2)}) collective-permute-start(bf16[3,768,768]{2,1,0:T(8,128)(2,1)} %dynamic-slice_bitcast_fusion), channel_id=1, source_target_pairs={{0,1},{1,0},{2,3},{3,2},{4,5},{5,4},{6,7},{7,6},{8,9},{9,8},{10,11... | collective-permute-start | bytes 10616840 | tf_op jit(solution)/shard_map/ppermute | solution.py:30
  22.6 26.8 %collective-permute-start = (f32[4,1536]{1,0:T(4,128)S(1)}, f32[4,1536]{1,0:T(4,128)S(1)}, u32[]{:S(2)}, u32[]{:S(2)}) collective-permute-start(f32[4,1536]{1,0:T(4,128)S(1)} %bitcast.138), channel_id=1, source_target_pairs={{0,1},{1,0},{2,3},{3,2},{4,5},{5,4},{6,7},{7,6},{8,9},{9,8},{10,11... | collective-permute-start | bytes 73736 | tf_op jit(solution)/shard_map/ppermute | solution.py:30
  22.8 30.7 %collective-permute-start.1 = (bf16[512,1536]{1,0:T(8,128)(2,1)S(1)}, bf16[512,1536]{1,0:T(8,128)(2,1)}, u32[]{:S(2)}, u32[]{:S(2)}) collective-permute-start(bf16[512,1536]{1,0:T(8,128)(2,1)S(1)} %bitcast.128), channel_id=1, source_target_pairs={{0,1},{1,0},{2,3},{3,2},{4,5},{5,4},{6,7},{7,6},{8,9},{9,8},{10,11... | collective-permute-start | bytes 4718600 | tf_op jit(solution)/shard_map/ppermute | solution.py:30
  23.1 23.1 %collective-permute-start.4 = (s32[2,512]{1,0:T(2,128)S(1)}, s32[2,512]{1,0:T(2,128)S(1)}, u32[]{:S(2)}, u32[]{:S(2)}) collective-permute-start(s32[2,512]{1,0:T(2,128)S(1)} %bitcast.151), channel_id=1, source_target_pairs={{0,1},{1,0},{2,3},{3,2},{4,5},{5,4},{6,7},{7,6},{8,9},{9,8},{10,11... | collective-permute-start | bytes 12296 | tf_op jit(solution)/shard_map/ppermute | solution.py:30
  210.6 76.0 %collective-permute-start.14 = (bf16[8,2,96,2048]{3,2,1,0:T(8,128)(2,1)}, bf16[8,2,96,2048]{3,2,1,0:T(8,128)(2,1)}, u32[]{:S(2)}, u32[]{:S(2)}) collective-permute-start(bf16[8,2,96,2048]{3,2,1,0:T(8,128)(2,1)} %get-tuple-element.143), channel_id=1, source_target_pairs={{0,2},{1,5},{2,0},{3,7},{4,6},{5,1},{6,4},{7,3},{8,10},{9,13},{10,... | collective-permute-start | bytes 18874376 | tf_op jit(solution)/shard_map/ppermute | solution.py:104
  214.2 72.4 %collective-permute-start.15 = (bf16[8,96,2048]{2,1,0:T(8,128)(2,1)}, bf16[8,96,2048]{2,1,0:T(8,128)(2,1)}, u32[]{:S(2)}, u32[]{:S(2)}) collective-permute-start(bf16[8,96,2048]{2,1,0:T(8,128)(2,1)} %get-tuple-element.144), channel_id=1, source_target_pairs={{0,8},{1,9},{2,10},{3,11},{4,12},{5,13},{6,14},{7,15},{8,0},{9,1},... | collective-permute-start | bytes 9437192 | tf_op jit(solution)/shard_map/ppermute | solution.py:104
  294.7 66.3 %collective-permute-start.17 = (bf16[4,2,96,2048]{3,2,1,0:T(8,128)(2,1)}, bf16[4,2,96,2048]{3,2,1,0:T(8,128)(2,1)}, u32[]{:S(2)}, u32[]{:S(2)}) collective-permute-start(bf16[4,2,96,2048]{3,2,1,0:T(8,128)(2,1)} %get-tuple-element.250), channel_id=1, source_target_pairs={{0,4},{1,3},{2,6},{3,1},{4,0},{5,7},{6,2},{7,5},{8,12},{9,11},{10,... | collective-permute-start | bytes 9437192 | tf_op jit(solution)/shard_map/ppermute | solution.py:104
  303.0 58.0 %collective-permute-start.18 = (bf16[4,96,2048]{2,1,0:T(8,128)(2,1)}, bf16[4,96,2048]{2,1,0:T(8,128)(2,1)}, u32[]{:S(2)}, u32[]{:S(2)}) collective-permute-start(bf16[4,96,2048]{2,1,0:T(8,128)(2,1)} %get-tuple-element.256), channel_id=1, source_target_pairs={{0,2},{1,5},{2,0},{3,7},{4,6},{5,1},{6,4},{7,3},{8,10},{9,13},{10,... | collective-permute-start | bytes 4718600 | tf_op jit(solution)/shard_map/ppermute | solution.py:104
  304.3 56.7 %collective-permute-start.19 = (bf16[8,96,768]{2,1,0:T(8,128)(2,1)}, bf16[8,96,768]{2,1,0:T(8,128)(2,1)}, u32[]{:S(2)}, u32[]{:S(2)}) collective-permute-start(bf16[8,96,768]{2,1,0:T(8,128)(2,1)} %get-tuple-element.160), channel_id=1, source_target_pairs={{0,2},{1,5},{2,0},{3,7},{4,6},{5,1},{6,4},{7,3},{8,10},{9,13},{10,... | collective-permute-start | bytes 3538952 | tf_op jit(solution)/shard_map/ppermute | solution.py:104
  352.6 61.1 %collective-permute-start.22 = (bf16[4,3,96,1536]{3,2,1,0:T(8,128)(2,1)}, bf16[4,3,96,1536]{3,2,1,0:T(8,128)(2,1)}, u32[]{:S(2)}, u32[]{:S(2)}) collective-permute-start(bf16[4,3,96,1536]{3,2,1,0:T(8,128)(2,1)} %get-tuple-element.165), channel_id=1, source_target_pairs={{0,2},{1,5},{2,0},{3,7},{4,6},{5,1},{6,4},{7,3},{8,10},{9,13},{10,... | collective-permute-start | bytes 10616840 | tf_op jit(solution)/shard_map/ppermute | solution.py:104
  367.3 46.4 %collective-permute-start.23 = (bf16[2,2,96,2048]{3,2,1,0:T(8,128)(2,1)}, bf16[2,2,96,2048]{3,2,1,0:T(8,128)(2,1)}, u32[]{:S(2)}, u32[]{:S(2)}) collective-permute-start(bf16[2,2,96,2048]{3,2,1,0:T(8,128)(2,1)} %get-tuple-element.254), channel_id=1, source_target_pairs={{0,8},{1,9},{2,10},{3,11},{4,12},{5,13},{6,14},{7,15},{8,0},{9,1},... | collective-permute-start | bytes 4718600 | tf_op jit(solution)/shard_map/ppermute | solution.py:104
  375.6 38.1 %collective-permute-start.25 = (bf16[4,96,768]{2,1,0:T(8,128)(2,1)}, bf16[4,96,768]{2,1,0:T(8,128)(2,1)}, u32[]{:S(2)}, u32[]{:S(2)}) collective-permute-start(bf16[4,96,768]{2,1,0:T(8,128)(2,1)} %get-tuple-element.266), channel_id=1, source_target_pairs={{0,4},{1,3},{2,6},{3,1},{4,0},{5,7},{6,2},{7,5},{8,12},{9,11},{10,... | collective-permute-start | bytes 1769480 | tf_op jit(solution)/shard_map/ppermute | solution.py:104
  380.3 33.4 %collective-permute-start.24 = (bf16[2,96,2048]{2,1,0:T(8,128)(2,1)}, bf16[2,96,2048]{2,1,0:T(8,128)(2,1)}, u32[]{:S(2)}, u32[]{:S(2)}) collective-permute-start(bf16[2,96,2048]{2,1,0:T(8,128)(2,1)} %get-tuple-element.264), channel_id=1, source_target_pairs={{0,4},{1,3},{2,6},{3,1},{4,0},{5,7},{6,2},{7,5},{8,12},{9,11},{10,... | collective-permute-start | bytes 2359304 | tf_op jit(solution)/shard_map/ppermute | solution.py:104
  395.1 34.9 %collective-permute-start.26 = (bf16[512,1536]{1,0:T(8,128)(2,1)}, bf16[512,1536]{1,0:T(8,128)(2,1)}, u32[]{:S(2)}, u32[]{:S(2)}) collective-permute-start(bf16[512,1536]{1,0:T(8,128)(2,1)} %get-tuple-element.175), channel_id=1, source_target_pairs={{0,1},{1,0},{2,3},{3,2},{4,5},{5,4},{6,7},{7,6},{8,9},{9,8},{10,11... | collective-permute-start | bytes 4718600 | tf_op jit(solution)/shard_map/ppermute | solution.py:54
  418.9 44.6 %collective-permute-start.27 = (bf16[2,3,96,1536]{3,2,1,0:T(8,128)(2,1)}, bf16[2,3,96,1536]{3,2,1,0:T(8,128)(2,1)}, u32[]{:S(2)}, u32[]{:S(2)}) collective-permute-start(bf16[2,3,96,1536]{3,2,1,0:T(8,128)(2,1)} %get-tuple-element.252), channel_id=1, source_target_pairs={{0,4},{1,3},{2,6},{3,1},{4,0},{5,7},{6,2},{7,5},{8,12},{9,11},{10,... | collective-permute-start | bytes 5308424 | tf_op jit(solution)/shard_map/ppermute | solution.py:104
  424.1 39.4 %collective-permute-start.29 = (bf16[2,96,768]{2,1,0:T(8,128)(2,1)}, bf16[2,96,768]{2,1,0:T(8,128)(2,1)}, u32[]{:S(2)}, u32[]{:S(2)}) collective-permute-start(bf16[2,96,768]{2,1,0:T(8,128)(2,1)} %get-tuple-element.279), channel_id=1, source_target_pairs={{0,8},{1,9},{2,10},{3,11},{4,12},{5,13},{6,14},{7,15},{8,0},{9,1},... | collective-permute-start | bytes 884744 | tf_op jit(solution)/shard_map/ppermute | solution.py:104
  427.4 36.1 %collective-permute-start.28 = (bf16[1,96,2048]{2,1,0:T(8,128)(2,1)}, bf16[1,96,2048]{2,1,0:T(8,128)(2,1)}, u32[]{:S(2)}, u32[]{:S(2)}) collective-permute-start(bf16[1,96,2048]{2,1,0:T(8,128)(2,1)} %add_convert_fusion.19), channel_id=1, source_target_pairs={{0,16},{1,17},{2,18},{3,19},{4,20},{5,21},{6,22},{7,23},{8,24},{9,... | collective-permute-start | bytes 1179656 | tf_op jit(solution)/shard_map/ppermute | solution.py:104
  468.4 59.2 %collective-permute-start.33 = (bf16[1,2,96,2048]{3,2,1,0:T(8,128)(2,1)}, bf16[1,2,96,2048]{3,2,1,0:T(8,128)(2,1)}, u32[]{:S(2)}, u32[]{:S(2)}) collective-permute-start(bf16[1,2,96,2048]{3,2,1,0:T(8,128)(2,1)} %add_convert_fusion.13), channel_id=1, source_target_pairs={{0,16},{1,17},{2,18},{3,19},{4,20},{5,21},{6,22},{7,23},{8,24},{9,... | collective-permute-start | bytes 2359304 | tf_op jit(solution)/shard_map/ppermute | solution.py:104
  476.6 40.3 %collective-permute-start.32 = (bf16[16,2,96,128]{3,2,1,0:T(8,128)(2,1)}, bf16[16,2,96,128]{3,2,1,0:T(8,128)(2,1)}, u32[]{:S(2)}, u32[]{:S(2)}) collective-permute-start(bf16[16,2,96,128]{3,2,1,0:T(8,128)(2,1)} %get-tuple-element.191), channel_id=1, source_target_pairs={{0,1},{1,0},{2,3},{3,2},{4,5},{5,4},{6,7},{7,6},{8,9},{9,8},{10,11... | collective-permute-start | bytes 2359304 | tf_op jit(solution)/shard_map/ppermute | solution.py:30
  480.9 33.0 %collective-permute-start.37 = (bf16[1,96,768]{2,1,0:T(8,128)(2,1)}, bf16[1,96,768]{2,1,0:T(8,128)(2,1)}, u32[]{:S(2)}, u32[]{:S(2)}) collective-permute-start(bf16[1,96,768]{2,1,0:T(8,128)(2,1)} %add_convert_fusion.22), channel_id=1, source_target_pairs={{0,16},{1,17},{2,18},{3,19},{4,20},{5,21},{6,22},{7,23},{8,24},{9,... | collective-permute-start | bytes 442376 | tf_op jit(solution)/shard_map/ppermute | solution.py:104
  481.0 46.6 %collective-permute-start.34 = (bf16[1,3,96,1536]{3,2,1,0:T(8,128)(2,1)}, bf16[1,3,96,1536]{3,2,1,0:T(8,128)(2,1)}, u32[]{:S(2)}, u32[]{:S(2)}) collective-permute-start(bf16[1,3,96,1536]{3,2,1,0:T(8,128)(2,1)} %get-tuple-element.261), channel_id=1, source_target_pairs={{0,8},{1,9},{2,10},{3,11},{4,12},{5,13},{6,14},{7,15},{8,0},{9,1},... | collective-permute-start | bytes 2654216 | tf_op jit(solution)/shard_map/ppermute | solution.py:104
  488.1 27.5 %collective-permute-start.30 = (bf16[128,2048]{1,0:T(8,128)(2,1)S(1)}, bf16[128,2048]{1,0:T(8,128)(2,1)S(1)}, u32[]{:S(2)}, u32[]{:S(2)}) collective-permute-start(bf16[128,2048]{1,0:T(8,128)(2,1)S(1)} %constant_dynamic-slice_fusion.1), channel_id=1, source_target_pairs={{0,1},{1,0},{2,3},{3,2},{4,5},{5,4},{6,7},{7,6},{8,9},{9,8},{10,11... | collective-permute-start | bytes 1572872 | tf_op jit(solution)/shard_map/ppermute | solution.py:30
  531.3 32.9 %collective-permute-start.36 = (bf16[1,3,96,768]{3,2,1,0:T(8,128)(2,1)S(1)}, bf16[1,3,96,768]{3,2,1,0:T(8,128)(2,1)S(1)}, u32[]{:S(2)}, u32[]{:S(2)}) collective-permute-start(bf16[1,3,96,768]{3,2,1,0:T(8,128)(2,1)S(1)} %get-tuple-element.200), channel_id=1, source_target_pairs={{0,16},{1,17},{2,18},{3,19},{4,20},{5,21},{6,22},{7,23},{8,24},{9,... | collective-permute-start | bytes 1327112 | tf_op jit(solution)/shard_map/ppermute | solution.py:104
  (69 other events, 1160.9 us)
Sparse Core Ops, SparseCore 0:
  12.9 194.2 all-gather.1

commit v14 on v13

--- a/solution.py
+++ b/solution.py
@@ -906,7 +906,7 @@
             ids, part_a[0], part_b[0], pre, stats, gain3, first_all, dpn, low_bits
         )
         part_a, part_b, grads = advance(
-            [wide_chain, down_chain, out_chain], (part_a[1:], part_b[1:], grads)
+            [wide_chain, down_chain], (part_a[1:], part_b[1:], grads)
         )
         qkv_chain = Halving(low_bits, keep, send)
         parts = project_back(ids, grads, w_flat, w_parts[1])
@@ -974,14 +974,14 @@
     text_grad = dot(pair_cols, text_all).reshape(2, share, TW // n)
     mods, text_grad = settle([wide_chain], (mods, text_grad))
     if paired:
-        mods = advance([qkv_chain], mods)
+        mods = advance([qkv_chain, out_chain], mods)
         own_side = f == (me >> low_bits[-1] + 1)
         mine, got = exchange_rot(qkv_chain.last[0].astype(BF16), 2)
         keep, send = jnp.where(own_side, mine, got)[None], jnp.where(own_side, got, mine)[None]
         mods, keep, send = lax.optimization_barrier((mods, keep, send))
         qkv_chain = Halving(bits[-1:], keep, send)
     mods, small = small_exchange(mods)
-    mods = settle([qkv_chain], mods)
+    mods = settle([qkv_chain, out_chain], mods)
     total = small[:, 5 : 5 + SUMS].reshape(-1)[: 6 * own_d].reshape(6, own_d)
     gate_total = jnp.sum(total[5].reshape(HEADS // n, HD), axis=1) * (
         1.0 - head_tanh * head_tanh

time: 581 us -> 590 us (1.015)
  Pallas kernels: 320 us -> 328 us
  transfers between devices with their start and end apart: 39 -> 39, of which waited for: 12 -> 12; matrix products, arithmetic and copies ran while one was open for 22% -> 21% of each run, Pallas kernels for 56% -> 56%
where the time goes in v14:
time: 590 us; the launch traced here: 585 us
  Pallas kernels  328 us (56%)
  other arithmetic  105 us (18%)
  waiting for transfers between devices  53.3 us (9%)
  starting transfers between devices  31.6 us (5%)
  local copies, waits for them, and re-layouts  27.5 us (5%)
  matrix products  21.5 us (4%)
  between operations  16.6 us (3%)
    pallas_call x1, Pallas kernels, ffn(): pl.pallas_call(functools.partial(ffn_kernel, orders), grid=(hid // bc,),...  90.2 us
    pallas_call x2, Pallas kernels, attn_backward(): pl.pallas_call(attn_bwd_kernel, grid=(blocks,), in_specs=[scalar, col, co...  68.8 us
    ppermute x16, waiting for transfers between devices, dp_swap(): return lax.ppermute(value, ('dp', 'fsdp'), pairs)  41.5 us
    pallas_call x1, Pallas kernels, text_bwd(): pl.pallas_call(text_bwd_kernel, grid=(depth // bk,), in_specs=[pl.BlockSp...  32.7 us
    convert_element_type x7, other arithmetic, step(): self.keep = add(slice(half)).astype(BF16)  32.2 us
    pallas_call x1, Pallas kernels, attn_forward(): pl.pallas_call(attn_fwd_kernel, grid=(blocks,), in_specs=[scalar, three,...  32.1 us
    pallas_call x1, Pallas kernels, small_exchange(): pl.pallas_call(small_kernel, in_specs=[vmem], out_specs=[vmem] * 2, out_s...  31.1 us
    ppermute x16, starting transfers between devices, dp_swap(): return lax.ppermute(value, ('dp', 'fsdp'), pairs)  26.5 us
  transfers between devices with their start and end apart: 39, of which 12 were waited for; matrix products, arithmetic and copies ran while one was open for 21% of the time, Pallas kernels for 56%

profile of v14, /device:TPU:0, one launch (start us, length us, event | category | flops | bytes accessed | tf_op | source)
XLA Modules:
  0.0 584.9 jit_solution(7605114019512049324)
XLA Ops:
  12.8 4.0 dynamic-slice_bitcast_fusion
  17.9 4.7 fusion.2
  23.3 16.2 %shard_map.222 = f32[2,256,1536]{2,1,0:T(8,128)} custom-call(bf16[256,2048]{1,0:T(8,128)(2,1)} %pad_maximum_fusion.2.x_ref, bf16[2048,2,1536]{2,1,0:T(2,128)(2,1)} %w_ref.5), custom_call_target="tpu_custom_call" | custom-call | tf_op jit(solution)/shard_map/pallas_call | solution.py:427
  53.4 14.4 %shard_map.221 = (bf16[1024,1536]{1,0:T(8,128)(2,1)}, f32[3,1024,768]{2,1,0:T(8,128)}, f32[8,1024]{1,0:T(8,128)}) custom-call(s32[2]{0:T(128)} %pad_add_fusion.1.id_ref, bf16[512,1536]{1,0:T(8,128)(2,1)} %bitcast.127, bf16[512,1536]{1,0:T(8,128)(2,1)} %collective-permute-done.1.xp_ref, f32[1,1536]{1,0:T(1,128)} %get-tuple-element.282.front_ref, ...), custom_call_target="tpu_custom_call" | custom-call | tf_op jit(solution)/shard_map/pallas_call | solution.py:615
  70.5 32.1 %shard_map.223 = (bf16[1024,768]{1,0:T(8,128)(2,1)}, bf16[1024,768]{1,0:T(8,128)(2,1)}, bf16[1024,768]{1,0:T(8,128)(2,1)}, bf16[1024,768]{1,0:T(8,128)(2,1)}, f3...) custom-call(s32[1]{0:T(128)S(6)} %copy.48.len_ref, ...), custom_call_target="tpu_custom_call" | custom-call | tf_op jit(solution)/shard_map/pallas_call | solution.py:370
  120.3 90.2 %shard_map.224 = (bf16[8,2,96,2048]{3,2,1,0:T(8,128)(2,1)}, bf16[8,2,96,2048]{3,2,1,0:T(8,128)(2,1)}, bf16[8,96,2048]{2,1,0:T(8,128)(2,1)}, bf16[8,96,2048]{2,1,...) custom-call(s32[2]{0:T(128)} %pad_add_fusion.1.id_ref, ...), custom_call_target="tpu_custom_call" | custom-call | tf_op jit(solution)/shard_map/pallas_call | solution.py:558
  217.3 4.3 multiply_reduce_fusion
  221.6 6.4 %fusion.7 = (f32[1536]{0:T(1024)}, bf16[1,512,1536]{2,1,0:T(8,128)(2,1)}, f32[1536]{0:T(1024)}, f32[512,1536]{1,0:T(8,128)S(1)}) fusion(f32[512,1536]{1,0:T(8,128)} %get-tuple-element.118, bf16[512,1536]{1,0:T(8,128)(2,1)S(1)} %collective-permute-done.11, bf16[1,512,1536]{2,1,0:T(8,128)(2,1)} %param.19, f32[512,1536]{1,0:T(8,128)S(1)} %copy-done.1, ...), kind=kLoop, calls=%fused_computation.18 | loop fusion | flops 16512000 | bytes 23627776 | tf_op jit(solution)/shard_map/reduce_sum | solution.py:877
  233.1 9.6 %shard_map.225 = (f32[1024,768]{1,0:T(8,128)}, bf16[8,96,768]{2,1,0:T(8,128)(2,1)}, bf16[8,96,768]{2,1,0:T(8,128)(2,1)}) custom-call(s32[2]{0:T(128)} %pad_add_fusion.1.id_ref, bf16[512,1536]{1,0:T(8,128)(2,1)} %copy-done.17, bf16[512,1536]{1,0:T(8,128)(2,1)} %collective-permute-done.13.refs_1_, bf16[768,1536]{1,0:T(8,128)(2,1)} %refs_2_.1, ...), custom_call_target="tpu_custom_call" | custom-call | tf_op jit(solution)/shard_map/pallas_call | solution.py:743
  242.7 44.5 %shard_map.226 = (f32[3,1024,512]{2,1,0:T(8,128)}, f32[256,512]{1,0:T(8,128)}, f32[256,512]{1,0:T(8,128)}, f32[8,1024]{1,0:T(8,128)}, f32[1,512]{1,0:T(1,128)}, /*index=5*/f32[1,512]{1,0:T(1,128)}, f32[1,512]{1,0:T(1,128)}) custom-call(s32[1]{0:T(128)S(6)} %copy.48.len_ref, bf16[1024,768]{1,0:T(8,128)(2,1)} %get-tuple-element.122.q_ref, ...), custom_call_target="tpu_custom_call" | custom-call | tf_op jit(solution)/shard_map/pallas_call | solution.py:385
  287.2 8.3 %add_convert_fusion = (bf16[4,2,96,2048]{3,2,1,0:T(8,128)(2,1)}, bf16[4,2,96,2048]{3,2,1,0:T(8,128)(2,1)}) fusion(bf16[8,2,96,2048]{3,2,1,0:T(8,128)(2,1)} %collective-permute-done.14, bf16[8,2,96,2048]{3,2,1,0:T(8,128)(2,1)} %get-tuple-element.157), kind=kLoop, calls=%fused_computation.4 | loop fusion | flops 12582912 | bytes 18874368 | tf_op jit(solution)/shard_map/convert_element_type | solution.py:130
  297.1 4.9 add_convert_fusion.5
  303.9 24.3 %shard_map.227 = (f32[3,1024,256]{2,1,0:T(8,128)}, f32[256,256]{1,0:T(8,128)}, f32[256,256]{1,0:T(8,128)}, f32[8,1024]{1,0:T(8,128)}, f32[1,256]{1,0:T(1,128)}, /*index=5*/f32[1,256]{1,0:T(1,128)}, f32[1,256]{1,0:T(1,128)}) custom-call(s32[1]{0:T(128)S(6)} %copy.48.len_ref, bf16[1024,768]{1,0:T(8,128)(2,1)} %get-tuple-element.122.q_ref, ...), custom_call_target="tpu_custom_call" | custom-call | tf_op jit(solution)/shard_map/pallas_call | solution.py:385
  331.4 18.6 %shard_map.228 = (bf16[4,3,96,1536]{3,2,1,0:T(8,128)(2,1)}, bf16[4,3,96,1536]{3,2,1,0:T(8,128)(2,1)}, bf16[3,1024,768]{2,1,0:T(8,128)(2,1)}) custom-call(s32[2]{0:T(128)} %pad_add_fusion.1.id_ref, f32[3,1024,512]{2,1,0:T(8,128)} %get-tuple-element.153.da_ref, f32[3,1024,256]{2,1,0:T(8,128)} %get-tuple-element.154.db_ref, ...), custom_call_target="tpu_custom_call" | custom-call | tf_op jit(solution)/shard_map/pallas_call | solution.py:662
  351.7 6.2 %add_convert_fusion.4 = (bf16[2,2,96,2048]{3,2,1,0:T(8,128)(2,1)}, bf16[2,2,96,2048]{3,2,1,0:T(8,128)(2,1)}) fusion(bf16[4,2,96,2048]{3,2,1,0:T(8,128)(2,1)} %get-tuple-element.251, bf16[4,2,96,2048]{3,2,1,0:T(8,128)(2,1)} %collective-permute-done.17), kind=kLoop, calls=%fused_computation.26 | loop fusion | flops 6291456 | bytes 9437184 | tf_op jit(solution)/shard_map/convert_element_type | solution.py:130
  369.2 13.7 %shard_map.230 = (f32[512,1536]{1,0:T(8,128)}, bf16[512,1536]{1,0:T(8,128)(2,1)}) custom-call(s32[2]{0:T(128)} %pad_add_fusion.1.id_ref, bf16[3,1024,768]{2,1,0:T(8,128)(2,1)} %get-tuple-element.172.g_ref, bf16[3,768,1536]{2,1,0:T(8,128)(2,1)} %bitcast.126, bf16[3,768,768]{2,1,0:T(8,128)(2,1)} %collective-permute-done.2.got_ref), custom_call_target="tpu_custom_call" | custom-call | tf_op jit(solution)/shard_map/pallas_call | solution.py:708
  393.7 19.3 %collective-permute-done.24 = bf16[8,96,768]{2,1,0:T(8,128)(2,1)} collective-permute-done((bf16[8,96,768]{2,1,0:T(8,128)(2,1)}, bf16[8,96,768]{2,1,0:T(8,128)(2,1)}, u32[]{:S(2)}, u32[]{:S(2)}) %collective-permute-start.24) | collective-permute-done | bytes 1179680 | tf_op jit(solution)/shard_map/ppermute | solution.py:104
  413.1 5.0 add_convert_fusion.2
  428.1 32.7 %shard_map.229 = (bf16[256,2048]{1,0:T(8,128)(2,1)}, bf16[16,2,96,128]{3,2,1,0:T(8,128)(2,1)}) custom-call(bf16[2,256,1536]{2,1,0:T(8,128)(2,1)} %pad_maximum_fusion.1.g_ref, bf16[2048,2,1536]{2,1,0:T(2,128)(2,1)} %w_ref.5, bf16[16,2,96,128]{3,2,1,0:T(8,128)(2,1)} %bitcast.131), custom_call_target="tpu_custom_call" | custom-call | tf_op jit(solution)/shard_map/pallas_call | solution.py:463
  469.2 5.6 collective-permute-start.32
  485.4 4.6 fusion.15
  496.6 8.8 %fusion = f32[2,96,2048]{2,1,0:T(8,128)} fusion(bf16[2,96,4096]{2,1,0:T(8,128)(2,1)S(1)} %bitcast.134, bf16[4096,2048]{1,0:T(8,128)(2,1)} %all-gather.2.cloned.1.call-done), kind=kOutput, calls=%fused_computation | convolution fusion | flops 3221225472 | bytes 19922944 | tf_op jit(solution)/shard_map/dot_general | solution.py:25
  509.6 18.0 %collective-permute-done.33 = bf16[1,3,96,1536]{3,2,1,0:T(8,128)(2,1)} collective-permute-done((bf16[1,3,96,1536]{3,2,1,0:T(8,128)(2,1)}, bf16[1,3,96,1536]{3,2,1,0:T(8,128)(2,1)}, u32[]{:S(2)}, u32[]{:S(2)}) %collective-permute-start.33) | collective-permute-done | bytes 884768 | tf_op jit(solution)/shard_map/ppermute | solution.py:104
  537.5 31.1 %shard_map.231 = (f32[16,8,128]{2,1,0:T(8,128)}, f32[16,8,128]{2,1,0:T(8,128)}) custom-call(f32[16,8,128]{2,1,0:T(8,128)} %select_maximum_fusion.mod_ref), custom_call_target="tpu_custom_call" | custom-call | tf_op jit(solution)/shard_map/pallas_call | solution.py:172
  (309 shorter events, 140.6 us)
Async XLA Ops:
  7.2 206.5 %all-gather.2.cloned.1.call-start = ((), (), s32[]{:S(2)}) async-start(), calls=%async_computation | async-start | bytes 17825792 | tf_op jit(solution)/shard_map/all_gather | solution.py:818
  16.8 36.6 %collective-permute-start.2 = (bf16[3,768,768]{2,1,0:T(8,128)(2,1)}, bf16[3,768,768]{2,1,0:T(8,128)(2,1)}, u32[]{:S(2)}, u32[]{:S(2)}) collective-permute-start(bf16[3,768,768]{2,1,0:T(8,128)(2,1)} %dynamic-slice_bitcast_fusion), channel_id=1, source_target_pairs={{0,1},{1,0},{2,3},{3,2},{4,5},{5,4},{6,7},{7,6},{8,9},{9,8},{10,11... | collective-permute-start | bytes 10616840 | tf_op jit(solution)/shard_map/ppermute | solution.py:30
  22.6 26.7 %collective-permute-start = (f32[4,1536]{1,0:T(4,128)S(1)}, f32[4,1536]{1,0:T(4,128)S(1)}, u32[]{:S(2)}, u32[]{:S(2)}) collective-permute-start(f32[4,1536]{1,0:T(4,128)S(1)} %bitcast.138), channel_id=1, source_target_pairs={{0,1},{1,0},{2,3},{3,2},{4,5},{5,4},{6,7},{7,6},{8,9},{9,8},{10,11... | collective-permute-start | bytes 73736 | tf_op jit(solution)/shard_map/ppermute | solution.py:30
  22.8 30.6 %collective-permute-start.1 = (bf16[512,1536]{1,0:T(8,128)(2,1)S(1)}, bf16[512,1536]{1,0:T(8,128)(2,1)}, u32[]{:S(2)}, u32[]{:S(2)}) collective-permute-start(bf16[512,1536]{1,0:T(8,128)(2,1)S(1)} %bitcast.128), channel_id=1, source_target_pairs={{0,1},{1,0},{2,3},{3,2},{4,5},{5,4},{6,7},{7,6},{8,9},{9,8},{10,11... | collective-permute-start | bytes 4718600 | tf_op jit(solution)/shard_map/ppermute | solution.py:30
  23.1 23.0 %collective-permute-start.4 = (s32[2,512]{1,0:T(2,128)S(1)}, s32[2,512]{1,0:T(2,128)S(1)}, u32[]{:S(2)}, u32[]{:S(2)}) collective-permute-start(s32[2,512]{1,0:T(2,128)S(1)} %bitcast.151), channel_id=1, source_target_pairs={{0,1},{1,0},{2,3},{3,2},{4,5},{5,4},{6,7},{7,6},{8,9},{9,8},{10,11... | collective-permute-start | bytes 12296 | tf_op jit(solution)/shard_map/ppermute | solution.py:30
  210.6 76.6 %collective-permute-start.14 = (bf16[8,2,96,2048]{3,2,1,0:T(8,128)(2,1)}, bf16[8,2,96,2048]{3,2,1,0:T(8,128)(2,1)}, u32[]{:S(2)}, u32[]{:S(2)}) collective-permute-start(bf16[8,2,96,2048]{3,2,1,0:T(8,128)(2,1)} %get-tuple-element.144), channel_id=1, source_target_pairs={{0,2},{1,5},{2,0},{3,7},{4,6},{5,1},{6,4},{7,3},{8,10},{9,13},{10,... | collective-permute-start | bytes 18874376 | tf_op jit(solution)/shard_map/ppermute | solution.py:104
  214.2 73.1 %collective-permute-start.15 = (bf16[8,96,2048]{2,1,0:T(8,128)(2,1)}, bf16[8,96,2048]{2,1,0:T(8,128)(2,1)}, u32[]{:S(2)}, u32[]{:S(2)}) collective-permute-start(bf16[8,96,2048]{2,1,0:T(8,128)(2,1)} %get-tuple-element.145), channel_id=1, source_target_pairs={{0,8},{1,9},{2,10},{3,11},{4,12},{5,13},{6,14},{7,15},{8,0},{9,1},... | collective-permute-start | bytes 9437192 | tf_op jit(solution)/shard_map/ppermute | solution.py:104
  295.6 56.1 %collective-permute-start.17 = (bf16[4,2,96,2048]{3,2,1,0:T(8,128)(2,1)}, bf16[4,2,96,2048]{3,2,1,0:T(8,128)(2,1)}, u32[]{:S(2)}, u32[]{:S(2)}) collective-permute-start(bf16[4,2,96,2048]{3,2,1,0:T(8,128)(2,1)} %get-tuple-element.252), channel_id=1, source_target_pairs={{0,4},{1,3},{2,6},{3,1},{4,0},{5,7},{6,2},{7,5},{8,12},{9,11},{10,... | collective-permute-start | bytes 9437192 | tf_op jit(solution)/shard_map/ppermute | solution.py:104
  301.9 49.7 %collective-permute-start.18 = (bf16[4,96,2048]{2,1,0:T(8,128)(2,1)}, bf16[4,96,2048]{2,1,0:T(8,128)(2,1)}, u32[]{:S(2)}, u32[]{:S(2)}) collective-permute-start(bf16[4,96,2048]{2,1,0:T(8,128)(2,1)} %get-tuple-element.258), channel_id=1, source_target_pairs={{0,2},{1,5},{2,0},{3,7},{4,6},{5,1},{6,4},{7,3},{8,10},{9,13},{10,... | collective-permute-start | bytes 4718600 | tf_op jit(solution)/shard_map/ppermute | solution.py:104
  350.1 62.9 %collective-permute-start.21 = (bf16[4,3,96,1536]{3,2,1,0:T(8,128)(2,1)}, bf16[4,3,96,1536]{3,2,1,0:T(8,128)(2,1)}, u32[]{:S(2)}, u32[]{:S(2)}) collective-permute-start(bf16[4,3,96,1536]{3,2,1,0:T(8,128)(2,1)} %get-tuple-element.165), channel_id=1, source_target_pairs={{0,2},{1,5},{2,0},{3,7},{4,6},{5,1},{6,4},{7,3},{8,10},{9,13},{10,... | collective-permute-start | bytes 10616840 | tf_op jit(solution)/shard_map/ppermute | solution.py:104
  357.9 55.1 %collective-permute-start.22 = (bf16[2,2,96,2048]{3,2,1,0:T(8,128)(2,1)}, bf16[2,2,96,2048]{3,2,1,0:T(8,128)(2,1)}, u32[]{:S(2)}, u32[]{:S(2)}) collective-permute-start(bf16[2,2,96,2048]{3,2,1,0:T(8,128)(2,1)} %get-tuple-element.256), channel_id=1, source_target_pairs={{0,8},{1,9},{2,10},{3,11},{4,12},{5,13},{6,14},{7,15},{8,0},{9,1},... | collective-permute-start | bytes 4718600 | tf_op jit(solution)/shard_map/ppermute | solution.py:104
  362.9 20.0 %collective-permute-start.20 = (bf16[2,256,768]{2,1,0:T(8,128)(2,1)}, bf16[2,256,768]{2,1,0:T(8,128)(2,1)}, u32[]{:S(2)}, u32[]{:S(2)}) collective-permute-start(bf16[2,256,768]{2,1,0:T(8,128)(2,1)} %maximum_maximum_fusion), channel_id=1, source_target_pairs={{0,1},{1,0},{2,3},{3,2},{4,5},{5,4},{6,7},{7,6},{8,9},{9,8},{10,11... | collective-permute-start | bytes 2359304 | tf_op jit(solution)/shard_map/ppermute | solution.py:30
  363.7 49.3 %collective-permute-start.24 = (bf16[8,96,768]{2,1,0:T(8,128)(2,1)}, bf16[8,96,768]{2,1,0:T(8,128)(2,1)}, u32[]{:S(2)}, u32[]{:S(2)}) collective-permute-start(bf16[8,96,768]{2,1,0:T(8,128)(2,1)} %get-tuple-element.168), channel_id=1, source_target_pairs={{0,2},{1,5},{2,0},{3,7},{4,6},{5,1},{6,4},{7,3},{8,10},{9,13},{10,... | collective-permute-start | bytes 3538952 | tf_op jit(solution)/shard_map/ppermute | solution.py:104
  367.3 45.7 %collective-permute-start.23 = (bf16[2,96,2048]{2,1,0:T(8,128)(2,1)}, bf16[2,96,2048]{2,1,0:T(8,128)(2,1)}, u32[]{:S(2)}, u32[]{:S(2)}) collective-permute-start(bf16[2,96,2048]{2,1,0:T(8,128)(2,1)} %get-tuple-element.266), channel_id=1, source_target_pairs={{0,4},{1,3},{2,6},{3,1},{4,0},{5,7},{6,2},{7,5},{8,12},{9,11},{10,... | collective-permute-start | bytes 2359304 | tf_op jit(solution)/shard_map/ppermute | solution.py:104
  382.9 78.0 %collective-permute-start.25 = (bf16[512,1536]{1,0:T(8,128)(2,1)}, bf16[512,1536]{1,0:T(8,128)(2,1)}, u32[]{:S(2)}, u32[]{:S(2)}) collective-permute-start(bf16[512,1536]{1,0:T(8,128)(2,1)} %get-tuple-element.174), channel_id=1, source_target_pairs={{0,1},{1,0},{2,3},{3,2},{4,5},{5,4},{6,7},{7,6},{8,9},{9,8},{10,11... | collective-permute-start | bytes 4718600 | tf_op jit(solution)/shard_map/ppermute | solution.py:54
  418.1 45.8 %collective-permute-start.26 = (bf16[2,3,96,1536]{3,2,1,0:T(8,128)(2,1)}, bf16[2,3,96,1536]{3,2,1,0:T(8,128)(2,1)}, u32[]{:S(2)}, u32[]{:S(2)}) collective-permute-start(bf16[2,3,96,1536]{3,2,1,0:T(8,128)(2,1)} %get-tuple-element.254), channel_id=1, source_target_pairs={{0,4},{1,3},{2,6},{3,1},{4,0},{5,7},{6,2},{7,5},{8,12},{9,11},{10,... | collective-permute-start | bytes 5308424 | tf_op jit(solution)/shard_map/ppermute | solution.py:104
  423.6 40.3 %collective-permute-start.28 = (bf16[4,96,768]{2,1,0:T(8,128)(2,1)}, bf16[4,96,768]{2,1,0:T(8,128)(2,1)}, u32[]{:S(2)}, u32[]{:S(2)}) collective-permute-start(bf16[4,96,768]{2,1,0:T(8,128)(2,1)} %get-tuple-element.268), channel_id=1, source_target_pairs={{0,4},{1,3},{2,6},{3,1},{4,0},{5,7},{6,2},{7,5},{8,12},{9,11},{10,... | collective-permute-start | bytes 1769480 | tf_op jit(solution)/shard_map/ppermute | solution.py:104
  425.6 38.3 %collective-permute-start.27 = (bf16[1,96,2048]{2,1,0:T(8,128)(2,1)S(1)}, bf16[1,96,2048]{2,1,0:T(8,128)(2,1)}, u32[]{:S(2)}, u32[]{:S(2)}) collective-permute-start(bf16[1,96,2048]{2,1,0:T(8,128)(2,1)S(1)} %add_convert_fusion.19), channel_id=1, source_target_pairs={{0,16},{1,17},{2,18},{3,19},{4,20},{5,21},{6,22},{7,23},{8,24},{9,... | collective-permute-start | bytes 1179656 | tf_op jit(solution)/shard_map/ppermute | solution.py:104
  469.2 39.8 %collective-permute-start.32 = (bf16[1,2,96,2048]{3,2,1,0:T(8,128)(2,1)}, bf16[1,2,96,2048]{3,2,1,0:T(8,128)(2,1)}, u32[]{:S(2)}, u32[]{:S(2)}) collective-permute-start(bf16[1,2,96,2048]{3,2,1,0:T(8,128)(2,1)} %add_convert_fusion.13), channel_id=1, source_target_pairs={{0,16},{1,17},{2,18},{3,19},{4,20},{5,21},{6,22},{7,23},{8,24},{9,... | collective-permute-start | bytes 2359304 | tf_op jit(solution)/shard_map/ppermute | solution.py:104
  477.9 16.9 %collective-permute-start.31 = (bf16[16,2,96,128]{3,2,1,0:T(8,128)(2,1)}, bf16[16,2,96,128]{3,2,1,0:T(8,128)(2,1)}, u32[]{:S(2)}, u32[]{:S(2)}) collective-permute-start(bf16[16,2,96,128]{3,2,1,0:T(8,128)(2,1)} %get-tuple-element.191), channel_id=1, source_target_pairs={{0,1},{1,0},{2,3},{3,2},{4,5},{5,4},{6,7},{7,6},{8,9},{9,8},{10,11... | collective-permute-start | bytes 2359304 | tf_op jit(solution)/shard_map/ppermute | solution.py:30
  482.6 26.9 %collective-permute-start.34 = (bf16[2,96,768]{2,1,0:T(8,128)(2,1)}, bf16[2,96,768]{2,1,0:T(8,128)(2,1)}, u32[]{:S(2)}, u32[]{:S(2)}) collective-permute-start(bf16[2,96,768]{2,1,0:T(8,128)(2,1)} %get-tuple-element.281), channel_id=1, source_target_pairs={{0,8},{1,9},{2,10},{3,11},{4,12},{5,13},{6,14},{7,15},{8,0},{9,1},... | collective-permute-start | bytes 884744 | tf_op jit(solution)/shard_map/ppermute | solution.py:104
  482.6 45.0 %collective-permute-start.33 = (bf16[1,3,96,1536]{3,2,1,0:T(8,128)(2,1)}, bf16[1,3,96,1536]{3,2,1,0:T(8,128)(2,1)}, u32[]{:S(2)}, u32[]{:S(2)}) collective-permute-start(bf16[1,3,96,1536]{3,2,1,0:T(8,128)(2,1)} %get-tuple-element.263), channel_id=1, source_target_pairs={{0,8},{1,9},{2,10},{3,11},{4,12},{5,13},{6,14},{7,15},{8,0},{9,1},... | collective-permute-start | bytes 2654216 | tf_op jit(solution)/shard_map/ppermute | solution.py:104
  533.5 38.0 %collective-permute-start.36 = (bf16[1,3,96,768]{3,2,1,0:T(8,128)(2,1)S(1)}, bf16[1,3,96,768]{3,2,1,0:T(8,128)(2,1)S(1)}, u32[]{:S(2)}, u32[]{:S(2)}) collective-permute-start(bf16[1,3,96,768]{3,2,1,0:T(8,128)(2,1)S(1)} %get-tuple-element.201), channel_id=1, source_target_pairs={{0,16},{1,17},{2,18},{3,19},{4,20},{5,21},{6,22},{7,23},{8,24},{9,... | collective-permute-start | bytes 1327112 | tf_op jit(solution)/shard_map/ppermute | solution.py:104
  534.6 37.0 %collective-permute-start.37 = (bf16[1,96,768]{2,1,0:T(8,128)(2,1)S(1)}, bf16[1,96,768]{2,1,0:T(8,128)(2,1)S(1)}, u32[]{:S(2)}, u32[]{:S(2)}) collective-permute-start(bf16[1,96,768]{2,1,0:T(8,128)(2,1)S(1)} %add_convert_fusion.23), channel_id=1, source_target_pairs={{0,16},{1,17},{2,18},{3,19},{4,20},{5,21},{6,22},{7,23},{8,24},{9,... | collective-permute-start | bytes 442376 | tf_op jit(solution)/shard_map/ppermute | solution.py:104
  (73 other events, 1193.8 us)
Sparse Core Ops, SparseCore 0:
  12.9 194.2 all-gather.1

commit v15 on v9

--- a/solution.py
+++ b/solution.py
@@ -192,11 +192,17 @@
     )(text, mods)
 
 
-def advance(chains, value):
+def settle(chains, value):
     live = [c for c in chains if c.got is not None]
     value, got = lax.optimization_barrier((value, [c.got for c in live]))
     for c, g in zip(live, got):
         c.got = g
+    return value
+
+
+def advance(chains, value):
+    value = settle(chains, value)
+    for c in chains:
         c.step()
     return value
 
@@ -911,6 +917,7 @@
     text_pair = jnp.stack([grad_tk, dtv.astype(BF16)])
     pair_all = jnp.concatenate(natural(gather_rot(text_pair)), axis=-1)
     pair_all = advance([qkv_chain, wide_chain, down_chain, out_chain], pair_all)
+    pair_all, wide_chain.keep = lax.optimization_barrier((pair_all, wide_chain.keep))
     text_in = text_bwd(pair_all, w_text)
     text_in, grad_first = advance([qkv_chain], (text_in, grad_first))
     text_in = jnp.concatenate(natural(exchange_rot(text_in, 0)), axis=1)
@@ -937,7 +944,7 @@
     mods = jnp.concatenate([mods, small.reshape(dpn, SUMS, 128)], axis=1)
     outgoing = block_of(pair_all.transpose(0, 2, 1), f, 2)
     outgoing = outgoing.reshape(2, dpn, share, TEXT // n).transpose(1, 0, 2, 3)
-    mods = advance([down_chain, out_chain], mods)
+    mods = settle([wide_chain], advance([down_chain, out_chain], mods))
     pair_cols, mods, small = swap_all(outgoing, mods)
     chains = [out_chain, down_chain] if paired else [qkv_chain, out_chain, down_chain]
     if paired:

time: 572 us -> 573 us (level)
  waiting for transfers between devices: 38.8 us -> 51.2 us
  Pallas kernels: 327 us -> 317 us
    ppermute x16, waiting for transfers between devices: 27 us -> 39.3 us  [dp_swap(): return lax.ppermute(value, ('dp', 'fsdp'), pairs)]
    pallas_call x1, Pallas kernels: 48.5 us -> 38.7 us  [swap_all(): pl.pallas_call(swap_all_kernel, in_specs=[vmem] * 2, out_specs=[vmem] * 3...]
  transfers between devices with their start and end apart: 39 -> 39, of which waited for: 11 -> 12; matrix products, arithmetic and copies ran while one was open for 24% -> 24% of each run, Pallas kernels for 58% -> 56%
where the time goes in v15:
time: 573 us; the launch traced here: 568 us
  Pallas kernels  317 us (55%)
  other arithmetic  103 us (18%)
  waiting for transfers between devices  51.2 us (9%)
  local copies, waits for them, and re-layouts  30.6 us (5%)
  starting transfers between devices  25.2 us (4%)
  matrix products  21.4 us (4%)
  between operations  16.4 us (3%)
    pallas_call x1, Pallas kernels, ffn(): pl.pallas_call(functools.partial(ffn_kernel, orders), grid=(hid // bc,),...  90.3 us
    pallas_call x2, Pallas kernels, attn_backward(): pl.pallas_call(attn_bwd_kernel, grid=(blocks,), in_specs=[scalar, col, co...  68.8 us
    ppermute x16, waiting for transfers between devices, dp_swap(): return lax.ppermute(value, ('dp', 'fsdp'), pairs)  39.3 us
    pallas_call x1, Pallas kernels, swap_all(): pl.pallas_call(swap_all_kernel, in_specs=[vmem] * 2, out_specs=[vmem] * 3...  38.7 us
    convert_element_type x7, other arithmetic, step(): self.keep = add(slice(half)).astype(BF16)  32.1 us
    pallas_call x1, Pallas kernels, attn_forward(): pl.pallas_call(attn_fwd_kernel, grid=(blocks,), in_specs=[scalar, three,...  32.1 us
    ppermute x16, starting transfers between devices, dp_swap(): return lax.ppermute(value, ('dp', 'fsdp'), pairs)  20.1 us
    pallas_call x1, Pallas kernels, project_grad(): pl.pallas_call(functools.partial(project_grad_kernel, order), grid=(3,),...  18.7 us
  transfers between devices with their start and end apart: 39, of which 12 were waited for; matrix products, arithmetic and copies ran while one was open for 24% of the time, Pallas kernels for 56%

profile of v15, /device:TPU:0, one launch (start us, length us, event | category | flops | bytes accessed | tf_op | source)
XLA Modules:
  0.0 567.6 jit_solution(8609647672675583741)
XLA Ops:
  17.9 4.7 fusion.2
  23.3 16.2 %shard_map.222 = f32[2,256,1536]{2,1,0:T(8,128)} custom-call(bf16[256,2048]{1,0:T(8,128)(2,1)} %pad_maximum_fusion.2.x_ref, bf16[2048,2,1536]{2,1,0:T(2,128)(2,1)} %w_ref.5), custom_call_target="tpu_custom_call" | custom-call | tf_op jit(solution)/shard_map/pallas_call | solution.py:436
  53.4 14.4 %shard_map.221 = (bf16[1024,1536]{1,0:T(8,128)(2,1)}, f32[3,1024,768]{2,1,0:T(8,128)}, f32[8,1024]{1,0:T(8,128)}) custom-call(s32[2]{0:T(128)} %pad_add_fusion.1.id_ref, bf16[512,1536]{1,0:T(8,128)(2,1)} %bitcast.129, bf16[512,1536]{1,0:T(8,128)(2,1)} %collective-permute-done.1.xp_ref, f32[1,1536]{1,0:T(1,128)} %get-tuple-element.274.front_ref, ...), custom_call_target="tpu_custom_call" | custom-call | tf_op jit(solution)/shard_map/pallas_call | solution.py:592
  70.6 32.1 %shard_map.223 = (bf16[1024,768]{1,0:T(8,128)(2,1)}, bf16[1024,768]{1,0:T(8,128)(2,1)}, bf16[1024,768]{1,0:T(8,128)(2,1)}, bf16[1024,768]{1,0:T(8,128)(2,1)}, f3...) custom-call(s32[1]{0:T(128)S(6)} %copy.48.len_ref, ...), custom_call_target="tpu_custom_call" | custom-call | tf_op jit(solution)/shard_map/pallas_call | solution.py:379
  120.4 90.3 %shard_map.224 = (bf16[8,2,96,2048]{3,2,1,0:T(8,128)(2,1)}, bf16[8,2,96,2048]{3,2,1,0:T(8,128)(2,1)}, bf16[8,96,2048]{2,1,0:T(8,128)(2,1)}, bf16[8,96,2048]{2,1,...) custom-call(s32[2]{0:T(128)} %pad_add_fusion.1.id_ref, ...), custom_call_target="tpu_custom_call" | custom-call | tf_op jit(solution)/shard_map/pallas_call | solution.py:535
  217.3 4.3 multiply_reduce_fusion
  221.6 5.8 %fusion.7 = (f32[1536]{0:T(1024)S(1)}, bf16[1,512,1536]{2,1,0:T(8,128)(2,1)}, f32[1536]{0:T(1024)S(1)}, f32[512,1536]{1,0:T(8,128)S(1)}) fusion(f32[512,1536]{1,0:T(8,128)} %get-tuple-element.115, bf16[512,1536]{1,0:T(8,128)(2,1)S(1)} %collective-permute-done.11, bf16[1,512,1536]{2,1,0:T(8,128)(2,1)} %param.19, f32[512,1536]{1,0:T(8,128)S(1)} %copy-done.1, ...), kind=kLoop, calls=%fused_computation.18 | loop fusion | flops 16512000 | bytes 23627776 | tf_op jit(solution)/shard_map/reduce_sum | solution.py:854
  232.5 9.6 %shard_map.225 = (f32[1024,768]{1,0:T(8,128)}, bf16[8,96,768]{2,1,0:T(8,128)(2,1)}, bf16[8,96,768]{2,1,0:T(8,128)(2,1)}) custom-call(s32[2]{0:T(128)} %pad_add_fusion.1.id_ref, bf16[512,1536]{1,0:T(8,128)(2,1)} %copy-done.18, bf16[512,1536]{1,0:T(8,128)(2,1)} %collective-permute-done.13.refs_1_, bf16[768,1536]{1,0:T(8,128)(2,1)} %refs_2_.1, ...), custom_call_target="tpu_custom_call" | custom-call | tf_op jit(solution)/shard_map/pallas_call | solution.py:720
  242.1 44.5 %shard_map.226 = (f32[3,1024,512]{2,1,0:T(8,128)}, f32[256,512]{1,0:T(8,128)}, f32[256,512]{1,0:T(8,128)}, f32[8,1024]{1,0:T(8,128)}, f32[1,512]{1,0:T(1,128)}, /*index=5*/f32[1,512]{1,0:T(1,128)}, f32[1,512]{1,0:T(1,128)}) custom-call(s32[1]{0:T(128)S(6)} %copy.48.len_ref, bf16[1024,768]{1,0:T(8,128)(2,1)} %get-tuple-element.119.q_ref, ...), custom_call_target="tpu_custom_call" | custom-call | tf_op jit(solution)/shard_map/pallas_call | solution.py:394
  286.7 8.1 %add_convert_fusion = (bf16[4,2,96,2048]{3,2,1,0:T(8,128)(2,1)}, bf16[4,2,96,2048]{3,2,1,0:T(8,128)(2,1)}) fusion(bf16[8,2,96,2048]{3,2,1,0:T(8,128)(2,1)} %collective-permute-done.14, bf16[8,2,96,2048]{3,2,1,0:T(8,128)(2,1)} %get-tuple-element.154), kind=kLoop, calls=%fused_computation.4 | loop fusion | flops 12582912 | bytes 18874368 | tf_op jit(solution)/shard_map/convert_element_type | solution.py:130
  297.0 6.1 %add_convert_fusion.5 = (bf16[4,96,2048]{2,1,0:T(8,128)(2,1)}, bf16[4,96,2048]{2,1,0:T(8,128)(2,1)}) fusion(bf16[8,96,2048]{2,1,0:T(8,128)(2,1)} %collective-permute-done.15, bf16[8,96,2048]{2,1,0:T(8,128)(2,1)} %get-tuple-element.156), kind=kLoop, calls=%fused_computation.34 | loop fusion | flops 6291456 | bytes 9437184 | tf_op jit(solution)/shard_map/convert_element_type | solution.py:130
  306.4 24.3 %shard_map.227 = (f32[3,1024,256]{2,1,0:T(8,128)}, f32[256,256]{1,0:T(8,128)}, f32[256,256]{1,0:T(8,128)}, f32[8,1024]{1,0:T(8,128)}, f32[1,256]{1,0:T(1,128)}, /*index=5*/f32[1,256]{1,0:T(1,128)}, f32[1,256]{1,0:T(1,128)}) custom-call(s32[1]{0:T(128)S(6)} %copy.48.len_ref, bf16[1024,768]{1,0:T(8,128)(2,1)} %get-tuple-element.119.q_ref, ...), custom_call_target="tpu_custom_call" | custom-call | tf_op jit(solution)/shard_map/pallas_call | solution.py:394
  334.0 18.7 %shard_map.228 = (bf16[4,3,96,1536]{3,2,1,0:T(8,128)(2,1)}, bf16[4,3,96,1536]{3,2,1,0:T(8,128)(2,1)}, bf16[3,1024,768]{2,1,0:T(8,128)(2,1)}) custom-call(s32[2]{0:T(128)} %pad_add_fusion.1.id_ref, f32[3,1024,512]{2,1,0:T(8,128)} %get-tuple-element.150.da_ref, f32[3,1024,256]{2,1,0:T(8,128)} %get-tuple-element.151.db_ref, ...), custom_call_target="tpu_custom_call" | custom-call | tf_op jit(solution)/shard_map/pallas_call | solution.py:639
  353.3 7.7 %collective-permute-done.19 = bf16[8,96,768]{2,1,0:T(8,128)(2,1)} collective-permute-done((bf16[8,96,768]{2,1,0:T(8,128)(2,1)}, bf16[8,96,768]{2,1,0:T(8,128)(2,1)}, u32[]{:S(2)}, u32[]{:S(2)}) %collective-permute-start.19) | collective-permute-done | bytes 1179680 | tf_op jit(solution)/shard_map/ppermute | solution.py:104
  365.4 5.0 add_convert_fusion.4
  388.3 13.7 %shard_map.230 = (f32[512,1536]{1,0:T(8,128)}, bf16[512,1536]{1,0:T(8,128)(2,1)}) custom-call(s32[2]{0:T(128)} %pad_add_fusion.1.id_ref, bf16[3,1024,768]{2,1,0:T(8,128)(2,1)} %get-tuple-element.171.g_ref, bf16[3,768,1536]{2,1,0:T(8,128)(2,1)} %bitcast.128, bf16[3,768,768]{2,1,0:T(8,128)(2,1)} %collective-permute-done.2.got_ref), custom_call_target="tpu_custom_call" | custom-call | tf_op jit(solution)/shard_map/pallas_call | solution.py:685
  404.9 8.7 %collective-permute-done.22 = bf16[4,3,96,1536]{3,2,1,0:T(8,128)(2,1)} collective-permute-done((bf16[4,3,96,1536]{3,2,1,0:T(8,128)(2,1)}, bf16[4,3,96,1536]{3,2,1,0:T(8,128)(2,1)}, u32[]{:S(2)}, u32[]{:S(2)}) %collective-permute-start.22) | collective-permute-done | bytes 3538976 | tf_op jit(solution)/shard_map/ppermute | solution.py:104
  417.1 5.0 add_convert_fusion.2
  431.1 14.7 %shard_map.229 = bf16[256,2048]{1,0:T(8,128)(2,1)} custom-call(bf16[2,256,1536]{2,1,0:T(8,128)(2,1)} %pad_maximum_fusion.1.g_ref, bf16[2048,2,1536]{2,1,0:T(2,128)(2,1)} %w_ref.5), custom_call_target="tpu_custom_call" | custom-call | tf_op jit(solution)/shard_map/pallas_call | solution.py:455
  463.3 4.2 fusion.15
  470.5 12.4 %collective-permute-done.32 = bf16[1,2,96,2048]{3,2,1,0:T(8,128)(2,1)} collective-permute-done((bf16[1,2,96,2048]{3,2,1,0:T(8,128)(2,1)}, bf16[1,2,96,2048]{3,2,1,0:T(8,128)(2,1)}, u32[]{:S(2)}, u32[]{:S(2)}) %collective-permute-start.32) | collective-permute-done | bytes 786464 | tf_op jit(solution)/shard_map/ppermute | solution.py:104
  482.9 38.7 %shard_map.231 = (bf16[16,2,96,128]{3,2,1,0:T(8,128)(2,1)}, f32[16,8,128]{2,1,0:T(8,128)}, f32[16,8,128]{2,1,0:T(8,128)}) custom-call(bf16[16,2,96,128]{3,2,1,0:T(8,128)(2,1)} %bitcast.133, f32[16,8,128]{2,1,0:T(8,128)} %select_maximum_fusion.mod_ref), custom_call_target="tpu_custom_call" | custom-call | tf_op jit(solution)/shard_map/pallas_call | solution.py:179
  540.2 8.7 %fusion = f32[2048,2,96]{0,2,1:T(8,128)} fusion(bf16[2,96,4096]{2,1,0:T(8,128)(2,1)S(1)} %bitcast.136, bf16[4096,2048]{1,0:T(8,128)(2,1)} %all-gather.2.cloned.1.call-done), kind=kOutput, calls=%fused_computation | convolution fusion | flops 3221225472 | bytes 19922944 | tf_op jit(solution)/shard_map/dot_general | solution.py:25
  549.0 10.5 %collective-permute-done.37 = bf16[1,3,96,768]{3,2,1,0:T(8,128)(2,1)S(1)} collective-permute-done((bf16[1,3,96,768]{3,2,1,0:T(8,128)(2,1)S(1)}, bf16[1,3,96,768]{3,2,1,0:T(8,128)(2,1)S(1)}, u32[]{:S(2)}, u32[]{:S(2)}) %collective-permute-start.37) | collective-permute-done | bytes 442400 | tf_op jit(solution)/shard_map/ppermute | solution.py:104
  (301 shorter events, 142.7 us)
Async XLA Ops:
  7.2 206.5 %all-gather.2.cloned.1.call-start = ((), (), s32[]{:S(2)}) async-start(), calls=%async_computation | async-start | bytes 17825792 | tf_op jit(solution)/shard_map/all_gather | solution.py:795
  16.7 36.6 %collective-permute-start.2 = (bf16[3,768,768]{2,1,0:T(8,128)(2,1)}, bf16[3,768,768]{2,1,0:T(8,128)(2,1)}, u32[]{:S(2)}, u32[]{:S(2)}) collective-permute-start(bf16[3,768,768]{2,1,0:T(8,128)(2,1)} %dynamic-slice_bitcast_fusion), channel_id=1, source_target_pairs={{0,1},{1,0},{2,3},{3,2},{4,5},{5,4},{6,7},{7,6},{8,9},{9,8},{10,11... | collective-permute-start | bytes 10616840 | tf_op jit(solution)/shard_map/ppermute | solution.py:30
  22.5 26.8 %collective-permute-start = (f32[4,1536]{1,0:T(4,128)S(1)}, f32[4,1536]{1,0:T(4,128)S(1)}, u32[]{:S(2)}, u32[]{:S(2)}) collective-permute-start(f32[4,1536]{1,0:T(4,128)S(1)} %bitcast.140), channel_id=1, source_target_pairs={{0,1},{1,0},{2,3},{3,2},{4,5},{5,4},{6,7},{7,6},{8,9},{9,8},{10,11... | collective-permute-start | bytes 73736 | tf_op jit(solution)/shard_map/ppermute | solution.py:30
  22.8 30.6 %collective-permute-start.1 = (bf16[512,1536]{1,0:T(8,128)(2,1)S(1)}, bf16[512,1536]{1,0:T(8,128)(2,1)}, u32[]{:S(2)}, u32[]{:S(2)}) collective-permute-start(bf16[512,1536]{1,0:T(8,128)(2,1)S(1)} %bitcast.130), channel_id=1, source_target_pairs={{0,1},{1,0},{2,3},{3,2},{4,5},{5,4},{6,7},{7,6},{8,9},{9,8},{10,11... | collective-permute-start | bytes 4718600 | tf_op jit(solution)/shard_map/ppermute | solution.py:30
  23.1 23.0 %collective-permute-start.4 = (s32[2,512]{1,0:T(2,128)S(1)}, s32[2,512]{1,0:T(2,128)S(1)}, u32[]{:S(2)}, u32[]{:S(2)}) collective-permute-start(s32[2,512]{1,0:T(2,128)S(1)} %bitcast.153), channel_id=1, source_target_pairs={{0,1},{1,0},{2,3},{3,2},{4,5},{5,4},{6,7},{7,6},{8,9},{9,8},{10,11... | collective-permute-start | bytes 12296 | tf_op jit(solution)/shard_map/ppermute | solution.py:30
  210.6 76.0 %collective-permute-start.14 = (bf16[8,2,96,2048]{3,2,1,0:T(8,128)(2,1)}, bf16[8,2,96,2048]{3,2,1,0:T(8,128)(2,1)}, u32[]{:S(2)}, u32[]{:S(2)}) collective-permute-start(bf16[8,2,96,2048]{3,2,1,0:T(8,128)(2,1)} %get-tuple-element.141), channel_id=1, source_target_pairs={{0,2},{1,5},{2,0},{3,7},{4,6},{5,1},{6,4},{7,3},{8,10},{9,13},{10,... | collective-permute-start | bytes 18874376 | tf_op jit(solution)/shard_map/ppermute | solution.py:104
  214.2 72.5 %collective-permute-start.15 = (bf16[8,96,2048]{2,1,0:T(8,128)(2,1)}, bf16[8,96,2048]{2,1,0:T(8,128)(2,1)}, u32[]{:S(2)}, u32[]{:S(2)}) collective-permute-start(bf16[8,96,2048]{2,1,0:T(8,128)(2,1)} %get-tuple-element.142), channel_id=1, source_target_pairs={{0,8},{1,9},{2,10},{3,11},{4,12},{5,13},{6,14},{7,15},{8,0},{9,1},... | collective-permute-start | bytes 9437192 | tf_op jit(solution)/shard_map/ppermute | solution.py:104
  294.8 66.2 %collective-permute-start.17 = (bf16[4,2,96,2048]{3,2,1,0:T(8,128)(2,1)}, bf16[4,2,96,2048]{3,2,1,0:T(8,128)(2,1)}, u32[]{:S(2)}, u32[]{:S(2)}) collective-permute-start(bf16[4,2,96,2048]{3,2,1,0:T(8,128)(2,1)} %get-tuple-element.246), channel_id=1, source_target_pairs={{0,4},{1,3},{2,6},{3,1},{4,0},{5,7},{6,2},{7,5},{8,12},{9,11},{10,... | collective-permute-start | bytes 9437192 | tf_op jit(solution)/shard_map/ppermute | solution.py:104
  303.1 57.9 %collective-permute-start.18 = (bf16[4,96,2048]{2,1,0:T(8,128)(2,1)}, bf16[4,96,2048]{2,1,0:T(8,128)(2,1)}, u32[]{:S(2)}, u32[]{:S(2)}) collective-permute-start(bf16[4,96,2048]{2,1,0:T(8,128)(2,1)} %get-tuple-element.252), channel_id=1, source_target_pairs={{0,2},{1,5},{2,0},{3,7},{4,6},{5,1},{6,4},{7,3},{8,10},{9,13},{10,... | collective-permute-start | bytes 4718600 | tf_op jit(solution)/shard_map/ppermute | solution.py:104
  304.3 56.7 %collective-permute-start.19 = (bf16[8,96,768]{2,1,0:T(8,128)(2,1)}, bf16[8,96,768]{2,1,0:T(8,128)(2,1)}, u32[]{:S(2)}, u32[]{:S(2)}) collective-permute-start(bf16[8,96,768]{2,1,0:T(8,128)(2,1)} %get-tuple-element.158), channel_id=1, source_target_pairs={{0,2},{1,5},{2,0},{3,7},{4,6},{5,1},{6,4},{7,3},{8,10},{9,13},{10,... | collective-permute-start | bytes 3538952 | tf_op jit(solution)/shard_map/ppermute | solution.py:104
  352.7 60.9 %collective-permute-start.22 = (bf16[4,3,96,1536]{3,2,1,0:T(8,128)(2,1)}, bf16[4,3,96,1536]{3,2,1,0:T(8,128)(2,1)}, u32[]{:S(2)}, u32[]{:S(2)}) collective-permute-start(bf16[4,3,96,1536]{3,2,1,0:T(8,128)(2,1)} %get-tuple-element.163), channel_id=1, source_target_pairs={{0,2},{1,5},{2,0},{3,7},{4,6},{5,1},{6,4},{7,3},{8,10},{9,13},{10,... | collective-permute-start | bytes 10616840 | tf_op jit(solution)/shard_map/ppermute | solution.py:104
  363.9 49.8 %collective-permute-start.25 = (bf16[4,96,768]{2,1,0:T(8,128)(2,1)}, bf16[4,96,768]{2,1,0:T(8,128)(2,1)}, u32[]{:S(2)}, u32[]{:S(2)}) collective-permute-start(bf16[4,96,768]{2,1,0:T(8,128)(2,1)} %get-tuple-element.262), channel_id=1, source_target_pairs={{0,4},{1,3},{2,6},{3,1},{4,0},{5,7},{6,2},{7,5},{8,12},{9,11},{10,... | collective-permute-start | bytes 1769480 | tf_op jit(solution)/shard_map/ppermute | solution.py:104
  370.4 43.2 %collective-permute-start.23 = (bf16[2,2,96,2048]{3,2,1,0:T(8,128)(2,1)}, bf16[2,2,96,2048]{3,2,1,0:T(8,128)(2,1)}, u32[]{:S(2)}, u32[]{:S(2)}) collective-permute-start(bf16[2,2,96,2048]{3,2,1,0:T(8,128)(2,1)} %get-tuple-element.250), channel_id=1, source_target_pairs={{0,8},{1,9},{2,10},{3,11},{4,12},{5,13},{6,14},{7,15},{8,0},{9,1},... | collective-permute-start | bytes 4718600 | tf_op jit(solution)/shard_map/ppermute | solution.py:104
  375.9 26.1 %collective-permute-start.21 = (bf16[2,256,768]{2,1,0:T(8,128)(2,1)}, bf16[2,256,768]{2,1,0:T(8,128)(2,1)}, u32[]{:S(2)}, u32[]{:S(2)}) collective-permute-start(bf16[2,256,768]{2,1,0:T(8,128)(2,1)} %maximum_maximum_fusion), channel_id=1, source_target_pairs={{0,1},{1,0},{2,3},{3,2},{4,5},{5,4},{6,7},{7,6},{8,9},{9,8},{10,11... | collective-permute-start | bytes 2359304 | tf_op jit(solution)/shard_map/ppermute | solution.py:30
  379.2 34.5 %collective-permute-start.24 = (bf16[2,96,2048]{2,1,0:T(8,128)(2,1)}, bf16[2,96,2048]{2,1,0:T(8,128)(2,1)}, u32[]{:S(2)}, u32[]{:S(2)}) collective-permute-start(bf16[2,96,2048]{2,1,0:T(8,128)(2,1)} %get-tuple-element.260), channel_id=1, source_target_pairs={{0,4},{1,3},{2,6},{3,1},{4,0},{5,7},{6,2},{7,5},{8,12},{9,11},{10,... | collective-permute-start | bytes 2359304 | tf_op jit(solution)/shard_map/ppermute | solution.py:104
  402.0 50.7 %collective-permute-start.26 = (bf16[512,1536]{1,0:T(8,128)(2,1)}, bf16[512,1536]{1,0:T(8,128)(2,1)}, u32[]{:S(2)}, u32[]{:S(2)}) collective-permute-start(bf16[512,1536]{1,0:T(8,128)(2,1)} %get-tuple-element.173), channel_id=1, source_target_pairs={{0,1},{1,0},{2,3},{3,2},{4,5},{5,4},{6,7},{7,6},{8,9},{9,8},{10,11... | collective-permute-start | bytes 4718600 | tf_op jit(solution)/shard_map/ppermute | solution.py:54
  415.6 53.9 %collective-permute-start.31 = (bf16[2,96,768]{2,1,0:T(8,128)(2,1)}, bf16[2,96,768]{2,1,0:T(8,128)(2,1)}, u32[]{:S(2)}, u32[]{:S(2)}) collective-permute-start(bf16[2,96,768]{2,1,0:T(8,128)(2,1)} %get-tuple-element.273), channel_id=1, source_target_pairs={{0,8},{1,9},{2,10},{3,11},{4,12},{5,13},{6,14},{7,15},{8,0},{9,1},... | collective-permute-start | bytes 884744 | tf_op jit(solution)/shard_map/ppermute | solution.py:104
  422.0 33.6 %collective-permute-start.27 = (bf16[2,3,96,1536]{3,2,1,0:T(8,128)(2,1)}, bf16[2,3,96,1536]{3,2,1,0:T(8,128)(2,1)}, u32[]{:S(2)}, u32[]{:S(2)}) collective-permute-start(bf16[2,3,96,1536]{3,2,1,0:T(8,128)(2,1)} %get-tuple-element.248), channel_id=1, source_target_pairs={{0,4},{1,3},{2,6},{3,1},{4,0},{5,7},{6,2},{7,5},{8,12},{9,11},{10,... | collective-permute-start | bytes 5308424 | tf_op jit(solution)/shard_map/ppermute | solution.py:104
  425.4 44.1 %collective-permute-start.30 = (bf16[1,96,2048]{2,1,0:T(8,128)(2,1)}, bf16[1,96,2048]{2,1,0:T(8,128)(2,1)}, u32[]{:S(2)}, u32[]{:S(2)}) collective-permute-start(bf16[1,96,2048]{2,1,0:T(8,128)(2,1)} %add_convert_fusion.19), channel_id=1, source_target_pairs={{0,16},{1,17},{2,18},{3,19},{4,20},{5,21},{6,22},{7,23},{8,24},{9,... | collective-permute-start | bytes 1179656 | tf_op jit(solution)/shard_map/ppermute | solution.py:104
  445.9 37.0 %collective-permute-start.32 = (bf16[1,2,96,2048]{3,2,1,0:T(8,128)(2,1)}, bf16[1,2,96,2048]{3,2,1,0:T(8,128)(2,1)}, u32[]{:S(2)}, u32[]{:S(2)}) collective-permute-start(bf16[1,2,96,2048]{3,2,1,0:T(8,128)(2,1)} %get-tuple-element.257), channel_id=1, source_target_pairs={{0,16},{1,17},{2,18},{3,19},{4,20},{5,21},{6,22},{7,23},{8,24},{9,... | collective-permute-start | bytes 2359304 | tf_op jit(solution)/shard_map/ppermute | solution.py:104
  462.0 63.1 %collective-permute-start.33 = (bf16[1,3,96,1536]{3,2,1,0:T(8,128)(2,1)}, bf16[1,3,96,1536]{3,2,1,0:T(8,128)(2,1)}, u32[]{:S(2)}, u32[]{:S(2)}) collective-permute-start(bf16[1,3,96,1536]{3,2,1,0:T(8,128)(2,1)} %add_convert_fusion.11), channel_id=1, source_target_pairs={{0,8},{1,9},{2,10},{3,11},{4,12},{5,13},{6,14},{7,15},{8,0},{9,1},... | collective-permute-start | bytes 2654216 | tf_op jit(solution)/shard_map/ppermute | solution.py:104
  467.6 56.3 %collective-permute-start.28 = (bf16[128,2048]{1,0:T(8,128)(2,1)S(1)}, bf16[128,2048]{1,0:T(8,128)(2,1)S(1)}, u32[]{:S(2)}, u32[]{:S(2)}) collective-permute-start(bf16[128,2048]{1,0:T(8,128)(2,1)S(1)} %constant_dynamic-slice_fusion.1), channel_id=1, source_target_pairs={{0,1},{1,0},{2,3},{3,2},{4,5},{5,4},{6,7},{7,6},{8,9},{9,8},{10,11... | collective-permute-start | bytes 1572872 | tf_op jit(solution)/shard_map/ppermute | solution.py:30
  482.9 45.2 %collective-permute-start.34 = (bf16[1,96,768]{2,1,0:T(8,128)(2,1)S(1)}, bf16[1,96,768]{2,1,0:T(8,128)(2,1)}, u32[]{:S(2)}, u32[]{:S(2)}) collective-permute-start(bf16[1,96,768]{2,1,0:T(8,128)(2,1)S(1)} %add_convert_fusion.23), channel_id=1, source_target_pairs={{0,16},{1,17},{2,18},{3,19},{4,20},{5,21},{6,22},{7,23},{8,24},{9,... | collective-permute-start | bytes 442376 | tf_op jit(solution)/shard_map/ppermute | solution.py:104
  537.2 22.3 %collective-permute-start.37 = (bf16[1,3,96,768]{3,2,1,0:T(8,128)(2,1)S(1)}, bf16[1,3,96,768]{3,2,1,0:T(8,128)(2,1)S(1)}, u32[]{:S(2)}, u32[]{:S(2)}) collective-permute-start(bf16[1,3,96,768]{3,2,1,0:T(8,128)(2,1)S(1)} %fusion.25), channel_id=1, source_target_pairs={{0,16},{1,17},{2,18},{3,19},{4,20},{5,21},{6,22},{7,23},{8,24},{9,... | collective-permute-start | bytes 1327112 | tf_op jit(solution)/shard_map/ppermute | solution.py:104
  (67 other events, 1164.0 us)
Sparse Core Ops, SparseCore 0:
  12.9 194.2 all-gather.1
